TPU v7x, 128 devices: a whole 4x4x4 slice. The times are simulated.
128 devices in a mesh: row: 8 (over x, core), col: 16 (over y, z).
Axes of the slice: x: 4, y: 4, z: 4, core: 2. Of those that a mesh axis runs over, the one named last changes fastest.
Arguments:
- left_factor: bfloat16 [4, 2048, 24, 4096], P(None, 'row', None, 'col'), may hold values from -0.01953125 to 0.01953125
- prev_solution: bfloat16 [24, 4096, 512], P('row', 'col'), may hold values from -6 to 6
- cross: bfloat16 [4, 2048, 512], P(None, 'row'), may hold values from -6 to 6
- inverses: bfloat16 [2, 2, 2048, 1, 4096], P(None, None, 'row', None, 'col'), as said below
- coupling: bfloat16 [2, 2048, 1, 4096], P(None, 'row', None, 'col'), may hold values from -0.09375 to 0.09375
- prior_cov: float32 [512, 512], P('col'), may hold values from -6 to 6
Outputs:
- solved: bfloat16 [4, 2048, 512], P(None, 'row')
- pred_cov: float32 [512, 512], P('col')
Inputs may be any that keep to these rules, and one draw needn't show every extreme that they name: Each block of inverses is lower triangular in natural order, with diagonal entries from 0.5 to 1.5.
All inputs are finite; a program needn't handle non-finite values.
Results may differ from a plain program's by a relative error of at most 0.0056.
Values may be sent and summed in bfloat16 or wider, within the bound.
No kernel may reach another device: no remote copies, remote signals or barrier semaphores. Data moves between devices by JAX's collectives and lax.ppermute only.
A program may use at most 64 MiB of HBM per device.

v0:
```python
import jax
import jax.numpy as jnp
from jax import lax
from jax.sharding import PartitionSpec as P

S = 8192


def from_root(shard, axis, root):
    return lax.dynamic_index_in_dim(lax.all_gather(shard, axis), root, 0, keepdims=False)


def filled_up(lines, peers):
    spare = -len(lines) % peers
    return jnp.pad(lines, [(0, spare)] + [(0, 0)] * (lines.ndim - 1))


def in_order(blocks, dim):
    shape = list(blocks.shape[1:])
    shape[dim] *= blocks.shape[0]
    return jnp.moveaxis(blocks, 0, dim).reshape(shape)


def from_everyone(shard, axis):
    peers = lax.axis_size(axis)
    return lax.all_to_all(
        jnp.broadcast_to(shard[None], (peers, *shard.shape)), axis, 0, 0, tiled=True
    )


def gather_directly(shard, axis, dim):
    return in_order(from_everyone(shard, axis), dim)


def cut_along(shard, dim, peers):
    shape = shard.shape
    blocks = shard.reshape(*shape[:dim], peers, shape[dim] // peers, *shape[dim + 1 :])
    return jnp.moveaxis(blocks, dim, 0)


def sent_and_summed(shard, axis, dim):
    blocks = cut_along(shard, dim, lax.axis_size(axis))
    arrived = lax.all_to_all(blocks, axis, split_axis=0, concat_axis=0, tiled=True)
    return arrived.sum(axis=0)


def sum_by_parts(shard, axes):
    lines = shard.reshape(-1, shard.shape[-1])
    padded = filled_up(lines, lax.axis_size(axes))
    whole = gather_directly(sent_and_summed(padded, axes, 0), axes, 0)
    return lax.slice_in_dim(whole, 0, len(lines)).reshape(shard.shape)


def over_copies(shard, axis):
    return from_everyone(shard, axis).astype(jnp.float32).sum(axis=0)


def apply_block(matrix, values):
    return jnp.einsum("atbu,bum->atm", matrix, values, preferred_element_type=jnp.float32)


def spread_rows(values):
    n_row = lax.axis_size("row")
    n_col = lax.axis_size("col")
    col_id = lax.axis_index("col")
    rounds, tile, sites = values.shape
    group = n_col // n_row
    grouped = values.reshape(rounds // group, group, tile, sites)
    picked = lax.dynamic_index_in_dim(grouped, col_id // n_row, 1, keepdims=False)
    return from_root(picked, "row", col_id % n_row)


def column_sum(values):
    return sum_by_parts(values, "col")


def solve_rounded(values):
    return sum_by_parts(values, "col").astype(jnp.bfloat16)


def outer_rows(solution):
    share = solution.shape[2] // lax.axis_size("col")
    own = lax.dynamic_slice_in_dim(solution, lax.axis_index("col") * share, share, 2)
    return jnp.einsum("atm,atn->mn", own, solution, preferred_element_type=jnp.float32)


def body(left_factor, prev_solution, cross, inverses, coupling, prior_cov):
    half = coupling.shape[0]
    pre = jnp.einsum(
        "atbu,bum->atm",
        left_factor,
        lax.all_gather(prev_solution, "row", axis=0, tiled=True),
        preferred_element_type=jnp.float32,
    )
    cross_first = cross[:half].astype(jnp.float32)
    cross_second = cross[half:].astype(jnp.float32)
    pre_first = sum_by_parts(pre[:half], "col")
    first_rhs = (cross_first - pre_first).astype(jnp.bfloat16)
    solved_first = solve_rounded(apply_block(inverses[0], spread_rows(first_rhs)))
    linked = column_sum(pre[half:] + apply_block(coupling, spread_rows(solved_first)))
    second_rhs = (cross_second - linked).astype(jnp.bfloat16)
    solved_second = solve_rounded(apply_block(inverses[1], spread_rows(second_rhs)))
    solved_all = jnp.concatenate([solved_first, solved_second], axis=0)
    outer_total = over_copies(outer_rows(solved_all).astype(jnp.bfloat16), "row").astype(
        jnp.float32
    )
    pred_cov = prior_cov - outer_total / S
    return (solved_all, pred_cov)


def solution(mesh):
    placed = (
        P(None, "row", None, "col"),
        P("row", "col", None),
        P(None, "row", None),
        P(None, None, "row", None, "col"),
        P(None, "row", None, "col"),
        P("col", None),
    )
    return jax.shard_map(
        body,
        mesh=mesh,
        in_specs=placed,
        out_specs=(P(None, "row", None), P("col", None)),
        check_vma=False,
    )
```

profile of v0, /device:TPU:0, one launch (start us, length us, event | category | flops | bytes accessed | tf_op | source)
XLA Modules:
  0.0 326.3 jit_solution(15073894378876235162)
XLA Ops:
  7.2 0.7 all-gather.8.cloned.1.call-update
  7.9 45.2 %all-gather.8.cloned.1.call-done = bf16[24,256,512]{2,1,0:T(8,128)(2,1)} async-done(((bf16[3,256,512]{2,1,0:T(8,128)(2,1)}), bf16[24,256,512]{2,1,0:T(8,128)(2,1)}) %all-gather.8.cloned.1.call-update) | async-done | bytes 6291472 | tf_op jit(solution)/shard_map/all_gather | solution.py:92
  53.1 14.2 %fusion.3 = f32[4,256,512]{2,1,0:T(8,128)S(1)} fusion(bf16[24,256,512]{2,1,0:T(8,128)(2,1)} %all-gather.8.cloned.1.call-done, bf16[4,256,24,256]{3,2,1,0:T(8,128)(2,1)} %param.6), kind=kOutput, calls=%fused_computation.3 | convolution fusion | flops 6442450944 | bytes 20971520 | tf_op jit(solution)/shard_map/atbu,bum->atm/dot_general | solution.py:89
  67.3 24.3 %all_to_all.45 = f32[16,32,512]{2,1,0:T(8,128)S(1)} all-to-all(f32[16,32,512]{2,1,0:T(8,128)S(1)} %bitcast.52), channel_id=1, replica_groups=mesh['row'=8,'col'=16] {'col'}, dimensions={0} | all-to-all | bytes 2097152 | tf_op jit(solution)/shard_map/all_to_all | solution.py:43
  91.7 1.1 broadcast_in_dim.10
  92.8 3.7 %all-to-all-start.1 = ((f32[16,32,512]{2,1,0:T(8,128)}), f32[16,32,512]{2,1,0:T(8,128)S(1)}, u32[]{:S(2)}, u32[]{:S(2)}) async-start(f32[16,32,512]{2,1,0:T(8,128)} %broadcast_in_dim.10), calls=%async_computation.1 | async-start | bytes 2097152 | tf_op jit(solution)/shard_map/all_to_all | solution.py:26
  96.5 2.3 fusion.26
  98.8 13.9 %all-to-all-done.1 = f32[16,32,512]{2,1,0:T(8,128)S(1)} async-done(((f32[16,32,512]{2,1,0:T(8,128)}), f32[16,32,512]{2,1,0:T(8,128)S(1)}, u32[]{:S(2)}, u32[]{:S(2)}) %all-to-all-start.1) | async-done | bytes 1048608 | tf_op jit(solution)/shard_map/all_to_all | solution.py:26
  112.7 1.7 fusion.11
  114.6 1.8 fusion.27
  116.3 20.0 %all-gather.10.cloned.1.call-done = bf16[8,256,512]{2,1,0:T(8,128)(2,1)} async-done(((bf16[1,256,512]{2,1,0:T(8,128)(2,1)}), bf16[8,256,512]{2,1,0:T(8,128)(2,1)}) %all-gather.10.cloned.1.call-update) | async-done | bytes 2097168 | tf_op jit(solution)/shard_map/all_gather | solution.py:10
  136.3 1.2 convolution_bitcast_fusion.2
  137.5 24.3 %all_to_all.46 = f32[16,32,512]{2,1,0:T(8,128)S(1)} all-to-all(f32[16,32,512]{2,1,0:T(8,128)S(1)} %convolution_bitcast_fusion.2), channel_id=1, replica_groups=mesh['row'=8,'col'=16] {'col'}, dimensions={0} | all-to-all | bytes 2097152 | tf_op jit(solution)/shard_map/all_to_all | solution.py:43
  161.8 0.1 reduce_sum.46
  162.0 14.0 %all_to_all.47 = bf16[16,32,512]{2,1,0:T(8,128)(2,1)S(1)} all-to-all(bf16[16,32,512]{2,1,0:T(8,128)(2,1)S(1)} %broadcast_in_dim.11), channel_id=1, replica_groups=mesh['row'=8,'col'=16] {'col'}, dimensions={0} | all-to-all | bytes 1048576 | tf_op jit(solution)/shard_map/all_to_all | solution.py:26
  176.0 0.7 constant_dynamic-slice_fusion
  176.8 22.0 %all-gather.12.cloned.1.call-done = bf16[8,256,512]{2,1,0:T(8,128)(2,1)} async-done(((bf16[1,256,512]{2,1,0:T(8,128)(2,1)}), bf16[8,256,512]{2,1,0:T(8,128)(2,1)}) %all-gather.12.cloned.1.call-update) | async-done | bytes 2097168 | tf_op jit(solution)/shard_map/all_gather | solution.py:10
  198.8 1.2 fusion.8
  200.0 24.3 %all_to_all.48 = f32[16,32,512]{2,1,0:T(8,128)S(1)} all-to-all(f32[16,32,512]{2,1,0:T(8,128)S(1)} %bitcast.51), channel_id=1, replica_groups=mesh['row'=8,'col'=16] {'col'}, dimensions={0} | all-to-all | bytes 2097152 | tf_op jit(solution)/shard_map/all_to_all | solution.py:43
  224.4 0.1 broadcast_in_dim.12
  224.5 19.8 %all_to_all.49 = f32[16,32,512]{2,1,0:T(8,128)S(1)} all-to-all(f32[16,32,512]{2,1,0:T(8,128)S(1)} %broadcast_in_dim.12), channel_id=1, replica_groups=mesh['row'=8,'col'=16] {'col'}, dimensions={0} | all-to-all | bytes 2097152 | tf_op jit(solution)/shard_map/all_to_all | solution.py:26
  244.3 0.8 fusion.10
  245.1 22.0 %all-gather.14.cloned.1.call-done = bf16[8,256,512]{2,1,0:T(8,128)(2,1)} async-done(((bf16[1,256,512]{2,1,0:T(8,128)(2,1)}), bf16[8,256,512]{2,1,0:T(8,128)(2,1)}) %all-gather.14.cloned.1.call-update) | async-done | bytes 2097168 | tf_op jit(solution)/shard_map/all_gather | solution.py:10
  267.1 1.2 convolution_bitcast_fusion
  268.4 24.3 %all_to_all.50 = f32[16,32,512]{2,1,0:T(8,128)S(1)} all-to-all(f32[16,32,512]{2,1,0:T(8,128)S(1)} %convolution_bitcast_fusion), channel_id=1, replica_groups=mesh['row'=8,'col'=16] {'col'}, dimensions={0} | all-to-all | bytes 2097152 | tf_op jit(solution)/shard_map/all_to_all | solution.py:43
  292.8 0.8 broadcast_in_dim.13
  293.6 3.6 %all-to-all-start.7 = ((bf16[16,32,512]{2,1,0:T(8,128)(2,1)}), bf16[16,32,512]{2,1,0:T(8,128)(2,1)S(1)}, u32[]{:S(2)}, u32[]{:S(2)}) async-start(bf16[16,32,512]{2,1,0:T(8,128)(2,1)} %broadcast_in_dim.13), calls=%async_computation.7 | async-start | bytes 1048576 | tf_op jit(solution)/shard_map/all_to_all | solution.py:26
  297.2 10.7 %all-to-all-done.7 = bf16[16,32,512]{2,1,0:T(8,128)(2,1)S(1)} async-done(((bf16[16,32,512]{2,1,0:T(8,128)(2,1)}), bf16[16,32,512]{2,1,0:T(8,128)(2,1)S(1)}, u32[]{:S(2)}, u32[]{:S(2)}) %all-to-all-start.7) | async-done | bytes 524320 | tf_op jit(solution)/shard_map/all_to_all | solution.py:26
  307.9 0.1 pad_maximum_fusion
  308.0 0.4 fusion.9
  308.4 10.6 %all_to_all.51 = bf16[8,32,512]{2,1,0:T(8,128)(2,1)S(1)} all-to-all(bf16[8,32,512]{2,1,0:T(8,128)(2,1)S(1)} %broadcast_in_dim.14), channel_id=1, replica_groups=mesh['row'=8,'col'=16] {'row'}, dimensions={0} | all-to-all | bytes 524288 | tf_op jit(solution)/shard_map/all_to_all | solution.py:26
  319.1 0.6 multiply_subtract_fusion
  (24 shorter events, 0.6 us)
Async XLA Ops:
  7.2 191.6 %copy-start = (bf16[2,256,1,256]{3,1,2,0:T(8,128)(2,1)S(1)}, bf16[2,256,1,256]{3,1,2,0:T(8,128)(2,1)}, u32[]{:S(2)}) copy-start(bf16[2,256,1,256]{3,1,2,0:T(8,128)(2,1)} %param.10) | copy-start | bytes 786436
  7.2 45.9 %all-gather.8.cloned.1.call-start = ((), (), s32[]{:S(2)}) async-start(), calls=%async_computation.9 | async-start | bytes 7077888 | tf_op jit(solution)/shard_map/all_gather | solution.py:92
  92.8 19.9 %all-to-all-start.1 = ((f32[16,32,512]{2,1,0:T(8,128)}), f32[16,32,512]{2,1,0:T(8,128)S(1)}, u32[]{:S(2)}, u32[]{:S(2)}) async-start(f32[16,32,512]{2,1,0:T(8,128)} %broadcast_in_dim.10), calls=%async_computation.1 | async-start | bytes 2097152 | tf_op jit(solution)/shard_map/all_to_all | solution.py:26
  96.5 39.8 %all-gather.10.cloned.1.call-start = ((), (), s32[]{:S(2)}) async-start(), calls=%async_computation.10 | async-start | bytes 2359296 | tf_op jit(solution)/shard_map/all_gather | solution.py:10
  114.5 84.3 %all-gather.12.cloned.1.call-start = ((), (), s32[]{:S(2)}) async-start(), calls=%async_computation.11 | async-start | bytes 2359296 | tf_op jit(solution)/shard_map/all_gather | solution.py:10
  176.7 90.4 %all-gather.14.cloned.1.call-start = ((), (), s32[]{:S(2)}) async-start(), calls=%async_computation.12 | async-start | bytes 2359296 | tf_op jit(solution)/shard_map/all_gather | solution.py:10
  224.3 20.0 %copy-start.2 = (bf16[2,256,512]{2,1,0:T(8,128)(2,1)S(1)}, bf16[2,256,512]{2,1,0:T(8,128)(2,1)}, u32[]{:S(2)}) copy-start(bf16[2,256,512]{2,1,0:T(8,128)(2,1)} %get-tuple-element.2) | copy-start | bytes 1572868
  224.4 42.7 %copy-start.3 = (bf16[1,2,256,1,256]{4,2,3,1,0:T(8,128)(2,1)S(1)}, bf16[1,2,256,1,256]{4,2,3,1,0:T(8,128)(2,1)}, u32[]{:S(2)}) copy-start(bf16[1,2,256,1,256]{4,2,3,1,0:T(8,128)(2,1)} %get-tuple-element.5) | copy-start | bytes 786436
  293.6 14.2 %all-to-all-start.7 = ((bf16[16,32,512]{2,1,0:T(8,128)(2,1)}), bf16[16,32,512]{2,1,0:T(8,128)(2,1)S(1)}, u32[]{:S(2)}, u32[]{:S(2)}) async-start(bf16[16,32,512]{2,1,0:T(8,128)(2,1)} %broadcast_in_dim.13), calls=%async_computation.7 | async-start | bytes 1048576 | tf_op jit(solution)/shard_map/all_to_all | solution.py:26
  307.9 11.8 %copy-start.1 = (bf16[4,256,512]{2,1,0:T(8,128)(2,1)}, bf16[4,256,512]{2,1,0:T(8,128)(2,1)S(1)}, u32[]{:S(2)}) copy-start(bf16[4,256,512]{2,1,0:T(8,128)(2,1)S(1)} %pad_maximum_fusion) | copy-start | bytes 3145732
  308.0 11.1 %copy-start.4 = (f32[32,512]{1,0:T(8,128)S(1)}, f32[32,512]{1,0:T(8,128)}, u32[]{:S(2)}) copy-start(f32[32,512]{1,0:T(8,128)} %param.11) | copy-start | bytes 196612
Sparse Core Ops, SparseCore 0:
  9.7 43.3 all-gather.7
  114.6 21.6 all-gather.9
  176.9 21.8 all-gather.11
  245.2 21.8 all-gather.13
where the time goes:
time: 327 us; the launch traced here: 326 us
  blocking collectives  142 us (43%)
  waiting for transfers between devices  134 us (41%)
  matrix products  18.3 us (6%)
  between operations  13.9 us (4%)
  starting transfers between devices  7.39 us (2%)
  local copies, waits for them, and re-layouts  7.02 us (2%)
  other arithmetic  3.55 us (1%)
    all_to_all x4, blocking collectives, sent_and_summed(): lax.all_to_all(blocks, axis, split_axis=0, concat_axis=0, tiled=True)  97.2 us
    all_gather x3, waiting for transfers between devices, from_root(): lax.all_gather(shard, axis)  64 us
    all_gather x1, waiting for transfers between devices, body(): lax.all_gather(prev_solution, 'row', axis=0, tiled=True)  45.2 us
    all_to_all x3, blocking collectives, from_everyone(): lax.all_to_all(jnp.broadcast_to(shard[None], (peers, *shard.shape)), axis...  44.4 us
    all_to_all x2, waiting for transfers between devices, from_everyone(): lax.all_to_all(jnp.broadcast_to(shard[None], (peers, *shard.shape)), axis...  24.6 us
    dot_general x1, matrix products, body(): jnp.einsum('atbu,bum->atm', left_factor, lax.all_gather(prev_solution, 'r...  14.2 us
    all_to_all x2, starting transfers between devices, from_everyone(): lax.all_to_all(jnp.broadcast_to(shard[None], (peers, *shard.shape)), axis...  7.23 us
  transfers between devices with their start and end apart: 6, of which 6 were waited for; matrix products, arithmetic and copies ran while one was open for 1% of the time, Pallas kernels for 0%

commit v1 on v0

v1 whole, which is shorter than its diff:
```python
import jax
import jax.numpy as jnp
from jax import lax
from jax.experimental import pallas as pl
from jax.experimental.pallas import tpu as pltpu
from jax.sharding import PartitionSpec as P

S = 8192
BF = jnp.bfloat16
F32 = jnp.float32
VMEM = pltpu.VMEM
NT = (((1,), (1,)), ((), ()))


def x_shift(v, step):
    return lax.ppermute(v, "row", [(r, (r + 2 * step) % 8) for r in range(8)])


def other_core(v):
    return lax.ppermute(v, "row", [(r, r ^ 1) for r in range(8)])


def y_shift(v, step):
    return lax.ppermute(v, "col", [(c, (c // 4 + step) % 4 * 4 + c % 4) for c in range(16)])


def z_shift(v, step):
    return lax.ppermute(v, "col", [(c, c // 4 * 4 + (c + step) % 4) for c in range(16)])


def whole(array):
    rank = len(array.shape)
    return pl.BlockSpec(array.shape, lambda i, *_: (0,) * rank)


def cost(flops, moved):
    return pl.CostEstimate(flops=flops, bytes_accessed=moved, transcendentals=0)


def split_tiles_kernel(src, dst):
    dst[:, 0] = pltpu.einshape("tbu->btu", src[0])


def split_tiles(left):
    rounds, tile, count, width = left.shape
    rows = 64
    out = pl.pallas_call(
        split_tiles_kernel,
        grid=(rounds, tile // rows),
        in_specs=[pl.BlockSpec((1, rows, count, width), lambda a, t: (a, t, 0, 0))],
        out_specs=pl.BlockSpec((count, 1, rows, width), lambda a, t: (0, a, t, 0)),
        out_shape=jax.ShapeDtypeStruct((count, rounds, tile, width), BF),
        cost_estimate=cost(0, 2 * left.size * 2),
    )(left)
    return out.reshape(count, rounds * tile, width)


def accumulate(acc, left, held, step):
    rows = 128

    def part(m, _):
        here = pl.ds(pl.multiple_of(m * rows, rows), rows)
        total = jnp.dot(left[0, here, :], held[0], preferred_element_type=F32)
        for t in range(1, 3):
            total += jnp.dot(left[t, here, :], held[t], preferred_element_type=F32)

        @pl.when(step == 0)
        def _():
            acc[here, :] = total

        @pl.when(step > 0)
        def _():
            acc[here, :] += total

        return 0

    lax.fori_loop(0, 8, part, 0)


def take_pieces(step, pieces, held):
    half = held.shape[2] // 2
    for j in range(len(pieces) // 2):

        @pl.when(step == j)
        def _():
            held[:, :, :half] = pieces[2 * j][...]
            held[:, :, half:] = pieces[2 * j + 1][...]


def first_products_kernel(order, left, *refs):
    del order
    *pieces, acc, held = refs
    step = pl.program_id(0)
    take_pieces(step, pieces, held)
    accumulate(acc, left, held, step)


def last_products_kernel(order, left, before, *refs):
    del order
    *pieces, first, second, acc, held = refs
    step = pl.program_id(0)

    @pl.when(step == 0)
    def _():
        acc[...] = before[...]

    take_pieces(step, pieces, held)
    accumulate(acc, left, held, step + 1)

    @pl.when(step == pl.num_programs(0) - 1)
    def _():
        for out, base in ((first, 0), (second, 512)):
            for m in range(4):
                block = acc[base + m * 128 : base + (m + 1) * 128, :]
                out[:, m * 128 : (m + 1) * 128] = jnp.transpose(block).astype(BF)


def piece_specs(pieces):
    specs = []
    for array, place in pieces:
        specs.append(pl.BlockSpec((3, 256, 256), lambda i, *_, place=place: (0, 0, place)))
    return specs


def products(order, left, pieces, before=None):
    blocks = len(pieces) // 2
    _, rows, width = left.shape
    left_spec = pl.BlockSpec((3, rows, width), lambda i, order: (order[i], 0, 0))
    arrays = [array for array, _ in pieces]
    held = VMEM((3, 256, 512), BF)
    flops = blocks * 2 * rows * 768 * 512
    moved = blocks * 3 * 2 * (rows * 256 + 256 * 512) + rows * 512 * 4
    if before is None:
        out = jax.ShapeDtypeStruct((rows, 512), F32)
        return pl.pallas_call(
            first_products_kernel,
            grid_spec=pltpu.PrefetchScalarGridSpec(
                num_scalar_prefetch=1,
                grid=(blocks,),
                in_specs=[left_spec, *piece_specs(pieces)],
                out_specs=whole(out),
                scratch_shapes=[held],
            ),
            out_shape=out,
            cost_estimate=cost(flops, moved),
        )(order, left, *arrays)
    out = jax.ShapeDtypeStruct((512, 512), BF)
    return pl.pallas_call(
        last_products_kernel,
        grid_spec=pltpu.PrefetchScalarGridSpec(
            num_scalar_prefetch=1,
            grid=(blocks,),
            in_specs=[left_spec, whole(before), *piece_specs(pieces)],
            out_specs=[whole(out), whole(out)],
            scratch_shapes=[VMEM((rows, 512), F32), held],
        ),
        out_shape=[out, out],
        cost_estimate=cost(flops, moved),
    )(order, left, before, *arrays)


def ring(block, shift):
    half = block.shape[0] // 2
    before = shift(block, 1)
    after = shift(block, -1)
    far_low = shift(before[:half], 1)
    far_high = shift(after[half:], -1)
    return [block, before, after, far_low, far_high]


def both_ways(block, first_shift, then_shift):
    lines = block.shape[1]
    near = ring(block.reshape(3 * lines, -1), first_shift)
    near = jnp.concatenate([*near[:3], *near[3:]], axis=0)
    return ring(near.reshape(4, 3, lines, -1), then_shift)


RELATIVE = (0, -1, 1, 2)


def far_gather(block):
    low, high = block[:, :, :256], block[:, :, 256:]
    before_low = x_shift(low, 1)
    after_high = x_shift(high, -1)
    before_high = x_shift(high, 1)
    after_low = x_shift(low, -1)
    far_low = x_shift(before_low, 1)
    far_high = x_shift(after_high, -1)
    return (low, high), (before_low, before_high), (after_low, after_high), (far_low, far_high)


def stage_kernel(mode, order, tiles, own, one, two, three, base, *refs):
    *weights, out, held = refs
    for i, source in enumerate((own, one, two, three)):
        for k in range(2):
            line = order[2 * i + k]
            held[line] = source[k, :, :256]
            held[8 + line] = source[k, :, 256:]
    for a in range(2):
        flow = mode[a]
        total = jnp.zeros((32, 256), F32)
        place = 0
        for ref in weights[5 * a : 5 * a + 5]:
            for i in range(ref.shape[0]):
                tile = held[tiles[16 * flow + place]]
                total += lax.dot_general(tile, ref[i, 0], NT, preferred_element_type=F32)
                place += 1
        lanes = slice(256 * a, 256 * (a + 1))
        if base is None:
            out[:, lanes] = total.astype(BF)
        else:
            out[:, lanes] = (base[:, lanes] - total).astype(BF)


def apply_stage(order, tiles, values, flows, picks, base=None):
    pair = jnp.stack([values, other_core(values)])
    moved = [pair, x_shift(pair, 1), x_shift(pair, -1), x_shift(pair, 2)]
    weights, specs = [], []
    for flow, q in picks:
        for array in flows[flow]:
            weights.append(array)
            specs.append(
                pl.BlockSpec((array.shape[0], 1, 256, 256), lambda i, *_, q=q: (0, q, 0, 0))
            )
    mode = [flow for flow, _ in picks]
    bases = [] if base is None else [base]

    def kernel(order, tiles, own, one, two, three, *refs):
        if base is None:
            stage_kernel(mode, order, tiles, own, one, two, three, None, *refs)
        else:
            stage_kernel(mode, order, tiles, own, one, two, three, refs[0], *refs[1:])

    out = jax.ShapeDtypeStruct(values.shape, BF)
    return pl.pallas_call(
        kernel,
        grid_spec=pltpu.PrefetchScalarGridSpec(
            num_scalar_prefetch=2,
            grid=(1,),
            in_specs=[*map(whole, moved), *map(whole, bases), *specs],
            out_specs=whole(out),
            scratch_shapes=[VMEM((16, 32, 256), BF)],
        ),
        out_shape=out,
        cost_estimate=cost(2 * 32 * 4096 * 512, 2 * 4096 * 512),
    )(order, tiles, *moved, *bases, *weights)


def over_sites(partial):
    return lax.all_to_all(partial.reshape(16, 32, 512), "col", 0, 0, tiled=True)


def all_sites(values):
    sent = jnp.broadcast_to(values[None], (16, *values.shape))
    return lax.all_to_all(sent, "col", 0, 0, tiled=True).reshape(512, 512)


def row_sum(values):
    values = values + other_core(values)
    return values + x_shift(values, 1) + x_shift(values, -1) + x_shift(values, 2)


def outer_part(own, every):
    return lax.dot_general(own, every, NT, preferred_element_type=F32)


def in_rows(every):
    return jnp.transpose(every).reshape(2, 256, 512)


def body(left_factor, prev_solution, cross, inverses, coupling, prior_cov):
    row, col = lax.axis_index("row"), lax.axis_index("col")
    x, k = row // 2, row % 2
    y, z = col // 4, col % 4
    order = jnp.stack([(x + d) % 4 * 2 + (k + e) % 2 for d in RELATIVE for e in range(2)])
    tiles = jnp.stack(
        [(y + d) % 4 * 4 + (z + e) % 4 for e in RELATIVE for d in RELATIVE]
        + [(y + d) % 4 * 4 + (z + e) % 4 for d in RELATIVE for e in RELATIVE]
    )
    order, tiles = order.astype(jnp.int32), tiles.astype(jnp.int32)

    own, before, after, far = far_gather(prev_solution)
    sibling = other_core(prev_solution)
    factor_lines = [
        *inverses[0, :, :, 0, :],
        *coupling[:, :, 0, :],
        *inverses[1, :, :, 0, :],
    ]
    flows = (
        both_ways(jnp.stack(factor_lines[:3]), y_shift, z_shift),
        both_ways(jnp.stack(factor_lines[3:]), z_shift, y_shift),
    )
    left = split_tiles(left_factor)
    pieces = [(prev_solution, 0), (prev_solution, 1), (sibling, 0), (sibling, 1)]
    for pair in (before, after):
        pieces += [(v, 0) for v in pair] + [(other_core(v), 0) for v in pair]
    started = products(order[:6], left, pieces)
    pieces = [(v, 0) for v in far] + [(other_core(v), 0) for v in far]
    first, second = products(order[6:], left, pieces, started)

    sites = jnp.transpose(cross.reshape(1024, 512))
    sites = lax.dynamic_slice_in_dim(sites, 32 * col, 32, 0).astype(F32)
    first_sum = over_sites(first).astype(F32).sum(axis=0)
    second_sum = over_sites(second).astype(F32).sum(axis=0)
    first_rhs = (sites[:, :512] - first_sum).astype(BF)
    solved_first = apply_stage(order, tiles, first_rhs, flows, ((0, 0), (0, 1)))
    second_rhs = apply_stage(
        order, tiles, solved_first, flows, ((0, 2), (1, 0)), sites[:, 512:] - second_sum
    )
    every_first = all_sites(solved_first)
    solved_second = apply_stage(order, tiles, second_rhs, flows, ((1, 1), (1, 2)))
    every_second = all_sites(solved_second)
    outer = outer_part(solved_first, every_first) + outer_part(solved_second, every_second)
    pred_cov = prior_cov - row_sum(outer) / S
    return jnp.concatenate([in_rows(every_first), in_rows(every_second)]), pred_cov


def solution(mesh):
    placed = (
        P(None, "row", None, "col"),
        P("row", "col", None),
        P(None, "row", None),
        P(None, None, "row", None, "col"),
        P(None, "row", None, "col"),
        P("col", None),
    )
    return jax.shard_map(
        body,
        mesh=mesh,
        in_specs=placed,
        out_specs=(P(None, "row", None), P("col", None)),
        check_vma=False,
    )
```

time: 327 us -> 242 us (0.74)
  blocking collectives: 142 us -> 30.1 us
  waiting for transfers between devices: 134 us -> 57 us
  Pallas kernels: 0 us -> 59.9 us
  starting transfers between devices: 7.39 us -> 56.9 us
  local copies, waits for them, and re-layouts: 7.02 us -> 28.6 us
  matrix products: 18.3 us -> 0.49 us
  between operations: 13.9 us -> 1.09 us
    all_to_all x7 -> x2, blocking collectives: 142 us -> 30.1 us  [the longest x1 16 us: over_sites(): return lax.all_to_all(partial.reshape(16, 32, 512), 'col', 0, 0, tiled=True)]
    all_gather x4 -> x0, waiting for transfers between devices: 109 us -> none  [the longest x3 64 us: from_root(): lax.all_gather(shard, axis)]
    pallas_call x0 -> x6, Pallas kernels: none -> 59.9 us  [the longest x1 19.5 us: products(): pl.pallas_call(first_products_kernel, grid_spec=pltpu.PrefetchScalarGridS...]
    ppermute x0 -> x45, starting transfers between devices: none -> 49.6 us  [the longest x18 20.1 us: x_shift(): return lax.ppermute(v, 'row', [(r, (r + 2 * step) % 8) for r in range(8)])]
    ppermute x0 -> x45, waiting for transfers between devices: none -> 46.8 us  [the longest x18 39.7 us: x_shift(): return lax.ppermute(v, 'row', [(r, (r + 2 * step) % 8) for r in range(8)])]
    dot_general x5 -> x2, matrix products: 18.3 us -> 0.49 us  [outer_part(): return lax.dot_general(own, every, NT, preferred_element_type=F32)]
    all_to_all x2, waiting for transfers between devices: 24.6 us -> 10.2 us  [the longest x1 9.8 us: all_sites(): return lax.all_to_all(sent, 'col', 0, 0, tiled=True).reshape(512, 512)]
    unnamed x10 -> x77, local copies, waits for them, and re-layouts: 0.03 us -> 11.5 us
  transfers between devices with their start and end apart: 6 -> 47, of which waited for: 6 -> 22; matrix products, arithmetic and copies ran while one was open for 1% -> 11% of each run, Pallas kernels for 0% -> 21%
where the time goes in v1:
time: 242 us; the launch traced here: 240 us
  Pallas kernels  59.9 us (25%)
  waiting for transfers between devices  57 us (24%)
  starting transfers between devices  56.9 us (24%)
  blocking collectives  30.1 us (12%)
  local copies, waits for them, and re-layouts  28.6 us (12%)
  other arithmetic  6.22 us (3%)
    ppermute x18, waiting for transfers between devices, x_shift(): return lax.ppermute(v, 'row', [(r, (r + 2 * step) % 8) for r in range(8)])  39.7 us
    ppermute x18, starting transfers between devices, x_shift(): return lax.ppermute(v, 'row', [(r, (r + 2 * step) % 8) for r in range(8)])  20.1 us
    pallas_call x1, Pallas kernels, products(): pl.pallas_call(first_products_kernel, grid_spec=pltpu.PrefetchScalarGridS...  19.5 us
    ppermute x8, starting transfers between devices, z_shift(): lax.ppermute(v, 'col', [(c, c // 4 * 4 + (c + step) % 4) for c in range(1...  16.7 us
    pallas_call x1, Pallas kernels, split_tiles(): pl.pallas_call(split_tiles_kernel, grid=(rounds, tile // rows), in_specs=...  16.3 us
    all_to_all x1, blocking collectives, over_sites(): return lax.all_to_all(partial.reshape(16, 32, 512), 'col', 0, 0, tiled=True)  16 us
    pallas_call x3, Pallas kernels, apply_stage(): pl.pallas_call(kernel, grid_spec=pltpu.PrefetchScalarGridSpec(num_scalar_...  14.7 us
    all_to_all x1, blocking collectives, all_sites(): return lax.all_to_all(sent, 'col', 0, 0, tiled=True).reshape(512, 512)  14 us
  transfers between devices with their start and end apart: 47, of which 22 were waited for; matrix products, arithmetic and copies ran while one was open for 11% of the time, Pallas kernels for 21%

profile of v1, /device:TPU:0, one launch (start us, length us, event | category | flops | bytes accessed | tf_op | source)
XLA Modules:
  0.0 240.2 jit_solution(14441178769879567762)
XLA Ops:
  0.7 2.2 fusion.1
  11.4 4.9 %collective-permute-done.1.refs_4_ = bf16[3,256,256]{2,1,0:T(8,128)(2,1)S(1)} collective-permute-done((bf16[3,256,256]{2,1,0:T(8,128)(2,1)}, bf16[3,256,256]{2,1,0:T(8,128)(2,1)S(1)}, u32[]{:S(2)}, u32[]{:S(2)}) %collective-permute-start.1) | collective-permute-done | bytes 393248 | tf_op jit(solution)/shard_map/ppermute | solution.py:16
  16.3 4.1 %collective-permute-start.30 = (bf16[768,256]{1,0:T(8,128)(2,1)S(1)}, bf16[768,256]{1,0:T(8,128)(2,1)}, u32[]{:S(2)}, u32[]{:S(2)}) collective-permute-start(bf16[768,256]{1,0:T(8,128)(2,1)S(1)} %bitcast.74), channel_id=1, source_target_pairs={{0,3},{1,0},{2,1},{3,2},{4,7},{5,4},{6,5},{7,6},{8,11},{9,8},{10,9... | collective-permute-start | bytes 1179656 | tf_op jit(solution)/shard_map/ppermute | solution.py:28
  20.4 3.0 %collective-permute-done.2.refs_5_ = bf16[3,256,256]{2,1,0:T(8,128)(2,1)S(1)} collective-permute-done((bf16[3,256,256]{2,1,0:T(8,128)(2,1)}, bf16[3,256,256]{2,1,0:T(8,128)(2,1)S(1)}, u32[]{:S(2)}, u32[]{:S(2)}) %collective-permute-start.2) | collective-permute-done | bytes 393248 | tf_op jit(solution)/shard_map/ppermute | solution.py:16
  26.0 16.3 %shard_map.77 = bf16[24,4,256,256]{3,2,1,0:T(8,128)(2,1)} custom-call(bf16[4,256,24,256]{3,2,1,0:T(8,128)(2,1)} %src.1), custom_call_target="tpu_custom_call" | custom-call | bytes 25165824 | tf_op jit(solution)/shard_map/pallas_call | solution.py:47
  52.5 2.2 collective-permute-start.32
  57.5 2.2 collective-permute-done.31
  64.4 3.0 %collective-permute-done.9.refs_0_ = bf16[3,256,256]{2,1,0:T(8,128)(2,1)S(1)} collective-permute-done((bf16[3,256,256]{2,1,0:T(8,128)(2,1)S(1)}, bf16[3,256,256]{2,1,0:T(8,128)(2,1)S(1)}, u32[]{:S(2)}, u32[]{:S(2)}) %collective-permute-start.9) | collective-permute-done | bytes 393248 | tf_op jit(solution)/shard_map/ppermute | solution.py:16
  68.9 3.2 %collective-permute-start.22 = (bf16[4,3,256,256]{3,2,1,0:T(8,128)(2,1)}, bf16[4,3,256,256]{3,2,1,0:T(8,128)(2,1)}, u32[]{:S(2)}, u32[]{:S(2)}) collective-permute-start(bf16[4,3,256,256]{3,2,1,0:T(8,128)(2,1)} %bitcast.34.refs_0_.refs_5_.refs_1_), channel_id=1, source_target_pairs={{0,3},{1,0},{2,1},{3,2},{4,7},{5,4},{6,5},{7,6},{8,11},{9,8},{10,9... | collective-permute-start | bytes 4718600 | tf_op jit(solution)/shard_map/ppermute | solution.py:28
  78.1 19.5 %shard_map.78.before = f32[1024,512]{1,0:T(8,128)} custom-call(s32[6]{0:T(128)} %stack.156.order, bf16[24,1024,256]{2,1,0:T(8,128)(2,1)} %bitcast.65, bf16[3,256,512]{2,1,0:T(8,128)(2,1)} %refs_1_.1, bf16[3,256,512]{2,1,0:T(8,128)(2,1)} %refs_1_.1, bf16[3,256,512]{2,1,0:T(8,128)(2,1)} %copy-done.4, bf16[3,256,512]{2,1,0:T(8,128)(2,1)} %copy-done.4, ...), custom_call_target="tpu_custom_call" | custom-call | flops 4831838208 | bytes 16252928 | tf_op jit(solution)/shard_map/pallas_call | solution.py:135
  97.6 9.4 %shard_map.79 = (bf16[512,512]{1,0:T(8,128)(2,1)}, bf16[512,512]{1,0:T(8,128)(2,1)}) custom-call(s32[2]{0:T(128)} %pad_add_fusion.order, bf16[24,1024,256]{2,1,0:T(8,128)(2,1)} %bitcast.66, f32[1024,512]{1,0:T(8,128)} %shard_map.78.before, bf16[3,256,256]{2,1,0:T(8,128)(2,1)} %copy-done.12, bf16[3,256,256]{2,1,0:T(8,128)(2,1)} %collective-permute-done.10.refs_1_, ...), custom_call_target="tpu_custom_call" | custom-call | flops 1610612736 | bytes 6815744 | tf_op jit(solution)/shard_map/pallas_call | solution.py:148
  107.0 16.0 %all_to_all.20 = bf16[16,32,512]{2,1,0:T(8,128)(2,1)} all-to-all(bf16[16,32,512]{2,1,0:T(8,128)(2,1)} %bitcast.81), channel_id=1, replica_groups=mesh['row'=8,'col'=16] {'col'}, dimensions={0} | all-to-all | bytes 1048576 | tf_op jit(solution)/shard_map/all_to_all | solution.py:250
  123.0 3.8 %all-to-all-start = ((bf16[16,32,512]{2,1,0:T(8,128)(2,1)}), bf16[16,32,512]{2,1,0:T(8,128)(2,1)S(1)}, u32[]{:S(2)}, u32[]{:S(2)}) async-start(bf16[16,32,512]{2,1,0:T(8,128)(2,1)} %bitcast.80), calls=%async_computation | async-start | bytes 1048576 | tf_op jit(solution)/shard_map/all_to_all | solution.py:250
  128.6 2.1 slice.67
  132.3 2.1 slice.68
  139.4 2.1 slice.73
  146.7 4.3 %collective-permute-done.14.one = bf16[2,32,512]{2,1,0:T(8,128)(2,1)S(1)} collective-permute-done((bf16[2,32,512]{2,1,0:T(8,128)(2,1)S(1)}, bf16[2,32,512]{2,1,0:T(8,128)(2,1)S(1)}, u32[]{:S(2)}, u32[]{:S(2)}) %collective-permute-start.14) | collective-permute-done | bytes 65568 | tf_op jit(solution)/shard_map/ppermute | solution.py:16
  151.5 3.7 %collective-permute-done.15.two = bf16[2,32,512]{2,1,0:T(8,128)(2,1)S(1)} collective-permute-done((bf16[2,32,512]{2,1,0:T(8,128)(2,1)S(1)}, bf16[2,32,512]{2,1,0:T(8,128)(2,1)S(1)}, u32[]{:S(2)}, u32[]{:S(2)}) %collective-permute-start.15) | collective-permute-done | bytes 65568 | tf_op jit(solution)/shard_map/ppermute | solution.py:16
  157.1 3.9 %collective-permute-done.16.three = bf16[2,32,512]{2,1,0:T(8,128)(2,1)S(1)} collective-permute-done((bf16[2,32,512]{2,1,0:T(8,128)(2,1)S(1)}, bf16[2,32,512]{2,1,0:T(8,128)(2,1)S(1)}, u32[]{:S(2)}, u32[]{:S(2)}) %collective-permute-start.16) | collective-permute-done | bytes 65568 | tf_op jit(solution)/shard_map/ppermute | solution.py:16
  161.6 4.9 %shard_map.80 = bf16[32,512]{1,0:T(8,128)(2,1)} custom-call(s32[8]{0:T(128)} %stack.137.order, s32[32]{0:T(128)} %stack.154.tiles, bf16[2,32,512]{2,1,0:T(8,128)(2,1)} %copy-done.19, bf16[2,32,512]{2,1,0:T(8,128)(2,1)} %copy-done.24, bf16[2,32,512]{2,1,0:T(8,128)(2,1)} %copy-done.25, bf16[2,32,512]{2,1,0:T(8,128)(2,1)} %copy-done.26, ...), custom_call_target="tpu_custom_call" | custom-call | flops 134217728 | bytes 4194304 | tf_op jit(solution)/shard_map/pallas_call | solution.py:235
  168.8 3.2 %collective-permute-start.27 = (bf16[2,32,512]{2,1,0:T(8,128)(2,1)S(1)}, bf16[2,32,512]{2,1,0:T(8,128)(2,1)S(1)}, u32[]{:S(2)}, u32[]{:S(2)}) collective-permute-start(bf16[2,32,512]{2,1,0:T(8,128)(2,1)S(1)} %pad_maximum_fusion.4.own), channel_id=1, source_target_pairs={{0,96},{16,112},{32,0},{48,16},{64,32},{80,48},{96,64},{112,80},{1... | collective-permute-start | bytes 196616 | tf_op jit(solution)/shard_map/ppermute | solution.py:16
  172.0 2.2 collective-permute-done.26.one
  174.3 3.5 %collective-permute-done.28.three = bf16[2,32,512]{2,1,0:T(8,128)(2,1)S(1)} collective-permute-done((bf16[2,32,512]{2,1,0:T(8,128)(2,1)S(1)}, bf16[2,32,512]{2,1,0:T(8,128)(2,1)S(1)}, u32[]{:S(2)}, u32[]{:S(2)}) %collective-permute-start.28) | collective-permute-done | bytes 65568 | tf_op jit(solution)/shard_map/ppermute | solution.py:16
  178.4 4.9 %shard_map.81 = bf16[32,512]{1,0:T(8,128)(2,1)} custom-call(s32[8]{0:T(128)} %stack.137.order, s32[32]{0:T(128)} %stack.154.tiles, bf16[2,32,512]{2,1,0:T(8,128)(2,1)} %copy-done.20, bf16[2,32,512]{2,1,0:T(8,128)(2,1)} %copy-done.27, bf16[2,32,512]{2,1,0:T(8,128)(2,1)} %copy-done.28, bf16[2,32,512]{2,1,0:T(8,128)(2,1)} %copy-done.29, ...), custom_call_target="tpu_custom_call" | custom-call | flops 134217728 | bytes 4194304 | tf_op jit(solution)/shard_map/pallas_call | solution.py:235
  185.6 3.2 %collective-permute-start.39 = (bf16[2,32,512]{2,1,0:T(8,128)(2,1)S(1)}, bf16[2,32,512]{2,1,0:T(8,128)(2,1)S(1)}, u32[]{:S(2)}, u32[]{:S(2)}) collective-permute-start(bf16[2,32,512]{2,1,0:T(8,128)(2,1)S(1)} %pad_maximum_fusion.5.own), channel_id=1, source_target_pairs={{0,96},{16,112},{32,0},{48,16},{64,32},{80,48},{96,64},{112,80},{1... | collective-permute-start | bytes 196616 | tf_op jit(solution)/shard_map/ppermute | solution.py:16
  188.8 2.2 collective-permute-done.38.one
  191.7 2.9 %collective-permute-done.40.three = bf16[2,32,512]{2,1,0:T(8,128)(2,1)S(1)} collective-permute-done((bf16[2,32,512]{2,1,0:T(8,128)(2,1)S(1)}, bf16[2,32,512]{2,1,0:T(8,128)(2,1)S(1)}, u32[]{:S(2)}, u32[]{:S(2)}) %collective-permute-start.40) | collective-permute-done | bytes 65568 | tf_op jit(solution)/shard_map/ppermute | solution.py:16
  195.3 4.9 %shard_map.82 = bf16[32,512]{1,0:T(8,128)(2,1)} custom-call(s32[8]{0:T(128)} %stack.137.order, s32[32]{0:T(128)} %stack.154.tiles, bf16[2,32,512]{2,1,0:T(8,128)(2,1)} %copy-done.21, bf16[2,32,512]{2,1,0:T(8,128)(2,1)} %copy-done.30, bf16[2,32,512]{2,1,0:T(8,128)(2,1)} %copy-done.31, bf16[2,32,512]{2,1,0:T(8,128)(2,1)} %copy-done.32, ...), custom_call_target="tpu_custom_call" | custom-call | flops 134217728 | bytes 4194304 | tf_op jit(solution)/shard_map/pallas_call | solution.py:235
  201.0 14.0 %all_to_all.21 = bf16[16,32,512]{2,1,0:T(8,128)(2,1)S(1)} all-to-all(bf16[16,32,512]{2,1,0:T(8,128)(2,1)S(1)} %broadcast_in_dim.16), channel_id=1, replica_groups=mesh['row'=8,'col'=16] {'col'}, dimensions={0} | all-to-all | bytes 1048576 | tf_op jit(solution)/shard_map/all_to_all | solution.py:255
  215.9 3.6 %all-to-all-start.1 = ((bf16[16,32,512]{2,1,0:T(8,128)(2,1)}), bf16[16,32,512]{2,1,0:T(8,128)(2,1)S(1)}, u32[]{:S(2)}, u32[]{:S(2)}) async-start(bf16[16,32,512]{2,1,0:T(8,128)(2,1)} %broadcast_in_dim.6), calls=%async_computation.1 | async-start | bytes 1048576 | tf_op jit(solution)/shard_map/all_to_all | solution.py:255
  219.8 9.8 %all-to-all-done.1 = bf16[16,32,512]{2,1,0:T(8,128)(2,1)S(1)} async-done(((bf16[16,32,512]{2,1,0:T(8,128)(2,1)}), bf16[16,32,512]{2,1,0:T(8,128)(2,1)S(1)}, u32[]{:S(2)}, u32[]{:S(2)}) %all-to-all-start.1) | async-done | bytes 524320 | tf_op jit(solution)/shard_map/all_to_all | solution.py:255
  231.5 2.6 %collective-permute-start.43 = (f32[32,512]{1,0:T(8,128)S(1)}, f32[32,512]{1,0:T(8,128)S(1)}, u32[]{:S(2)}, u32[]{:S(2)}) collective-permute-start(f32[32,512]{1,0:T(8,128)S(1)} %add.353), channel_id=1, source_target_pairs={{0,96},{16,112},{32,0},{48,16},{64,32},{80,48},{96,64},{112,80},{1... | collective-permute-start | bytes 196616 | tf_op jit(solution)/shard_map/ppermute | solution.py:16
  (183 shorter events, 69.1 us)
Async XLA Ops:
  2.9 13.4 %collective-permute-start.1 = (bf16[3,256,256]{2,1,0:T(8,128)(2,1)}, bf16[3,256,256]{2,1,0:T(8,128)(2,1)S(1)}, u32[]{:S(2)}, u32[]{:S(2)}) collective-permute-start(bf16[3,256,256]{2,1,0:T(8,128)(2,1)} %get-tuple-element.7), channel_id=1, source_target_pairs={{0,32},{16,48},{32,64},{48,80},{64,96},{80,112},{96,0},{112,16},{1... | collective-permute-start | bytes 1179656 | tf_op jit(solution)/shard_map/ppermute | solution.py:16
  4.4 19.0 %collective-permute-start.2 = (bf16[3,256,256]{2,1,0:T(8,128)(2,1)}, bf16[3,256,256]{2,1,0:T(8,128)(2,1)S(1)}, u32[]{:S(2)}, u32[]{:S(2)}) collective-permute-start(bf16[3,256,256]{2,1,0:T(8,128)(2,1)} %get-tuple-element.6), channel_id=1, source_target_pairs={{0,32},{16,48},{32,64},{48,80},{64,96},{80,112},{96,0},{112,16},{1... | collective-permute-start | bytes 1179656 | tf_op jit(solution)/shard_map/ppermute | solution.py:16
  6.1 19.1 %collective-permute-start.17 = (bf16[768,256]{1,0:T(8,128)(2,1)S(1)}, bf16[768,256]{1,0:T(8,128)(2,1)S(1)}, u32[]{:S(2)}, u32[]{:S(2)}) collective-permute-start(bf16[768,256]{1,0:T(8,128)(2,1)S(1)} %bitcast.76), channel_id=1, source_target_pairs={{0,4},{1,5},{2,6},{3,7},{4,8},{5,9},{6,10},{7,11},{8,12},{9,13},{1... | collective-permute-start | bytes 1179656 | tf_op jit(solution)/shard_map/ppermute | solution.py:24
  7.7 35.2 %collective-permute-start.18 = (bf16[768,256]{1,0:T(8,128)(2,1)S(1)}, bf16[768,256]{1,0:T(8,128)(2,1)S(1)}, u32[]{:S(2)}, u32[]{:S(2)}) collective-permute-start(bf16[768,256]{1,0:T(8,128)(2,1)S(1)} %bitcast.77), channel_id=1, source_target_pairs={{0,12},{1,13},{2,14},{3,15},{4,0},{5,1},{6,2},{7,3},{8,4},{9,5},{1... | collective-permute-start | bytes 1179656 | tf_op jit(solution)/shard_map/ppermute | solution.py:24
  9.4 34.5 %collective-permute-start.29 = (bf16[768,256]{1,0:T(8,128)(2,1)S(1)}, bf16[768,256]{1,0:T(8,128)(2,1)}, u32[]{:S(2)}, u32[]{:S(2)}) collective-permute-start(bf16[768,256]{1,0:T(8,128)(2,1)S(1)} %bitcast.73), channel_id=1, source_target_pairs={{0,1},{1,2},{2,3},{3,0},{4,5},{5,6},{6,7},{7,4},{8,9},{9,10},{10,1... | collective-permute-start | bytes 1179656 | tf_op jit(solution)/shard_map/ppermute | solution.py:28
  16.3 29.2 %collective-permute-start.30 = (bf16[768,256]{1,0:T(8,128)(2,1)S(1)}, bf16[768,256]{1,0:T(8,128)(2,1)}, u32[]{:S(2)}, u32[]{:S(2)}) collective-permute-start(bf16[768,256]{1,0:T(8,128)(2,1)S(1)} %bitcast.74), channel_id=1, source_target_pairs={{0,3},{1,0},{2,1},{3,2},{4,7},{5,4},{6,5},{7,6},{8,11},{9,8},{10,9... | collective-permute-start | bytes 1179656 | tf_op jit(solution)/shard_map/ppermute | solution.py:28
  23.4 27.0 %collective-permute-start.5 = (bf16[3,256,256]{2,1,0:T(8,128)(2,1)}, bf16[3,256,256]{2,1,0:T(8,128)(2,1)}, u32[]{:S(2)}, u32[]{:S(2)}) collective-permute-start(bf16[3,256,256]{2,1,0:T(8,128)(2,1)} %get-tuple-element.7), channel_id=1, source_target_pairs={{0,96},{16,112},{32,0},{48,16},{64,32},{80,48},{96,64},{112,80},{1... | collective-permute-start | bytes 1179656 | tf_op jit(solution)/shard_map/ppermute | solution.py:16
  25.2 27.3 %collective-permute-start.6 = (bf16[3,256,256]{2,1,0:T(8,128)(2,1)}, bf16[3,256,256]{2,1,0:T(8,128)(2,1)}, u32[]{:S(2)}, u32[]{:S(2)}) collective-permute-start(bf16[3,256,256]{2,1,0:T(8,128)(2,1)} %get-tuple-element.6), channel_id=1, source_target_pairs={{0,96},{16,112},{32,0},{48,16},{64,32},{80,48},{96,64},{112,80},{1... | collective-permute-start | bytes 1179656 | tf_op jit(solution)/shard_map/ppermute | solution.py:16
  42.9 20.9 %collective-permute-start = (bf16[3,256,512]{2,1,0:T(8,128)(2,1)S(1)}, bf16[3,256,512]{2,1,0:T(8,128)(2,1)S(1)}, u32[]{:S(2)}, u32[]{:S(2)}) collective-permute-start(bf16[3,256,512]{2,1,0:T(8,128)(2,1)S(1)} %copy-done.2), channel_id=1, source_target_pairs={{0,16},{16,0},{32,48},{48,32},{64,80},{80,64},{96,112},{112,96},{1... | collective-permute-start | bytes 2359304 | tf_op jit(solution)/shard_map/ppermute | solution.py:20
  43.9 10.8 %collective-permute-start.19 = (bf16[384,256]{1,0:T(8,128)(2,1)S(1)}, bf16[384,256]{1,0:T(8,128)(2,1)S(1)}, u32[]{:S(2)}, u32[]{:S(2)}) collective-permute-start(bf16[384,256]{1,0:T(8,128)(2,1)S(1)} %slice.65), channel_id=1, source_target_pairs={{0,4},{1,5},{2,6},{3,7},{4,8},{5,9},{6,10},{7,11},{8,12},{9,13},{1... | collective-permute-start | bytes 589832 | tf_op jit(solution)/shard_map/ppermute | solution.py:24
  45.5 9.1 %collective-permute-start.20 = (bf16[384,256]{1,0:T(8,128)(2,1)S(1)}, bf16[384,256]{1,0:T(8,128)(2,1)S(1)}, u32[]{:S(2)}, u32[]{:S(2)}) collective-permute-start(bf16[384,256]{1,0:T(8,128)(2,1)S(1)} %slice.66), channel_id=1, source_target_pairs={{0,12},{1,13},{2,14},{3,15},{4,0},{5,1},{6,2},{7,3},{8,4},{9,5},{1... | collective-permute-start | bytes 589832 | tf_op jit(solution)/shard_map/ppermute | solution.py:24
  50.5 9.2 %collective-permute-start.31 = (bf16[384,256]{1,0:T(8,128)(2,1)S(1)}, bf16[384,256]{1,0:T(8,128)(2,1)S(1)}, u32[]{:S(2)}, u32[]{:S(2)}) collective-permute-start(bf16[384,256]{1,0:T(8,128)(2,1)S(1)} %slice.70), channel_id=1, source_target_pairs={{0,1},{1,2},{2,3},{3,0},{4,5},{5,6},{6,7},{7,4},{8,9},{9,10},{10,1... | collective-permute-start | bytes 589832 | tf_op jit(solution)/shard_map/ppermute | solution.py:28
  52.5 7.3 %collective-permute-start.32 = (bf16[384,256]{1,0:T(8,128)(2,1)S(1)}, bf16[384,256]{1,0:T(8,128)(2,1)S(1)}, u32[]{:S(2)}, u32[]{:S(2)}) collective-permute-start(bf16[384,256]{1,0:T(8,128)(2,1)S(1)} %slice.71), channel_id=1, source_target_pairs={{0,3},{1,0},{2,1},{3,2},{4,7},{5,4},{6,5},{7,6},{8,11},{9,8},{10,9... | collective-permute-start | bytes 589832 | tf_op jit(solution)/shard_map/ppermute | solution.py:28
  54.7 9.2 %collective-permute-start.3 = (bf16[3,256,256]{2,1,0:T(8,128)(2,1)S(1)}, bf16[3,256,256]{2,1,0:T(8,128)(2,1)S(1)}, u32[]{:S(2)}, u32[]{:S(2)}) collective-permute-start(bf16[3,256,256]{2,1,0:T(8,128)(2,1)S(1)} %copy-done.9), channel_id=1, source_target_pairs={{0,16},{16,0},{32,48},{48,32},{64,80},{80,64},{96,112},{112,96},{1... | collective-permute-start | bytes 1179656 | tf_op jit(solution)/shard_map/ppermute | solution.py:20
  54.7 12.7 %collective-permute-start.9 = (bf16[3,256,256]{2,1,0:T(8,128)(2,1)S(1)}, bf16[3,256,256]{2,1,0:T(8,128)(2,1)S(1)}, u32[]{:S(2)}, u32[]{:S(2)}) collective-permute-start(bf16[3,256,256]{2,1,0:T(8,128)(2,1)S(1)} %copy-done.9), channel_id=1, source_target_pairs={{0,32},{16,48},{32,64},{48,80},{64,96},{80,112},{96,0},{112,16},{1... | collective-permute-start | bytes 1179656 | tf_op jit(solution)/shard_map/ppermute | solution.py:16
  59.7 9.2 %collective-permute-start.4 = (bf16[3,256,256]{2,1,0:T(8,128)(2,1)S(1)}, bf16[3,256,256]{2,1,0:T(8,128)(2,1)S(1)}, u32[]{:S(2)}, u32[]{:S(2)}) collective-permute-start(bf16[3,256,256]{2,1,0:T(8,128)(2,1)S(1)} %copy-done.11), channel_id=1, source_target_pairs={{0,16},{16,0},{32,48},{48,32},{64,80},{80,64},{96,112},{112,96},{1... | collective-permute-start | bytes 1179656 | tf_op jit(solution)/shard_map/ppermute | solution.py:20
  59.7 9.2 %collective-permute-start.7 = (bf16[3,256,256]{2,1,0:T(8,128)(2,1)}, bf16[3,256,256]{2,1,0:T(8,128)(2,1)S(1)}, u32[]{:S(2)}, u32[]{:S(2)}) collective-permute-start(bf16[3,256,256]{2,1,0:T(8,128)(2,1)} %collective-permute-done.5.refs_8_), channel_id=1, source_target_pairs={{0,16},{16,0},{32,48},{48,32},{64,80},{80,64},{96,112},{112,96},{1... | collective-permute-start | bytes 1179656 | tf_op jit(solution)/shard_map/ppermute | solution.py:20
  63.8 9.7 %collective-permute-start.8 = (bf16[3,256,256]{2,1,0:T(8,128)(2,1)}, bf16[3,256,256]{2,1,0:T(8,128)(2,1)S(1)}, u32[]{:S(2)}, u32[]{:S(2)}) collective-permute-start(bf16[3,256,256]{2,1,0:T(8,128)(2,1)} %collective-permute-done.6.refs_9_), channel_id=1, source_target_pairs={{0,16},{16,0},{32,48},{48,32},{64,80},{80,64},{96,112},{112,96},{1... | collective-permute-start | bytes 1179656 | tf_op jit(solution)/shard_map/ppermute | solution.py:20
  63.9 11.8 %collective-permute-start.10 = (bf16[3,256,256]{2,1,0:T(8,128)(2,1)}, bf16[3,256,256]{2,1,0:T(8,128)(2,1)}, u32[]{:S(2)}, u32[]{:S(2)}) collective-permute-start(bf16[3,256,256]{2,1,0:T(8,128)(2,1)} %collective-permute-done.6.refs_9_), channel_id=1, source_target_pairs={{0,96},{16,112},{32,0},{48,16},{64,32},{80,48},{96,64},{112,80},{1... | collective-permute-start | bytes 1179656 | tf_op jit(solution)/shard_map/ppermute | solution.py:16
  67.4 9.9 %collective-permute-start.11 = (bf16[3,256,256]{2,1,0:T(8,128)(2,1)S(1)}, bf16[3,256,256]{2,1,0:T(8,128)(2,1)S(1)}, u32[]{:S(2)}, u32[]{:S(2)}) collective-permute-start(bf16[3,256,256]{2,1,0:T(8,128)(2,1)S(1)} %collective-permute-done.9.refs_0_), channel_id=1, source_target_pairs={{0,16},{16,0},{32,48},{48,32},{64,80},{80,64},{96,112},{112,96},{1... | collective-permute-start | bytes 1179656 | tf_op jit(solution)/shard_map/ppermute | solution.py:20
  68.9 59.7 %collective-permute-start.21 = (bf16[4,3,256,256]{3,2,1,0:T(8,128)(2,1)}, bf16[4,3,256,256]{3,2,1,0:T(8,128)(2,1)}, u32[]{:S(2)}, u32[]{:S(2)}) collective-permute-start(bf16[4,3,256,256]{3,2,1,0:T(8,128)(2,1)} %bitcast.34.refs_0_.refs_5_.refs_1_), channel_id=1, source_target_pairs={{0,1},{1,2},{2,3},{3,0},{4,5},{5,6},{6,7},{7,4},{8,9},{9,10},{10,1... | collective-permute-start | bytes 4718600 | tf_op jit(solution)/shard_map/ppermute | solution.py:28
  68.9 63.4 %collective-permute-start.22 = (bf16[4,3,256,256]{3,2,1,0:T(8,128)(2,1)}, bf16[4,3,256,256]{3,2,1,0:T(8,128)(2,1)}, u32[]{:S(2)}, u32[]{:S(2)}) collective-permute-start(bf16[4,3,256,256]{3,2,1,0:T(8,128)(2,1)} %bitcast.34.refs_0_.refs_5_.refs_1_), channel_id=1, source_target_pairs={{0,3},{1,0},{2,1},{3,2},{4,7},{5,4},{6,5},{7,6},{8,11},{9,8},{10,9... | collective-permute-start | bytes 4718600 | tf_op jit(solution)/shard_map/ppermute | solution.py:28
  73.5 63.7 %collective-permute-start.33 = (bf16[4,3,256,256]{3,2,1,0:T(8,128)(2,1)}, bf16[4,3,256,256]{3,2,1,0:T(8,128)(2,1)S(1)}, u32[]{:S(2)}, u32[]{:S(2)}) collective-permute-start(bf16[4,3,256,256]{3,2,1,0:T(8,128)(2,1)} %bitcast.45.refs_6_.refs_0_.refs_5_), channel_id=1, source_target_pairs={{0,4},{1,5},{2,6},{3,7},{4,8},{5,9},{6,10},{7,11},{8,12},{9,13},{1... | collective-permute-start | bytes 4718600 | tf_op jit(solution)/shard_map/ppermute | solution.py:24
  75.7 63.8 %collective-permute-start.34 = (bf16[4,3,256,256]{3,2,1,0:T(8,128)(2,1)}, bf16[4,3,256,256]{3,2,1,0:T(8,128)(2,1)}, u32[]{:S(2)}, u32[]{:S(2)}) collective-permute-start(bf16[4,3,256,256]{3,2,1,0:T(8,128)(2,1)} %bitcast.45.refs_6_.refs_0_.refs_5_), channel_id=1, source_target_pairs={{0,12},{1,13},{2,14},{3,15},{4,0},{5,1},{6,2},{7,3},{8,4},{9,5},{1... | collective-permute-start | bytes 4718600 | tf_op jit(solution)/shard_map/ppermute | solution.py:24
  77.3 20.3 %collective-permute-start.12 = (bf16[3,256,256]{2,1,0:T(8,128)(2,1)}, bf16[3,256,256]{2,1,0:T(8,128)(2,1)}, u32[]{:S(2)}, u32[]{:S(2)}) collective-permute-start(bf16[3,256,256]{2,1,0:T(8,128)(2,1)} %collective-permute-done.10.refs_1_), channel_id=1, source_target_pairs={{0,16},{16,0},{32,48},{48,32},{64,80},{80,64},{96,112},{112,96},{1... | collective-permute-start | bytes 1179656 | tf_op jit(solution)/shard_map/ppermute | solution.py:20
  123.0 14.1 %all-to-all-start = ((bf16[16,32,512]{2,1,0:T(8,128)(2,1)}), bf16[16,32,512]{2,1,0:T(8,128)(2,1)S(1)}, u32[]{:S(2)}, u32[]{:S(2)}) async-start(bf16[16,32,512]{2,1,0:T(8,128)(2,1)} %bitcast.80), calls=%async_computation | async-start | bytes 1048576 | tf_op jit(solution)/shard_map/all_to_all | solution.py:250
  130.7 30.3 %collective-permute-start.23 = (bf16[2,3,256,256]{3,2,1,0:T(8,128)(2,1)}, bf16[2,3,256,256]{3,2,1,0:T(8,128)(2,1)}, u32[]{:S(2)}, u32[]{:S(2)}) collective-permute-start(bf16[2,3,256,256]{3,2,1,0:T(8,128)(2,1)} %slice.67), channel_id=1, source_target_pairs={{0,1},{1,2},{2,3},{3,0},{4,5},{5,6},{6,7},{7,4},{8,9},{9,10},{10,1... | collective-permute-start | bytes 2359304 | tf_op jit(solution)/shard_map/ppermute | solution.py:28
  134.4 26.6 %collective-permute-start.24 = (bf16[2,3,256,256]{3,2,1,0:T(8,128)(2,1)}, bf16[2,3,256,256]{3,2,1,0:T(8,128)(2,1)}, u32[]{:S(2)}, u32[]{:S(2)}) collective-permute-start(bf16[2,3,256,256]{3,2,1,0:T(8,128)(2,1)} %slice.68), channel_id=1, source_target_pairs={{0,3},{1,0},{2,1},{3,2},{4,7},{5,4},{6,5},{7,6},{8,11},{9,8},{10,9... | collective-permute-start | bytes 2359304 | tf_op jit(solution)/shard_map/ppermute | solution.py:28
  138.2 33.8 %collective-permute-start.35 = (bf16[2,3,256,256]{3,2,1,0:T(8,128)(2,1)}, bf16[2,3,256,256]{3,2,1,0:T(8,128)(2,1)S(1)}, u32[]{:S(2)}, u32[]{:S(2)}) collective-permute-start(bf16[2,3,256,256]{3,2,1,0:T(8,128)(2,1)} %slice.72), channel_id=1, source_target_pairs={{0,4},{1,5},{2,6},{3,7},{4,8},{5,9},{6,10},{7,11},{8,12},{9,13},{1... | collective-permute-start | bytes 2359304 | tf_op jit(solution)/shard_map/ppermute | solution.py:24
  141.5 30.5 %collective-permute-start.36 = (bf16[2,3,256,256]{3,2,1,0:T(8,128)(2,1)}, bf16[2,3,256,256]{3,2,1,0:T(8,128)(2,1)}, u32[]{:S(2)}, u32[]{:S(2)}) collective-permute-start(bf16[2,3,256,256]{3,2,1,0:T(8,128)(2,1)} %slice.73), channel_id=1, source_target_pairs={{0,12},{1,13},{2,14},{3,15},{4,0},{5,1},{6,2},{7,3},{8,4},{9,5},{1... | collective-permute-start | bytes 2359304 | tf_op jit(solution)/shard_map/ppermute | solution.py:24
  215.9 13.6 %all-to-all-start.1 = ((bf16[16,32,512]{2,1,0:T(8,128)(2,1)}), bf16[16,32,512]{2,1,0:T(8,128)(2,1)S(1)}, u32[]{:S(2)}, u32[]{:S(2)}) async-start(bf16[16,32,512]{2,1,0:T(8,128)(2,1)} %broadcast_in_dim.6), calls=%async_computation.1 | async-start | bytes 1048576 | tf_op jit(solution)/shard_map/all_to_all | solution.py:255
  231.5 6.9 %collective-permute-start.43 = (f32[32,512]{1,0:T(8,128)S(1)}, f32[32,512]{1,0:T(8,128)S(1)}, u32[]{:S(2)}, u32[]{:S(2)}) collective-permute-start(f32[32,512]{1,0:T(8,128)S(1)} %add.353), channel_id=1, source_target_pairs={{0,96},{16,112},{32,0},{48,16},{64,32},{80,48},{96,64},{112,80},{1... | collective-permute-start | bytes 196616 | tf_op jit(solution)/shard_map/ppermute | solution.py:16
  (49 other events, 436.3 us)

commit v2 on v1

v2 whole, which is shorter than its diff:
```python
import jax
import jax.numpy as jnp
from jax import lax
from jax.experimental import pallas as pl
from jax.experimental.pallas import tpu as pltpu
from jax.sharding import PartitionSpec as P

S = 8192
BF = jnp.bfloat16
F32 = jnp.float32
VMEM = pltpu.VMEM
ROOMY = pltpu.CompilerParams(vmem_limit_bytes=20 << 20)
NT = (((1,), (1,)), ((), ()))


def x_shift(v, step):
    return lax.ppermute(v, "row", [(r, (r + 2 * step) % 8) for r in range(8)])


def other_core(v):
    return lax.ppermute(v, "row", [(r, r ^ 1) for r in range(8)])


def y_shift(v, step):
    return lax.ppermute(v, "col", [(c, (c // 4 + step) % 4 * 4 + c % 4) for c in range(16)])


def z_shift(v, step):
    return lax.ppermute(v, "col", [(c, c // 4 * 4 + (c + step) % 4) for c in range(16)])


def whole(array):
    rank = len(array.shape)
    return pl.BlockSpec(array.shape, lambda i, *_: (0,) * rank)


def cost(flops, moved):
    return pl.CostEstimate(flops=flops, bytes_accessed=moved, transcendentals=0)


def split_tiles_kernel(src, dst):
    dst[:, 0] = pltpu.einshape("tbu->btu", src[0])


def split_tiles(left):
    rounds, tile, count, width = left.shape
    rows = 256
    out = pl.pallas_call(
        split_tiles_kernel,
        grid=(rounds, tile // rows),
        in_specs=[pl.BlockSpec((1, rows, count, width), lambda a, t: (a, t, 0, 0))],
        out_specs=pl.BlockSpec((count, 1, rows, width), lambda a, t: (0, a, t, 0)),
        out_shape=jax.ShapeDtypeStruct((count, rounds, tile, width), BF),
        cost_estimate=cost(0, 2 * left.size * 2),
        compiler_params=ROOMY,
    )(left)
    return out.reshape(count, rounds * tile, width)


def accumulate(acc, left, held, step):
    for base in (0, 512):
        here = slice(base, base + 512)
        total = jnp.dot(left[0, here, :], held[0], preferred_element_type=F32)
        for t in range(1, 3):
            total += jnp.dot(left[t, here, :], held[t], preferred_element_type=F32)

        @pl.when(step == 0)
        def _():
            acc[here, :] = total

        @pl.when(step > 0)
        def _():
            acc[here, :] += total


def take_pieces(step, pieces, held):
    half = held.shape[1] // 2
    for j in range(len(pieces) // 2):

        @pl.when(step == j)
        def _():
            held[:, :half, :] = pieces[2 * j][...]
            held[:, half:, :] = pieces[2 * j + 1][...]


def first_products_kernel(order, left, *refs):
    del order
    *pieces, acc, held = refs
    step = pl.program_id(0)
    take_pieces(step, pieces, held)
    accumulate(acc, left, held, step)


def next_products_kernel(order, left, before, *refs):
    del order
    *pieces, acc, held = refs
    step = pl.program_id(0)

    @pl.when(step == 0)
    def _():
        acc[...] = before[...]

    take_pieces(step, pieces, held)
    accumulate(acc, left, held, step + 1)


def last_products_kernel(order, left, before, *refs):
    *pieces, first, second, acc, held = refs
    next_products_kernel(order, left, before, *pieces, acc, held)

    @pl.when(pl.program_id(0) == pl.num_programs(0) - 1)
    def _():
        for out, base in ((first, 0), (second, 512)):
            for m in range(4):
                block = acc[base + m * 128 : base + (m + 1) * 128, :]
                out[:, m * 128 : (m + 1) * 128] = jnp.transpose(block).astype(BF)


def piece_specs(pieces):
    specs = []
    for array, place in pieces:
        specs.append(pl.BlockSpec((3, 128, 512), lambda i, *_, place=place: (0, place, 0)))
    return specs


def products(order, left, pieces, before=None, last=False):
    blocks = len(pieces) // 2
    _, rows, width = left.shape
    left_spec = pl.BlockSpec((3, rows, width), lambda i, order: (order[i], 0, 0))
    arrays = [array for array, _ in pieces]
    scratch = [VMEM((3, 256, 512), BF)]
    flops = blocks * 2 * rows * 768 * 512
    moved = blocks * 3 * 2 * (rows * 256 + 256 * 512) + rows * 512 * 4
    starts = [] if before is None else [before]
    out = jax.ShapeDtypeStruct((rows, 512), F32)
    kernel = first_products_kernel if before is None else next_products_kernel
    if last:
        out = [jax.ShapeDtypeStruct((512, 512), BF)] * 2
        kernel = last_products_kernel
        scratch = [VMEM((rows, 512), F32), *scratch]
    return pl.pallas_call(
        kernel,
        grid_spec=pltpu.PrefetchScalarGridSpec(
            num_scalar_prefetch=1,
            grid=(blocks,),
            in_specs=[left_spec, *map(whole, starts), *piece_specs(pieces)],
            out_specs=jax.tree.map(whole, out),
            scratch_shapes=scratch,
        ),
        out_shape=out,
        cost_estimate=cost(flops, moved),
        compiler_params=ROOMY,
    )(order, left, *starts, *arrays)


def spread_panel(block):
    ways = (0, 1, -1, 2)
    near = jnp.stack([z_shift(block, d) if d else block for d in ways])
    return [y_shift(near, d) if d else near for d in ways]


RELATIVE = (0, -1, 1, 2)


def far_gather(block):
    low, high = block[:, :128, :], block[:, 128:, :]
    before_low = x_shift(low, 1)
    after_high = x_shift(high, -1)
    before_high = x_shift(high, 1)
    after_low = x_shift(low, -1)
    far_low = x_shift(before_low, 1)
    far_high = x_shift(after_high, -1)
    return (low, high), (before_low, before_high), (after_low, after_high), (far_low, far_high)


def place_values(order, sources, held):
    for i, source in enumerate(sources):
        for k in range(2):
            line = order[2 * i + k]
            held[line] = source[k, :, :256]
            held[8 + line] = source[k, :, 256:]


def block_product(tile, block):
    return lax.dot_general(tile, block, NT, preferred_element_type=F32)


def gathered_stage_kernel(subtract, order, own, one, two, three, *refs):
    *base, weights, out, held, total = refs
    step = pl.program_id(0)

    @pl.when(step == 0)
    def _():
        place_values(order, (own, one, two, three), held)
        total[...] = jnp.zeros_like(total)

    for a in range(2):
        rows = slice(256 * a, 256 * (a + 1))
        part = total[:, rows]
        for i in range(4):
            part += block_product(held[4 * step + i], weights[i, rows, :])
        total[:, rows] = part

    @pl.when(step == pl.num_programs(0) - 1)
    def _():
        result = total[...]
        if subtract:
            result = base[0][...] - result
        out[...] = result.astype(BF)


def spread_stage_kernel(order, tiles, own, one, two, three, *refs):
    *weights, out, held = refs
    place_values(order, (own, one, two, three), held)
    for a in range(2):
        rows = slice(256 * a, 256 * (a + 1))
        total = jnp.zeros((32, 256), F32)
        for j, ref in enumerate(weights):
            for i in range(4):
                total += block_product(held[tiles[4 * j + i]], ref[i, rows, :])
        out[:, rows] = total.astype(BF)


def over_cores(values):
    return jnp.stack([values, other_core(values)])


def over_chips(pair):
    return [pair, x_shift(pair, 1), x_shift(pair, -1), x_shift(pair, 2)]


STAGE_COST = cost(2 * 32 * 4096 * 512, 2 * 4096 * 512)
STAGE_OUT = jax.ShapeDtypeStruct((32, 512), BF)
LEAN = pltpu.CompilerParams(vmem_limit_bytes=12 << 20)
SCALARS = pl.BlockSpec(memory_space=pltpu.SMEM)
NEAR = pl.BlockSpec(memory_space=VMEM)


def gathered_stage(order, moved, panels, which, base=None):
    bases = [] if base is None else [base]
    return pl.pallas_call(
        lambda *refs: gathered_stage_kernel(base is not None, *refs),
        grid=(4,),
        in_specs=[
            SCALARS,
            *map(whole, moved),
            *map(whole, bases),
            pl.BlockSpec((4, None, 512, 256), lambda i: (i, which, 0, 0)),
        ],
        out_specs=whole(STAGE_OUT),
        scratch_shapes=[VMEM((16, 32, 256), BF), VMEM((32, 512), F32)],
        out_shape=STAGE_OUT,
        cost_estimate=STAGE_COST,
        compiler_params=LEAN,
    )(order, *moved, *bases, panels)


def spread_stage(order, tiles, moved, panels):
    return pl.pallas_call(
        spread_stage_kernel,
        in_specs=[SCALARS, SCALARS] + [NEAR] * 8,
        out_specs=NEAR,
        scratch_shapes=[VMEM((16, 32, 256), BF)],
        out_shape=STAGE_OUT,
        cost_estimate=STAGE_COST,
        compiler_params=LEAN,
    )(order, tiles, *moved, *panels)


def over_sites(partial):
    return lax.all_to_all(partial.reshape(16, 32, 512), "col", 0, 0, tiled=True)


def all_sites(values):
    sent = jnp.broadcast_to(values[None], (16, *values.shape))
    return lax.all_to_all(sent, "col", 0, 0, tiled=True).reshape(512, 512)


def row_sum(values):
    values = values + other_core(values)
    return values + x_shift(values, 1) + x_shift(values, -1) + x_shift(values, 2)


def outer_part(own, every):
    return lax.dot_general(own, every, NT, preferred_element_type=F32)


def in_rows(every):
    return jnp.transpose(every).reshape(2, 256, 512)


def body(left_factor, prev_solution, cross, inverses, coupling, prior_cov):
    row, col = lax.axis_index("row"), lax.axis_index("col")
    x, k = row // 2, row % 2
    y, z = col // 4, col % 4
    order = jnp.stack([(x + d) % 4 * 2 + (k + e) % 2 for d in RELATIVE for e in range(2)])
    tiles = jnp.stack([(y + d) % 4 * 4 + (z + e) % 4 for d in RELATIVE for e in RELATIVE])
    order, tiles = order.astype(jnp.int32), tiles.astype(jnp.int32)

    own, before, after, far = far_gather(prev_solution)
    sibling = other_core(prev_solution)
    early = jnp.stack([inverses[0].reshape(512, 256), coupling.reshape(512, 256)])
    panels = lax.all_gather(early, "col")
    late_panels = spread_panel(inverses[1].reshape(512, 256))
    left = split_tiles(left_factor)
    pieces = [(prev_solution, 0), (prev_solution, 1), (sibling, 0), (sibling, 1)]
    started = products(order[:2], left, pieces)
    pieces = []
    for pair in (before, after):
        pieces += [(v, 0) for v in pair] + [(other_core(v), 0) for v in pair]
    started = products(order[2:6], left, pieces, started)
    pieces = [(v, 0) for v in far] + [(other_core(v), 0) for v in far]
    first, second = products(order[6:], left, pieces, started, last=True)

    sites = jnp.transpose(cross.reshape(1024, 512))
    sites = lax.dynamic_slice_in_dim(sites, 32 * col, 32, 0).astype(F32)
    first_sum = over_sites(first).astype(F32).sum(axis=0)
    second_sum = over_sites(second).astype(F32).sum(axis=0)
    first_rhs = (sites[:, :512] - first_sum).astype(BF)
    solved_first = gathered_stage(order, over_chips(over_cores(first_rhs)), panels, 0)
    pair = over_cores(solved_first)
    sent, pair = lax.optimization_barrier((solved_first, pair))
    every_first = all_sites(sent)
    base = sites[:, 512:] - second_sum
    second_rhs = gathered_stage(order, over_chips(pair), panels, 1, base)
    second_rhs, every_first = lax.optimization_barrier((second_rhs, every_first))
    moved = over_chips(over_cores(second_rhs))
    solved_second = spread_stage(order, tiles, moved, late_panels)
    every_second = all_sites(solved_second)
    outer = outer_part(solved_first, every_first) + outer_part(solved_second, every_second)
    pred_cov = prior_cov - row_sum(outer) / S
    return jnp.concatenate([in_rows(every_first), in_rows(every_second)]), pred_cov


def solution(mesh):
    placed = (
        P(None, "row", None, "col"),
        P("row", "col", None),
        P(None, "row", None),
        P(None, None, "row", None, "col"),
        P(None, "row", None, "col"),
        P("col", None),
    )
    return jax.shard_map(
        body,
        mesh=mesh,
        in_specs=placed,
        out_specs=(P(None, "row", None), P("col", None)),
        check_vma=False,
    )
```

time: 242 us -> 219 us (0.905)
  Pallas kernels: 59.9 us -> 29.3 us
  starting transfers between devices: 56.9 us -> 43.4 us
  between operations: 1.09 us -> 14.3 us
  waiting for transfers between devices: 57 us -> 68 us
  local copies, waits for them, and re-layouts: 28.6 us -> 17.9 us
  blocking collectives: 30.1 us -> 39 us
    pallas_call x5 -> x6, Pallas kernels: 43.6 us -> 25 us  [the longest x3 17.1 us: products(): pl.pallas_call(kernel, grid_spec=pltpu.PrefetchScalarGridSpec(num_scalar_...]
    pallas_call x1, Pallas kernels: 16.3 us -> 4.31 us  [split_tiles(): pl.pallas_call(split_tiles_kernel, grid=(rounds, tile // rows), in_specs=...]
    ppermute x8 -> x3, starting transfers between devices: 16.7 us -> 5.53 us  [z_shift(): lax.ppermute(v, 'col', [(c, c // 4 * 4 + (c + step) % 4) for c in range(1...]
    all_to_all x1, blocking collectives: 16 us -> 23.8 us  [over_sites(): return lax.all_to_all(partial.reshape(16, 32, 512), 'col', 0, 0, tiled=True)]
    slice x9 -> x2, local copies, waits for them, and re-layouts: 11.3 us -> 3.78 us  [the longest x1 1.95 us: far_gather(): low, high = (block[:, :128, :], block[:, 128:, :])]
    ppermute x8 -> x3, starting transfers between devices: 11.9 us -> 4.78 us  [y_shift(): lax.ppermute(v, 'col', [(c, (c // 4 + step) % 4 * 4 + c % 4) for c in ran...]
    all_to_all x1, waiting for transfers between devices: 0.42 us -> 7.4 us  [over_sites(): return lax.all_to_all(partial.reshape(16, 32, 512), 'col', 0, 0, tiled=True)]
    ppermute x8 -> x3, waiting for transfers between devices: 2.23 us -> 6.5 us  [z_shift(): lax.ppermute(v, 'col', [(c, c // 4 * 4 + (c + step) % 4) for c in range(1...]
  transfers between devices with their start and end apart: 47 -> 38, of which waited for: 22 -> 20; matrix products, arithmetic and copies ran while one was open for 11% -> 3% of each run, Pallas kernels for 21% -> 12%
where the time goes in v2:
time: 219 us
  waiting for transfers between devices  68 us (31%)
  starting transfers between devices  43.4 us (20%)
  blocking collectives  39 us (18%)
  Pallas kernels  29.3 us (13%)
  local copies, waits for them, and re-layouts  17.9 us (8%)
  between operations  14.3 us (7%)
  other arithmetic  5.05 us (2%)
    ppermute x18, waiting for transfers between devices, x_shift(): return lax.ppermute(v, 'row', [(r, (r + 2 * step) % 8) for r in range(8)])  42.1 us
    all_to_all x1, blocking collectives, over_sites(): return lax.all_to_all(partial.reshape(16, 32, 512), 'col', 0, 0, tiled=True)  23.8 us
    ppermute x18, starting transfers between devices, x_shift(): return lax.ppermute(v, 'row', [(r, (r + 2 * step) % 8) for r in range(8)])  20.9 us
    pallas_call x3, Pallas kernels, products(): pl.pallas_call(kernel, grid_spec=pltpu.PrefetchScalarGridSpec(num_scalar_...  17.1 us
    all_to_all x1, blocking collectives, all_sites(): return lax.all_to_all(sent, 'col', 0, 0, tiled=True).reshape(512, 512)  15.2 us
    unnamed x15, local copies, waits for them, and re-layouts  11.5 us
    all_to_all x1, waiting for transfers between devices, all_sites(): return lax.all_to_all(sent, 'col', 0, 0, tiled=True).reshape(512, 512)  9.6 us
    all_to_all x1, waiting for transfers between devices, over_sites(): return lax.all_to_all(partial.reshape(16, 32, 512), 'col', 0, 0, tiled=True)  7.4 us
  transfers between devices with their start and end apart: 38, of which 20 were waited for; matrix products, arithmetic and copies ran while one was open for 3% of the time, Pallas kernels for 12%

profile of v2, /device:TPU:0, one launch (start us, length us, event | category | flops | bytes accessed | tf_op | source)
XLA Modules:
  0.0 218.6 jit_solution(17653628172792959942)
XLA Ops:
  18.2 8.1 %collective-permute-done.1.refs_0_ = bf16[3,128,512]{2,1,0:T(8,128)(2,1)S(1)} collective-permute-done((bf16[3,128,512]{2,1,0:T(8,128)(2,1)}, bf16[3,128,512]{2,1,0:T(8,128)(2,1)S(1)}, u32[]{:S(2)}, u32[]{:S(2)}) %collective-permute-start.1) | collective-permute-done | bytes 393248 | tf_op jit(solution)/shard_map/ppermute | solution.py:17
  26.3 8.0 %collective-permute-done.2.refs_1_ = bf16[3,128,512]{2,1,0:T(8,128)(2,1)S(1)} collective-permute-done((bf16[3,128,512]{2,1,0:T(8,128)(2,1)S(1)}, bf16[3,128,512]{2,1,0:T(8,128)(2,1)S(1)}, u32[]{:S(2)}, u32[]{:S(2)}) %collective-permute-start.2) | collective-permute-done | bytes 393248 | tf_op jit(solution)/shard_map/ppermute | solution.py:17
  34.6 2.9 %collective-permute-start.10 = (bf16[3,128,512]{2,1,0:T(8,128)(2,1)S(1)}, bf16[3,128,512]{2,1,0:T(8,128)(2,1)}, u32[]{:S(2)}, u32[]{:S(2)}) collective-permute-start(bf16[3,128,512]{2,1,0:T(8,128)(2,1)S(1)} %collective-permute-done.6.refs_5_), channel_id=1, source_target_pairs={{0,96},{16,112},{32,0},{48,16},{64,32},{80,48},{96,64},{112,80},{1... | collective-permute-start | bytes 1179656 | tf_op jit(solution)/shard_map/ppermute | solution.py:17
  38.2 4.6 %copy-done.3 = bf16[4,256,24,256]{3,2,1,0:T(8,128)(2,1)S(1)} copy-done((bf16[4,256,24,256]{3,2,1,0:T(8,128)(2,1)S(1)}, bf16[4,256,24,256]{3,2,1,0:T(8,128)(2,1)}, u32[]{:S(2)}) %copy-start.3) | copy-done | bytes 12582936
  42.8 4.3 %shard_map.77 = bf16[24,4,256,256]{3,2,1,0:T(8,128)(2,1)S(1)} custom-call(bf16[4,256,24,256]{3,2,1,0:T(8,128)(2,1)S(1)} %copy-done.3), custom_call_target="tpu_custom_call" | custom-call | bytes 25165824 | tf_op jit(solution)/shard_map/pallas_call | solution.py:48
  47.8 3.4 %shard_map.78.before = f32[1024,512]{1,0:T(8,128)S(1)} custom-call(s32[2]{0:T(128)S(1)} %pad_add_fusion.2.order, bf16[24,1024,256]{2,1,0:T(8,128)(2,1)S(1)} %bitcast.56, bf16[3,256,512]{2,1,0:T(8,128)(2,1)S(1)} %copy-done.4, bf16[3,256,512]{2,1,0:T(8,128)(2,1)S(1)} %copy-done.4, bf16[3,256,512]{2,1,0:T(8,128)(2,1)S(1)} %collective-permute-done.refs_2_.refs_3_, ...), custom_call_target="tpu_custom_call" | custom-call | flops 1610612736 | bytes 6815744 | tf_op jit(solution)/shard_map/pallas_call | solution.py:141
  51.3 8.1 %shard_map.79.before = f32[1024,512]{1,0:T(8,128)S(1)} custom-call(s32[4]{0:T(128)S(1)} %pad_add_fusion.1.order, bf16[24,1024,256]{2,1,0:T(8,128)(2,1)S(1)} %bitcast.57, f32[1024,512]{1,0:T(8,128)S(1)} %shard_map.78.before, bf16[3,128,512]{2,1,0:T(8,128)(2,1)S(1)} %collective-permute-done.1.refs_0_, bf16[3,128,512]{2,1,0:T(8,128)(2,1)S(1)} %collective-permute-done.2.refs_1_, ...), custom_call_target="tpu_custom_call" | custom-call | flops 3221225472 | bytes 11534336 | tf_op jit(solution)/shard_map/pallas_call | solution.py:141
  59.4 5.6 %shard_map.80 = (bf16[512,512]{1,0:T(8,128)(2,1)}, bf16[512,512]{1,0:T(8,128)(2,1)S(1)}) custom-call(s32[2]{0:T(128)S(1)} %pad_add_fusion.order, bf16[24,1024,256]{2,1,0:T(8,128)(2,1)S(1)} %bitcast.58, f32[1024,512]{1,0:T(8,128)S(1)} %shard_map.79.before, bf16[3,128,512]{2,1,0:T(8,128)(2,1)S(1)} %collective-permute-done.9.refs_0_, ...), custom_call_target="tpu_custom_call" | custom-call | flops 1610612736 | bytes 6815744 | tf_op jit(solution)/shard_map/pallas_call | solution.py:141
  65.0 23.8 %all_to_all.20 = bf16[16,32,512]{2,1,0:T(8,128)(2,1)S(1)} all-to-all(bf16[16,32,512]{2,1,0:T(8,128)(2,1)S(1)} %bitcast.62), channel_id=1, replica_groups=mesh['row'=8,'col'=16] {'col'}, dimensions={0} | all-to-all | bytes 1048576 | tf_op jit(solution)/shard_map/all_to_all | solution.py:271
  88.8 5.8 %all-to-all-start = ((bf16[16,32,512]{2,1,0:T(8,128)(2,1)}), bf16[16,32,512]{2,1,0:T(8,128)(2,1)S(1)}, u32[]{:S(2)}, u32[]{:S(2)}) async-start(bf16[16,32,512]{2,1,0:T(8,128)(2,1)} %bitcast.11), calls=%async_computation | async-start | bytes 1048576 | tf_op jit(solution)/shard_map/all_to_all | solution.py:271
  94.6 3.5 %collective-permute-start.27 = (bf16[512,256]{1,0:T(8,128)(2,1)S(1)}, bf16[512,256]{1,0:T(8,128)(2,1)S(1)}, u32[]{:S(2)}, u32[]{:S(2)}) collective-permute-start(bf16[512,256]{1,0:T(8,128)(2,1)S(1)} %bitcast.69), channel_id=1, source_target_pairs={{0,2},{1,3},{2,0},{3,1},{4,6},{5,7},{6,4},{7,5},{8,10},{9,11},{10,... | collective-permute-start | bytes 786440 | tf_op jit(solution)/shard_map/ppermute | solution.py:29
  100.5 7.4 %all-to-all-done = bf16[16,32,512]{2,1,0:T(8,128)(2,1)S(1)} async-done(((bf16[16,32,512]{2,1,0:T(8,128)(2,1)}), bf16[16,32,512]{2,1,0:T(8,128)(2,1)S(1)}, u32[]{:S(2)}, u32[]{:S(2)}) %all-to-all-start) | async-done | bytes 524320 | tf_op jit(solution)/shard_map/all_to_all | solution.py:271
  108.3 2.5 %collective-permute-done.27 = bf16[512,256]{1,0:T(8,128)(2,1)S(1)} collective-permute-done((bf16[512,256]{1,0:T(8,128)(2,1)S(1)}, bf16[512,256]{1,0:T(8,128)(2,1)S(1)}, u32[]{:S(2)}, u32[]{:S(2)}) %collective-permute-start.27) | collective-permute-done | bytes 262176 | tf_op jit(solution)/shard_map/ppermute | solution.py:29
  110.8 3.3 %collective-permute-done.26 = bf16[512,256]{1,0:T(8,128)(2,1)S(1)} collective-permute-done((bf16[512,256]{1,0:T(8,128)(2,1)S(1)}, bf16[512,256]{1,0:T(8,128)(2,1)S(1)}, u32[]{:S(2)}, u32[]{:S(2)}) %collective-permute-start.26) | collective-permute-done | bytes 262176 | tf_op jit(solution)/shard_map/ppermute | solution.py:29
  120.8 3.2 %collective-permute-start.15 = (bf16[2,32,512]{2,1,0:T(8,128)(2,1)S(1)}, bf16[2,32,512]{2,1,0:T(8,128)(2,1)S(1)}, u32[]{:S(2)}, u32[]{:S(2)}) collective-permute-start(bf16[2,32,512]{2,1,0:T(8,128)(2,1)S(1)} %pad_maximum_fusion.3.refs_1_), channel_id=1, source_target_pairs={{0,96},{16,112},{32,0},{48,16},{64,32},{80,48},{96,64},{112,80},{1... | collective-permute-start | bytes 196616 | tf_op jit(solution)/shard_map/ppermute | solution.py:17
  124.0 2.2 %collective-permute-done.14.refs_2_ = bf16[2,32,512]{2,1,0:T(8,128)(2,1)S(1)} collective-permute-done((bf16[2,32,512]{2,1,0:T(8,128)(2,1)S(1)}, bf16[2,32,512]{2,1,0:T(8,128)(2,1)S(1)}, u32[]{:S(2)}, u32[]{:S(2)}) %collective-permute-start.14) | collective-permute-done | bytes 65568 | tf_op jit(solution)/shard_map/ppermute | solution.py:17
  126.5 5.5 %collective-permute-done.16.refs_4_ = bf16[2,32,512]{2,1,0:T(8,128)(2,1)S(1)} collective-permute-done((bf16[2,32,512]{2,1,0:T(8,128)(2,1)S(1)}, bf16[2,32,512]{2,1,0:T(8,128)(2,1)S(1)}, u32[]{:S(2)}, u32[]{:S(2)}) %collective-permute-start.16) | collective-permute-done | bytes 65568 | tf_op jit(solution)/shard_map/ppermute | solution.py:17
  132.0 3.4 %copy-done.1 = bf16[32,512,256]{2,1,0:T(8,128)(2,1)S(1)} copy-done((bf16[32,512,256]{2,1,0:T(8,128)(2,1)S(1)}, bf16[32,512,256]{2,1,0:T(8,128)(2,1)}, u32[]{:S(2)}) %copy-start.1) | copy-done | bytes 8388632
  135.4 2.5 %shard_map.81 = bf16[32,512]{1,0:T(8,128)(2,1)S(1)} custom-call(s32[8]{0:T(128)S(1)} %stack.134.refs_0_.order, bf16[2,32,512]{2,1,0:T(8,128)(2,1)S(1)} %pad_maximum_fusion.3.refs_1_, bf16[2,32,512]{2,1,0:T(8,128)(2,1)S(1)} %collective-permute-done.14.refs_2_, bf16[2,32,512]{2,1,0:T(8,128)(2,1)S(1)} %collective-permute-done.15.refs_3_, ...), custom_call_target="tpu_custom_call" | custom-call | flops 134217728 | bytes 4194304 | tf_op jit(solution)/shard_map/pallas_call | solution.py:241
  140.0 4.7 %all-to-all-start.2 = ((bf16[16,32,512]{2,1,0:T(8,128)(2,1)}), bf16[16,32,512]{2,1,0:T(8,128)(2,1)}, u32[]{:S(2)}, u32[]{:S(2)}) async-start(bf16[16,32,512]{2,1,0:T(8,128)(2,1)} %broadcast_in_dim.4), calls=%async_computation.2 | async-start | bytes 1048576 | tf_op jit(solution)/shard_map/all_to_all | solution.py:276
  144.8 3.2 %collective-permute-start.19 = (bf16[2,32,512]{2,1,0:T(8,128)(2,1)S(1)}, bf16[2,32,512]{2,1,0:T(8,128)(2,1)S(1)}, u32[]{:S(2)}, u32[]{:S(2)}) collective-permute-start(bf16[2,32,512]{2,1,0:T(8,128)(2,1)S(1)} %pad_maximum_fusion.4.refs_1_), channel_id=1, source_target_pairs={{0,96},{16,112},{32,0},{48,16},{64,32},{80,48},{96,64},{112,80},{1... | collective-permute-start | bytes 196616 | tf_op jit(solution)/shard_map/ppermute | solution.py:17
  148.0 2.2 %collective-permute-done.18.refs_2_ = bf16[2,32,512]{2,1,0:T(8,128)(2,1)S(1)} collective-permute-done((bf16[2,32,512]{2,1,0:T(8,128)(2,1)S(1)}, bf16[2,32,512]{2,1,0:T(8,128)(2,1)S(1)}, u32[]{:S(2)}, u32[]{:S(2)}) %collective-permute-start.18) | collective-permute-done | bytes 65568 | tf_op jit(solution)/shard_map/ppermute | solution.py:17
  150.5 5.5 %collective-permute-done.20.refs_4_ = bf16[2,32,512]{2,1,0:T(8,128)(2,1)S(1)} collective-permute-done((bf16[2,32,512]{2,1,0:T(8,128)(2,1)S(1)}, bf16[2,32,512]{2,1,0:T(8,128)(2,1)S(1)}, u32[]{:S(2)}, u32[]{:S(2)}) %collective-permute-start.20) | collective-permute-done | bytes 65568 | tf_op jit(solution)/shard_map/ppermute | solution.py:17
  156.0 3.4 %copy-done.2 = bf16[32,512,256]{2,1,0:T(8,128)(2,1)S(1)} copy-done((bf16[32,512,256]{2,1,0:T(8,128)(2,1)S(1)}, bf16[32,512,256]{2,1,0:T(8,128)(2,1)}, u32[]{:S(2)}) %copy-start.2) | copy-done | bytes 8388632
  159.4 2.5 %shard_map.82 = bf16[32,512]{1,0:T(8,128)(2,1)S(1)} custom-call(s32[8]{0:T(128)S(1)} %stack.134.refs_0_.order, bf16[2,32,512]{2,1,0:T(8,128)(2,1)S(1)} %pad_maximum_fusion.4.refs_1_, bf16[2,32,512]{2,1,0:T(8,128)(2,1)S(1)} %collective-permute-done.18.refs_2_, bf16[2,32,512]{2,1,0:T(8,128)(2,1)S(1)} %collective-permute-done.19.refs_3_, ...), custom_call_target="tpu_custom_call" | custom-call | flops 134217728 | bytes 4194304 | tf_op jit(solution)/shard_map/pallas_call | solution.py:241
  161.9 9.6 %all-to-all-done.2 = bf16[16,32,512]{2,1,0:T(8,128)(2,1)} async-done(((bf16[16,32,512]{2,1,0:T(8,128)(2,1)}), bf16[16,32,512]{2,1,0:T(8,128)(2,1)}, u32[]{:S(2)}, u32[]{:S(2)}) %all-to-all-start.2) | async-done | bytes 524320 | tf_op jit(solution)/shard_map/all_to_all | solution.py:276
  172.8 3.2 %collective-permute-start.23 = (bf16[2,32,512]{2,1,0:T(8,128)(2,1)S(1)}, bf16[2,32,512]{2,1,0:T(8,128)(2,1)S(1)}, u32[]{:S(2)}, u32[]{:S(2)}) collective-permute-start(bf16[2,32,512]{2,1,0:T(8,128)(2,1)S(1)} %pad_maximum_fusion.5.own), channel_id=1, source_target_pairs={{0,96},{16,112},{32,0},{48,16},{64,32},{80,48},{96,64},{112,80},{1... | collective-permute-start | bytes 196616 | tf_op jit(solution)/shard_map/ppermute | solution.py:17
  178.4 3.4 %collective-permute-done.24.three = bf16[2,32,512]{2,1,0:T(8,128)(2,1)S(1)} collective-permute-done((bf16[2,32,512]{2,1,0:T(8,128)(2,1)S(1)}, bf16[2,32,512]{2,1,0:T(8,128)(2,1)S(1)}, u32[]{:S(2)}, u32[]{:S(2)}) %collective-permute-start.24) | collective-permute-done | bytes 65568 | tf_op jit(solution)/shard_map/ppermute | solution.py:17
  181.8 2.9 %shard_map.83 = bf16[32,512]{1,0:T(8,128)(2,1)S(1)} custom-call(s32[8]{0:T(128)S(1)} %stack.134.refs_0_.order, s32[16]{0:T(128)S(1)} %stack.161.tiles, bf16[2,32,512]{2,1,0:T(8,128)(2,1)S(1)} %pad_maximum_fusion.5.own, bf16[2,32,512]{2,1,0:T(8,128)(2,1)S(1)} %collective-permute-done.22.one, bf16[2,32,512]{2,1,0:T(8,128)(2,1)S(1)} %collective-permute-done.23.two, ...), custom_call_target="tpu_custom_call" | custom-call | flops 134217728 | bytes 4194304 | tf_op jit(solution)/shard_map/pallas_call | solution.py:259
  184.7 15.2 %all_to_all.21 = bf16[16,32,512]{2,1,0:T(8,128)(2,1)S(1)} all-to-all(bf16[16,32,512]{2,1,0:T(8,128)(2,1)S(1)} %broadcast_in_dim.5), channel_id=1, replica_groups=mesh['row'=8,'col'=16] {'col'}, dimensions={0} | all-to-all | bytes 1048576 | tf_op jit(solution)/shard_map/all_to_all | solution.py:276
  203.4 2.2 collective-permute-start.33
  206.7 2.5 %collective-permute-done.34 = f32[32,512]{1,0:T(8,128)S(1)} collective-permute-done((f32[32,512]{1,0:T(8,128)S(1)}, f32[32,512]{1,0:T(8,128)S(1)}, u32[]{:S(2)}, u32[]{:S(2)}) %collective-permute-start.34) | collective-permute-done | bytes 65568 | tf_op jit(solution)/shard_map/ppermute | solution.py:17
  (95 shorter events, 35.6 us)
Async XLA Ops:
  7.2 124.8 %all-gather.3.cloned.1.call-start = ((), (), s32[]{:S(2)}) async-start(), calls=%async_computation.4 | async-start | bytes 8912896 | tf_op jit(solution)/shard_map/all_gather | solution.py:303
  10.9 26.7 %collective-permute-start = (bf16[3,256,512]{2,1,0:T(8,128)(2,1)}, bf16[3,256,512]{2,1,0:T(8,128)(2,1)S(1)}, u32[]{:S(2)}, u32[]{:S(2)}) collective-permute-start(bf16[3,256,512]{2,1,0:T(8,128)(2,1)} %refs_1_.1), channel_id=1, source_target_pairs={{0,16},{16,0},{32,48},{48,32},{64,80},{80,64},{96,112},{112,96},{1... | collective-permute-start | bytes 2359304 | tf_op jit(solution)/shard_map/ppermute | solution.py:21
  12.9 13.3 %collective-permute-start.1 = (bf16[3,128,512]{2,1,0:T(8,128)(2,1)}, bf16[3,128,512]{2,1,0:T(8,128)(2,1)S(1)}, u32[]{:S(2)}, u32[]{:S(2)}) collective-permute-start(bf16[3,128,512]{2,1,0:T(8,128)(2,1)} %get-tuple-element.15), channel_id=1, source_target_pairs={{0,32},{16,48},{32,64},{48,80},{64,96},{80,112},{96,0},{112,16},{1... | collective-permute-start | bytes 1179656 | tf_op jit(solution)/shard_map/ppermute | solution.py:17
  14.5 19.8 %collective-permute-start.2 = (bf16[3,128,512]{2,1,0:T(8,128)(2,1)S(1)}, bf16[3,128,512]{2,1,0:T(8,128)(2,1)S(1)}, u32[]{:S(2)}, u32[]{:S(2)}) collective-permute-start(bf16[3,128,512]{2,1,0:T(8,128)(2,1)S(1)} %get-tuple-element.14), channel_id=1, source_target_pairs={{0,32},{16,48},{32,64},{48,80},{64,96},{80,112},{96,0},{112,16},{1... | collective-permute-start | bytes 1179656 | tf_op jit(solution)/shard_map/ppermute | solution.py:17
  16.0 18.7 %collective-permute-start.6 = (bf16[3,128,512]{2,1,0:T(8,128)(2,1)S(1)}, bf16[3,128,512]{2,1,0:T(8,128)(2,1)S(1)}, u32[]{:S(2)}, u32[]{:S(2)}) collective-permute-start(bf16[3,128,512]{2,1,0:T(8,128)(2,1)S(1)} %get-tuple-element.14), channel_id=1, source_target_pairs={{0,96},{16,112},{32,0},{48,16},{64,32},{80,48},{96,64},{112,80},{1... | collective-permute-start | bytes 1179656 | tf_op jit(solution)/shard_map/ppermute | solution.py:17
  17.7 19.8 %collective-permute-start.5 = (bf16[3,128,512]{2,1,0:T(8,128)(2,1)}, bf16[3,128,512]{2,1,0:T(8,128)(2,1)}, u32[]{:S(2)}, u32[]{:S(2)}) collective-permute-start(bf16[3,128,512]{2,1,0:T(8,128)(2,1)} %get-tuple-element.15), channel_id=1, source_target_pairs={{0,96},{16,112},{32,0},{48,16},{64,32},{80,48},{96,64},{112,80},{1... | collective-permute-start | bytes 1179656 | tf_op jit(solution)/shard_map/ppermute | solution.py:17
  26.3 11.8 %collective-permute-start.3 = (bf16[3,128,512]{2,1,0:T(8,128)(2,1)S(1)}, bf16[3,128,512]{2,1,0:T(8,128)(2,1)}, u32[]{:S(2)}, u32[]{:S(2)}) collective-permute-start(bf16[3,128,512]{2,1,0:T(8,128)(2,1)S(1)} %collective-permute-done.1.refs_0_), channel_id=1, source_target_pairs={{0,16},{16,0},{32,48},{48,32},{64,80},{80,64},{96,112},{112,96},{1... | collective-permute-start | bytes 1179656 | tf_op jit(solution)/shard_map/ppermute | solution.py:21
  34.3 13.0 %collective-permute-start.9 = (bf16[3,128,512]{2,1,0:T(8,128)(2,1)S(1)}, bf16[3,128,512]{2,1,0:T(8,128)(2,1)S(1)}, u32[]{:S(2)}, u32[]{:S(2)}) collective-permute-start(bf16[3,128,512]{2,1,0:T(8,128)(2,1)S(1)} %collective-permute-done.1.refs_0_), channel_id=1, source_target_pairs={{0,32},{16,48},{32,64},{48,80},{64,96},{80,112},{96,0},{112,16},{1... | collective-permute-start | bytes 1179656 | tf_op jit(solution)/shard_map/ppermute | solution.py:17
  34.6 13.1 %collective-permute-start.10 = (bf16[3,128,512]{2,1,0:T(8,128)(2,1)S(1)}, bf16[3,128,512]{2,1,0:T(8,128)(2,1)}, u32[]{:S(2)}, u32[]{:S(2)}) collective-permute-start(bf16[3,128,512]{2,1,0:T(8,128)(2,1)S(1)} %collective-permute-done.6.refs_5_), channel_id=1, source_target_pairs={{0,96},{16,112},{32,0},{48,16},{64,32},{80,48},{96,64},{112,80},{1... | collective-permute-start | bytes 1179656 | tf_op jit(solution)/shard_map/ppermute | solution.py:17
  37.5 13.8 %collective-permute-start.8 = (bf16[3,128,512]{2,1,0:T(8,128)(2,1)S(1)}, bf16[3,128,512]{2,1,0:T(8,128)(2,1)}, u32[]{:S(2)}, u32[]{:S(2)}) collective-permute-start(bf16[3,128,512]{2,1,0:T(8,128)(2,1)S(1)} %collective-permute-done.6.refs_5_), channel_id=1, source_target_pairs={{0,16},{16,0},{32,48},{48,32},{64,80},{80,64},{96,112},{112,96},{1... | collective-permute-start | bytes 1179656 | tf_op jit(solution)/shard_map/ppermute | solution.py:21
  37.5 13.7 %collective-permute-start.4 = (bf16[3,128,512]{2,1,0:T(8,128)(2,1)S(1)}, bf16[3,128,512]{2,1,0:T(8,128)(2,1)}, u32[]{:S(2)}, u32[]{:S(2)}) collective-permute-start(bf16[3,128,512]{2,1,0:T(8,128)(2,1)S(1)} %collective-permute-done.2.refs_1_), channel_id=1, source_target_pairs={{0,16},{16,0},{32,48},{48,32},{64,80},{80,64},{96,112},{112,96},{1... | collective-permute-start | bytes 1179656 | tf_op jit(solution)/shard_map/ppermute | solution.py:21
  38.0 13.2 %collective-permute-start.7 = (bf16[3,128,512]{2,1,0:T(8,128)(2,1)}, bf16[3,128,512]{2,1,0:T(8,128)(2,1)}, u32[]{:S(2)}, u32[]{:S(2)}) collective-permute-start(bf16[3,128,512]{2,1,0:T(8,128)(2,1)} %collective-permute-done.5.refs_4_), channel_id=1, source_target_pairs={{0,16},{16,0},{32,48},{48,32},{64,80},{80,64},{96,112},{112,96},{1... | collective-permute-start | bytes 1179656 | tf_op jit(solution)/shard_map/ppermute | solution.py:21
  47.3 12.1 %collective-permute-start.11 = (bf16[3,128,512]{2,1,0:T(8,128)(2,1)S(1)}, bf16[3,128,512]{2,1,0:T(8,128)(2,1)S(1)}, u32[]{:S(2)}, u32[]{:S(2)}) collective-permute-start(bf16[3,128,512]{2,1,0:T(8,128)(2,1)S(1)} %collective-permute-done.9.refs_0_), channel_id=1, source_target_pairs={{0,16},{16,0},{32,48},{48,32},{64,80},{80,64},{96,112},{112,96},{1... | collective-permute-start | bytes 1179656 | tf_op jit(solution)/shard_map/ppermute | solution.py:21
  47.7 11.7 %collective-permute-start.12 = (bf16[3,128,512]{2,1,0:T(8,128)(2,1)}, bf16[3,128,512]{2,1,0:T(8,128)(2,1)S(1)}, u32[]{:S(2)}, u32[]{:S(2)}) collective-permute-start(bf16[3,128,512]{2,1,0:T(8,128)(2,1)} %collective-permute-done.10.refs_1_), channel_id=1, source_target_pairs={{0,16},{16,0},{32,48},{48,32},{64,80},{80,64},{96,112},{112,96},{1... | collective-permute-start | bytes 1179656 | tf_op jit(solution)/shard_map/ppermute | solution.py:21
  88.8 19.1 %all-to-all-start = ((bf16[16,32,512]{2,1,0:T(8,128)(2,1)}), bf16[16,32,512]{2,1,0:T(8,128)(2,1)S(1)}, u32[]{:S(2)}, u32[]{:S(2)}) async-start(bf16[16,32,512]{2,1,0:T(8,128)(2,1)} %bitcast.11), calls=%async_computation | async-start | bytes 1048576 | tf_op jit(solution)/shard_map/all_to_all | solution.py:271
  94.6 16.2 %collective-permute-start.27 = (bf16[512,256]{1,0:T(8,128)(2,1)S(1)}, bf16[512,256]{1,0:T(8,128)(2,1)S(1)}, u32[]{:S(2)}, u32[]{:S(2)}) collective-permute-start(bf16[512,256]{1,0:T(8,128)(2,1)S(1)} %bitcast.69), channel_id=1, source_target_pairs={{0,2},{1,3},{2,0},{3,1},{4,6},{5,7},{6,4},{7,5},{8,10},{9,11},{10,... | collective-permute-start | bytes 786440 | tf_op jit(solution)/shard_map/ppermute | solution.py:29
  98.1 16.0 %collective-permute-start.26 = (bf16[512,256]{1,0:T(8,128)(2,1)S(1)}, bf16[512,256]{1,0:T(8,128)(2,1)S(1)}, u32[]{:S(2)}, u32[]{:S(2)}) collective-permute-start(bf16[512,256]{1,0:T(8,128)(2,1)S(1)} %bitcast.70), channel_id=1, source_target_pairs={{0,3},{1,0},{2,1},{3,2},{4,7},{5,4},{6,5},{7,6},{8,11},{9,8},{10,9... | collective-permute-start | bytes 786440 | tf_op jit(solution)/shard_map/ppermute | solution.py:29
  99.3 15.5 %collective-permute-start.25 = (bf16[512,256]{1,0:T(8,128)(2,1)S(1)}, bf16[512,256]{1,0:T(8,128)(2,1)}, u32[]{:S(2)}, u32[]{:S(2)}) collective-permute-start(bf16[512,256]{1,0:T(8,128)(2,1)S(1)} %bitcast.71), channel_id=1, source_target_pairs={{0,1},{1,2},{2,3},{3,0},{4,5},{5,6},{6,7},{7,4},{8,9},{9,10},{10,1... | collective-permute-start | bytes 786440 | tf_op jit(solution)/shard_map/ppermute | solution.py:29
  108.0 12.6 %collective-permute-start.13 = (bf16[32,512]{1,0:T(8,128)(2,1)S(1)}, bf16[32,512]{1,0:T(8,128)(2,1)S(1)}, u32[]{:S(2)}, u32[]{:S(2)}) collective-permute-start(bf16[32,512]{1,0:T(8,128)(2,1)S(1)} %get-tuple-element.19), channel_id=1, source_target_pairs={{0,16},{16,0},{32,48},{48,32},{64,80},{80,64},{96,112},{112,96},{1... | collective-permute-start | bytes 98312 | tf_op jit(solution)/shard_map/ppermute | solution.py:21
  115.9 60.2 %collective-permute-start.28 = (bf16[4,512,256]{2,1,0:T(8,128)(2,1)S(1)}, bf16[4,512,256]{2,1,0:T(8,128)(2,1)S(1)}, u32[]{:S(2)}, u32[]{:S(2)}) collective-permute-start(bf16[4,512,256]{2,1,0:T(8,128)(2,1)S(1)} %pad_maximum_fusion.refs_0_), channel_id=1, source_target_pairs={{0,4},{1,5},{2,6},{3,7},{4,8},{5,9},{6,10},{7,11},{8,12},{9,13},{1... | collective-permute-start | bytes 3145736 | tf_op jit(solution)/shard_map/ppermute | solution.py:25
  117.4 58.7 %collective-permute-start.29 = (bf16[4,512,256]{2,1,0:T(8,128)(2,1)S(1)}, bf16[4,512,256]{2,1,0:T(8,128)(2,1)}, u32[]{:S(2)}, u32[]{:S(2)}) collective-permute-start(bf16[4,512,256]{2,1,0:T(8,128)(2,1)S(1)} %pad_maximum_fusion.refs_0_), channel_id=1, source_target_pairs={{0,12},{1,13},{2,14},{3,15},{4,0},{5,1},{6,2},{7,3},{8,4},{9,5},{1... | collective-permute-start | bytes 3145736 | tf_op jit(solution)/shard_map/ppermute | solution.py:25
  119.2 57.0 %collective-permute-start.30 = (bf16[4,512,256]{2,1,0:T(8,128)(2,1)S(1)}, bf16[4,512,256]{2,1,0:T(8,128)(2,1)}, u32[]{:S(2)}, u32[]{:S(2)}) collective-permute-start(bf16[4,512,256]{2,1,0:T(8,128)(2,1)S(1)} %pad_maximum_fusion.refs_0_), channel_id=1, source_target_pairs={{0,8},{1,9},{2,10},{3,11},{4,12},{5,13},{6,14},{7,15},{8,0},{9,1},... | collective-permute-start | bytes 3145736 | tf_op jit(solution)/shard_map/ppermute | solution.py:25
  120.7 5.5 %collective-permute-start.14 = (bf16[2,32,512]{2,1,0:T(8,128)(2,1)S(1)}, bf16[2,32,512]{2,1,0:T(8,128)(2,1)S(1)}, u32[]{:S(2)}, u32[]{:S(2)}) collective-permute-start(bf16[2,32,512]{2,1,0:T(8,128)(2,1)S(1)} %pad_maximum_fusion.3.refs_1_), channel_id=1, source_target_pairs={{0,32},{16,48},{32,64},{48,80},{64,96},{80,112},{96,0},{112,16},{1... | collective-permute-start | bytes 196616 | tf_op jit(solution)/shard_map/ppermute | solution.py:17
  120.8 5.7 %collective-permute-start.15 = (bf16[2,32,512]{2,1,0:T(8,128)(2,1)S(1)}, bf16[2,32,512]{2,1,0:T(8,128)(2,1)S(1)}, u32[]{:S(2)}, u32[]{:S(2)}) collective-permute-start(bf16[2,32,512]{2,1,0:T(8,128)(2,1)S(1)} %pad_maximum_fusion.3.refs_1_), channel_id=1, source_target_pairs={{0,96},{16,112},{32,0},{48,16},{64,32},{80,48},{96,64},{112,80},{1... | collective-permute-start | bytes 196616 | tf_op jit(solution)/shard_map/ppermute | solution.py:17
  126.2 5.8 %collective-permute-start.16 = (bf16[2,32,512]{2,1,0:T(8,128)(2,1)S(1)}, bf16[2,32,512]{2,1,0:T(8,128)(2,1)S(1)}, u32[]{:S(2)}, u32[]{:S(2)}) collective-permute-start(bf16[2,32,512]{2,1,0:T(8,128)(2,1)S(1)} %pad_maximum_fusion.3.refs_1_), channel_id=1, source_target_pairs={{0,64},{16,80},{32,96},{48,112},{64,0},{80,16},{96,32},{112,48},{1... | collective-permute-start | bytes 196616 | tf_op jit(solution)/shard_map/ppermute | solution.py:17
  140.0 31.5 %all-to-all-start.2 = ((bf16[16,32,512]{2,1,0:T(8,128)(2,1)}), bf16[16,32,512]{2,1,0:T(8,128)(2,1)}, u32[]{:S(2)}, u32[]{:S(2)}) async-start(bf16[16,32,512]{2,1,0:T(8,128)(2,1)} %broadcast_in_dim.4), calls=%async_computation.2 | async-start | bytes 1048576 | tf_op jit(solution)/shard_map/all_to_all | solution.py:276
  144.8 5.7 %collective-permute-start.19 = (bf16[2,32,512]{2,1,0:T(8,128)(2,1)S(1)}, bf16[2,32,512]{2,1,0:T(8,128)(2,1)S(1)}, u32[]{:S(2)}, u32[]{:S(2)}) collective-permute-start(bf16[2,32,512]{2,1,0:T(8,128)(2,1)S(1)} %pad_maximum_fusion.4.refs_1_), channel_id=1, source_target_pairs={{0,96},{16,112},{32,0},{48,16},{64,32},{80,48},{96,64},{112,80},{1... | collective-permute-start | bytes 196616 | tf_op jit(solution)/shard_map/ppermute | solution.py:17
  150.2 5.8 %collective-permute-start.20 = (bf16[2,32,512]{2,1,0:T(8,128)(2,1)S(1)}, bf16[2,32,512]{2,1,0:T(8,128)(2,1)S(1)}, u32[]{:S(2)}, u32[]{:S(2)}) collective-permute-start(bf16[2,32,512]{2,1,0:T(8,128)(2,1)S(1)} %pad_maximum_fusion.4.refs_1_), channel_id=1, source_target_pairs={{0,64},{16,80},{32,96},{48,112},{64,0},{80,16},{96,32},{112,48},{1... | collective-permute-start | bytes 196616 | tf_op jit(solution)/shard_map/ppermute | solution.py:17
  172.8 5.6 %collective-permute-start.23 = (bf16[2,32,512]{2,1,0:T(8,128)(2,1)S(1)}, bf16[2,32,512]{2,1,0:T(8,128)(2,1)S(1)}, u32[]{:S(2)}, u32[]{:S(2)}) collective-permute-start(bf16[2,32,512]{2,1,0:T(8,128)(2,1)S(1)} %pad_maximum_fusion.5.own), channel_id=1, source_target_pairs={{0,96},{16,112},{32,0},{48,16},{64,32},{80,48},{96,64},{112,80},{1... | collective-permute-start | bytes 196616 | tf_op jit(solution)/shard_map/ppermute | solution.py:17
  176.0 5.8 %collective-permute-start.24 = (bf16[2,32,512]{2,1,0:T(8,128)(2,1)S(1)}, bf16[2,32,512]{2,1,0:T(8,128)(2,1)S(1)}, u32[]{:S(2)}, u32[]{:S(2)}) collective-permute-start(bf16[2,32,512]{2,1,0:T(8,128)(2,1)S(1)} %pad_maximum_fusion.5.own), channel_id=1, source_target_pairs={{0,64},{16,80},{32,96},{48,112},{64,0},{80,16},{96,32},{112,48},{1... | collective-permute-start | bytes 196616 | tf_op jit(solution)/shard_map/ppermute | solution.py:17
  203.1 6.1 %collective-permute-start.34 = (f32[32,512]{1,0:T(8,128)S(1)}, f32[32,512]{1,0:T(8,128)S(1)}, u32[]{:S(2)}, u32[]{:S(2)}) collective-permute-start(f32[32,512]{1,0:T(8,128)S(1)} %add.281), channel_id=1, source_target_pairs={{0,64},{16,80},{32,96},{48,112},{64,0},{80,16},{96,32},{112,48},{1... | collective-permute-start | bytes 196616 | tf_op jit(solution)/shard_map/ppermute | solution.py:17
  203.4 5.8 %collective-permute-start.33 = (f32[32,512]{1,0:T(8,128)S(1)}, f32[32,512]{1,0:T(8,128)S(1)}, u32[]{:S(2)}, u32[]{:S(2)}) collective-permute-start(f32[32,512]{1,0:T(8,128)S(1)} %add.281), channel_id=1, source_target_pairs={{0,96},{16,112},{32,0},{48,16},{64,32},{80,48},{96,64},{112,80},{1... | collective-permute-start | bytes 196616 | tf_op jit(solution)/shard_map/ppermute | solution.py:17
  (13 other events, 216.9 us)
Sparse Core Ops, SparseCore 0:
  11.0 78.9 all-gather.2

commit v3 on v2

--- a/solution.py
+++ b/solution.py
@@ -50,7 +50,7 @@
         grid=(rounds, tile // rows),
         in_specs=[pl.BlockSpec((1, rows, count, width), lambda a, t: (a, t, 0, 0))],
         out_specs=pl.BlockSpec((count, 1, rows, width), lambda a, t: (0, a, t, 0)),
-        out_shape=jax.ShapeDtypeStruct((count, rounds, tile, width), BF),
+        out_shape=pltpu.HBM((count, rounds, tile, width), BF),
         cost_estimate=cost(0, 2 * left.size * 2),
         compiler_params=ROOMY,
     )(left)
@@ -127,6 +127,7 @@
     blocks = len(pieces) // 2
     _, rows, width = left.shape
     left_spec = pl.BlockSpec((3, rows, width), lambda i, order: (order[i], 0, 0))
+    left = pltpu.with_memory_space_constraint(left, pltpu.HBM)
     arrays = [array for array, _ in pieces]
     scratch = [VMEM((3, 256, 512), BF)]
     flops = blocks * 2 * rows * 768 * 512
@@ -153,24 +154,11 @@
     )(order, left, *starts, *arrays)
 
 
-def spread_panel(block):
-    ways = (0, 1, -1, 2)
-    near = jnp.stack([z_shift(block, d) if d else block for d in ways])
-    return [y_shift(near, d) if d else near for d in ways]
+def four_ways(block, shift):
+    return [shift(block, -d) if d else block for d in RELATIVE]
 
 
 RELATIVE = (0, -1, 1, 2)
-
-
-def far_gather(block):
-    low, high = block[:, :128, :], block[:, 128:, :]
-    before_low = x_shift(low, 1)
-    after_high = x_shift(high, -1)
-    before_high = x_shift(high, 1)
-    after_low = x_shift(low, -1)
-    far_low = x_shift(before_low, 1)
-    far_high = x_shift(after_high, -1)
-    return (low, high), (before_low, before_high), (after_low, after_high), (far_low, far_high)
 
 
 def place_values(order, sources, held):
@@ -297,18 +285,30 @@
     tiles = jnp.stack([(y + d) % 4 * 4 + (z + e) % 4 for d in RELATIVE for e in RELATIVE])
     order, tiles = order.astype(jnp.int32), tiles.astype(jnp.int32)
 
-    own, before, after, far = far_gather(prev_solution)
-    sibling = other_core(prev_solution)
     early = jnp.stack([inverses[0].reshape(512, 256), coupling.reshape(512, 256)])
     panels = lax.all_gather(early, "col")
-    late_panels = spread_panel(inverses[1].reshape(512, 256))
-    left = split_tiles(left_factor)
+    panels = pltpu.with_memory_space_constraint(panels, pltpu.HBM)
+    sibling = other_core(prev_solution)
+    low, high = prev_solution[:, :128, :], prev_solution[:, 128:, :]
+    before_low, after_high = x_shift(low, 1), x_shift(high, -1)
+    before_high, after_low = x_shift(high, 1), x_shift(low, -1)
+    left = split_tiles(pltpu.with_memory_space_constraint(left_factor, pltpu.HBM))
+    late = inverses[1].reshape(512, 256)
+    before_low, after_high, left, late = lax.optimization_barrier(
+        (before_low, after_high, left, late)
+    )
+    far_low, far_high = x_shift(before_low, 1), x_shift(after_high, -1)
+    near = jnp.stack(four_ways(late, z_shift))
     pieces = [(prev_solution, 0), (prev_solution, 1), (sibling, 0), (sibling, 1)]
     started = products(order[:2], left, pieces)
+    before_high, after_low, started = lax.optimization_barrier((before_high, after_low, started))
+    started, near = lax.optimization_barrier((started, near))
+    late_panels = four_ways(near, y_shift)
     pieces = []
-    for pair in (before, after):
+    for pair in ((before_low, before_high), (after_low, after_high)):
         pieces += [(v, 0) for v in pair] + [(other_core(v), 0) for v in pair]
     started = products(order[2:6], left, pieces, started)
+    far = (far_low, far_high)
     pieces = [(v, 0) for v in far] + [(other_core(v), 0) for v in far]
     first, second = products(order[6:], left, pieces, started, last=True)
 
@@ -323,9 +323,9 @@
     every_first = all_sites(sent)
     base = sites[:, 512:] - second_sum
     second_rhs = gathered_stage(order, over_chips(pair), panels, 1, base)
-    second_rhs, every_first = lax.optimization_barrier((second_rhs, every_first))
     moved = over_chips(over_cores(second_rhs))
     solved_second = spread_stage(order, tiles, moved, late_panels)
+    solved_second, every_first = lax.optimization_barrier((solved_second, every_first))
     every_second = all_sites(solved_second)
     outer = outer_part(solved_first, every_first) + outer_part(solved_second, every_second)
     pred_cov = prior_cov - row_sum(outer) / S

time: 219 us -> 203 us (0.927)
  waiting for transfers between devices: 68 us -> 40 us
  Pallas kernels: 29.3 us -> 40.7 us
  local copies, waits for them, and re-layouts: 17.9 us -> 9.22 us
  starting transfers between devices: 43.4 us -> 49.7 us
  other arithmetic: 5.05 us -> 9.18 us
    ppermute x18, waiting for transfers between devices: 42.1 us -> 24.5 us  [x_shift(): return lax.ppermute(v, 'row', [(r, (r + 2 * step) % 8) for r in range(8)])]
    all_to_all x1, waiting for transfers between devices: 9.6 us -> 0.01 us  [all_sites(): return lax.all_to_all(sent, 'col', 0, 0, tiled=True).reshape(512, 512)]
    unnamed x15 -> x13, local copies, waits for them, and re-layouts: 11.5 us -> 3.49 us
    pallas_call x1, Pallas kernels: 4.31 us -> 10.5 us  [split_tiles(): pl.pallas_call(split_tiles_kernel, grid=(rounds, tile // rows), in_specs=...]
    all_to_all x1, blocking collectives: 23.8 us -> 20.7 us  [over_sites(): return lax.all_to_all(partial.reshape(16, 32, 512), 'col', 0, 0, tiled=True)]
    pallas_call x2, Pallas kernels: 5 us -> 7.71 us  [gathered_stage(): pl.pallas_call(lambda *refs: gathered_stage_kernel(base is not None, *ref...]
    ppermute x18, starting transfers between devices: 20.9 us -> 23.6 us  [x_shift(): return lax.ppermute(v, 'row', [(r, (r + 2 * step) % 8) for r in range(8)])]
    ppermute x3, starting transfers between devices: 5.53 us -> 8.19 us  [z_shift(): lax.ppermute(v, 'col', [(c, c // 4 * 4 + (c + step) % 4) for c in range(1...]
  transfers between devices with their start and end apart: 38 -> 38, of which waited for: 20 -> 16; matrix products, arithmetic and copies ran while one was open for 3% -> 5% of each run, Pallas kernels for 12% -> 20%
where the time goes in v3:
time: 203 us; the launch traced here: 202 us
  starting transfers between devices  49.7 us (24%)
  Pallas kernels  40.7 us (20%)
  waiting for transfers between devices  40 us (20%)
  blocking collectives  37.7 us (19%)
  between operations  14.4 us (7%)
  local copies, waits for them, and re-layouts  9.22 us (5%)
  other arithmetic  9.18 us (5%)
    ppermute x18, waiting for transfers between devices, x_shift(): return lax.ppermute(v, 'row', [(r, (r + 2 * step) % 8) for r in range(8)])  24.5 us
    ppermute x18, starting transfers between devices, x_shift(): return lax.ppermute(v, 'row', [(r, (r + 2 * step) % 8) for r in range(8)])  23.6 us
    all_to_all x1, blocking collectives, over_sites(): return lax.all_to_all(partial.reshape(16, 32, 512), 'col', 0, 0, tiled=True)  20.7 us
    pallas_call x3, Pallas kernels, products(): pl.pallas_call(kernel, grid_spec=pltpu.PrefetchScalarGridSpec(num_scalar_...  19.6 us
    all_to_all x1, blocking collectives, all_sites(): return lax.all_to_all(sent, 'col', 0, 0, tiled=True).reshape(512, 512)  17 us
    pallas_call x1, Pallas kernels, split_tiles(): pl.pallas_call(split_tiles_kernel, grid=(rounds, tile // rows), in_specs=...  10.5 us
    ppermute x3, starting transfers between devices, z_shift(): lax.ppermute(v, 'col', [(c, c // 4 * 4 + (c + step) % 4) for c in range(1...  8.19 us
    pallas_call x2, Pallas kernels, gathered_stage(): pl.pallas_call(lambda *refs: gathered_stage_kernel(base is not None, *ref...  7.71 us
  transfers between devices with their start and end apart: 38, of which 16 were waited for; matrix products, arithmetic and copies ran while one was open for 5% of the time, Pallas kernels for 20%

profile of v3, /device:TPU:0, one launch (start us, length us, event | category | flops | bytes accessed | tf_op | source)
XLA Modules:
  0.0 202.4 jit_solution(1333696137255067197)
XLA Ops:
  7.2 1.9 fusion.2
  15.9 2.9 %collective-permute-start.3 = (bf16[3,128,512]{2,1,0:T(8,128)(2,1)S(1)}, bf16[3,128,512]{2,1,0:T(8,128)(2,1)}, u32[]{:S(2)}, u32[]{:S(2)}) collective-permute-start(bf16[3,128,512]{2,1,0:T(8,128)(2,1)S(1)} %get-tuple-element.33), channel_id=1, source_target_pairs={{0,96},{16,112},{32,0},{48,16},{64,32},{80,48},{96,64},{112,80},{1... | collective-permute-start | bytes 1179656 | tf_op jit(solution)/shard_map/ppermute | solution.py:17
  18.8 10.5 %shard_map.77 = bf16[24,4,256,256]{3,2,1,0:T(8,128)(2,1)} custom-call(bf16[4,256,24,256]{3,2,1,0:T(8,128)(2,1)} %src.1), custom_call_target="tpu_custom_call" | custom-call | bytes 25165824 | tf_op jit(solution)/shard_map/pallas_call | solution.py:48
  29.2 4.1 %collective-permute-start.7 = (bf16[512,256]{1,0:T(8,128)(2,1)}, bf16[512,256]{1,0:T(8,128)(2,1)}, u32[]{:S(2)}, u32[]{:S(2)}) collective-permute-start(bf16[512,256]{1,0:T(8,128)(2,1)} %bitcast.27), channel_id=1, source_target_pairs={{0,2},{1,3},{2,0},{3,1},{4,6},{5,7},{6,4},{7,5},{8,10},{9,11},{10,... | collective-permute-start | bytes 786440 | tf_op jit(solution)/shard_map/ppermute | solution.py:29
  33.5 4.1 %collective-permute-start.6 = (bf16[512,256]{1,0:T(8,128)(2,1)}, bf16[512,256]{1,0:T(8,128)(2,1)}, u32[]{:S(2)}, u32[]{:S(2)}) collective-permute-start(bf16[512,256]{1,0:T(8,128)(2,1)} %bitcast.27), channel_id=1, source_target_pairs={{0,3},{1,0},{2,1},{3,2},{4,7},{5,4},{6,5},{7,6},{8,11},{9,8},{10,9... | collective-permute-start | bytes 786440 | tf_op jit(solution)/shard_map/ppermute | solution.py:29
  37.7 7.0 %collective-permute-done.7 = bf16[512,256]{1,0:T(8,128)(2,1)} collective-permute-done((bf16[512,256]{1,0:T(8,128)(2,1)}, bf16[512,256]{1,0:T(8,128)(2,1)}, u32[]{:S(2)}, u32[]{:S(2)}) %collective-permute-start.7) | collective-permute-done | bytes 262176 | tf_op jit(solution)/shard_map/ppermute | solution.py:29
  45.6 3.2 %collective-permute-start.13 = (bf16[3,128,512]{2,1,0:T(8,128)(2,1)}, bf16[3,128,512]{2,1,0:T(8,128)(2,1)}, u32[]{:S(2)}, u32[]{:S(2)}) collective-permute-start(bf16[3,128,512]{2,1,0:T(8,128)(2,1)} %collective-permute-done.1.refs_5_), channel_id=1, source_target_pairs={{0,96},{16,112},{32,0},{48,16},{64,32},{80,48},{96,64},{112,80},{1... | collective-permute-start | bytes 1179656 | tf_op jit(solution)/shard_map/ppermute | solution.py:17
  51.1 4.7 %shard_map.78.before = f32[1024,512]{1,0:T(8,128)S(1)} custom-call(s32[2]{0:T(128)S(1)} %pad_add_fusion.2.order, bf16[24,1024,256]{2,1,0:T(8,128)(2,1)} %bitcast.59, bf16[3,256,512]{2,1,0:T(8,128)(2,1)S(1)} %copy-done.1, bf16[3,256,512]{2,1,0:T(8,128)(2,1)S(1)} %copy-done.1, bf16[3,256,512]{2,1,0:T(8,128)(2,1)S(1)} %copy-done.4, ...), custom_call_target="tpu_custom_call" | custom-call | flops 1610612736 | bytes 6815744 | tf_op jit(solution)/shard_map/pallas_call | solution.py:142
  57.8 2.3 %pad_maximum_fusion.refs_0_ = bf16[4,512,256]{2,1,0:T(8,128)(2,1)} fusion(bf16[1,512,256]{2,1,0:T(8,128)(2,1)} %bitcast.31, bf16[1,512,256]{2,1,0:T(8,128)(2,1)} %bitcast.30, bf16[1,512,256]{2,1,0:T(8,128)(2,1)} %bitcast.70, bf16[1,512,256]{2,1,0:T(8,128)(2,1)} %bitcast.28), kind=kLoop, calls=%fused_computation.1 | loop fusion | flops 1572864 | bytes 2097152 | tf_op jit(solution)/shard_map/stack | solution.py:301
  60.1 8.7 %shard_map.79.before = f32[1024,512]{1,0:T(8,128)S(1)} custom-call(s32[4]{0:T(128)S(1)} %pad_add_fusion.1.order, bf16[24,1024,256]{2,1,0:T(8,128)(2,1)} %bitcast.60, f32[1024,512]{1,0:T(8,128)S(1)} %shard_map.78.before, bf16[3,128,512]{2,1,0:T(8,128)(2,1)S(1)} %collective-permute-done.refs_0_, bf16[3,128,512]{2,1,0:T(8,128)(2,1)} %collective-permute-done.2.refs_1_, ...), custom_call_target="tpu_custom_call" | custom-call | flops 3221225472 | bytes 11534336 | tf_op jit(solution)/shard_map/pallas_call | solution.py:142
  68.8 6.3 %shard_map.80 = (bf16[512,512]{1,0:T(8,128)(2,1)}, bf16[512,512]{1,0:T(8,128)(2,1)S(1)}) custom-call(s32[2]{0:T(128)S(1)} %pad_add_fusion.order, bf16[24,1024,256]{2,1,0:T(8,128)(2,1)} %bitcast.61, f32[1024,512]{1,0:T(8,128)S(1)} %shard_map.79.before, bf16[3,128,512]{2,1,0:T(8,128)(2,1)} %collective-permute-done.12.refs_0_, ...), custom_call_target="tpu_custom_call" | custom-call | flops 1610612736 | bytes 6815744 | tf_op jit(solution)/shard_map/pallas_call | solution.py:142
  75.1 20.7 %all_to_all.20 = bf16[16,32,512]{2,1,0:T(8,128)(2,1)} all-to-all(bf16[16,32,512]{2,1,0:T(8,128)(2,1)S(1)} %bitcast.57), channel_id=1, replica_groups=mesh['row'=8,'col'=16] {'col'}, dimensions={0} | all-to-all | bytes 1048576 | tf_op jit(solution)/shard_map/all_to_all | solution.py:259
  95.8 5.7 %all-to-all-start = ((bf16[16,32,512]{2,1,0:T(8,128)(2,1)}), bf16[16,32,512]{2,1,0:T(8,128)(2,1)}, u32[]{:S(2)}, u32[]{:S(2)}) async-start(bf16[16,32,512]{2,1,0:T(8,128)(2,1)} %bitcast.32), calls=%async_computation | async-start | bytes 1048576 | tf_op jit(solution)/shard_map/all_to_all | solution.py:259
  101.8 1.9 collective-permute-start.28
  105.2 2.1 %collective-permute-start.30 = (bf16[4,512,256]{2,1,0:T(8,128)(2,1)S(1)}, bf16[4,512,256]{2,1,0:T(8,128)(2,1)}, u32[]{:S(2)}, u32[]{:S(2)}) collective-permute-start(bf16[4,512,256]{2,1,0:T(8,128)(2,1)S(1)} %copy-done.2), channel_id=1, source_target_pairs={{0,8},{1,9},{2,10},{3,11},{4,12},{5,13},{6,14},{7,15},{8,0},{9,1},... | collective-permute-start | bytes 3145736 | tf_op jit(solution)/shard_map/ppermute | solution.py:25
  108.4 4.9 %all-to-all-done = bf16[16,32,512]{2,1,0:T(8,128)(2,1)} async-done(((bf16[16,32,512]{2,1,0:T(8,128)(2,1)}), bf16[16,32,512]{2,1,0:T(8,128)(2,1)}, u32[]{:S(2)}, u32[]{:S(2)}) %all-to-all-start) | async-done | bytes 524320 | tf_op jit(solution)/shard_map/all_to_all | solution.py:259
  116.9 2.1 %collective-permute-start.18 = (bf16[2,32,512]{2,1,0:T(8,128)(2,1)S(1)}, bf16[2,32,512]{2,1,0:T(8,128)(2,1)S(1)}, u32[]{:S(2)}, u32[]{:S(2)}) collective-permute-start(bf16[2,32,512]{2,1,0:T(8,128)(2,1)S(1)} %pad_maximum_fusion.3.refs_1_), channel_id=1, source_target_pairs={{0,96},{16,112},{32,0},{48,16},{64,32},{80,48},{96,64},{112,80},{1... | collective-permute-start | bytes 196616 | tf_op jit(solution)/shard_map/ppermute | solution.py:17
  119.1 2.2 %collective-permute-done.17.refs_2_ = bf16[2,32,512]{2,1,0:T(8,128)(2,1)S(1)} collective-permute-done((bf16[2,32,512]{2,1,0:T(8,128)(2,1)S(1)}, bf16[2,32,512]{2,1,0:T(8,128)(2,1)S(1)}, u32[]{:S(2)}, u32[]{:S(2)}) %collective-permute-start.17) | collective-permute-done | bytes 65568 | tf_op jit(solution)/shard_map/ppermute | solution.py:17
  122.5 4.6 %collective-permute-done.19.refs_4_ = bf16[2,32,512]{2,1,0:T(8,128)(2,1)S(1)} collective-permute-done((bf16[2,32,512]{2,1,0:T(8,128)(2,1)S(1)}, bf16[2,32,512]{2,1,0:T(8,128)(2,1)S(1)}, u32[]{:S(2)}, u32[]{:S(2)}) %collective-permute-start.19) | collective-permute-done | bytes 65568 | tf_op jit(solution)/shard_map/ppermute | solution.py:17
  127.1 3.9 %shard_map.81 = bf16[32,512]{1,0:T(8,128)(2,1)S(1)} custom-call(s32[8]{0:T(128)S(1)} %stack.137.refs_0_.order, bf16[2,32,512]{2,1,0:T(8,128)(2,1)S(1)} %pad_maximum_fusion.3.refs_1_, bf16[2,32,512]{2,1,0:T(8,128)(2,1)S(1)} %collective-permute-done.17.refs_2_, bf16[2,32,512]{2,1,0:T(8,128)(2,1)S(1)} %collective-permute-done.18.refs_3_, ...), custom_call_target="tpu_custom_call" | custom-call | flops 134217728 | bytes 4194304 | tf_op jit(solution)/shard_map/pallas_call | solution.py:229
  133.1 4.7 %all-to-all-start.2 = ((bf16[16,32,512]{2,1,0:T(8,128)(2,1)}), bf16[16,32,512]{2,1,0:T(8,128)(2,1)}, u32[]{:S(2)}, u32[]{:S(2)}) async-start(bf16[16,32,512]{2,1,0:T(8,128)(2,1)} %broadcast_in_dim.4), calls=%async_computation.2 | async-start | bytes 1048576 | tf_op jit(solution)/shard_map/all_to_all | solution.py:264
  137.9 3.2 %collective-permute-start.22 = (bf16[2,32,512]{2,1,0:T(8,128)(2,1)S(1)}, bf16[2,32,512]{2,1,0:T(8,128)(2,1)S(1)}, u32[]{:S(2)}, u32[]{:S(2)}) collective-permute-start(bf16[2,32,512]{2,1,0:T(8,128)(2,1)S(1)} %pad_maximum_fusion.4.refs_1_), channel_id=1, source_target_pairs={{0,96},{16,112},{32,0},{48,16},{64,32},{80,48},{96,64},{112,80},{1... | collective-permute-start | bytes 196616 | tf_op jit(solution)/shard_map/ppermute | solution.py:17
  141.1 2.2 %collective-permute-done.21.refs_2_ = bf16[2,32,512]{2,1,0:T(8,128)(2,1)S(1)} collective-permute-done((bf16[2,32,512]{2,1,0:T(8,128)(2,1)S(1)}, bf16[2,32,512]{2,1,0:T(8,128)(2,1)S(1)}, u32[]{:S(2)}, u32[]{:S(2)}) %collective-permute-start.21) | collective-permute-done | bytes 65568 | tf_op jit(solution)/shard_map/ppermute | solution.py:17
  143.3 5.8 %collective-permute-done.23.refs_4_ = bf16[2,32,512]{2,1,0:T(8,128)(2,1)S(1)} collective-permute-done((bf16[2,32,512]{2,1,0:T(8,128)(2,1)S(1)}, bf16[2,32,512]{2,1,0:T(8,128)(2,1)S(1)}, u32[]{:S(2)}, u32[]{:S(2)}) %collective-permute-start.23) | collective-permute-done | bytes 65568 | tf_op jit(solution)/shard_map/ppermute | solution.py:17
  149.1 3.9 %shard_map.82 = bf16[32,512]{1,0:T(8,128)(2,1)S(1)} custom-call(s32[8]{0:T(128)S(1)} %stack.137.refs_0_.order, bf16[2,32,512]{2,1,0:T(8,128)(2,1)S(1)} %pad_maximum_fusion.4.refs_1_, bf16[2,32,512]{2,1,0:T(8,128)(2,1)S(1)} %collective-permute-done.21.refs_2_, bf16[2,32,512]{2,1,0:T(8,128)(2,1)S(1)} %collective-permute-done.22.refs_3_, ...), custom_call_target="tpu_custom_call" | custom-call | flops 134217728 | bytes 4194304 | tf_op jit(solution)/shard_map/pallas_call | solution.py:229
  154.4 3.2 %collective-permute-start.26 = (bf16[2,32,512]{2,1,0:T(8,128)(2,1)S(1)}, bf16[2,32,512]{2,1,0:T(8,128)(2,1)S(1)}, u32[]{:S(2)}, u32[]{:S(2)}) collective-permute-start(bf16[2,32,512]{2,1,0:T(8,128)(2,1)S(1)} %pad_maximum_fusion.5.own), channel_id=1, source_target_pairs={{0,96},{16,112},{32,0},{48,16},{64,32},{80,48},{96,64},{112,80},{1... | collective-permute-start | bytes 196616 | tf_op jit(solution)/shard_map/ppermute | solution.py:17
  157.7 2.1 %collective-permute-done.25.one = bf16[2,32,512]{2,1,0:T(8,128)(2,1)S(1)} collective-permute-done((bf16[2,32,512]{2,1,0:T(8,128)(2,1)S(1)}, bf16[2,32,512]{2,1,0:T(8,128)(2,1)S(1)}, u32[]{:S(2)}, u32[]{:S(2)}) %collective-permute-start.25) | collective-permute-done | bytes 65568 | tf_op jit(solution)/shard_map/ppermute | solution.py:17
  160.4 3.0 %collective-permute-done.27.three = bf16[2,32,512]{2,1,0:T(8,128)(2,1)S(1)} collective-permute-done((bf16[2,32,512]{2,1,0:T(8,128)(2,1)S(1)}, bf16[2,32,512]{2,1,0:T(8,128)(2,1)S(1)}, u32[]{:S(2)}, u32[]{:S(2)}) %collective-permute-start.27) | collective-permute-done | bytes 65568 | tf_op jit(solution)/shard_map/ppermute | solution.py:17
  163.4 2.9 %shard_map.83 = bf16[32,512]{1,0:T(8,128)(2,1)S(1)} custom-call(s32[8]{0:T(128)S(1)} %stack.137.refs_0_.order, s32[16]{0:T(128)S(1)} %stack.154.tiles, bf16[2,32,512]{2,1,0:T(8,128)(2,1)S(1)} %pad_maximum_fusion.5.own, bf16[2,32,512]{2,1,0:T(8,128)(2,1)S(1)} %collective-permute-done.25.one, bf16[2,32,512]{2,1,0:T(8,128)(2,1)S(1)} %collective-permute-done.26.two, ...), custom_call_target="tpu_custom_call" | custom-call | flops 134217728 | bytes 4194304 | tf_op jit(solution)/shard_map/pallas_call | solution.py:247
  166.3 17.0 %all_to_all.21 = bf16[16,32,512]{2,1,0:T(8,128)(2,1)S(1)} all-to-all(bf16[16,32,512]{2,1,0:T(8,128)(2,1)S(1)} %broadcast_in_dim.5), channel_id=1, replica_groups=mesh['row'=8,'col'=16] {'col'}, dimensions={0} | all-to-all | bytes 1048576 | tf_op jit(solution)/shard_map/all_to_all | solution.py:264
  186.8 1.8 collective-permute-start.33
  190.3 2.2 %collective-permute-done.34 = f32[32,512]{1,0:T(8,128)S(1)} collective-permute-done((f32[32,512]{1,0:T(8,128)S(1)}, f32[32,512]{1,0:T(8,128)S(1)}, u32[]{:S(2)}, u32[]{:S(2)}) %collective-permute-start.34) | collective-permute-done | bytes 65568 | tf_op jit(solution)/shard_map/ppermute | solution.py:17
  (93 shorter events, 32.4 us)
Async XLA Ops:
  7.2 119.9 %all-gather.3.cloned.1.call-start = ((), (), s32[]{:S(2)}) async-start(), calls=%async_computation.4 | async-start | bytes 8912896 | tf_op jit(solution)/shard_map/all_gather | solution.py:289
  10.9 33.8 %collective-permute-start.4 = (bf16[3,256,512]{2,1,0:T(8,128)(2,1)}, bf16[3,256,512]{2,1,0:T(8,128)(2,1)S(1)}, u32[]{:S(2)}, u32[]{:S(2)}) collective-permute-start(bf16[3,256,512]{2,1,0:T(8,128)(2,1)} %refs_1_.1), channel_id=1, source_target_pairs={{0,16},{16,0},{32,48},{48,32},{64,80},{80,64},{96,112},{112,96},{1... | collective-permute-start | bytes 2359304 | tf_op jit(solution)/shard_map/ppermute | solution.py:21
  12.2 17.0 %collective-permute-start = (bf16[3,128,512]{2,1,0:T(8,128)(2,1)S(1)}, bf16[3,128,512]{2,1,0:T(8,128)(2,1)S(1)}, u32[]{:S(2)}, u32[]{:S(2)}) collective-permute-start(bf16[3,128,512]{2,1,0:T(8,128)(2,1)S(1)} %get-tuple-element.33), channel_id=1, source_target_pairs={{0,32},{16,48},{32,64},{48,80},{64,96},{80,112},{96,0},{112,16},{1... | collective-permute-start | bytes 1179656 | tf_op jit(solution)/shard_map/ppermute | solution.py:17
  13.9 15.4 %collective-permute-start.1 = (bf16[3,128,512]{2,1,0:T(8,128)(2,1)S(1)}, bf16[3,128,512]{2,1,0:T(8,128)(2,1)}, u32[]{:S(2)}, u32[]{:S(2)}) collective-permute-start(bf16[3,128,512]{2,1,0:T(8,128)(2,1)S(1)} %get-tuple-element.32), channel_id=1, source_target_pairs={{0,96},{16,112},{32,0},{48,16},{64,32},{80,48},{96,64},{112,80},{1... | collective-permute-start | bytes 1179656 | tf_op jit(solution)/shard_map/ppermute | solution.py:17
  15.5 18.0 %collective-permute-start.2 = (bf16[3,128,512]{2,1,0:T(8,128)(2,1)S(1)}, bf16[3,128,512]{2,1,0:T(8,128)(2,1)}, u32[]{:S(2)}, u32[]{:S(2)}) collective-permute-start(bf16[3,128,512]{2,1,0:T(8,128)(2,1)S(1)} %get-tuple-element.32), channel_id=1, source_target_pairs={{0,32},{16,48},{32,64},{48,80},{64,96},{80,112},{96,0},{112,16},{1... | collective-permute-start | bytes 1179656 | tf_op jit(solution)/shard_map/ppermute | solution.py:17
  15.9 21.8 %collective-permute-start.3 = (bf16[3,128,512]{2,1,0:T(8,128)(2,1)S(1)}, bf16[3,128,512]{2,1,0:T(8,128)(2,1)}, u32[]{:S(2)}, u32[]{:S(2)}) collective-permute-start(bf16[3,128,512]{2,1,0:T(8,128)(2,1)S(1)} %get-tuple-element.33), channel_id=1, source_target_pairs={{0,96},{16,112},{32,0},{48,16},{64,32},{80,48},{96,64},{112,80},{1... | collective-permute-start | bytes 1179656 | tf_op jit(solution)/shard_map/ppermute | solution.py:17
  29.2 15.5 %collective-permute-start.7 = (bf16[512,256]{1,0:T(8,128)(2,1)}, bf16[512,256]{1,0:T(8,128)(2,1)}, u32[]{:S(2)}, u32[]{:S(2)}) collective-permute-start(bf16[512,256]{1,0:T(8,128)(2,1)} %bitcast.27), channel_id=1, source_target_pairs={{0,2},{1,3},{2,0},{3,1},{4,6},{5,7},{6,4},{7,5},{8,10},{9,11},{10,... | collective-permute-start | bytes 786440 | tf_op jit(solution)/shard_map/ppermute | solution.py:29
  33.3 23.1 %collective-permute-start.8 = (bf16[3,128,512]{2,1,0:T(8,128)(2,1)S(1)}, bf16[3,128,512]{2,1,0:T(8,128)(2,1)}, u32[]{:S(2)}, u32[]{:S(2)}) collective-permute-start(bf16[3,128,512]{2,1,0:T(8,128)(2,1)S(1)} %collective-permute-done.refs_0_), channel_id=1, source_target_pairs={{0,16},{16,0},{32,48},{48,32},{64,80},{80,64},{96,112},{112,96},{1... | collective-permute-start | bytes 1179656 | tf_op jit(solution)/shard_map/ppermute | solution.py:21
  33.5 22.2 %collective-permute-start.6 = (bf16[512,256]{1,0:T(8,128)(2,1)}, bf16[512,256]{1,0:T(8,128)(2,1)}, u32[]{:S(2)}, u32[]{:S(2)}) collective-permute-start(bf16[512,256]{1,0:T(8,128)(2,1)} %bitcast.27), channel_id=1, source_target_pairs={{0,3},{1,0},{2,1},{3,2},{4,7},{5,4},{6,5},{7,6},{8,11},{9,8},{10,9... | collective-permute-start | bytes 786440 | tf_op jit(solution)/shard_map/ppermute | solution.py:29
  37.7 18.2 %collective-permute-start.5 = (bf16[512,256]{1,0:T(8,128)(2,1)}, bf16[512,256]{1,0:T(8,128)(2,1)S(1)}, u32[]{:S(2)}, u32[]{:S(2)}) collective-permute-start(bf16[512,256]{1,0:T(8,128)(2,1)} %bitcast.27), channel_id=1, source_target_pairs={{0,1},{1,2},{2,3},{3,0},{4,5},{5,6},{6,7},{7,4},{8,9},{9,10},{10,1... | collective-permute-start | bytes 786440 | tf_op jit(solution)/shard_map/ppermute | solution.py:29
  44.7 12.5 %collective-permute-start.12 = (bf16[3,128,512]{2,1,0:T(8,128)(2,1)S(1)}, bf16[3,128,512]{2,1,0:T(8,128)(2,1)}, u32[]{:S(2)}, u32[]{:S(2)}) collective-permute-start(bf16[3,128,512]{2,1,0:T(8,128)(2,1)S(1)} %collective-permute-done.refs_0_), channel_id=1, source_target_pairs={{0,32},{16,48},{32,64},{48,80},{64,96},{80,112},{96,0},{112,16},{1... | collective-permute-start | bytes 1179656 | tf_op jit(solution)/shard_map/ppermute | solution.py:17
  45.6 11.7 %collective-permute-start.13 = (bf16[3,128,512]{2,1,0:T(8,128)(2,1)}, bf16[3,128,512]{2,1,0:T(8,128)(2,1)}, u32[]{:S(2)}, u32[]{:S(2)}) collective-permute-start(bf16[3,128,512]{2,1,0:T(8,128)(2,1)} %collective-permute-done.1.refs_5_), channel_id=1, source_target_pairs={{0,96},{16,112},{32,0},{48,16},{64,32},{80,48},{96,64},{112,80},{1... | collective-permute-start | bytes 1179656 | tf_op jit(solution)/shard_map/ppermute | solution.py:17
  55.8 4.3 %collective-permute-start.11 = (bf16[3,128,512]{2,1,0:T(8,128)(2,1)}, bf16[3,128,512]{2,1,0:T(8,128)(2,1)}, u32[]{:S(2)}, u32[]{:S(2)}) collective-permute-start(bf16[3,128,512]{2,1,0:T(8,128)(2,1)} %collective-permute-done.1.refs_5_), channel_id=1, source_target_pairs={{0,16},{16,0},{32,48},{48,32},{64,80},{80,64},{96,112},{112,96},{1... | collective-permute-start | bytes 1179656 | tf_op jit(solution)/shard_map/ppermute | solution.py:21
  57.2 11.5 %collective-permute-start.14 = (bf16[3,128,512]{2,1,0:T(8,128)(2,1)}, bf16[3,128,512]{2,1,0:T(8,128)(2,1)S(1)}, u32[]{:S(2)}, u32[]{:S(2)}) collective-permute-start(bf16[3,128,512]{2,1,0:T(8,128)(2,1)} %collective-permute-done.12.refs_0_), channel_id=1, source_target_pairs={{0,16},{16,0},{32,48},{48,32},{64,80},{80,64},{96,112},{112,96},{1... | collective-permute-start | bytes 1179656 | tf_op jit(solution)/shard_map/ppermute | solution.py:21
  57.3 11.5 %collective-permute-start.15 = (bf16[3,128,512]{2,1,0:T(8,128)(2,1)}, bf16[3,128,512]{2,1,0:T(8,128)(2,1)S(1)}, u32[]{:S(2)}, u32[]{:S(2)}) collective-permute-start(bf16[3,128,512]{2,1,0:T(8,128)(2,1)} %collective-permute-done.13.refs_1_), channel_id=1, source_target_pairs={{0,16},{16,0},{32,48},{48,32},{64,80},{80,64},{96,112},{112,96},{1... | collective-permute-start | bytes 1179656 | tf_op jit(solution)/shard_map/ppermute | solution.py:21
  95.8 17.5 %all-to-all-start = ((bf16[16,32,512]{2,1,0:T(8,128)(2,1)}), bf16[16,32,512]{2,1,0:T(8,128)(2,1)}, u32[]{:S(2)}, u32[]{:S(2)}) async-start(bf16[16,32,512]{2,1,0:T(8,128)(2,1)} %bitcast.32), calls=%async_computation | async-start | bytes 1048576 | tf_op jit(solution)/shard_map/all_to_all | solution.py:259
  101.8 55.8 %collective-permute-start.28 = (bf16[4,512,256]{2,1,0:T(8,128)(2,1)S(1)}, bf16[4,512,256]{2,1,0:T(8,128)(2,1)S(1)}, u32[]{:S(2)}, u32[]{:S(2)}) collective-permute-start(bf16[4,512,256]{2,1,0:T(8,128)(2,1)S(1)} %copy-done.2), channel_id=1, source_target_pairs={{0,4},{1,5},{2,6},{3,7},{4,8},{5,9},{6,10},{7,11},{8,12},{9,13},{1... | collective-permute-start | bytes 3145736 | tf_op jit(solution)/shard_map/ppermute | solution.py:25
  103.7 54.0 %collective-permute-start.29 = (bf16[4,512,256]{2,1,0:T(8,128)(2,1)S(1)}, bf16[4,512,256]{2,1,0:T(8,128)(2,1)}, u32[]{:S(2)}, u32[]{:S(2)}) collective-permute-start(bf16[4,512,256]{2,1,0:T(8,128)(2,1)S(1)} %copy-done.2), channel_id=1, source_target_pairs={{0,12},{1,13},{2,14},{3,15},{4,0},{5,1},{6,2},{7,3},{8,4},{9,5},{1... | collective-permute-start | bytes 3145736 | tf_op jit(solution)/shard_map/ppermute | solution.py:25
  105.2 52.5 %collective-permute-start.30 = (bf16[4,512,256]{2,1,0:T(8,128)(2,1)S(1)}, bf16[4,512,256]{2,1,0:T(8,128)(2,1)}, u32[]{:S(2)}, u32[]{:S(2)}) collective-permute-start(bf16[4,512,256]{2,1,0:T(8,128)(2,1)S(1)} %copy-done.2), channel_id=1, source_target_pairs={{0,8},{1,9},{2,10},{3,11},{4,12},{5,13},{6,14},{7,15},{8,0},{9,1},... | collective-permute-start | bytes 3145736 | tf_op jit(solution)/shard_map/ppermute | solution.py:25
  115.8 5.5 %collective-permute-start.17 = (bf16[2,32,512]{2,1,0:T(8,128)(2,1)S(1)}, bf16[2,32,512]{2,1,0:T(8,128)(2,1)S(1)}, u32[]{:S(2)}, u32[]{:S(2)}) collective-permute-start(bf16[2,32,512]{2,1,0:T(8,128)(2,1)S(1)} %pad_maximum_fusion.3.refs_1_), channel_id=1, source_target_pairs={{0,32},{16,48},{32,64},{48,80},{64,96},{80,112},{96,0},{112,16},{1... | collective-permute-start | bytes 196616 | tf_op jit(solution)/shard_map/ppermute | solution.py:17
  116.9 5.5 %collective-permute-start.18 = (bf16[2,32,512]{2,1,0:T(8,128)(2,1)S(1)}, bf16[2,32,512]{2,1,0:T(8,128)(2,1)S(1)}, u32[]{:S(2)}, u32[]{:S(2)}) collective-permute-start(bf16[2,32,512]{2,1,0:T(8,128)(2,1)S(1)} %pad_maximum_fusion.3.refs_1_), channel_id=1, source_target_pairs={{0,96},{16,112},{32,0},{48,16},{64,32},{80,48},{96,64},{112,80},{1... | collective-permute-start | bytes 196616 | tf_op jit(solution)/shard_map/ppermute | solution.py:17
  121.3 5.8 %collective-permute-start.19 = (bf16[2,32,512]{2,1,0:T(8,128)(2,1)S(1)}, bf16[2,32,512]{2,1,0:T(8,128)(2,1)S(1)}, u32[]{:S(2)}, u32[]{:S(2)}) collective-permute-start(bf16[2,32,512]{2,1,0:T(8,128)(2,1)S(1)} %pad_maximum_fusion.3.refs_1_), channel_id=1, source_target_pairs={{0,64},{16,80},{32,96},{48,112},{64,0},{80,16},{96,32},{112,48},{1... | collective-permute-start | bytes 196616 | tf_op jit(solution)/shard_map/ppermute | solution.py:17
  133.1 33.1 %all-to-all-start.2 = ((bf16[16,32,512]{2,1,0:T(8,128)(2,1)}), bf16[16,32,512]{2,1,0:T(8,128)(2,1)}, u32[]{:S(2)}, u32[]{:S(2)}) async-start(bf16[16,32,512]{2,1,0:T(8,128)(2,1)} %broadcast_in_dim.4), calls=%async_computation.2 | async-start | bytes 1048576 | tf_op jit(solution)/shard_map/all_to_all | solution.py:264
  137.8 5.5 %collective-permute-start.21 = (bf16[2,32,512]{2,1,0:T(8,128)(2,1)S(1)}, bf16[2,32,512]{2,1,0:T(8,128)(2,1)S(1)}, u32[]{:S(2)}, u32[]{:S(2)}) collective-permute-start(bf16[2,32,512]{2,1,0:T(8,128)(2,1)S(1)} %pad_maximum_fusion.4.refs_1_), channel_id=1, source_target_pairs={{0,32},{16,48},{32,64},{48,80},{64,96},{80,112},{96,0},{112,16},{1... | collective-permute-start | bytes 196616 | tf_op jit(solution)/shard_map/ppermute | solution.py:17
  137.9 5.5 %collective-permute-start.22 = (bf16[2,32,512]{2,1,0:T(8,128)(2,1)S(1)}, bf16[2,32,512]{2,1,0:T(8,128)(2,1)S(1)}, u32[]{:S(2)}, u32[]{:S(2)}) collective-permute-start(bf16[2,32,512]{2,1,0:T(8,128)(2,1)S(1)} %pad_maximum_fusion.4.refs_1_), channel_id=1, source_target_pairs={{0,96},{16,112},{32,0},{48,16},{64,32},{80,48},{96,64},{112,80},{1... | collective-permute-start | bytes 196616 | tf_op jit(solution)/shard_map/ppermute | solution.py:17
  143.3 5.8 %collective-permute-start.23 = (bf16[2,32,512]{2,1,0:T(8,128)(2,1)S(1)}, bf16[2,32,512]{2,1,0:T(8,128)(2,1)S(1)}, u32[]{:S(2)}, u32[]{:S(2)}) collective-permute-start(bf16[2,32,512]{2,1,0:T(8,128)(2,1)S(1)} %pad_maximum_fusion.4.refs_1_), channel_id=1, source_target_pairs={{0,64},{16,80},{32,96},{48,112},{64,0},{80,16},{96,32},{112,48},{1... | collective-permute-start | bytes 196616 | tf_op jit(solution)/shard_map/ppermute | solution.py:17
  154.3 5.5 %collective-permute-start.25 = (bf16[2,32,512]{2,1,0:T(8,128)(2,1)S(1)}, bf16[2,32,512]{2,1,0:T(8,128)(2,1)S(1)}, u32[]{:S(2)}, u32[]{:S(2)}) collective-permute-start(bf16[2,32,512]{2,1,0:T(8,128)(2,1)S(1)} %pad_maximum_fusion.5.own), channel_id=1, source_target_pairs={{0,32},{16,48},{32,64},{48,80},{64,96},{80,112},{96,0},{112,16},{1... | collective-permute-start | bytes 196616 | tf_op jit(solution)/shard_map/ppermute | solution.py:17
  154.4 6.0 %collective-permute-start.26 = (bf16[2,32,512]{2,1,0:T(8,128)(2,1)S(1)}, bf16[2,32,512]{2,1,0:T(8,128)(2,1)S(1)}, u32[]{:S(2)}, u32[]{:S(2)}) collective-permute-start(bf16[2,32,512]{2,1,0:T(8,128)(2,1)S(1)} %pad_maximum_fusion.5.own), channel_id=1, source_target_pairs={{0,96},{16,112},{32,0},{48,16},{64,32},{80,48},{96,64},{112,80},{1... | collective-permute-start | bytes 196616 | tf_op jit(solution)/shard_map/ppermute | solution.py:17
  157.6 5.8 %collective-permute-start.27 = (bf16[2,32,512]{2,1,0:T(8,128)(2,1)S(1)}, bf16[2,32,512]{2,1,0:T(8,128)(2,1)S(1)}, u32[]{:S(2)}, u32[]{:S(2)}) collective-permute-start(bf16[2,32,512]{2,1,0:T(8,128)(2,1)S(1)} %pad_maximum_fusion.5.own), channel_id=1, source_target_pairs={{0,64},{16,80},{32,96},{48,112},{64,0},{80,16},{96,32},{112,48},{1... | collective-permute-start | bytes 196616 | tf_op jit(solution)/shard_map/ppermute | solution.py:17
  186.4 6.1 %collective-permute-start.34 = (f32[32,512]{1,0:T(8,128)S(1)}, f32[32,512]{1,0:T(8,128)S(1)}, u32[]{:S(2)}, u32[]{:S(2)}) collective-permute-start(f32[32,512]{1,0:T(8,128)S(1)} %add.281), channel_id=1, source_target_pairs={{0,64},{16,80},{32,96},{48,112},{64,0},{80,16},{96,32},{112,48},{1... | collective-permute-start | bytes 196616 | tf_op jit(solution)/shard_map/ppermute | solution.py:17
  186.8 6.4 %collective-permute-start.33 = (f32[32,512]{1,0:T(8,128)S(1)}, f32[32,512]{1,0:T(8,128)S(1)}, u32[]{:S(2)}, u32[]{:S(2)}) collective-permute-start(f32[32,512]{1,0:T(8,128)S(1)} %add.281), channel_id=1, source_target_pairs={{0,96},{16,112},{32,0},{48,16},{64,32},{80,48},{96,64},{112,80},{1... | collective-permute-start | bytes 196616 | tf_op jit(solution)/shard_map/ppermute | solution.py:17
  188.6 5.5 %collective-permute-start.32 = (f32[32,512]{1,0:T(8,128)S(1)}, f32[32,512]{1,0:T(8,128)S(1)}, u32[]{:S(2)}, u32[]{:S(2)}) collective-permute-start(f32[32,512]{1,0:T(8,128)S(1)} %add.281), channel_id=1, source_target_pairs={{0,32},{16,48},{32,64},{48,80},{64,96},{80,112},{96,0},{112,16},{1... | collective-permute-start | bytes 196616 | tf_op jit(solution)/shard_map/ppermute | solution.py:17
  (12 other events, 144.3 us)
Sparse Core Ops, SparseCore 0:
  11.1 84.9 all-gather.2

commit v4 on v3

--- a/solution.py
+++ b/solution.py
@@ -21,14 +21,6 @@
     return lax.ppermute(v, "row", [(r, r ^ 1) for r in range(8)])
 
 
-def y_shift(v, step):
-    return lax.ppermute(v, "col", [(c, (c // 4 + step) % 4 * 4 + c % 4) for c in range(16)])
-
-
-def z_shift(v, step):
-    return lax.ppermute(v, "col", [(c, c // 4 * 4 + (c + step) % 4) for c in range(16)])
-
-
 def whole(array):
     rank = len(array.shape)
     return pl.BlockSpec(array.shape, lambda i, *_: (0,) * rank)
@@ -36,6 +28,38 @@
 
 def cost(flops, moved):
     return pl.CostEstimate(flops=flops, bytes_accessed=moved, transcendentals=0)
+
+
+def in_hbm(array):
+    return pltpu.with_memory_space_constraint(array, pltpu.HBM)
+
+
+def prepare_kernel(values, first, second, linking, low, high, lines):
+    low[...] = values[:, :128, :]
+    high[...] = values[:, 128:, :]
+    lines[0] = first[...]
+    lines[1] = linking[...]
+    lines[2] = second[...]
+
+
+def prepare(values, inverses, coupling):
+    inverses = in_hbm(inverses.reshape(2, 512, 256))
+    coupling = in_hbm(coupling.reshape(512, 256))
+    half = jax.ShapeDtypeStruct((3, 128, 512), BF)
+    out = [half, half, pltpu.HBM((3, 512, 256), BF)]
+    return pl.pallas_call(
+        prepare_kernel,
+        grid=(1,),
+        in_specs=[
+            whole(values),
+            pl.BlockSpec((None, 512, 256), lambda i: (0, 0, 0)),
+            pl.BlockSpec((None, 512, 256), lambda i: (1, 0, 0)),
+            whole(coupling),
+        ],
+        out_specs=list(map(whole, out)),
+        out_shape=out,
+        compiler_params=ROOMY,
+    )(in_hbm(values), inverses, inverses, coupling)
 
 
 def split_tiles_kernel(src, dst):
@@ -154,10 +178,6 @@
     )(order, left, *starts, *arrays)
 
 
-def four_ways(block, shift):
-    return [shift(block, -d) if d else block for d in RELATIVE]
-
-
 RELATIVE = (0, -1, 1, 2)
 
 
@@ -197,18 +217,6 @@
         out[...] = result.astype(BF)
 
 
-def spread_stage_kernel(order, tiles, own, one, two, three, *refs):
-    *weights, out, held = refs
-    place_values(order, (own, one, two, three), held)
-    for a in range(2):
-        rows = slice(256 * a, 256 * (a + 1))
-        total = jnp.zeros((32, 256), F32)
-        for j, ref in enumerate(weights):
-            for i in range(4):
-                total += block_product(held[tiles[4 * j + i]], ref[i, rows, :])
-        out[:, rows] = total.astype(BF)
-
-
 def over_cores(values):
     return jnp.stack([values, other_core(values)])
 
@@ -221,7 +229,6 @@
 STAGE_OUT = jax.ShapeDtypeStruct((32, 512), BF)
 LEAN = pltpu.CompilerParams(vmem_limit_bytes=12 << 20)
 SCALARS = pl.BlockSpec(memory_space=pltpu.SMEM)
-NEAR = pl.BlockSpec(memory_space=VMEM)
 
 
 def gathered_stage(order, moved, panels, which, base=None):
@@ -243,18 +250,6 @@
     )(order, *moved, *bases, panels)
 
 
-def spread_stage(order, tiles, moved, panels):
-    return pl.pallas_call(
-        spread_stage_kernel,
-        in_specs=[SCALARS, SCALARS] + [NEAR] * 8,
-        out_specs=NEAR,
-        scratch_shapes=[VMEM((16, 32, 256), BF)],
-        out_shape=STAGE_OUT,
-        cost_estimate=STAGE_COST,
-        compiler_params=LEAN,
-    )(order, tiles, *moved, *panels)
-
-
 def over_sites(partial):
     return lax.all_to_all(partial.reshape(16, 32, 512), "col", 0, 0, tiled=True)
 
@@ -280,34 +275,27 @@
 def body(left_factor, prev_solution, cross, inverses, coupling, prior_cov):
     row, col = lax.axis_index("row"), lax.axis_index("col")
     x, k = row // 2, row % 2
-    y, z = col // 4, col % 4
     order = jnp.stack([(x + d) % 4 * 2 + (k + e) % 2 for d in RELATIVE for e in range(2)])
-    tiles = jnp.stack([(y + d) % 4 * 4 + (z + e) % 4 for d in RELATIVE for e in RELATIVE])
-    order, tiles = order.astype(jnp.int32), tiles.astype(jnp.int32)
-
-    early = jnp.stack([inverses[0].reshape(512, 256), coupling.reshape(512, 256)])
-    panels = lax.all_gather(early, "col")
-    panels = pltpu.with_memory_space_constraint(panels, pltpu.HBM)
-    sibling = other_core(prev_solution)
-    low, high = prev_solution[:, :128, :], prev_solution[:, 128:, :]
+    order = order.astype(jnp.int32)
+
+    low, high, lines = prepare(prev_solution, inverses, coupling)
+    panels = in_hbm(lax.all_gather(lines, "col"))
     before_low, after_high = x_shift(low, 1), x_shift(high, -1)
     before_high, after_low = x_shift(high, 1), x_shift(low, -1)
-    left = split_tiles(pltpu.with_memory_space_constraint(left_factor, pltpu.HBM))
-    late = inverses[1].reshape(512, 256)
-    before_low, after_high, left, late = lax.optimization_barrier(
-        (before_low, after_high, left, late)
-    )
+    sibling = other_core(prev_solution)
+    left = split_tiles(in_hbm(left_factor))
+    before_low, after_high, left = lax.optimization_barrier((before_low, after_high, left))
     far_low, far_high = x_shift(before_low, 1), x_shift(after_high, -1)
-    near = jnp.stack(four_ways(late, z_shift))
     pieces = [(prev_solution, 0), (prev_solution, 1), (sibling, 0), (sibling, 1)]
     started = products(order[:2], left, pieces)
-    before_high, after_low, started = lax.optimization_barrier((before_high, after_low, started))
-    started, near = lax.optimization_barrier((started, near))
-    late_panels = four_ways(near, y_shift)
+    before_high, after_low, _ = lax.optimization_barrier(
+        (before_high, after_low, started[:8, :128])
+    )
     pieces = []
     for pair in ((before_low, before_high), (after_low, after_high)):
         pieces += [(v, 0) for v in pair] + [(other_core(v), 0) for v in pair]
     started = products(order[2:6], left, pieces, started)
+    far_low, far_high, _ = lax.optimization_barrier((far_low, far_high, started[:8, :128]))
     far = (far_low, far_high)
     pieces = [(v, 0) for v in far] + [(other_core(v), 0) for v in far]
     first, second = products(order[6:], left, pieces, started, last=True)
@@ -315,16 +303,18 @@
     sites = jnp.transpose(cross.reshape(1024, 512))
     sites = lax.dynamic_slice_in_dim(sites, 32 * col, 32, 0).astype(F32)
     first_sum = over_sites(first).astype(F32).sum(axis=0)
+    first_rhs = (sites[:, :512] - first_sum).astype(BF)
+    first_rhs, second = lax.optimization_barrier((first_rhs, second))
     second_sum = over_sites(second).astype(F32).sum(axis=0)
-    first_rhs = (sites[:, :512] - first_sum).astype(BF)
     solved_first = gathered_stage(order, over_chips(over_cores(first_rhs)), panels, 0)
     pair = over_cores(solved_first)
-    sent, pair = lax.optimization_barrier((solved_first, pair))
+    moved = over_chips(pair)
+    sent, moved[1] = lax.optimization_barrier((solved_first, moved[1]))
     every_first = all_sites(sent)
     base = sites[:, 512:] - second_sum
-    second_rhs = gathered_stage(order, over_chips(pair), panels, 1, base)
+    second_rhs = gathered_stage(order, moved, panels, 1, base)
     moved = over_chips(over_cores(second_rhs))
-    solved_second = spread_stage(order, tiles, moved, late_panels)
+    solved_second = gathered_stage(order, moved, panels, 2)
     solved_second, every_first = lax.optimization_barrier((solved_second, every_first))
     every_second = all_sites(solved_second)
     outer = outer_part(solved_first, every_first) + outer_part(solved_second, every_second)

time: 203 us -> 192 us (0.946)
  waiting for transfers between devices: 40 us -> 66.5 us
  blocking collectives: 37.7 us -> 17.1 us
  local copies, waits for them, and re-layouts: 9.22 us -> 1.68 us
  other arithmetic: 9.18 us -> 2.17 us
  starting transfers between devices: 49.7 us -> 44.3 us
  Pallas kernels: 40.7 us -> 44.8 us
    all_to_all x1 -> x0, blocking collectives: 20.7 us -> none  [over_sites(): return lax.all_to_all(partial.reshape(16, 32, 512), 'col', 0, 0, tiled=True)]
    all_gather x1, waiting for transfers between devices: 0.01 us -> 13.9 us  [body(): panels = in_hbm(lax.all_gather(lines, 'col'))]
    ppermute x6 -> x0, starting transfers between devices: 13.7 us -> none  [the longest x3 8.19 us: z_shift(): lax.ppermute(v, 'col', [(c, c // 4 * 4 + (c + step) % 4) for c in range(1...]
    all_to_all x1 -> x2, waiting for transfers between devices: 4.94 us -> 15.5 us  [over_sites(): return lax.all_to_all(partial.reshape(16, 32, 512), 'col', 0, 0, tiled=True)]
    ppermute x18, waiting for transfers between devices: 24.5 us -> 32.6 us  [x_shift(): return lax.ppermute(v, 'row', [(r, (r + 2 * step) % 8) for r in range(8)])]
    all_to_all x1 -> x2, starting transfers between devices: 5.68 us -> 13.7 us  [over_sites(): return lax.all_to_all(partial.reshape(16, 32, 512), 'col', 0, 0, tiled=True)]
    ppermute x6 -> x0, waiting for transfers between devices: 6.97 us -> none  [the longest x3 6.96 us: z_shift(): lax.ppermute(v, 'col', [(c, c // 4 * 4 + (c + step) % 4) for c in range(1...]
    another operation x2 -> x0, other arithmetic: 4.09 us -> none  [the longest x1 2.29 us: body(): near = jnp.stack(four_ways(late, z_shift))]
  transfers between devices with their start and end apart: 38 -> 33, of which waited for: 16 -> 20; matrix products, arithmetic and copies ran while one was open for 5% -> 1% of each run, Pallas kernels for 20% -> 22%
where the time goes in v4:
time: 192 us; the launch traced here: 191 us
  waiting for transfers between devices  66.5 us (35%)
  Pallas kernels  44.8 us (23%)
  starting transfers between devices  44.3 us (23%)
  blocking collectives  17.1 us (9%)
  between operations  14.3 us (7%)
  other arithmetic  2.17 us (1%)
    ppermute x18, waiting for transfers between devices, x_shift(): return lax.ppermute(v, 'row', [(r, (r + 2 * step) % 8) for r in range(8)])  32.6 us
    ppermute x18, starting transfers between devices, x_shift(): return lax.ppermute(v, 'row', [(r, (r + 2 * step) % 8) for r in range(8)])  23.8 us
    pallas_call x3, Pallas kernels, products(): pl.pallas_call(kernel, grid_spec=pltpu.PrefetchScalarGridSpec(num_scalar_...  20 us
    all_to_all x1, blocking collectives, all_sites(): return lax.all_to_all(sent, 'col', 0, 0, tiled=True).reshape(512, 512)  17.1 us
    all_to_all x2, waiting for transfers between devices, over_sites(): return lax.all_to_all(partial.reshape(16, 32, 512), 'col', 0, 0, tiled=True)  15.5 us
    all_gather x1, waiting for transfers between devices, body(): panels = in_hbm(lax.all_gather(lines, 'col'))  13.9 us
    all_to_all x2, starting transfers between devices, over_sites(): return lax.all_to_all(partial.reshape(16, 32, 512), 'col', 0, 0, tiled=True)  13.7 us
    pallas_call x3, Pallas kernels, gathered_stage(): pl.pallas_call(lambda *refs: gathered_stage_kernel(base is not None, *ref...  11.6 us
  transfers between devices with their start and end apart: 33, of which 20 were waited for; matrix products, arithmetic and copies ran while one was open for 1% of the time, Pallas kernels for 22%

profile of v4, /device:TPU:0, one launch (start us, length us, event | category | flops | bytes accessed | tf_op | source)
XLA Modules:
  0.0 191.4 jit_solution(10593922454676299488)
XLA Ops:
  7.2 2.6 %shard_map.77 = (bf16[3,128,512]{2,1,0:T(8,128)(2,1)}, bf16[3,128,512]{2,1,0:T(8,128)(2,1)}, bf16[3,512,256]{2,1,0:T(8,128)(2,1)}) custom-call(bf16[3,256,512]{2,1,0:T(8,128)(2,1)} %refs_1_.1, bf16[2,512,256]{2,1,0:T(8,128)(2,1)} %bitcast.49, bf16[2,512,256]{2,1,0:T(8,128)(2,1)} %bitcast.50, bf16[512,256]{1,0:T(8,128)(2,1)} %bitcast.51), custom_call_target="tpu_custom_call" | custom-call | tf_op jit(solution)/shard_map/pallas_call | solution.py:50
  9.8 1.6 collective-permute-start
  11.5 1.7 collective-permute-start.1
  13.5 2.8 %collective-permute-start.4 = (bf16[3,128,512]{2,1,0:T(8,128)(2,1)}, bf16[3,128,512]{2,1,0:T(8,128)(2,1)}, u32[]{:S(2)}, u32[]{:S(2)}) collective-permute-start(bf16[3,128,512]{2,1,0:T(8,128)(2,1)} %get-tuple-element.20), channel_id=1, source_target_pairs={{0,96},{16,112},{32,0},{48,16},{64,32},{80,48},{96,64},{112,80},{1... | collective-permute-start | bytes 1179656 | tf_op jit(solution)/shard_map/ppermute | solution.py:17
  16.4 10.7 %shard_map.78 = bf16[24,4,256,256]{3,2,1,0:T(8,128)(2,1)} custom-call(bf16[4,256,24,256]{3,2,1,0:T(8,128)(2,1)} %src.1), custom_call_target="tpu_custom_call" | custom-call | bytes 25165824 | tf_op jit(solution)/shard_map/pallas_call | solution.py:72
  27.1 3.2 %collective-permute-start.10 = (bf16[3,128,512]{2,1,0:T(8,128)(2,1)S(1)}, bf16[3,128,512]{2,1,0:T(8,128)(2,1)}, u32[]{:S(2)}, u32[]{:S(2)}) collective-permute-start(bf16[3,128,512]{2,1,0:T(8,128)(2,1)S(1)} %collective-permute-done.1.refs_5_), channel_id=1, source_target_pairs={{0,96},{16,112},{32,0},{48,16},{64,32},{80,48},{96,64},{112,80},{1... | collective-permute-start | bytes 1179656 | tf_op jit(solution)/shard_map/ppermute | solution.py:17
  31.7 7.7 %collective-permute-done.9.refs_0_ = bf16[3,128,512]{2,1,0:T(8,128)(2,1)} collective-permute-done((bf16[3,128,512]{2,1,0:T(8,128)(2,1)S(1)}, bf16[3,128,512]{2,1,0:T(8,128)(2,1)}, u32[]{:S(2)}, u32[]{:S(2)}) %collective-permute-start.9) | collective-permute-done | bytes 393248 | tf_op jit(solution)/shard_map/ppermute | solution.py:17
  40.7 4.7 %shard_map.79.before = f32[1024,512]{1,0:T(8,128)S(1)} custom-call(s32[2]{0:T(128)S(1)} %pad_add_fusion.2.order, bf16[24,1024,256]{2,1,0:T(8,128)(2,1)} %bitcast.37, bf16[3,256,512]{2,1,0:T(8,128)(2,1)S(1)} %copy-done.1, bf16[3,256,512]{2,1,0:T(8,128)(2,1)S(1)} %copy-done.1, bf16[3,256,512]{2,1,0:T(8,128)(2,1)S(1)} %collective-permute-done.2.refs_2_.refs_3_, ...), custom_call_target="tpu_custom_call" | custom-call | flops 1610612736 | bytes 6815744 | tf_op jit(solution)/shard_map/pallas_call | solution.py:166
  45.4 8.9 %shard_map.80.before = f32[1024,512]{1,0:T(8,128)S(1)} custom-call(s32[4]{0:T(128)S(1)} %pad_add_fusion.1.order, bf16[24,1024,256]{2,1,0:T(8,128)(2,1)} %bitcast.38, f32[1024,512]{1,0:T(8,128)S(1)} %shard_map.79.before, bf16[3,128,512]{2,1,0:T(8,128)(2,1)S(1)} %collective-permute-done.refs_0_, bf16[3,128,512]{2,1,0:T(8,128)(2,1)} %collective-permute-done.3.refs_1_, ...), custom_call_target="tpu_custom_call" | custom-call | flops 3221225472 | bytes 11534336 | tf_op jit(solution)/shard_map/pallas_call | solution.py:166
  54.3 6.4 %shard_map.81 = (bf16[512,512]{1,0:T(8,128)(2,1)}, bf16[512,512]{1,0:T(8,128)(2,1)}) custom-call(s32[2]{0:T(128)S(1)} %pad_add_fusion.order, bf16[24,1024,256]{2,1,0:T(8,128)(2,1)} %bitcast.39, f32[1024,512]{1,0:T(8,128)S(1)} %shard_map.80.before, bf16[3,128,512]{2,1,0:T(8,128)(2,1)} %collective-permute-done.9.refs_0_, ...), custom_call_target="tpu_custom_call" | custom-call | flops 1610612736 | bytes 6815744 | tf_op jit(solution)/shard_map/pallas_call | solution.py:166
  60.7 7.9 %all-to-all-start = ((bf16[16,32,512]{2,1,0:T(8,128)(2,1)}), bf16[16,32,512]{2,1,0:T(8,128)(2,1)S(1)}, u32[]{:S(2)}, u32[]{:S(2)}) async-start(bf16[16,32,512]{2,1,0:T(8,128)(2,1)} %bitcast.13), calls=%async_computation | async-start | bytes 1048576 | tf_op jit(solution)/shard_map/all_to_all | solution.py:254
  69.0 15.5 %all-to-all-done = bf16[16,32,512]{2,1,0:T(8,128)(2,1)S(1)} async-done(((bf16[16,32,512]{2,1,0:T(8,128)(2,1)}), bf16[16,32,512]{2,1,0:T(8,128)(2,1)S(1)}, u32[]{:S(2)}, u32[]{:S(2)}) %all-to-all-start) | async-done | bytes 524320 | tf_op jit(solution)/shard_map/all_to_all | solution.py:254
  84.6 5.7 %all-to-all-start.1 = ((bf16[16,32,512]{2,1,0:T(8,128)(2,1)}), bf16[16,32,512]{2,1,0:T(8,128)(2,1)S(1)}, u32[]{:S(2)}, u32[]{:S(2)}) async-start(bf16[16,32,512]{2,1,0:T(8,128)(2,1)} %bitcast.19), calls=%async_computation.1 | async-start | bytes 1048576 | tf_op jit(solution)/shard_map/all_to_all | solution.py:254
  92.6 2.3 %collective-permute-start.15 = (bf16[2,32,512]{2,1,0:T(8,128)(2,1)S(1)}, bf16[2,32,512]{2,1,0:T(8,128)(2,1)S(1)}, u32[]{:S(2)}, u32[]{:S(2)}) collective-permute-start(bf16[2,32,512]{2,1,0:T(8,128)(2,1)S(1)} %pad_maximum_fusion.1.refs_1_), channel_id=1, source_target_pairs={{0,96},{16,112},{32,0},{48,16},{64,32},{80,48},{96,64},{112,80},{1... | collective-permute-start | bytes 196616 | tf_op jit(solution)/shard_map/ppermute | solution.py:17
  97.5 3.3 %collective-permute-done.16.refs_4_ = bf16[2,32,512]{2,1,0:T(8,128)(2,1)S(1)} collective-permute-done((bf16[2,32,512]{2,1,0:T(8,128)(2,1)S(1)}, bf16[2,32,512]{2,1,0:T(8,128)(2,1)S(1)}, u32[]{:S(2)}, u32[]{:S(2)}) %collective-permute-start.16) | collective-permute-done | bytes 65568 | tf_op jit(solution)/shard_map/ppermute | solution.py:17
  100.7 13.9 %all-gather.3.cloned.1.call-done = bf16[48,512,256]{2,1,0:T(8,128)(2,1)} async-done(((bf16[3,512,256]{2,1,0:T(8,128)(2,1)}), bf16[48,512,256]{2,1,0:T(8,128)(2,1)}) %all-gather.3.cloned.1.call-update) | async-done | bytes 12582928 | tf_op jit(solution)/shard_map/all_gather | solution.py:282
  114.7 3.9 %shard_map.82 = bf16[32,512]{1,0:T(8,128)(2,1)S(1)} custom-call(s32[8]{0:T(128)S(1)} %stack.68.refs_0_, bf16[2,32,512]{2,1,0:T(8,128)(2,1)S(1)} %pad_maximum_fusion.1.refs_1_, bf16[2,32,512]{2,1,0:T(8,128)(2,1)S(1)} %collective-permute-done.14.refs_2_, bf16[2,32,512]{2,1,0:T(8,128)(2,1)S(1)} %collective-permute-done.15.refs_3_, ...), custom_call_target="tpu_custom_call" | custom-call | flops 134217728 | bytes 4194304 | tf_op jit(solution)/shard_map/pallas_call | solution.py:236
  120.0 1.5 collective-permute-start.18
  121.5 4.0 %collective-permute-done.18.refs_2_ = bf16[2,32,512]{2,1,0:T(8,128)(2,1)S(1)} collective-permute-done((bf16[2,32,512]{2,1,0:T(8,128)(2,1)S(1)}, bf16[2,32,512]{2,1,0:T(8,128)(2,1)S(1)}, u32[]{:S(2)}, u32[]{:S(2)}) %collective-permute-start.18) | collective-permute-done | bytes 65568 | tf_op jit(solution)/shard_map/ppermute | solution.py:17
  126.4 5.3 %all-to-all-start.2 = ((bf16[16,32,512]{2,1,0:T(8,128)(2,1)}), bf16[16,32,512]{2,1,0:T(8,128)(2,1)S(1)}, u32[]{:S(2)}, u32[]{:S(2)}) async-start(bf16[16,32,512]{2,1,0:T(8,128)(2,1)} %broadcast_in_dim.4), calls=%async_computation.2 | async-start | bytes 1048576 | tf_op jit(solution)/shard_map/all_to_all | solution.py:259
  131.8 1.5 collective-permute-start.19
  134.2 1.9 %collective-permute-done.19.refs_3_ = bf16[2,32,512]{2,1,0:T(8,128)(2,1)S(1)} collective-permute-done((bf16[2,32,512]{2,1,0:T(8,128)(2,1)S(1)}, bf16[2,32,512]{2,1,0:T(8,128)(2,1)S(1)}, u32[]{:S(2)}, u32[]{:S(2)}) %collective-permute-start.19) | collective-permute-done | bytes 65568 | tf_op jit(solution)/shard_map/ppermute | solution.py:17
  136.1 3.0 %collective-permute-done.20.refs_4_ = bf16[2,32,512]{2,1,0:T(8,128)(2,1)S(1)} collective-permute-done((bf16[2,32,512]{2,1,0:T(8,128)(2,1)S(1)}, bf16[2,32,512]{2,1,0:T(8,128)(2,1)S(1)}, u32[]{:S(2)}, u32[]{:S(2)}) %collective-permute-start.20) | collective-permute-done | bytes 65568 | tf_op jit(solution)/shard_map/ppermute | solution.py:17
  139.1 3.9 %shard_map.83 = bf16[32,512]{1,0:T(8,128)(2,1)S(1)} custom-call(s32[8]{0:T(128)S(1)} %stack.68.refs_0_, bf16[2,32,512]{2,1,0:T(8,128)(2,1)S(1)} %pad_maximum_fusion.2.refs_1_, bf16[2,32,512]{2,1,0:T(8,128)(2,1)S(1)} %collective-permute-done.18.refs_2_, bf16[2,32,512]{2,1,0:T(8,128)(2,1)S(1)} %collective-permute-done.19.refs_3_, ...), custom_call_target="tpu_custom_call" | custom-call | flops 134217728 | bytes 4194304 | tf_op jit(solution)/shard_map/pallas_call | solution.py:236
  144.9 2.7 %collective-permute-start.23 = (bf16[2,32,512]{2,1,0:T(8,128)(2,1)S(1)}, bf16[2,32,512]{2,1,0:T(8,128)(2,1)S(1)}, u32[]{:S(2)}, u32[]{:S(2)}) collective-permute-start(bf16[2,32,512]{2,1,0:T(8,128)(2,1)S(1)} %pad_maximum_fusion.3.refs_1_), channel_id=1, source_target_pairs={{0,96},{16,112},{32,0},{48,16},{64,32},{80,48},{96,64},{112,80},{1... | collective-permute-start | bytes 196616 | tf_op jit(solution)/shard_map/ppermute | solution.py:17
  147.6 2.2 %collective-permute-done.22.refs_2_ = bf16[2,32,512]{2,1,0:T(8,128)(2,1)S(1)} collective-permute-done((bf16[2,32,512]{2,1,0:T(8,128)(2,1)S(1)}, bf16[2,32,512]{2,1,0:T(8,128)(2,1)S(1)}, u32[]{:S(2)}, u32[]{:S(2)}) %collective-permute-start.22) | collective-permute-done | bytes 65568 | tf_op jit(solution)/shard_map/ppermute | solution.py:17
  150.4 3.0 %collective-permute-done.24.refs_4_ = bf16[2,32,512]{2,1,0:T(8,128)(2,1)S(1)} collective-permute-done((bf16[2,32,512]{2,1,0:T(8,128)(2,1)S(1)}, bf16[2,32,512]{2,1,0:T(8,128)(2,1)S(1)}, u32[]{:S(2)}, u32[]{:S(2)}) %collective-permute-start.24) | collective-permute-done | bytes 65568 | tf_op jit(solution)/shard_map/ppermute | solution.py:17
  153.3 3.9 %shard_map.84 = bf16[32,512]{1,0:T(8,128)(2,1)S(1)} custom-call(s32[8]{0:T(128)S(1)} %stack.68.refs_0_, bf16[2,32,512]{2,1,0:T(8,128)(2,1)S(1)} %pad_maximum_fusion.3.refs_1_, bf16[2,32,512]{2,1,0:T(8,128)(2,1)S(1)} %collective-permute-done.22.refs_2_, bf16[2,32,512]{2,1,0:T(8,128)(2,1)S(1)} %collective-permute-done.23.refs_3_, ...), custom_call_target="tpu_custom_call" | custom-call | flops 134217728 | bytes 4194304 | tf_op jit(solution)/shard_map/pallas_call | solution.py:236
  157.3 17.1 %all_to_all.20 = bf16[16,32,512]{2,1,0:T(8,128)(2,1)S(1)} all-to-all(bf16[16,32,512]{2,1,0:T(8,128)(2,1)S(1)} %broadcast_in_dim.5), channel_id=1, replica_groups=mesh['row'=8,'col'=16] {'col'}, dimensions={0} | all-to-all | bytes 1048576 | tf_op jit(solution)/shard_map/all_to_all | solution.py:259
  176.5 1.8 collective-permute-start.27
  179.6 2.5 %collective-permute-done.28 = f32[32,512]{1,0:T(8,128)S(1)} collective-permute-done((f32[32,512]{1,0:T(8,128)S(1)}, f32[32,512]{1,0:T(8,128)S(1)}, u32[]{:S(2)}, u32[]{:S(2)}) %collective-permute-start.28) | collective-permute-done | bytes 65568 | tf_op jit(solution)/shard_map/ppermute | solution.py:17
  182.2 1.7 collective-permute-done.26
  (73 shorter events, 18.1 us)
Async XLA Ops:
  7.2 107.5 %all-gather.3.cloned.1.call-start = ((), (), s32[]{:S(2)}) async-start(), calls=%async_computation.4 | async-start | bytes 13369344 | tf_op jit(solution)/shard_map/all_gather | solution.py:282
  9.8 17.2 %collective-permute-start = (bf16[3,128,512]{2,1,0:T(8,128)(2,1)}, bf16[3,128,512]{2,1,0:T(8,128)(2,1)S(1)}, u32[]{:S(2)}, u32[]{:S(2)}) collective-permute-start(bf16[3,128,512]{2,1,0:T(8,128)(2,1)} %get-tuple-element.20), channel_id=1, source_target_pairs={{0,32},{16,48},{32,64},{48,80},{64,96},{80,112},{96,0},{112,16},{1... | collective-permute-start | bytes 1179656 | tf_op jit(solution)/shard_map/ppermute | solution.py:17
  11.5 15.6 %collective-permute-start.1 = (bf16[3,128,512]{2,1,0:T(8,128)(2,1)}, bf16[3,128,512]{2,1,0:T(8,128)(2,1)S(1)}, u32[]{:S(2)}, u32[]{:S(2)}) collective-permute-start(bf16[3,128,512]{2,1,0:T(8,128)(2,1)} %get-tuple-element.21), channel_id=1, source_target_pairs={{0,96},{16,112},{32,0},{48,16},{64,32},{80,48},{96,64},{112,80},{1... | collective-permute-start | bytes 1179656 | tf_op jit(solution)/shard_map/ppermute | solution.py:17
  13.1 27.0 %collective-permute-start.2 = (bf16[3,256,512]{2,1,0:T(8,128)(2,1)}, bf16[3,256,512]{2,1,0:T(8,128)(2,1)S(1)}, u32[]{:S(2)}, u32[]{:S(2)}) collective-permute-start(bf16[3,256,512]{2,1,0:T(8,128)(2,1)} %refs_1_.1), channel_id=1, source_target_pairs={{0,16},{16,0},{32,48},{48,32},{64,80},{80,64},{96,112},{112,96},{1... | collective-permute-start | bytes 2359304 | tf_op jit(solution)/shard_map/ppermute | solution.py:21
  13.1 17.5 %collective-permute-start.3 = (bf16[3,128,512]{2,1,0:T(8,128)(2,1)}, bf16[3,128,512]{2,1,0:T(8,128)(2,1)}, u32[]{:S(2)}, u32[]{:S(2)}) collective-permute-start(bf16[3,128,512]{2,1,0:T(8,128)(2,1)} %get-tuple-element.21), channel_id=1, source_target_pairs={{0,32},{16,48},{32,64},{48,80},{64,96},{80,112},{96,0},{112,16},{1... | collective-permute-start | bytes 1179656 | tf_op jit(solution)/shard_map/ppermute | solution.py:17
  13.5 18.1 %collective-permute-start.4 = (bf16[3,128,512]{2,1,0:T(8,128)(2,1)}, bf16[3,128,512]{2,1,0:T(8,128)(2,1)}, u32[]{:S(2)}, u32[]{:S(2)}) collective-permute-start(bf16[3,128,512]{2,1,0:T(8,128)(2,1)} %get-tuple-element.20), channel_id=1, source_target_pairs={{0,96},{16,112},{32,0},{48,16},{64,32},{80,48},{96,64},{112,80},{1... | collective-permute-start | bytes 1179656 | tf_op jit(solution)/shard_map/ppermute | solution.py:17
  27.1 12.3 %collective-permute-start.9 = (bf16[3,128,512]{2,1,0:T(8,128)(2,1)S(1)}, bf16[3,128,512]{2,1,0:T(8,128)(2,1)}, u32[]{:S(2)}, u32[]{:S(2)}) collective-permute-start(bf16[3,128,512]{2,1,0:T(8,128)(2,1)S(1)} %collective-permute-done.refs_0_), channel_id=1, source_target_pairs={{0,32},{16,48},{32,64},{48,80},{64,96},{80,112},{96,0},{112,16},{1... | collective-permute-start | bytes 1179656 | tf_op jit(solution)/shard_map/ppermute | solution.py:17
  27.1 12.3 %collective-permute-start.10 = (bf16[3,128,512]{2,1,0:T(8,128)(2,1)S(1)}, bf16[3,128,512]{2,1,0:T(8,128)(2,1)}, u32[]{:S(2)}, u32[]{:S(2)}) collective-permute-start(bf16[3,128,512]{2,1,0:T(8,128)(2,1)S(1)} %collective-permute-done.1.refs_5_), channel_id=1, source_target_pairs={{0,96},{16,112},{32,0},{48,16},{64,32},{80,48},{96,64},{112,80},{1... | collective-permute-start | bytes 1179656 | tf_op jit(solution)/shard_map/ppermute | solution.py:17
  30.6 9.6 %collective-permute-start.5 = (bf16[3,128,512]{2,1,0:T(8,128)(2,1)S(1)}, bf16[3,128,512]{2,1,0:T(8,128)(2,1)}, u32[]{:S(2)}, u32[]{:S(2)}) collective-permute-start(bf16[3,128,512]{2,1,0:T(8,128)(2,1)S(1)} %collective-permute-done.refs_0_), channel_id=1, source_target_pairs={{0,16},{16,0},{32,48},{48,32},{64,80},{80,64},{96,112},{112,96},{1... | collective-permute-start | bytes 1179656 | tf_op jit(solution)/shard_map/ppermute | solution.py:21
  31.7 13.7 %collective-permute-start.8 = (bf16[3,128,512]{2,1,0:T(8,128)(2,1)S(1)}, bf16[3,128,512]{2,1,0:T(8,128)(2,1)}, u32[]{:S(2)}, u32[]{:S(2)}) collective-permute-start(bf16[3,128,512]{2,1,0:T(8,128)(2,1)S(1)} %collective-permute-done.1.refs_5_), channel_id=1, source_target_pairs={{0,16},{16,0},{32,48},{48,32},{64,80},{80,64},{96,112},{112,96},{1... | collective-permute-start | bytes 1179656 | tf_op jit(solution)/shard_map/ppermute | solution.py:21
  39.4 6.0 %collective-permute-start.6 = (bf16[3,128,512]{2,1,0:T(8,128)(2,1)}, bf16[3,128,512]{2,1,0:T(8,128)(2,1)}, u32[]{:S(2)}, u32[]{:S(2)}) collective-permute-start(bf16[3,128,512]{2,1,0:T(8,128)(2,1)} %collective-permute-done.3.refs_1_), channel_id=1, source_target_pairs={{0,16},{16,0},{32,48},{48,32},{64,80},{80,64},{96,112},{112,96},{1... | collective-permute-start | bytes 1179656 | tf_op jit(solution)/shard_map/ppermute | solution.py:21
  39.4 6.0 %collective-permute-start.7 = (bf16[3,128,512]{2,1,0:T(8,128)(2,1)}, bf16[3,128,512]{2,1,0:T(8,128)(2,1)}, u32[]{:S(2)}, u32[]{:S(2)}) collective-permute-start(bf16[3,128,512]{2,1,0:T(8,128)(2,1)} %collective-permute-done.4.refs_4_), channel_id=1, source_target_pairs={{0,16},{16,0},{32,48},{48,32},{64,80},{80,64},{96,112},{112,96},{1... | collective-permute-start | bytes 1179656 | tf_op jit(solution)/shard_map/ppermute | solution.py:21
  40.1 14.1 %collective-permute-start.11 = (bf16[3,128,512]{2,1,0:T(8,128)(2,1)}, bf16[3,128,512]{2,1,0:T(8,128)(2,1)S(1)}, u32[]{:S(2)}, u32[]{:S(2)}) collective-permute-start(bf16[3,128,512]{2,1,0:T(8,128)(2,1)} %collective-permute-done.9.refs_0_), channel_id=1, source_target_pairs={{0,16},{16,0},{32,48},{48,32},{64,80},{80,64},{96,112},{112,96},{1... | collective-permute-start | bytes 1179656 | tf_op jit(solution)/shard_map/ppermute | solution.py:21
  40.2 14.1 %collective-permute-start.12 = (bf16[3,128,512]{2,1,0:T(8,128)(2,1)}, bf16[3,128,512]{2,1,0:T(8,128)(2,1)S(1)}, u32[]{:S(2)}, u32[]{:S(2)}) collective-permute-start(bf16[3,128,512]{2,1,0:T(8,128)(2,1)} %collective-permute-done.10.refs_1_), channel_id=1, source_target_pairs={{0,16},{16,0},{32,48},{48,32},{64,80},{80,64},{96,112},{112,96},{1... | collective-permute-start | bytes 1179656 | tf_op jit(solution)/shard_map/ppermute | solution.py:21
  60.7 23.8 %all-to-all-start = ((bf16[16,32,512]{2,1,0:T(8,128)(2,1)}), bf16[16,32,512]{2,1,0:T(8,128)(2,1)S(1)}, u32[]{:S(2)}, u32[]{:S(2)}) async-start(bf16[16,32,512]{2,1,0:T(8,128)(2,1)} %bitcast.13), calls=%async_computation | async-start | bytes 1048576 | tf_op jit(solution)/shard_map/all_to_all | solution.py:254
  84.6 40.9 %all-to-all-start.1 = ((bf16[16,32,512]{2,1,0:T(8,128)(2,1)}), bf16[16,32,512]{2,1,0:T(8,128)(2,1)S(1)}, u32[]{:S(2)}, u32[]{:S(2)}) async-start(bf16[16,32,512]{2,1,0:T(8,128)(2,1)} %bitcast.19), calls=%async_computation.1 | async-start | bytes 1048576 | tf_op jit(solution)/shard_map/all_to_all | solution.py:254
  90.3 1.3 collective-permute-start.13
  91.6 5.5 %collective-permute-start.14 = (bf16[2,32,512]{2,1,0:T(8,128)(2,1)S(1)}, bf16[2,32,512]{2,1,0:T(8,128)(2,1)S(1)}, u32[]{:S(2)}, u32[]{:S(2)}) collective-permute-start(bf16[2,32,512]{2,1,0:T(8,128)(2,1)S(1)} %pad_maximum_fusion.1.refs_1_), channel_id=1, source_target_pairs={{0,32},{16,48},{32,64},{48,80},{64,96},{80,112},{96,0},{112,16},{1... | collective-permute-start | bytes 196616 | tf_op jit(solution)/shard_map/ppermute | solution.py:17
  92.6 4.8 %collective-permute-start.15 = (bf16[2,32,512]{2,1,0:T(8,128)(2,1)S(1)}, bf16[2,32,512]{2,1,0:T(8,128)(2,1)S(1)}, u32[]{:S(2)}, u32[]{:S(2)}) collective-permute-start(bf16[2,32,512]{2,1,0:T(8,128)(2,1)S(1)} %pad_maximum_fusion.1.refs_1_), channel_id=1, source_target_pairs={{0,96},{16,112},{32,0},{48,16},{64,32},{80,48},{96,64},{112,80},{1... | collective-permute-start | bytes 196616 | tf_op jit(solution)/shard_map/ppermute | solution.py:17
  94.9 5.8 %collective-permute-start.16 = (bf16[2,32,512]{2,1,0:T(8,128)(2,1)S(1)}, bf16[2,32,512]{2,1,0:T(8,128)(2,1)S(1)}, u32[]{:S(2)}, u32[]{:S(2)}) collective-permute-start(bf16[2,32,512]{2,1,0:T(8,128)(2,1)S(1)} %pad_maximum_fusion.1.refs_1_), channel_id=1, source_target_pairs={{0,64},{16,80},{32,96},{48,112},{64,0},{80,16},{96,32},{112,48},{1... | collective-permute-start | bytes 196616 | tf_op jit(solution)/shard_map/ppermute | solution.py:17
  118.5 1.5 collective-permute-start.17
  120.0 5.5 %collective-permute-start.18 = (bf16[2,32,512]{2,1,0:T(8,128)(2,1)S(1)}, bf16[2,32,512]{2,1,0:T(8,128)(2,1)S(1)}, u32[]{:S(2)}, u32[]{:S(2)}) collective-permute-start(bf16[2,32,512]{2,1,0:T(8,128)(2,1)S(1)} %pad_maximum_fusion.2.refs_1_), channel_id=1, source_target_pairs={{0,32},{16,48},{32,64},{48,80},{64,96},{80,112},{96,0},{112,16},{1... | collective-permute-start | bytes 196616 | tf_op jit(solution)/shard_map/ppermute | solution.py:17
  126.4 30.8 %all-to-all-start.2 = ((bf16[16,32,512]{2,1,0:T(8,128)(2,1)}), bf16[16,32,512]{2,1,0:T(8,128)(2,1)S(1)}, u32[]{:S(2)}, u32[]{:S(2)}) async-start(bf16[16,32,512]{2,1,0:T(8,128)(2,1)} %broadcast_in_dim.4), calls=%async_computation.2 | async-start | bytes 1048576 | tf_op jit(solution)/shard_map/all_to_all | solution.py:259
  131.8 4.3 %collective-permute-start.19 = (bf16[2,32,512]{2,1,0:T(8,128)(2,1)S(1)}, bf16[2,32,512]{2,1,0:T(8,128)(2,1)S(1)}, u32[]{:S(2)}, u32[]{:S(2)}) collective-permute-start(bf16[2,32,512]{2,1,0:T(8,128)(2,1)S(1)} %pad_maximum_fusion.2.refs_1_), channel_id=1, source_target_pairs={{0,96},{16,112},{32,0},{48,16},{64,32},{80,48},{96,64},{112,80},{1... | collective-permute-start | bytes 196616 | tf_op jit(solution)/shard_map/ppermute | solution.py:17
  133.3 5.8 %collective-permute-start.20 = (bf16[2,32,512]{2,1,0:T(8,128)(2,1)S(1)}, bf16[2,32,512]{2,1,0:T(8,128)(2,1)S(1)}, u32[]{:S(2)}, u32[]{:S(2)}) collective-permute-start(bf16[2,32,512]{2,1,0:T(8,128)(2,1)S(1)} %pad_maximum_fusion.2.refs_1_), channel_id=1, source_target_pairs={{0,64},{16,80},{32,96},{48,112},{64,0},{80,16},{96,32},{112,48},{1... | collective-permute-start | bytes 196616 | tf_op jit(solution)/shard_map/ppermute | solution.py:17
  144.3 5.5 %collective-permute-start.22 = (bf16[2,32,512]{2,1,0:T(8,128)(2,1)S(1)}, bf16[2,32,512]{2,1,0:T(8,128)(2,1)S(1)}, u32[]{:S(2)}, u32[]{:S(2)}) collective-permute-start(bf16[2,32,512]{2,1,0:T(8,128)(2,1)S(1)} %pad_maximum_fusion.3.refs_1_), channel_id=1, source_target_pairs={{0,32},{16,48},{32,64},{48,80},{64,96},{80,112},{96,0},{112,16},{1... | collective-permute-start | bytes 196616 | tf_op jit(solution)/shard_map/ppermute | solution.py:17
  144.9 5.5 %collective-permute-start.23 = (bf16[2,32,512]{2,1,0:T(8,128)(2,1)S(1)}, bf16[2,32,512]{2,1,0:T(8,128)(2,1)S(1)}, u32[]{:S(2)}, u32[]{:S(2)}) collective-permute-start(bf16[2,32,512]{2,1,0:T(8,128)(2,1)S(1)} %pad_maximum_fusion.3.refs_1_), channel_id=1, source_target_pairs={{0,96},{16,112},{32,0},{48,16},{64,32},{80,48},{96,64},{112,80},{1... | collective-permute-start | bytes 196616 | tf_op jit(solution)/shard_map/ppermute | solution.py:17
  147.6 5.8 %collective-permute-start.24 = (bf16[2,32,512]{2,1,0:T(8,128)(2,1)S(1)}, bf16[2,32,512]{2,1,0:T(8,128)(2,1)S(1)}, u32[]{:S(2)}, u32[]{:S(2)}) collective-permute-start(bf16[2,32,512]{2,1,0:T(8,128)(2,1)S(1)} %pad_maximum_fusion.3.refs_1_), channel_id=1, source_target_pairs={{0,64},{16,80},{32,96},{48,112},{64,0},{80,16},{96,32},{112,48},{1... | collective-permute-start | bytes 196616 | tf_op jit(solution)/shard_map/ppermute | solution.py:17
  174.9 1.3 collective-permute-start.25
  176.2 5.9 %collective-permute-start.28 = (f32[32,512]{1,0:T(8,128)S(1)}, f32[32,512]{1,0:T(8,128)S(1)}, u32[]{:S(2)}, u32[]{:S(2)}) collective-permute-start(f32[32,512]{1,0:T(8,128)S(1)} %add.114), channel_id=1, source_target_pairs={{0,64},{16,80},{32,96},{48,112},{64,0},{80,16},{96,32},{112,48},{1... | collective-permute-start | bytes 196616 | tf_op jit(solution)/shard_map/ppermute | solution.py:17
  176.5 5.6 %collective-permute-start.27 = (f32[32,512]{1,0:T(8,128)S(1)}, f32[32,512]{1,0:T(8,128)S(1)}, u32[]{:S(2)}, u32[]{:S(2)}) collective-permute-start(f32[32,512]{1,0:T(8,128)S(1)} %add.114), channel_id=1, source_target_pairs={{0,96},{16,112},{32,0},{48,16},{64,32},{80,48},{96,64},{112,80},{1... | collective-permute-start | bytes 196616 | tf_op jit(solution)/shard_map/ppermute | solution.py:17
  178.4 5.5 %collective-permute-start.26 = (f32[32,512]{1,0:T(8,128)S(1)}, f32[32,512]{1,0:T(8,128)S(1)}, u32[]{:S(2)}, u32[]{:S(2)}) collective-permute-start(f32[32,512]{1,0:T(8,128)S(1)} %add.114), channel_id=1, source_target_pairs={{0,32},{16,48},{32,64},{48,80},{64,96},{80,112},{96,0},{112,16},{1... | collective-permute-start | bytes 196616 | tf_op jit(solution)/shard_map/ppermute | solution.py:17
  (4 other events, 132.9 us)
Sparse Core Ops, SparseCore 0:
  10.8 103.8 all-gather.2

commit v5 on v4

v5 whole, which is shorter than its diff:
```python
import jax
import jax.numpy as jnp
from jax import lax
from jax.experimental import pallas as pl
from jax.experimental.pallas import tpu as pltpu
from jax.sharding import PartitionSpec as P

S = 8192
BF = jnp.bfloat16
F32 = jnp.float32
VMEM = pltpu.VMEM
ROOMY = pltpu.CompilerParams(vmem_limit_bytes=20 << 20)


def x_shift(v, step):
    return lax.ppermute(v, "row", [(r, (r + 2 * step) % 8) for r in range(8)])


def other_core(v):
    return lax.ppermute(v, "row", [(r, r ^ 1) for r in range(8)])


def z_exchange(v):
    groups = [[4 * y + z for z in range(4)] for y in range(4)]
    return lax.all_to_all(v, "col", 0, 0, axis_index_groups=groups, tiled=True)


def y_gather(v):
    groups = [[4 * y + z for y in range(4)] for z in range(4)]
    return lax.all_gather(v, "col", axis=0, axis_index_groups=groups, tiled=True)


def whole(array):
    rank = len(array.shape)
    return pl.BlockSpec(array.shape, lambda i, *_: (0,) * rank)


def cost(flops, moved):
    return pl.CostEstimate(flops=flops, bytes_accessed=moved, transcendentals=0)


def in_hbm(array):
    return pltpu.with_memory_space_constraint(array, pltpu.HBM)


def prepare_kernel(values, first, second, linking, low, high, lines):
    low[...] = values[:, :128, :]
    high[...] = values[:, 128:, :]
    for m, source in enumerate((first, linking, second)):
        turned = jnp.transpose(source[...].astype(F32)).astype(BF)
        for q in range(4):
            lines[q, m] = turned[64 * q : 64 * (q + 1), :]


def prepare(values, inverses, coupling):
    inverses = in_hbm(inverses.reshape(2, 512, 256))
    coupling = in_hbm(coupling.reshape(512, 256))
    half = jax.ShapeDtypeStruct((3, 128, 512), BF)
    out = [half, half, jax.ShapeDtypeStruct((4, 3, 64, 512), BF)]
    return pl.pallas_call(
        prepare_kernel,
        grid=(1,),
        in_specs=[
            whole(values),
            pl.BlockSpec((None, 512, 256), lambda i: (0, 0, 0)),
            pl.BlockSpec((None, 512, 256), lambda i: (1, 0, 0)),
            whole(coupling),
        ],
        out_specs=list(map(whole, out)),
        out_shape=out,
        compiler_params=ROOMY,
    )(in_hbm(values), inverses, inverses, coupling)


def split_tiles_kernel(src, dst):
    dst[:, 0] = pltpu.einshape("tbu->btu", src[0])


def split_tiles(left):
    rounds, tile, count, width = left.shape
    rows = 256
    out = pl.pallas_call(
        split_tiles_kernel,
        grid=(rounds, tile // rows),
        in_specs=[pl.BlockSpec((1, rows, count, width), lambda a, t: (a, t, 0, 0))],
        out_specs=pl.BlockSpec((count, 1, rows, width), lambda a, t: (0, a, t, 0)),
        out_shape=pltpu.HBM((count, rounds, tile, width), BF),
        cost_estimate=cost(0, 2 * left.size * 2),
        compiler_params=ROOMY,
    )(left)
    return out.reshape(count, rounds * tile, width)


def accumulate(acc, left, held, step):
    for base in (0, 512):
        here = slice(base, base + 512)
        total = jnp.dot(left[0, here, :], held[0], preferred_element_type=F32)
        for t in range(1, 3):
            total += jnp.dot(left[t, here, :], held[t], preferred_element_type=F32)

        @pl.when(step == 0)
        def _():
            acc[here, :] = total

        @pl.when(step > 0)
        def _():
            acc[here, :] += total


def take_pieces(step, pieces, held):
    half = held.shape[1] // 2
    for j in range(len(pieces) // 2):

        @pl.when(step == j)
        def _():
            held[:, :half, :] = pieces[2 * j][...]
            held[:, half:, :] = pieces[2 * j + 1][...]


def first_products_kernel(order, left, *refs):
    del order
    *pieces, acc, held = refs
    step = pl.program_id(0)
    take_pieces(step, pieces, held)
    accumulate(acc, left, held, step)


def next_products_kernel(order, left, before, token, *refs):
    del order, token
    *pieces, acc, held = refs
    step = pl.program_id(0)

    @pl.when(step == 0)
    def _():
        acc[...] = before[...]

    take_pieces(step, pieces, held)
    accumulate(acc, left, held, step + 1)


def last_products_kernel(order, left, before, token, *refs):
    *pieces, first, second, acc, held = refs
    next_products_kernel(order, left, before, token, *pieces, acc, held)

    @pl.when(pl.program_id(0) == pl.num_programs(0) - 1)
    def _():
        for out, base in ((first, 0), (second, 512)):
            for y in range(4):
                for z in range(4):
                    for a in range(2):
                        top = base + 256 * a + 64 * z
                        block = acc[top : top + 64, 128 * y : 128 * (y + 1)]
                        out[4 * y + z, 64 * a : 64 * (a + 1), :] = block.astype(BF)


def piece_specs(pieces):
    specs = []
    for array, place in pieces:
        specs.append(pl.BlockSpec((3, 128, 512), lambda i, *_, place=place: (0, place, 0)))
    return specs


def products(order, left, pieces, before=None, token=None, last=False):
    blocks = len(pieces) // 2
    _, rows, width = left.shape
    left_spec = pl.BlockSpec((3, rows, width), lambda i, order: (order[i], 0, 0))
    left = pltpu.with_memory_space_constraint(left, pltpu.HBM)
    arrays = [array for array, _ in pieces]
    scratch = [VMEM((3, 256, 512), BF)]
    flops = blocks * 2 * rows * 768 * 512
    moved = blocks * 3 * 2 * (rows * 256 + 256 * 512) + rows * 512 * 4
    starts = [] if before is None else [before, token]
    out = jax.ShapeDtypeStruct((rows, 512), F32)
    kernel = first_products_kernel if before is None else next_products_kernel
    if last:
        out = [jax.ShapeDtypeStruct((16, 128, 128), BF)] * 2
        kernel = last_products_kernel
        scratch = [VMEM((rows, 512), F32), *scratch]
    return pl.pallas_call(
        kernel,
        grid_spec=pltpu.PrefetchScalarGridSpec(
            num_scalar_prefetch=1,
            grid=(blocks,),
            in_specs=[left_spec, *map(whole, starts), *piece_specs(pieces)],
            out_specs=jax.tree.map(whole, out),
            scratch_shapes=scratch,
        ),
        out_shape=out,
        cost_estimate=cost(flops, moved),
        compiler_params=ROOMY,
    )(order, left, *starts, *arrays)


RELATIVE = (0, -1, 1, 2)


def stage_kernel(order, own, one, two, three, weights, out, held):
    for i, source in enumerate((own, one, two, three)):
        for k in range(2):
            line = order[2 * i + k]
            held[line] = source[k, :64, :]
            held[8 + line] = source[k, 64:, :]
    values = held[...].reshape(1024, 128).astype(F32)
    values = jnp.transpose(values).astype(BF)
    factor = weights[...].reshape(1024, 512)
    total = jnp.dot(values, factor, preferred_element_type=F32)
    total = jnp.transpose(total).astype(BF)
    for q in range(4):
        for a in range(2):
            top = 256 * a + 64 * q
            out[q, 64 * a : 64 * (a + 1), :] = total[top : top + 64, :]


def over_cores(values):
    return jnp.stack([values, other_core(values)])


def over_chips(pair):
    return [pair, x_shift(pair, 1), x_shift(pair, -1), x_shift(pair, 2)]


SCALARS = pl.BlockSpec(memory_space=pltpu.SMEM)


def stage(order, values, panels, which):
    moved = over_chips(over_cores(values))
    out = jax.ShapeDtypeStruct((4, 128, 128), BF)
    partial = pl.pallas_call(
        stage_kernel,
        grid=(1,),
        in_specs=[
            SCALARS,
            *map(whole, moved),
            pl.BlockSpec((16, None, 64, 512), lambda i: (0, which, 0, 0)),
        ],
        out_specs=whole(out),
        scratch_shapes=[VMEM((16, 64, 128), BF)],
        out_shape=out,
        cost_estimate=cost(2 * 128 * 1024 * 512, 2 * 1024 * 512),
        compiler_params=ROOMY,
    )(order, *moved, panels)
    return z_exchange(partial).astype(F32).sum(axis=0)


def over_sites(partial):
    return lax.all_to_all(partial, "col", 0, 0, tiled=True).astype(F32).sum(axis=0)


def all_sites(values):
    sent = jnp.broadcast_to(values[None], (16, 128, 128))
    every = lax.all_to_all(sent, "col", 0, 0, tiled=True).reshape(4, 4, 2, 64, 128)
    return jnp.transpose(every, (2, 1, 3, 0, 4)).reshape(2, 256, 512)


def row_sum(values):
    values = values + other_core(values)
    return values + x_shift(values, 1) + x_shift(values, -1) + x_shift(values, 2)


def outer_part(every, col):
    own = lax.dynamic_slice_in_dim(every, 32 * col, 32, 2)
    return jnp.einsum("atm,atn->mn", own, every, preferred_element_type=F32)


def body(left_factor, prev_solution, cross, inverses, coupling, prior_cov):
    row, col = lax.axis_index("row"), lax.axis_index("col")
    x, k = row // 2, row % 2
    y, z = col // 4, col % 4
    order = jnp.stack([(x + d) % 4 * 2 + (k + e) % 2 for d in RELATIVE for e in range(2)])
    order = order.astype(jnp.int32)

    low, high, lines = prepare(prev_solution, inverses, coupling)
    before_low, after_high = x_shift(low, 1), x_shift(high, -1)
    before_high, after_low = x_shift(high, 1), x_shift(low, -1)
    sibling = in_hbm(other_core(prev_solution))
    left = split_tiles(in_hbm(left_factor))
    before_low, after_high, left, lines = lax.optimization_barrier(
        (before_low, after_high, left, lines)
    )
    panels = in_hbm(y_gather(z_exchange(lines)))
    far_low, far_high = x_shift(before_low, 1), x_shift(after_high, -1)
    pieces = [(prev_solution, 0), (prev_solution, 1), (sibling, 0), (sibling, 1)]
    started = products(order[:2], left, pieces)
    before_high, after_low, token = lax.optimization_barrier(
        (before_high, after_low, started[:8, :128])
    )
    pieces = []
    for pair in ((before_low, before_high), (after_low, after_high)):
        pieces += [(v, 0) for v in pair] + [(other_core(v), 0) for v in pair]
    started = products(order[2:6], left, pieces, started, token)
    far_low, far_high, token = lax.optimization_barrier(
        (far_low, far_high, started[:8, :128])
    )
    far = (far_low, far_high)
    pieces = [(v, 0) for v in far] + [(other_core(v), 0) for v in far]
    first, second = products(order[6:], left, pieces, started, token, last=True)

    known = lax.dynamic_slice(cross, (0, 64 * z, 128 * y), (4, 64, 128))
    known = known.astype(F32).reshape(2, 128, 128)
    first_rhs = (known[0] - over_sites(first)).astype(BF)
    first_rhs, second = lax.optimization_barrier((first_rhs, second))
    rest = known[1] - over_sites(second)
    solved_first = stage(order, first_rhs, panels, 0).astype(BF)
    every_first = all_sites(solved_first)
    second_rhs = (rest - stage(order, solved_first, panels, 1)).astype(BF)
    second_rhs, every_first = lax.optimization_barrier((second_rhs, every_first))
    solved_second = stage(order, second_rhs, panels, 2).astype(BF)
    every_second = all_sites(solved_second)
    outer = outer_part(every_first, col) + outer_part(every_second, col)
    pred_cov = prior_cov - row_sum(outer) / S
    return jnp.concatenate([every_first, every_second]), pred_cov


def solution(mesh):
    placed = (
        P(None, "row", None, "col"),
        P("row", "col", None),
        P(None, "row", None),
        P(None, None, "row", None, "col"),
        P(None, "row", None, "col"),
        P("col", None),
    )
    return jax.shard_map(
        body,
        mesh=mesh,
        in_specs=placed,
        out_specs=(P(None, "row", None), P("col", None)),
        check_vma=False,
    )
```

time: 192 us -> 211 us (1.099)
  blocking collectives: 17.1 us -> 44.1 us
  Pallas kernels: 44.8 us -> 37.4 us
  waiting for transfers between devices: 66.5 us -> 61.6 us
  local copies, waits for them, and re-layouts: 1.68 us -> 6.25 us
    all_to_all x1 -> x4, blocking collectives: 17.1 us -> 44.1 us  [z_exchange(): return lax.all_to_all(v, 'col', 0, 0, axis_index_groups=groups, tiled=True)]
    all_to_all x3 -> x4, waiting for transfers between devices: 15.5 us -> 30.5 us  [the longest x2 19.6 us: all_sites(): lax.all_to_all(sent, 'col', 0, 0, tiled=True).reshape(4, 4, 2, 64, 128)]
    all_gather x1, waiting for transfers between devices: 13.9 us -> 0.01 us  [y_gather(): lax.all_gather(v, 'col', axis=0, axis_index_groups=groups, tiled=True)]
    ppermute x18, waiting for transfers between devices: 32.6 us -> 24.3 us  [x_shift(): return lax.ppermute(v, 'row', [(r, (r + 2 * step) % 8) for r in range(8)])]
    pallas_call x3, Pallas kernels: 11.6 us -> 5.03 us  [stage(): pl.pallas_call(stage_kernel, grid=(1,), in_specs=[SCALARS, *map(whole, mo...]
    unnamed x7 -> x8, local copies, waits for them, and re-layouts: 0.14 us -> 2.93 us
    ppermute x11, waiting for transfers between devices: 4.41 us -> 6.76 us  [other_core(): return lax.ppermute(v, 'row', [(r, r ^ 1) for r in range(8)])]
    all_to_all x3 -> x4, starting transfers between devices: 19 us -> 17.3 us  [the longest x2 8.75 us: over_sites(): lax.all_to_all(partial, 'col', 0, 0, tiled=True).astype(F32).sum(axis=0)]
  transfers between devices with their start and end apart: 33 -> 34, of which waited for: 20 -> 21; matrix products, arithmetic and copies ran while one was open for 1% -> 1% of each run, Pallas kernels for 22% -> 15%
where the time goes in v5:
time: 211 us; the launch traced here: 210 us
  waiting for transfers between devices  61.6 us (29%)
  blocking collectives  44.1 us (21%)
  starting transfers between devices  42.4 us (20%)
  Pallas kernels  37.4 us (18%)
  between operations  14.4 us (7%)
  local copies, waits for them, and re-layouts  6.25 us (3%)
  other arithmetic  3.09 us (1%)
    all_to_all x4, blocking collectives, z_exchange(): return lax.all_to_all(v, 'col', 0, 0, axis_index_groups=groups, tiled=True)  44.1 us
    ppermute x18, waiting for transfers between devices, x_shift(): return lax.ppermute(v, 'row', [(r, (r + 2 * step) % 8) for r in range(8)])  24.3 us
    ppermute x18, starting transfers between devices, x_shift(): return lax.ppermute(v, 'row', [(r, (r + 2 * step) % 8) for r in range(8)])  22.9 us
    all_to_all x2, waiting for transfers between devices, all_sites(): lax.all_to_all(sent, 'col', 0, 0, tiled=True).reshape(4, 4, 2, 64, 128)  19.6 us
    pallas_call x3, Pallas kernels, products(): pl.pallas_call(kernel, grid_spec=pltpu.PrefetchScalarGridSpec(num_scalar_...  19.5 us
    all_to_all x2, waiting for transfers between devices, over_sites(): lax.all_to_all(partial, 'col', 0, 0, tiled=True).astype(F32).sum(axis=0)  10.9 us
    pallas_call x1, Pallas kernels, split_tiles(): pl.pallas_call(split_tiles_kernel, grid=(rounds, tile // rows), in_specs=...  10.5 us
    all_to_all x2, starting transfers between devices, over_sites(): lax.all_to_all(partial, 'col', 0, 0, tiled=True).astype(F32).sum(axis=0)  8.75 us
  transfers between devices with their start and end apart: 34, of which 21 were waited for; matrix products, arithmetic and copies ran while one was open for 1% of the time, Pallas kernels for 15%

profile of v5, /device:TPU:0, one launch (start us, length us, event | category | flops | bytes accessed | tf_op | source)
XLA Modules:
  0.0 209.7 jit_solution(17335213606138758865)
XLA Ops:
  7.2 2.5 %shard_map.77 = (bf16[3,128,512]{2,1,0:T(8,128)(2,1)}, bf16[3,128,512]{2,1,0:T(8,128)(2,1)}, bf16[4,3,64,512]{3,2,1,0:T(8,128)(2,1)S(1)}) custom-call(bf16[3,256,512]{2,1,0:T(8,128)(2,1)} %refs_1_.1, bf16[2,512,256]{2,1,0:T(8,128)(2,1)} %bitcast.46, bf16[2,512,256]{2,1,0:T(8,128)(2,1)} %bitcast.47, bf16[512,256]{1,0:T(8,128)(2,1)} %bitcast.49), custom_call_target="tpu_custom_call" | custom-call | tf_op jit(solution)/shard_map/pallas_call | solution.py:60
  11.3 1.7 collective-permute-start.1
  12.9 10.5 %shard_map.78 = bf16[24,4,256,256]{3,2,1,0:T(8,128)(2,1)} custom-call(bf16[4,256,24,256]{3,2,1,0:T(8,128)(2,1)} %src.1), custom_call_target="tpu_custom_call" | custom-call | bytes 25165824 | tf_op jit(solution)/shard_map/pallas_call | solution.py:82
  23.4 17.0 %all_to_all.40 = bf16[4,3,64,512]{3,2,1,0:T(8,128)(2,1)} all-to-all(bf16[4,3,64,512]{3,2,1,0:T(8,128)(2,1)S(1)} %get-tuple-element.37), channel_id=1, replica_groups={{0,1,2,3},{4,5,6,7},{8,9,10,11},{12,13,14,15},{16,17,18,19},{20,21,22,2..., dimensions={0} | all-to-all | bytes 1572864 | tf_op jit(solution)/shard_map/all_to_all | solution.py:25
  40.9 3.0 %collective-permute-start.4 = (bf16[3,128,512]{2,1,0:T(8,128)(2,1)}, bf16[3,128,512]{2,1,0:T(8,128)(2,1)}, u32[]{:S(2)}, u32[]{:S(2)}) collective-permute-start(bf16[3,128,512]{2,1,0:T(8,128)(2,1)} %get-tuple-element.21), channel_id=1, source_target_pairs={{0,96},{16,112},{32,0},{48,16},{64,32},{80,48},{96,64},{112,80},{1... | collective-permute-start | bytes 1179656 | tf_op jit(solution)/shard_map/ppermute | solution.py:16
  44.4 4.9 %shard_map.79.before = f32[1024,512]{1,0:T(8,128)S(1)} custom-call(s32[2]{0:T(128)S(1)} %pad_add_fusion.2.order, bf16[24,1024,256]{2,1,0:T(8,128)(2,1)} %bitcast.41, bf16[3,256,512]{2,1,0:T(8,128)(2,1)S(1)} %copy-done.2, bf16[3,256,512]{2,1,0:T(8,128)(2,1)S(1)} %copy-done.2, bf16[3,256,512]{2,1,0:T(8,128)(2,1)} %collective-permute-done.2.refs_2_.refs_3_, ...), custom_call_target="tpu_custom_call" | custom-call | flops 1610612736 | bytes 6815744 | tf_op jit(solution)/shard_map/pallas_call | solution.py:179
  49.3 4.3 %collective-permute-done.3.refs_1_ = bf16[3,128,512]{2,1,0:T(8,128)(2,1)} collective-permute-done((bf16[3,128,512]{2,1,0:T(8,128)(2,1)}, bf16[3,128,512]{2,1,0:T(8,128)(2,1)}, u32[]{:S(2)}, u32[]{:S(2)}) %collective-permute-start.3) | collective-permute-done | bytes 393248 | tf_op jit(solution)/shard_map/ppermute | solution.py:16
  54.4 3.0 %collective-permute-start.10 = (bf16[3,128,512]{2,1,0:T(8,128)(2,1)}, bf16[3,128,512]{2,1,0:T(8,128)(2,1)}, u32[]{:S(2)}, u32[]{:S(2)}) collective-permute-start(bf16[3,128,512]{2,1,0:T(8,128)(2,1)} %collective-permute-done.1.refs_5_), channel_id=1, source_target_pairs={{0,96},{16,112},{32,0},{48,16},{64,32},{80,48},{96,64},{112,80},{1... | collective-permute-start | bytes 1179656 | tf_op jit(solution)/shard_map/ppermute | solution.py:16
  57.4 8.5 %shard_map.80.before = f32[1024,512]{1,0:T(8,128)S(1)} custom-call(s32[4]{0:T(128)S(1)} %pad_add_fusion.1.order, bf16[24,1024,256]{2,1,0:T(8,128)(2,1)} %bitcast.42, f32[1024,512]{1,0:T(8,128)S(1)} %shard_map.79.before, f32[8,128]{1,0:T(8,128)S(1)} %slice.26.token, bf16[3,128,512]{2,1,0:T(8,128)(2,1)S(1)} %collective-permute-done.refs_0_, ...), custom_call_target="tpu_custom_call" | custom-call | flops 3221225472 | bytes 11534336 | tf_op jit(solution)/shard_map/pallas_call | solution.py:179
  71.4 6.1 %shard_map.81 = (bf16[16,128,128]{2,1,0:T(8,128)(2,1)}, bf16[16,128,128]{2,1,0:T(8,128)(2,1)}) custom-call(s32[2]{0:T(128)S(1)} %pad_add_fusion.order, bf16[24,1024,256]{2,1,0:T(8,128)(2,1)} %bitcast.43, f32[1024,512]{1,0:T(8,128)S(1)} %copy-done.1, f32[8,128]{1,0:T(8,128)S(1)} %slice.27.token, bf16[3,128,512]{2,1,0:T(8,128)(2,1)S(1)} %collective-permute-done.9.refs_0_, ...), custom_call_target="tpu_custom_call" | custom-call | flops 1610612736 | bytes 6815744 | tf_op jit(solution)/shard_map/pallas_call | solution.py:179
  77.5 5.2 %all-to-all-start = ((bf16[16,128,128]{2,1,0:T(8,128)(2,1)}), bf16[16,128,128]{2,1,0:T(8,128)(2,1)S(1)}, u32[]{:S(2)}, u32[]{:S(2)}) async-start(bf16[16,128,128]{2,1,0:T(8,128)(2,1)} %get-tuple-element.33), calls=%async_computation | async-start | bytes 1048576 | tf_op jit(solution)/shard_map/all_to_all | solution.py:246
  83.6 10.9 %all-to-all-done = bf16[16,128,128]{2,1,0:T(8,128)(2,1)S(1)} async-done(((bf16[16,128,128]{2,1,0:T(8,128)(2,1)}), bf16[16,128,128]{2,1,0:T(8,128)(2,1)S(1)}, u32[]{:S(2)}, u32[]{:S(2)}) %all-to-all-start) | async-done | bytes 524320 | tf_op jit(solution)/shard_map/all_to_all | solution.py:246
  96.4 2.7 %collective-permute-start.15 = (bf16[2,128,128]{2,1,0:T(8,128)(2,1)S(1)}, bf16[2,128,128]{2,1,0:T(8,128)(2,1)S(1)}, u32[]{:S(2)}, u32[]{:S(2)}) collective-permute-start(bf16[2,128,128]{2,1,0:T(8,128)(2,1)S(1)} %pad_maximum_fusion.1.own), channel_id=1, source_target_pairs={{0,96},{16,112},{32,0},{48,16},{64,32},{80,48},{96,64},{112,80},{1... | collective-permute-start | bytes 196616 | tf_op jit(solution)/shard_map/ppermute | solution.py:16
  101.7 3.3 %collective-permute-done.16.three = bf16[2,128,128]{2,1,0:T(8,128)(2,1)S(1)} collective-permute-done((bf16[2,128,128]{2,1,0:T(8,128)(2,1)S(1)}, bf16[2,128,128]{2,1,0:T(8,128)(2,1)S(1)}, u32[]{:S(2)}, u32[]{:S(2)}) %collective-permute-start.16) | collective-permute-done | bytes 65568 | tf_op jit(solution)/shard_map/ppermute | solution.py:16
  104.9 1.7 shard_map.82
  106.6 8.4 %all_to_all.41 = bf16[4,128,128]{2,1,0:T(8,128)(2,1)S(1)} all-to-all(bf16[4,128,128]{2,1,0:T(8,128)(2,1)S(1)} %shard_map.82), channel_id=1, replica_groups={{0,1,2,3},{4,5,6,7},{8,9,10,11},{12,13,14,15},{16,17,18,19},{20,21,22,2..., dimensions={0} | all-to-all | bytes 262144 | tf_op jit(solution)/shard_map/all_to_all | solution.py:25
  115.0 3.6 %all-to-all-start.1 = ((bf16[16,128,128]{2,1,0:T(8,128)(2,1)}), bf16[16,128,128]{2,1,0:T(8,128)(2,1)S(1)}, u32[]{:S(2)}, u32[]{:S(2)}) async-start(bf16[16,128,128]{2,1,0:T(8,128)(2,1)} %get-tuple-element.35), calls=%async_computation.1 | async-start | bytes 1048576 | tf_op jit(solution)/shard_map/all_to_all | solution.py:246
  120.1 3.2 %collective-permute-start.19 = (bf16[2,128,128]{2,1,0:T(8,128)(2,1)S(1)}, bf16[2,128,128]{2,1,0:T(8,128)(2,1)S(1)}, u32[]{:S(2)}, u32[]{:S(2)}) collective-permute-start(bf16[2,128,128]{2,1,0:T(8,128)(2,1)S(1)} %pad_maximum_fusion.2.own), channel_id=1, source_target_pairs={{0,96},{16,112},{32,0},{48,16},{64,32},{80,48},{96,64},{112,80},{1... | collective-permute-start | bytes 196616 | tf_op jit(solution)/shard_map/ppermute | solution.py:16
  123.4 2.2 %collective-permute-done.18.one = bf16[2,128,128]{2,1,0:T(8,128)(2,1)S(1)} collective-permute-done((bf16[2,128,128]{2,1,0:T(8,128)(2,1)S(1)}, bf16[2,128,128]{2,1,0:T(8,128)(2,1)S(1)}, u32[]{:S(2)}, u32[]{:S(2)}) %collective-permute-start.18) | collective-permute-done | bytes 65568 | tf_op jit(solution)/shard_map/ppermute | solution.py:16
  126.2 3.0 %collective-permute-done.20.three = bf16[2,128,128]{2,1,0:T(8,128)(2,1)S(1)} collective-permute-done((bf16[2,128,128]{2,1,0:T(8,128)(2,1)S(1)}, bf16[2,128,128]{2,1,0:T(8,128)(2,1)S(1)}, u32[]{:S(2)}, u32[]{:S(2)}) %collective-permute-start.20) | collective-permute-done | bytes 65568 | tf_op jit(solution)/shard_map/ppermute | solution.py:16
  129.1 1.7 shard_map.83
  130.8 10.4 %all_to_all.42 = bf16[4,128,128]{2,1,0:T(8,128)(2,1)S(1)} all-to-all(bf16[4,128,128]{2,1,0:T(8,128)(2,1)S(1)} %shard_map.83), channel_id=1, replica_groups={{0,1,2,3},{4,5,6,7},{8,9,10,11},{12,13,14,15},{16,17,18,19},{20,21,22,2..., dimensions={0} | all-to-all | bytes 262144 | tf_op jit(solution)/shard_map/all_to_all | solution.py:25
  142.1 5.0 %all-to-all-start.5 = ((bf16[16,128,128]{2,1,0:T(8,128)(2,1)}), bf16[16,128,128]{2,1,0:T(8,128)(2,1)S(1)}, u32[]{:S(2)}, u32[]{:S(2)}) async-start(bf16[16,128,128]{2,1,0:T(8,128)(2,1)} %broadcast_in_dim.4), calls=%async_computation.5 | async-start | bytes 1048576 | tf_op jit(solution)/shard_map/all_to_all | solution.py:251
  147.2 10.0 %all-to-all-done.5 = bf16[16,128,128]{2,1,0:T(8,128)(2,1)S(1)} async-done(((bf16[16,128,128]{2,1,0:T(8,128)(2,1)}), bf16[16,128,128]{2,1,0:T(8,128)(2,1)S(1)}, u32[]{:S(2)}, u32[]{:S(2)}) %all-to-all-start.5) | async-done | bytes 524320 | tf_op jit(solution)/shard_map/all_to_all | solution.py:251
  159.2 3.2 %collective-permute-start.23 = (bf16[2,128,128]{2,1,0:T(8,128)(2,1)S(1)}, bf16[2,128,128]{2,1,0:T(8,128)(2,1)S(1)}, u32[]{:S(2)}, u32[]{:S(2)}) collective-permute-start(bf16[2,128,128]{2,1,0:T(8,128)(2,1)S(1)} %pad_maximum_fusion.3.own), channel_id=1, source_target_pairs={{0,96},{16,112},{32,0},{48,16},{64,32},{80,48},{96,64},{112,80},{1... | collective-permute-start | bytes 196616 | tf_op jit(solution)/shard_map/ppermute | solution.py:16
  162.4 2.2 %collective-permute-done.22.one = bf16[2,128,128]{2,1,0:T(8,128)(2,1)S(1)} collective-permute-done((bf16[2,128,128]{2,1,0:T(8,128)(2,1)S(1)}, bf16[2,128,128]{2,1,0:T(8,128)(2,1)S(1)}, u32[]{:S(2)}, u32[]{:S(2)}) %collective-permute-start.22) | collective-permute-done | bytes 65568 | tf_op jit(solution)/shard_map/ppermute | solution.py:16
  165.2 3.0 %collective-permute-done.24.three = bf16[2,128,128]{2,1,0:T(8,128)(2,1)S(1)} collective-permute-done((bf16[2,128,128]{2,1,0:T(8,128)(2,1)S(1)}, bf16[2,128,128]{2,1,0:T(8,128)(2,1)S(1)}, u32[]{:S(2)}, u32[]{:S(2)}) %collective-permute-start.24) | collective-permute-done | bytes 65568 | tf_op jit(solution)/shard_map/ppermute | solution.py:16
  168.2 1.7 shard_map.84
  169.9 8.4 %all_to_all.43 = bf16[4,128,128]{2,1,0:T(8,128)(2,1)S(1)} all-to-all(bf16[4,128,128]{2,1,0:T(8,128)(2,1)S(1)} %shard_map.84), channel_id=1, replica_groups={{0,1,2,3},{4,5,6,7},{8,9,10,11},{12,13,14,15},{16,17,18,19},{20,21,22,2..., dimensions={0} | all-to-all | bytes 262144 | tf_op jit(solution)/shard_map/all_to_all | solution.py:25
  179.2 3.6 %all-to-all-start.7 = ((bf16[16,128,128]{2,1,0:T(8,128)(2,1)}), bf16[16,128,128]{2,1,0:T(8,128)(2,1)S(1)}, u32[]{:S(2)}, u32[]{:S(2)}) async-start(bf16[16,128,128]{2,1,0:T(8,128)(2,1)} %broadcast_in_dim.5), calls=%async_computation.7 | async-start | bytes 1048576 | tf_op jit(solution)/shard_map/all_to_all | solution.py:251
  183.2 9.7 %all-to-all-done.7 = bf16[16,128,128]{2,1,0:T(8,128)(2,1)S(1)} async-done(((bf16[16,128,128]{2,1,0:T(8,128)(2,1)}), bf16[16,128,128]{2,1,0:T(8,128)(2,1)S(1)}, u32[]{:S(2)}, u32[]{:S(2)}) %all-to-all-start.7) | async-done | bytes 524320 | tf_op jit(solution)/shard_map/all_to_all | solution.py:251
  198.3 2.7 %collective-permute-done.28 = f32[32,512]{1,0:T(8,128)S(1)} collective-permute-done((f32[32,512]{1,0:T(8,128)S(1)}, f32[32,512]{1,0:T(8,128)S(1)}, u32[]{:S(2)}, u32[]{:S(2)}) %collective-permute-start.28) | collective-permute-done | bytes 65568 | tf_op jit(solution)/shard_map/ppermute | solution.py:16
  (87 shorter events, 28.6 us)
Async XLA Ops:
  7.2 97.8 %all-gather.2.cloned.1.call-start = ((), (), s32[]{:S(2)}) async-start(), calls=%async_computation.8 | async-start | bytes 3932160 | tf_op jit(solution)/shard_map/all_gather | solution.py:30
  9.7 13.7 %collective-permute-start = (bf16[3,128,512]{2,1,0:T(8,128)(2,1)}, bf16[3,128,512]{2,1,0:T(8,128)(2,1)S(1)}, u32[]{:S(2)}, u32[]{:S(2)}) collective-permute-start(bf16[3,128,512]{2,1,0:T(8,128)(2,1)} %get-tuple-element.21), channel_id=1, source_target_pairs={{0,32},{16,48},{32,64},{48,80},{64,96},{80,112},{96,0},{112,16},{1... | collective-permute-start | bytes 1179656 | tf_op jit(solution)/shard_map/ppermute | solution.py:16
  11.3 12.1 %collective-permute-start.1 = (bf16[3,128,512]{2,1,0:T(8,128)(2,1)}, bf16[3,128,512]{2,1,0:T(8,128)(2,1)}, u32[]{:S(2)}, u32[]{:S(2)}) collective-permute-start(bf16[3,128,512]{2,1,0:T(8,128)(2,1)} %get-tuple-element.22), channel_id=1, source_target_pairs={{0,96},{16,112},{32,0},{48,16},{64,32},{80,48},{96,64},{112,80},{1... | collective-permute-start | bytes 1179656 | tf_op jit(solution)/shard_map/ppermute | solution.py:16
  40.4 4.0 %collective-permute-start.2 = (bf16[3,256,512]{2,1,0:T(8,128)(2,1)S(1)}, bf16[3,256,512]{2,1,0:T(8,128)(2,1)}, u32[]{:S(2)}, u32[]{:S(2)}) collective-permute-start(bf16[3,256,512]{2,1,0:T(8,128)(2,1)S(1)} %copy-done.2), channel_id=1, source_target_pairs={{0,16},{16,0},{32,48},{48,32},{64,80},{80,64},{96,112},{112,96},{1... | collective-permute-start | bytes 2359304 | tf_op jit(solution)/shard_map/ppermute | solution.py:20
  40.5 13.1 %collective-permute-start.3 = (bf16[3,128,512]{2,1,0:T(8,128)(2,1)}, bf16[3,128,512]{2,1,0:T(8,128)(2,1)}, u32[]{:S(2)}, u32[]{:S(2)}) collective-permute-start(bf16[3,128,512]{2,1,0:T(8,128)(2,1)} %get-tuple-element.22), channel_id=1, source_target_pairs={{0,32},{16,48},{32,64},{48,80},{64,96},{80,112},{96,0},{112,16},{1... | collective-permute-start | bytes 1179656 | tf_op jit(solution)/shard_map/ppermute | solution.py:16
  40.9 12.7 %collective-permute-start.4 = (bf16[3,128,512]{2,1,0:T(8,128)(2,1)}, bf16[3,128,512]{2,1,0:T(8,128)(2,1)}, u32[]{:S(2)}, u32[]{:S(2)}) collective-permute-start(bf16[3,128,512]{2,1,0:T(8,128)(2,1)} %get-tuple-element.21), channel_id=1, source_target_pairs={{0,96},{16,112},{32,0},{48,16},{64,32},{80,48},{96,64},{112,80},{1... | collective-permute-start | bytes 1179656 | tf_op jit(solution)/shard_map/ppermute | solution.py:16
  43.9 10.5 %collective-permute-start.5 = (bf16[3,128,512]{2,1,0:T(8,128)(2,1)S(1)}, bf16[3,128,512]{2,1,0:T(8,128)(2,1)}, u32[]{:S(2)}, u32[]{:S(2)}) collective-permute-start(bf16[3,128,512]{2,1,0:T(8,128)(2,1)S(1)} %collective-permute-done.refs_0_), channel_id=1, source_target_pairs={{0,16},{16,0},{32,48},{48,32},{64,80},{80,64},{96,112},{112,96},{1... | collective-permute-start | bytes 1179656 | tf_op jit(solution)/shard_map/ppermute | solution.py:20
  43.9 13.5 %collective-permute-start.8 = (bf16[3,128,512]{2,1,0:T(8,128)(2,1)}, bf16[3,128,512]{2,1,0:T(8,128)(2,1)}, u32[]{:S(2)}, u32[]{:S(2)}) collective-permute-start(bf16[3,128,512]{2,1,0:T(8,128)(2,1)} %collective-permute-done.1.refs_5_), channel_id=1, source_target_pairs={{0,16},{16,0},{32,48},{48,32},{64,80},{80,64},{96,112},{112,96},{1... | collective-permute-start | bytes 1179656 | tf_op jit(solution)/shard_map/ppermute | solution.py:20
  53.6 3.8 %collective-permute-start.6 = (bf16[3,128,512]{2,1,0:T(8,128)(2,1)}, bf16[3,128,512]{2,1,0:T(8,128)(2,1)S(1)}, u32[]{:S(2)}, u32[]{:S(2)}) collective-permute-start(bf16[3,128,512]{2,1,0:T(8,128)(2,1)} %collective-permute-done.3.refs_1_), channel_id=1, source_target_pairs={{0,16},{16,0},{32,48},{48,32},{64,80},{80,64},{96,112},{112,96},{1... | collective-permute-start | bytes 1179656 | tf_op jit(solution)/shard_map/ppermute | solution.py:20
  53.6 3.8 %collective-permute-start.7 = (bf16[3,128,512]{2,1,0:T(8,128)(2,1)}, bf16[3,128,512]{2,1,0:T(8,128)(2,1)}, u32[]{:S(2)}, u32[]{:S(2)}) collective-permute-start(bf16[3,128,512]{2,1,0:T(8,128)(2,1)} %collective-permute-done.4.refs_4_), channel_id=1, source_target_pairs={{0,16},{16,0},{32,48},{48,32},{64,80},{80,64},{96,112},{112,96},{1... | collective-permute-start | bytes 1179656 | tf_op jit(solution)/shard_map/ppermute | solution.py:20
  54.1 13.2 %collective-permute-start.9 = (bf16[3,128,512]{2,1,0:T(8,128)(2,1)S(1)}, bf16[3,128,512]{2,1,0:T(8,128)(2,1)S(1)}, u32[]{:S(2)}, u32[]{:S(2)}) collective-permute-start(bf16[3,128,512]{2,1,0:T(8,128)(2,1)S(1)} %collective-permute-done.refs_0_), channel_id=1, source_target_pairs={{0,32},{16,48},{32,64},{48,80},{64,96},{80,112},{96,0},{112,16},{1... | collective-permute-start | bytes 1179656 | tf_op jit(solution)/shard_map/ppermute | solution.py:16
  54.4 12.9 %collective-permute-start.10 = (bf16[3,128,512]{2,1,0:T(8,128)(2,1)}, bf16[3,128,512]{2,1,0:T(8,128)(2,1)}, u32[]{:S(2)}, u32[]{:S(2)}) collective-permute-start(bf16[3,128,512]{2,1,0:T(8,128)(2,1)} %collective-permute-done.1.refs_5_), channel_id=1, source_target_pairs={{0,96},{16,112},{32,0},{48,16},{64,32},{80,48},{96,64},{112,80},{1... | collective-permute-start | bytes 1179656 | tf_op jit(solution)/shard_map/ppermute | solution.py:16
  67.3 1.7 collective-permute-start.11
  67.3 2.5 %collective-permute-start.12 = (bf16[3,128,512]{2,1,0:T(8,128)(2,1)}, bf16[3,128,512]{2,1,0:T(8,128)(2,1)S(1)}, u32[]{:S(2)}, u32[]{:S(2)}) collective-permute-start(bf16[3,128,512]{2,1,0:T(8,128)(2,1)} %collective-permute-done.10.refs_1_), channel_id=1, source_target_pairs={{0,16},{16,0},{32,48},{48,32},{64,80},{80,64},{96,112},{112,96},{1... | collective-permute-start | bytes 1179656 | tf_op jit(solution)/shard_map/ppermute | solution.py:20
  77.5 17.0 %all-to-all-start = ((bf16[16,128,128]{2,1,0:T(8,128)(2,1)}), bf16[16,128,128]{2,1,0:T(8,128)(2,1)S(1)}, u32[]{:S(2)}, u32[]{:S(2)}) async-start(bf16[16,128,128]{2,1,0:T(8,128)(2,1)} %get-tuple-element.33), calls=%async_computation | async-start | bytes 1048576 | tf_op jit(solution)/shard_map/all_to_all | solution.py:246
  94.5 1.3 collective-permute-start.13
  95.8 5.5 %collective-permute-start.14 = (bf16[2,128,128]{2,1,0:T(8,128)(2,1)S(1)}, bf16[2,128,128]{2,1,0:T(8,128)(2,1)S(1)}, u32[]{:S(2)}, u32[]{:S(2)}) collective-permute-start(bf16[2,128,128]{2,1,0:T(8,128)(2,1)S(1)} %pad_maximum_fusion.1.own), channel_id=1, source_target_pairs={{0,32},{16,48},{32,64},{48,80},{64,96},{80,112},{96,0},{112,16},{1... | collective-permute-start | bytes 196616 | tf_op jit(solution)/shard_map/ppermute | solution.py:16
  96.4 5.2 %collective-permute-start.15 = (bf16[2,128,128]{2,1,0:T(8,128)(2,1)S(1)}, bf16[2,128,128]{2,1,0:T(8,128)(2,1)S(1)}, u32[]{:S(2)}, u32[]{:S(2)}) collective-permute-start(bf16[2,128,128]{2,1,0:T(8,128)(2,1)S(1)} %pad_maximum_fusion.1.own), channel_id=1, source_target_pairs={{0,96},{16,112},{32,0},{48,16},{64,32},{80,48},{96,64},{112,80},{1... | collective-permute-start | bytes 196616 | tf_op jit(solution)/shard_map/ppermute | solution.py:16
  99.2 5.8 %collective-permute-start.16 = (bf16[2,128,128]{2,1,0:T(8,128)(2,1)S(1)}, bf16[2,128,128]{2,1,0:T(8,128)(2,1)S(1)}, u32[]{:S(2)}, u32[]{:S(2)}) collective-permute-start(bf16[2,128,128]{2,1,0:T(8,128)(2,1)S(1)} %pad_maximum_fusion.1.own), channel_id=1, source_target_pairs={{0,64},{16,80},{32,96},{48,112},{64,0},{80,16},{96,32},{112,48},{1... | collective-permute-start | bytes 196616 | tf_op jit(solution)/shard_map/ppermute | solution.py:16
  115.0 15.9 %all-to-all-start.1 = ((bf16[16,128,128]{2,1,0:T(8,128)(2,1)}), bf16[16,128,128]{2,1,0:T(8,128)(2,1)S(1)}, u32[]{:S(2)}, u32[]{:S(2)}) async-start(bf16[16,128,128]{2,1,0:T(8,128)(2,1)} %get-tuple-element.35), calls=%async_computation.1 | async-start | bytes 1048576 | tf_op jit(solution)/shard_map/all_to_all | solution.py:246
  118.6 1.5 collective-permute-start.17
  120.1 5.5 %collective-permute-start.18 = (bf16[2,128,128]{2,1,0:T(8,128)(2,1)S(1)}, bf16[2,128,128]{2,1,0:T(8,128)(2,1)S(1)}, u32[]{:S(2)}, u32[]{:S(2)}) collective-permute-start(bf16[2,128,128]{2,1,0:T(8,128)(2,1)S(1)} %pad_maximum_fusion.2.own), channel_id=1, source_target_pairs={{0,32},{16,48},{32,64},{48,80},{64,96},{80,112},{96,0},{112,16},{1... | collective-permute-start | bytes 196616 | tf_op jit(solution)/shard_map/ppermute | solution.py:16
  120.1 6.0 %collective-permute-start.19 = (bf16[2,128,128]{2,1,0:T(8,128)(2,1)S(1)}, bf16[2,128,128]{2,1,0:T(8,128)(2,1)S(1)}, u32[]{:S(2)}, u32[]{:S(2)}) collective-permute-start(bf16[2,128,128]{2,1,0:T(8,128)(2,1)S(1)} %pad_maximum_fusion.2.own), channel_id=1, source_target_pairs={{0,96},{16,112},{32,0},{48,16},{64,32},{80,48},{96,64},{112,80},{1... | collective-permute-start | bytes 196616 | tf_op jit(solution)/shard_map/ppermute | solution.py:16
  123.4 5.8 %collective-permute-start.20 = (bf16[2,128,128]{2,1,0:T(8,128)(2,1)S(1)}, bf16[2,128,128]{2,1,0:T(8,128)(2,1)S(1)}, u32[]{:S(2)}, u32[]{:S(2)}) collective-permute-start(bf16[2,128,128]{2,1,0:T(8,128)(2,1)S(1)} %pad_maximum_fusion.2.own), channel_id=1, source_target_pairs={{0,64},{16,80},{32,96},{48,112},{64,0},{80,16},{96,32},{112,48},{1... | collective-permute-start | bytes 196616 | tf_op jit(solution)/shard_map/ppermute | solution.py:16
  142.1 15.1 %all-to-all-start.5 = ((bf16[16,128,128]{2,1,0:T(8,128)(2,1)}), bf16[16,128,128]{2,1,0:T(8,128)(2,1)S(1)}, u32[]{:S(2)}, u32[]{:S(2)}) async-start(bf16[16,128,128]{2,1,0:T(8,128)(2,1)} %broadcast_in_dim.4), calls=%async_computation.5 | async-start | bytes 1048576 | tf_op jit(solution)/shard_map/all_to_all | solution.py:251
  159.1 5.5 %collective-permute-start.22 = (bf16[2,128,128]{2,1,0:T(8,128)(2,1)S(1)}, bf16[2,128,128]{2,1,0:T(8,128)(2,1)S(1)}, u32[]{:S(2)}, u32[]{:S(2)}) collective-permute-start(bf16[2,128,128]{2,1,0:T(8,128)(2,1)S(1)} %pad_maximum_fusion.3.own), channel_id=1, source_target_pairs={{0,32},{16,48},{32,64},{48,80},{64,96},{80,112},{96,0},{112,16},{1... | collective-permute-start | bytes 196616 | tf_op jit(solution)/shard_map/ppermute | solution.py:16
  159.2 6.0 %collective-permute-start.23 = (bf16[2,128,128]{2,1,0:T(8,128)(2,1)S(1)}, bf16[2,128,128]{2,1,0:T(8,128)(2,1)S(1)}, u32[]{:S(2)}, u32[]{:S(2)}) collective-permute-start(bf16[2,128,128]{2,1,0:T(8,128)(2,1)S(1)} %pad_maximum_fusion.3.own), channel_id=1, source_target_pairs={{0,96},{16,112},{32,0},{48,16},{64,32},{80,48},{96,64},{112,80},{1... | collective-permute-start | bytes 196616 | tf_op jit(solution)/shard_map/ppermute | solution.py:16
  162.4 5.8 %collective-permute-start.24 = (bf16[2,128,128]{2,1,0:T(8,128)(2,1)S(1)}, bf16[2,128,128]{2,1,0:T(8,128)(2,1)S(1)}, u32[]{:S(2)}, u32[]{:S(2)}) collective-permute-start(bf16[2,128,128]{2,1,0:T(8,128)(2,1)S(1)} %pad_maximum_fusion.3.own), channel_id=1, source_target_pairs={{0,64},{16,80},{32,96},{48,112},{64,0},{80,16},{96,32},{112,48},{1... | collective-permute-start | bytes 196616 | tf_op jit(solution)/shard_map/ppermute | solution.py:16
  179.2 13.6 %all-to-all-start.7 = ((bf16[16,128,128]{2,1,0:T(8,128)(2,1)}), bf16[16,128,128]{2,1,0:T(8,128)(2,1)S(1)}, u32[]{:S(2)}, u32[]{:S(2)}) async-start(bf16[16,128,128]{2,1,0:T(8,128)(2,1)} %broadcast_in_dim.5), calls=%async_computation.7 | async-start | bytes 1048576 | tf_op jit(solution)/shard_map/all_to_all | solution.py:251
  195.0 5.9 %collective-permute-start.28 = (f32[32,512]{1,0:T(8,128)S(1)}, f32[32,512]{1,0:T(8,128)S(1)}, u32[]{:S(2)}, u32[]{:S(2)}) collective-permute-start(f32[32,512]{1,0:T(8,128)S(1)} %add.128), channel_id=1, source_target_pairs={{0,64},{16,80},{32,96},{48,112},{64,0},{80,16},{96,32},{112,48},{1... | collective-permute-start | bytes 196616 | tf_op jit(solution)/shard_map/ppermute | solution.py:16
  195.1 5.9 %collective-permute-start.27 = (f32[32,512]{1,0:T(8,128)S(1)}, f32[32,512]{1,0:T(8,128)S(1)}, u32[]{:S(2)}, u32[]{:S(2)}) collective-permute-start(f32[32,512]{1,0:T(8,128)S(1)} %add.128), channel_id=1, source_target_pairs={{0,96},{16,112},{32,0},{48,16},{64,32},{80,48},{96,64},{112,80},{1... | collective-permute-start | bytes 196616 | tf_op jit(solution)/shard_map/ppermute | solution.py:16
  196.6 5.5 %collective-permute-start.26 = (f32[32,512]{1,0:T(8,128)S(1)}, f32[32,512]{1,0:T(8,128)S(1)}, u32[]{:S(2)}, u32[]{:S(2)}) collective-permute-start(f32[32,512]{1,0:T(8,128)S(1)} %add.128), channel_id=1, source_target_pairs={{0,32},{16,48},{32,64},{48,80},{64,96},{80,112},{96,0},{112,16},{1... | collective-permute-start | bytes 196616 | tf_op jit(solution)/shard_map/ppermute | solution.py:16
  (6 other events, 54.1 us)
Sparse Core Ops, SparseCore 0:
  40.5 37.8 all-gather.1

commit v6 on v3

--- a/solution.py
+++ b/solution.py
@@ -36,6 +36,39 @@
 
 def cost(flops, moved):
     return pl.CostEstimate(flops=flops, bytes_accessed=moved, transcendentals=0)
+
+
+def in_hbm(array):
+    return pltpu.with_memory_space_constraint(array, pltpu.HBM)
+
+
+def prepare_kernel(values, first, second, linking, low, high, early, late):
+    low[...] = values[:, :128, :]
+    high[...] = values[:, 128:, :]
+    early[0] = first[...]
+    early[1] = linking[...]
+    late[...] = second[...]
+
+
+def prepare(values, inverses, coupling):
+    inverses = in_hbm(inverses.reshape(2, 512, 256))
+    coupling = in_hbm(coupling.reshape(512, 256))
+    half = jax.ShapeDtypeStruct((3, 128, 512), BF)
+    late = jax.ShapeDtypeStruct((512, 256), BF)
+    out = [half, half, pltpu.HBM((2, 512, 256), BF), late]
+    return pl.pallas_call(
+        prepare_kernel,
+        grid=(1,),
+        in_specs=[
+            whole(values),
+            pl.BlockSpec((None, 512, 256), lambda i: (0, 0, 0)),
+            pl.BlockSpec((None, 512, 256), lambda i: (1, 0, 0)),
+            whole(coupling),
+        ],
+        out_specs=list(map(whole, out)),
+        out_shape=out,
+        compiler_params=ROOMY,
+    )(in_hbm(values), inverses, inverses, coupling)
 
 
 def split_tiles_kernel(src, dst):
@@ -91,8 +124,8 @@
     accumulate(acc, left, held, step)
 
 
-def next_products_kernel(order, left, before, *refs):
-    del order
+def next_products_kernel(order, left, before, token, *refs):
+    del order, token
     *pieces, acc, held = refs
     step = pl.program_id(0)
 
@@ -104,9 +137,9 @@
     accumulate(acc, left, held, step + 1)
 
 
-def last_products_kernel(order, left, before, *refs):
+def last_products_kernel(order, left, before, token, *refs):
     *pieces, first, second, acc, held = refs
-    next_products_kernel(order, left, before, *pieces, acc, held)
+    next_products_kernel(order, left, before, token, *pieces, acc, held)
 
     @pl.when(pl.program_id(0) == pl.num_programs(0) - 1)
     def _():
@@ -123,7 +156,7 @@
     return specs
 
 
-def products(order, left, pieces, before=None, last=False):
+def products(order, left, pieces, before=None, token=None, last=False):
     blocks = len(pieces) // 2
     _, rows, width = left.shape
     left_spec = pl.BlockSpec((3, rows, width), lambda i, order: (order[i], 0, 0))
@@ -132,7 +165,7 @@
     scratch = [VMEM((3, 256, 512), BF)]
     flops = blocks * 2 * rows * 768 * 512
     moved = blocks * 3 * 2 * (rows * 256 + 256 * 512) + rows * 512 * 4
-    starts = [] if before is None else [before]
+    starts = [] if before is None else [before, token]
     out = jax.ShapeDtypeStruct((rows, 512), F32)
     kernel = first_products_kernel if before is None else next_products_kernel
     if last:
@@ -280,49 +313,50 @@
 def body(left_factor, prev_solution, cross, inverses, coupling, prior_cov):
     row, col = lax.axis_index("row"), lax.axis_index("col")
     x, k = row // 2, row % 2
+    order = jnp.stack([(x + d) % 4 * 2 + (k + e) % 2 for d in RELATIVE for e in range(2)])
     y, z = col // 4, col % 4
-    order = jnp.stack([(x + d) % 4 * 2 + (k + e) % 2 for d in RELATIVE for e in range(2)])
     tiles = jnp.stack([(y + d) % 4 * 4 + (z + e) % 4 for d in RELATIVE for e in RELATIVE])
     order, tiles = order.astype(jnp.int32), tiles.astype(jnp.int32)
 
-    early = jnp.stack([inverses[0].reshape(512, 256), coupling.reshape(512, 256)])
-    panels = lax.all_gather(early, "col")
-    panels = pltpu.with_memory_space_constraint(panels, pltpu.HBM)
-    sibling = other_core(prev_solution)
-    low, high = prev_solution[:, :128, :], prev_solution[:, 128:, :]
+    low, high, early, late = prepare(prev_solution, inverses, coupling)
+    panels = in_hbm(lax.all_gather(early, "col"))
     before_low, after_high = x_shift(low, 1), x_shift(high, -1)
     before_high, after_low = x_shift(high, 1), x_shift(low, -1)
-    left = split_tiles(pltpu.with_memory_space_constraint(left_factor, pltpu.HBM))
-    late = inverses[1].reshape(512, 256)
-    before_low, after_high, left, late = lax.optimization_barrier(
-        (before_low, after_high, left, late)
-    )
+    sibling = in_hbm(other_core(prev_solution))
+    left = split_tiles(in_hbm(left_factor))
+    before_low, after_high, left = lax.optimization_barrier((before_low, after_high, left))
     far_low, far_high = x_shift(before_low, 1), x_shift(after_high, -1)
-    near = jnp.stack(four_ways(late, z_shift))
     pieces = [(prev_solution, 0), (prev_solution, 1), (sibling, 0), (sibling, 1)]
     started = products(order[:2], left, pieces)
-    before_high, after_low, started = lax.optimization_barrier((before_high, after_low, started))
-    started, near = lax.optimization_barrier((started, near))
-    late_panels = four_ways(near, y_shift)
+    before_high, after_low, token = lax.optimization_barrier(
+        (before_high, after_low, started[:8, :128])
+    )
     pieces = []
     for pair in ((before_low, before_high), (after_low, after_high)):
         pieces += [(v, 0) for v in pair] + [(other_core(v), 0) for v in pair]
-    started = products(order[2:6], left, pieces, started)
+    started = products(order[2:6], left, pieces, started, token)
+    far_low, far_high, token = lax.optimization_barrier(
+        (far_low, far_high, started[:8, :128])
+    )
     far = (far_low, far_high)
     pieces = [(v, 0) for v in far] + [(other_core(v), 0) for v in far]
-    first, second = products(order[6:], left, pieces, started, last=True)
+    first, second = products(order[6:], left, pieces, started, token, last=True)
+    first, second, late = lax.optimization_barrier((first, second, late))
+    near = jnp.stack(four_ways(late, z_shift))
 
     sites = jnp.transpose(cross.reshape(1024, 512))
     sites = lax.dynamic_slice_in_dim(sites, 32 * col, 32, 0).astype(F32)
     first_sum = over_sites(first).astype(F32).sum(axis=0)
-    second_sum = over_sites(second).astype(F32).sum(axis=0)
     first_rhs = (sites[:, :512] - first_sum).astype(BF)
-    solved_first = gathered_stage(order, over_chips(over_cores(first_rhs)), panels, 0)
-    pair = over_cores(solved_first)
-    sent, pair = lax.optimization_barrier((solved_first, pair))
+    first_rhs, near = lax.optimization_barrier((first_rhs, near))
+    late_panels = four_ways(near, y_shift)
+    *moved, second = lax.optimization_barrier((*over_chips(over_cores(first_rhs)), second))
+    solved_first = gathered_stage(order, moved, panels, 0)
+    base = sites[:, 512:] - over_sites(second).astype(F32).sum(axis=0)
+    moved = over_chips(over_cores(solved_first))
+    *moved, sent = lax.optimization_barrier((*moved, solved_first))
     every_first = all_sites(sent)
-    base = sites[:, 512:] - second_sum
-    second_rhs = gathered_stage(order, over_chips(pair), panels, 1, base)
+    second_rhs = gathered_stage(order, moved, panels, 1, base)
     moved = over_chips(over_cores(second_rhs))
     solved_second = spread_stage(order, tiles, moved, late_panels)
     solved_second, every_first = lax.optimization_barrier((solved_second, every_first))

time: 203 us -> 221 us (1.089)
  starting transfers between devices: 49.7 us -> 78.8 us
  blocking collectives: 37.7 us -> 17.3 us
  waiting for transfers between devices: 40 us -> 51.1 us
  other arithmetic: 9.18 us -> 5.14 us
  Pallas kernels: 40.7 us -> 43.6 us
    ppermute x18, starting transfers between devices: 23.6 us -> 46.1 us  [x_shift(): return lax.ppermute(v, 'row', [(r, (r + 2 * step) % 8) for r in range(8)])]
    all_to_all x1 -> x0, blocking collectives: 20.7 us -> none  [over_sites(): return lax.all_to_all(partial.reshape(16, 32, 512), 'col', 0, 0, tiled=True)]
    ppermute x3, waiting for transfers between devices: 6.96 us -> 26.6 us  [z_shift(): lax.ppermute(v, 'col', [(c, c // 4 * 4 + (c + step) % 4) for c in range(1...]
    all_to_all x1 -> x2, starting transfers between devices: 5.68 us -> 14.8 us  [over_sites(): return lax.all_to_all(partial.reshape(16, 32, 512), 'col', 0, 0, tiled=True)]
    ppermute x18, waiting for transfers between devices: 24.5 us -> 17.3 us  [x_shift(): return lax.ppermute(v, 'row', [(r, (r + 2 * step) % 8) for r in range(8)])]
    all_to_all x1 -> x2, waiting for transfers between devices: 4.94 us -> 1.63 us  [over_sites(): return lax.all_to_all(partial.reshape(16, 32, 512), 'col', 0, 0, tiled=True)]
    slice x2, local copies, waits for them, and re-layouts: 3.06 us -> 0.01 us  [body(): started[:8, :128]]
    ppermute x3, starting transfers between devices: 8.19 us -> 5.53 us  [z_shift(): lax.ppermute(v, 'col', [(c, c // 4 * 4 + (c + step) % 4) for c in range(1...]
  transfers between devices with their start and end apart: 38 -> 39, of which waited for: 16 -> 16; matrix products, arithmetic and copies ran while one was open for 5% -> 3% of each run, Pallas kernels for 20% -> 19%
where the time goes in v6:
time: 221 us; the launch traced here: 220 us
  starting transfers between devices  78.8 us (36%)
  waiting for transfers between devices  51.1 us (23%)
  Pallas kernels  43.6 us (20%)
  blocking collectives  17.3 us (8%)
  between operations  14.4 us (7%)
  local copies, waits for them, and re-layouts  7.96 us (4%)
  other arithmetic  5.14 us (2%)
    ppermute x18, starting transfers between devices, x_shift(): return lax.ppermute(v, 'row', [(r, (r + 2 * step) % 8) for r in range(8)])  46.1 us
    ppermute x3, waiting for transfers between devices, z_shift(): lax.ppermute(v, 'col', [(c, c // 4 * 4 + (c + step) % 4) for c in range(1...  26.6 us
    pallas_call x3, Pallas kernels, products(): pl.pallas_call(kernel, grid_spec=pltpu.PrefetchScalarGridSpec(num_scalar_...  19.8 us
    ppermute x18, waiting for transfers between devices, x_shift(): return lax.ppermute(v, 'row', [(r, (r + 2 * step) % 8) for r in range(8)])  17.3 us
    all_to_all x1, blocking collectives, all_sites(): return lax.all_to_all(sent, 'col', 0, 0, tiled=True).reshape(512, 512)  17.3 us
    all_to_all x2, starting transfers between devices, over_sites(): return lax.all_to_all(partial.reshape(16, 32, 512), 'col', 0, 0, tiled=True)  14.8 us
    pallas_call x1, Pallas kernels, split_tiles(): pl.pallas_call(split_tiles_kernel, grid=(rounds, tile // rows), in_specs=...  10.7 us
    pallas_call x2, Pallas kernels, gathered_stage(): pl.pallas_call(lambda *refs: gathered_stage_kernel(base is not None, *ref...  7.77 us
  transfers between devices with their start and end apart: 39, of which 16 were waited for; matrix products, arithmetic and copies ran while one was open for 3% of the time, Pallas kernels for 19%

profile of v6, /device:TPU:0, one launch (start us, length us, event | category | flops | bytes accessed | tf_op | source)
XLA Modules:
  0.0 219.9 jit_solution(4964705344711629231)
XLA Ops:
  7.2 2.5 %shard_map.77 = (bf16[3,128,512]{2,1,0:T(8,128)(2,1)}, bf16[3,128,512]{2,1,0:T(8,128)(2,1)}, bf16[2,512,256]{2,1,0:T(8,128)(2,1)}, bf16[512,256]{1,0:T(8,128)(2,1)S(1)}) custom-call(bf16[3,256,512]{2,1,0:T(8,128)(2,1)} %refs_1_.1, bf16[2,512,256]{2,1,0:T(8,128)(2,1)} %bitcast.68, bf16[2,512,256]{2,1,0:T(8,128)(2,1)} %bitcast.69, bf16[512,256]{1,0:T(8,128)(2,1)} %bitcast.70), custom_call_target="tpu_custom_call" | custom-call | tf_op jit(solution)/shard_map/pallas_call | solution.py:59
  10.6 1.6 collective-permute-start
  12.2 1.7 collective-permute-start.1
  14.2 2.9 %collective-permute-start.4 = (bf16[3,128,512]{2,1,0:T(8,128)(2,1)}, bf16[3,128,512]{2,1,0:T(8,128)(2,1)}, u32[]{:S(2)}, u32[]{:S(2)}) collective-permute-start(bf16[3,128,512]{2,1,0:T(8,128)(2,1)} %get-tuple-element.34), channel_id=1, source_target_pairs={{0,96},{16,112},{32,0},{48,16},{64,32},{80,48},{96,64},{112,80},{1... | collective-permute-start | bytes 1179656 | tf_op jit(solution)/shard_map/ppermute | solution.py:17
  17.1 10.7 %shard_map.78 = bf16[24,4,256,256]{3,2,1,0:T(8,128)(2,1)} custom-call(bf16[4,256,24,256]{3,2,1,0:T(8,128)(2,1)} %src.1), custom_call_target="tpu_custom_call" | custom-call | bytes 25165824 | tf_op jit(solution)/shard_map/pallas_call | solution.py:81
  28.5 4.9 %shard_map.79.before = f32[1024,512]{1,0:T(8,128)S(1)} custom-call(s32[2]{0:T(128)S(1)} %pad_add_fusion.2.order, bf16[24,1024,256]{2,1,0:T(8,128)(2,1)} %bitcast.59, bf16[3,256,512]{2,1,0:T(8,128)(2,1)S(1)} %copy-done.3, bf16[3,256,512]{2,1,0:T(8,128)(2,1)S(1)} %copy-done.3, bf16[3,256,512]{2,1,0:T(8,128)(2,1)} %collective-permute-done.2.refs_2_.refs_3_, ...), custom_call_target="tpu_custom_call" | custom-call | flops 1610612736 | bytes 6815744 | tf_op jit(solution)/shard_map/pallas_call | solution.py:175
  34.1 3.1 %collective-permute-start.10 = (bf16[3,128,512]{2,1,0:T(8,128)(2,1)}, bf16[3,128,512]{2,1,0:T(8,128)(2,1)}, u32[]{:S(2)}, u32[]{:S(2)}) collective-permute-start(bf16[3,128,512]{2,1,0:T(8,128)(2,1)} %collective-permute-done.1.refs_5_), channel_id=1, source_target_pairs={{0,96},{16,112},{32,0},{48,16},{64,32},{80,48},{96,64},{112,80},{1... | collective-permute-start | bytes 1179656 | tf_op jit(solution)/shard_map/ppermute | solution.py:17
  37.3 8.6 %shard_map.80.before = f32[1024,512]{1,0:T(8,128)S(1)} custom-call(s32[4]{0:T(128)S(1)} %pad_add_fusion.1.order, bf16[24,1024,256]{2,1,0:T(8,128)(2,1)} %bitcast.60, f32[1024,512]{1,0:T(8,128)S(1)} %shard_map.79.before, f32[8,128]{1,0:T(8,128)S(1)} %slice.23.token, bf16[3,128,512]{2,1,0:T(8,128)(2,1)S(1)} %collective-permute-done.refs_0_, ...), custom_call_target="tpu_custom_call" | custom-call | flops 3221225472 | bytes 11534336 | tf_op jit(solution)/shard_map/pallas_call | solution.py:175
  49.8 1.6 copy-done.2
  51.4 6.2 %shard_map.81 = (bf16[512,512]{1,0:T(8,128)(2,1)}, bf16[512,512]{1,0:T(8,128)(2,1)S(1)}) custom-call(s32[2]{0:T(128)S(1)} %pad_add_fusion.order, bf16[24,1024,256]{2,1,0:T(8,128)(2,1)} %bitcast.61, f32[1024,512]{1,0:T(8,128)S(1)} %copy-done.2, f32[8,128]{1,0:T(8,128)S(1)} %slice.24.token, bf16[3,128,512]{2,1,0:T(8,128)(2,1)} %collective-permute-done.9.refs_0_, ...), custom_call_target="tpu_custom_call" | custom-call | flops 1610612736 | bytes 6815744 | tf_op jit(solution)/shard_map/pallas_call | solution.py:175
  58.4 8.1 %all-to-all-start = ((bf16[16,32,512]{2,1,0:T(8,128)(2,1)}), bf16[16,32,512]{2,1,0:T(8,128)(2,1)S(1)}, u32[]{:S(2)}, u32[]{:S(2)}) async-start(bf16[16,32,512]{2,1,0:T(8,128)(2,1)} %bitcast.29), calls=%async_computation | async-start | bytes 1048576 | tf_op jit(solution)/shard_map/all_to_all | solution.py:292
  66.6 3.5 %collective-permute-start.15 = (bf16[512,256]{1,0:T(8,128)(2,1)S(1)}, bf16[512,256]{1,0:T(8,128)(2,1)S(1)}, u32[]{:S(2)}, u32[]{:S(2)}) collective-permute-start(bf16[512,256]{1,0:T(8,128)(2,1)S(1)} %copy-done.6), channel_id=1, source_target_pairs={{0,2},{1,3},{2,0},{3,1},{4,6},{5,7},{6,4},{7,5},{8,10},{9,11},{10,... | collective-permute-start | bytes 786440 | tf_op jit(solution)/shard_map/ppermute | solution.py:29
  72.4 17.6 %collective-permute-done.15 = bf16[512,256]{1,0:T(8,128)(2,1)S(1)} collective-permute-done((bf16[512,256]{1,0:T(8,128)(2,1)S(1)}, bf16[512,256]{1,0:T(8,128)(2,1)S(1)}, u32[]{:S(2)}, u32[]{:S(2)}) %collective-permute-start.15) | collective-permute-done | bytes 262176 | tf_op jit(solution)/shard_map/ppermute | solution.py:29
  90.0 9.1 %collective-permute-done.14 = bf16[512,256]{1,0:T(8,128)(2,1)S(1)} collective-permute-done((bf16[512,256]{1,0:T(8,128)(2,1)S(1)}, bf16[512,256]{1,0:T(8,128)(2,1)S(1)}, u32[]{:S(2)}, u32[]{:S(2)}) %collective-permute-start.14) | collective-permute-done | bytes 262176 | tf_op jit(solution)/shard_map/ppermute | solution.py:29
  102.3 3.2 %collective-permute-start.18 = (bf16[2,32,512]{2,1,0:T(8,128)(2,1)S(1)}, bf16[2,32,512]{2,1,0:T(8,128)(2,1)S(1)}, u32[]{:S(2)}, u32[]{:S(2)}) collective-permute-start(bf16[2,32,512]{2,1,0:T(8,128)(2,1)S(1)} %pad_maximum_fusion.2.refs_1_), channel_id=1, source_target_pairs={{0,96},{16,112},{32,0},{48,16},{64,32},{80,48},{96,64},{112,80},{1... | collective-permute-start | bytes 196616 | tf_op jit(solution)/shard_map/ppermute | solution.py:17
  106.3 1.5 collective-permute-start.28
  108.1 3.3 %collective-permute-done.19.refs_4_ = bf16[2,32,512]{2,1,0:T(8,128)(2,1)S(1)} collective-permute-done((bf16[2,32,512]{2,1,0:T(8,128)(2,1)S(1)}, bf16[2,32,512]{2,1,0:T(8,128)(2,1)S(1)}, u32[]{:S(2)}, u32[]{:S(2)}) %collective-permute-start.19) | collective-permute-done | bytes 65568 | tf_op jit(solution)/shard_map/ppermute | solution.py:17
  111.3 6.7 %all-to-all-start.1 = ((bf16[16,32,512]{2,1,0:T(8,128)(2,1)}), bf16[16,32,512]{2,1,0:T(8,128)(2,1)}, u32[]{:S(2)}, u32[]{:S(2)}) async-start(bf16[16,32,512]{2,1,0:T(8,128)(2,1)} %bitcast.56), calls=%async_computation.1 | async-start | bytes 1048576 | tf_op jit(solution)/shard_map/all_to_all | solution.py:292
  118.0 3.1 %collective-permute-start.29 = (bf16[4,512,256]{2,1,0:T(8,128)(2,1)S(1)}, bf16[4,512,256]{2,1,0:T(8,128)(2,1)}, u32[]{:S(2)}, u32[]{:S(2)}) collective-permute-start(bf16[4,512,256]{2,1,0:T(8,128)(2,1)S(1)} %pad_maximum_fusion.refs_0_), channel_id=1, source_target_pairs={{0,12},{1,13},{2,14},{3,15},{4,0},{5,1},{6,2},{7,3},{8,4},{9,5},{1... | collective-permute-start | bytes 3145736 | tf_op jit(solution)/shard_map/ppermute | solution.py:25
  122.0 3.9 %shard_map.82 = bf16[32,512]{1,0:T(8,128)(2,1)S(1)} custom-call(s32[8]{0:T(128)S(1)} %stack.134.refs_0_.order, bf16[2,32,512]{2,1,0:T(8,128)(2,1)S(1)} %pad_maximum_fusion.2.refs_1_, bf16[2,32,512]{2,1,0:T(8,128)(2,1)S(1)} %collective-permute-done.17.refs_2_, bf16[2,32,512]{2,1,0:T(8,128)(2,1)S(1)} %collective-permute-done.18.refs_3_, ...), custom_call_target="tpu_custom_call" | custom-call | flops 134217728 | bytes 4194304 | tf_op jit(solution)/shard_map/pallas_call | solution.py:262
  127.3 3.2 %collective-permute-start.22 = (bf16[2,32,512]{2,1,0:T(8,128)(2,1)S(1)}, bf16[2,32,512]{2,1,0:T(8,128)(2,1)S(1)}, u32[]{:S(2)}, u32[]{:S(2)}) collective-permute-start(bf16[2,32,512]{2,1,0:T(8,128)(2,1)S(1)} %pad_maximum_fusion.3.refs_1_), channel_id=1, source_target_pairs={{0,96},{16,112},{32,0},{48,16},{64,32},{80,48},{96,64},{112,80},{1... | collective-permute-start | bytes 196616 | tf_op jit(solution)/shard_map/ppermute | solution.py:17
  130.5 2.2 %collective-permute-done.21.refs_2_ = bf16[2,32,512]{2,1,0:T(8,128)(2,1)S(1)} collective-permute-done((bf16[2,32,512]{2,1,0:T(8,128)(2,1)S(1)}, bf16[2,32,512]{2,1,0:T(8,128)(2,1)S(1)}, u32[]{:S(2)}, u32[]{:S(2)}) %collective-permute-start.21) | collective-permute-done | bytes 65568 | tf_op jit(solution)/shard_map/ppermute | solution.py:17
  132.8 5.8 %collective-permute-done.23.refs_4_ = bf16[2,32,512]{2,1,0:T(8,128)(2,1)S(1)} collective-permute-done((bf16[2,32,512]{2,1,0:T(8,128)(2,1)S(1)}, bf16[2,32,512]{2,1,0:T(8,128)(2,1)S(1)}, u32[]{:S(2)}, u32[]{:S(2)}) %collective-permute-start.23) | collective-permute-done | bytes 65568 | tf_op jit(solution)/shard_map/ppermute | solution.py:17
  138.5 1.6 all-to-all-done.1
  141.0 4.9 %all-to-all-start.2 = ((bf16[16,32,512]{2,1,0:T(8,128)(2,1)}), bf16[16,32,512]{2,1,0:T(8,128)(2,1)}, u32[]{:S(2)}, u32[]{:S(2)}) async-start(bf16[16,32,512]{2,1,0:T(8,128)(2,1)} %broadcast_in_dim.4), calls=%async_computation.2 | async-start | bytes 1048576 | tf_op jit(solution)/shard_map/all_to_all | solution.py:297
  147.9 3.9 %shard_map.83 = bf16[32,512]{1,0:T(8,128)(2,1)S(1)} custom-call(s32[8]{0:T(128)S(1)} %stack.134.refs_0_.order, bf16[2,32,512]{2,1,0:T(8,128)(2,1)S(1)} %pad_maximum_fusion.3.refs_1_, bf16[2,32,512]{2,1,0:T(8,128)(2,1)S(1)} %collective-permute-done.21.refs_2_, bf16[2,32,512]{2,1,0:T(8,128)(2,1)S(1)} %collective-permute-done.22.refs_3_, ...), custom_call_target="tpu_custom_call" | custom-call | flops 134217728 | bytes 4194304 | tf_op jit(solution)/shard_map/pallas_call | solution.py:262
  153.1 20.1 %collective-permute-start.25 = (bf16[2,32,512]{2,1,0:T(8,128)(2,1)S(1)}, bf16[2,32,512]{2,1,0:T(8,128)(2,1)S(1)}, u32[]{:S(2)}, u32[]{:S(2)}) collective-permute-start(bf16[2,32,512]{2,1,0:T(8,128)(2,1)S(1)} %pad_maximum_fusion.4.own), channel_id=1, source_target_pairs={{0,32},{16,48},{32,64},{48,80},{64,96},{80,112},{96,0},{112,16},{1... | collective-permute-start | bytes 196616 | tf_op jit(solution)/shard_map/ppermute | solution.py:17
  173.2 3.5 %collective-permute-start.27 = (bf16[2,32,512]{2,1,0:T(8,128)(2,1)S(1)}, bf16[2,32,512]{2,1,0:T(8,128)(2,1)S(1)}, u32[]{:S(2)}, u32[]{:S(2)}) collective-permute-start(bf16[2,32,512]{2,1,0:T(8,128)(2,1)S(1)} %pad_maximum_fusion.4.own), channel_id=1, source_target_pairs={{0,64},{16,80},{32,96},{48,112},{64,0},{80,16},{96,32},{112,48},{1... | collective-permute-start | bytes 196616 | tf_op jit(solution)/shard_map/ppermute | solution.py:17
  179.0 2.9 %shard_map.84 = bf16[32,512]{1,0:T(8,128)(2,1)S(1)} custom-call(s32[8]{0:T(128)S(1)} %stack.134.refs_0_.order, s32[16]{0:T(128)S(1)} %stack.151.tiles, bf16[2,32,512]{2,1,0:T(8,128)(2,1)S(1)} %pad_maximum_fusion.4.own, bf16[2,32,512]{2,1,0:T(8,128)(2,1)S(1)} %collective-permute-done.25.one, bf16[2,32,512]{2,1,0:T(8,128)(2,1)S(1)} %collective-permute-done.26.two, ...), custom_call_target="tpu_custom_call" | custom-call | flops 134217728 | bytes 4194304 | tf_op jit(solution)/shard_map/pallas_call | solution.py:280
  181.9 17.3 %all_to_all.20 = bf16[16,32,512]{2,1,0:T(8,128)(2,1)S(1)} all-to-all(bf16[16,32,512]{2,1,0:T(8,128)(2,1)S(1)} %broadcast_in_dim.5), channel_id=1, replica_groups=mesh['row'=8,'col'=16] {'col'}, dimensions={0} | all-to-all | bytes 1048576 | tf_op jit(solution)/shard_map/all_to_all | solution.py:297
  202.4 3.3 %collective-permute-start.34 = (f32[32,512]{1,0:T(8,128)S(1)}, f32[32,512]{1,0:T(8,128)S(1)}, u32[]{:S(2)}, u32[]{:S(2)}) collective-permute-start(f32[32,512]{1,0:T(8,128)S(1)} %add.281), channel_id=1, source_target_pairs={{0,64},{16,80},{32,96},{48,112},{64,0},{80,16},{96,32},{112,48},{1... | collective-permute-start | bytes 196616 | tf_op jit(solution)/shard_map/ppermute | solution.py:17
  210.0 2.4 %collective-permute-done.32 = f32[32,512]{1,0:T(8,128)S(1)} collective-permute-done((f32[32,512]{1,0:T(8,128)S(1)}, f32[32,512]{1,0:T(8,128)S(1)}, u32[]{:S(2)}, u32[]{:S(2)}) %collective-permute-start.32) | collective-permute-done | bytes 65568 | tf_op jit(solution)/shard_map/ppermute | solution.py:17
  (103 shorter events, 30.6 us)
Async XLA Ops:
  7.2 114.9 %all-gather.3.cloned.1.call-start = ((), (), s32[]{:S(2)}) async-start(), calls=%async_computation.4 | async-start | bytes 8912896 | tf_op jit(solution)/shard_map/all_gather | solution.py:322
  10.5 18.0 %collective-permute-start.2 = (bf16[3,256,512]{2,1,0:T(8,128)(2,1)}, bf16[3,256,512]{2,1,0:T(8,128)(2,1)}, u32[]{:S(2)}, u32[]{:S(2)}) collective-permute-start(bf16[3,256,512]{2,1,0:T(8,128)(2,1)} %refs_1_.1), channel_id=1, source_target_pairs={{0,16},{16,0},{32,48},{48,32},{64,80},{80,64},{96,112},{112,96},{1... | collective-permute-start | bytes 2359304 | tf_op jit(solution)/shard_map/ppermute | solution.py:21
  10.6 17.3 %collective-permute-start = (bf16[3,128,512]{2,1,0:T(8,128)(2,1)}, bf16[3,128,512]{2,1,0:T(8,128)(2,1)S(1)}, u32[]{:S(2)}, u32[]{:S(2)}) collective-permute-start(bf16[3,128,512]{2,1,0:T(8,128)(2,1)} %get-tuple-element.34), channel_id=1, source_target_pairs={{0,32},{16,48},{32,64},{48,80},{64,96},{80,112},{96,0},{112,16},{1... | collective-permute-start | bytes 1179656 | tf_op jit(solution)/shard_map/ppermute | solution.py:17
  12.2 15.7 %collective-permute-start.1 = (bf16[3,128,512]{2,1,0:T(8,128)(2,1)}, bf16[3,128,512]{2,1,0:T(8,128)(2,1)}, u32[]{:S(2)}, u32[]{:S(2)}) collective-permute-start(bf16[3,128,512]{2,1,0:T(8,128)(2,1)} %get-tuple-element.35), channel_id=1, source_target_pairs={{0,96},{16,112},{32,0},{48,16},{64,32},{80,48},{96,64},{112,80},{1... | collective-permute-start | bytes 1179656 | tf_op jit(solution)/shard_map/ppermute | solution.py:17
  13.9 19.5 %collective-permute-start.3 = (bf16[3,128,512]{2,1,0:T(8,128)(2,1)}, bf16[3,128,512]{2,1,0:T(8,128)(2,1)}, u32[]{:S(2)}, u32[]{:S(2)}) collective-permute-start(bf16[3,128,512]{2,1,0:T(8,128)(2,1)} %get-tuple-element.35), channel_id=1, source_target_pairs={{0,32},{16,48},{32,64},{48,80},{64,96},{80,112},{96,0},{112,16},{1... | collective-permute-start | bytes 1179656 | tf_op jit(solution)/shard_map/ppermute | solution.py:17
  14.2 19.2 %collective-permute-start.4 = (bf16[3,128,512]{2,1,0:T(8,128)(2,1)}, bf16[3,128,512]{2,1,0:T(8,128)(2,1)}, u32[]{:S(2)}, u32[]{:S(2)}) collective-permute-start(bf16[3,128,512]{2,1,0:T(8,128)(2,1)} %get-tuple-element.34), channel_id=1, source_target_pairs={{0,96},{16,112},{32,0},{48,16},{64,32},{80,48},{96,64},{112,80},{1... | collective-permute-start | bytes 1179656 | tf_op jit(solution)/shard_map/ppermute | solution.py:17
  27.9 6.2 %collective-permute-start.5 = (bf16[3,128,512]{2,1,0:T(8,128)(2,1)S(1)}, bf16[3,128,512]{2,1,0:T(8,128)(2,1)}, u32[]{:S(2)}, u32[]{:S(2)}) collective-permute-start(bf16[3,128,512]{2,1,0:T(8,128)(2,1)S(1)} %collective-permute-done.refs_0_), channel_id=1, source_target_pairs={{0,16},{16,0},{32,48},{48,32},{64,80},{80,64},{96,112},{112,96},{1... | collective-permute-start | bytes 1179656 | tf_op jit(solution)/shard_map/ppermute | solution.py:21
  28.0 9.4 %collective-permute-start.8 = (bf16[3,128,512]{2,1,0:T(8,128)(2,1)}, bf16[3,128,512]{2,1,0:T(8,128)(2,1)}, u32[]{:S(2)}, u32[]{:S(2)}) collective-permute-start(bf16[3,128,512]{2,1,0:T(8,128)(2,1)} %collective-permute-done.1.refs_5_), channel_id=1, source_target_pairs={{0,16},{16,0},{32,48},{48,32},{64,80},{80,64},{96,112},{112,96},{1... | collective-permute-start | bytes 1179656 | tf_op jit(solution)/shard_map/ppermute | solution.py:21
  33.4 3.9 %collective-permute-start.6 = (bf16[3,128,512]{2,1,0:T(8,128)(2,1)}, bf16[3,128,512]{2,1,0:T(8,128)(2,1)}, u32[]{:S(2)}, u32[]{:S(2)}) collective-permute-start(bf16[3,128,512]{2,1,0:T(8,128)(2,1)} %collective-permute-done.3.refs_1_), channel_id=1, source_target_pairs={{0,16},{16,0},{32,48},{48,32},{64,80},{80,64},{96,112},{112,96},{1... | collective-permute-start | bytes 1179656 | tf_op jit(solution)/shard_map/ppermute | solution.py:21
  34.0 13.3 %collective-permute-start.9 = (bf16[3,128,512]{2,1,0:T(8,128)(2,1)S(1)}, bf16[3,128,512]{2,1,0:T(8,128)(2,1)}, u32[]{:S(2)}, u32[]{:S(2)}) collective-permute-start(bf16[3,128,512]{2,1,0:T(8,128)(2,1)S(1)} %collective-permute-done.refs_0_), channel_id=1, source_target_pairs={{0,32},{16,48},{32,64},{48,80},{64,96},{80,112},{96,0},{112,16},{1... | collective-permute-start | bytes 1179656 | tf_op jit(solution)/shard_map/ppermute | solution.py:17
  34.1 13.2 %collective-permute-start.10 = (bf16[3,128,512]{2,1,0:T(8,128)(2,1)}, bf16[3,128,512]{2,1,0:T(8,128)(2,1)}, u32[]{:S(2)}, u32[]{:S(2)}) collective-permute-start(bf16[3,128,512]{2,1,0:T(8,128)(2,1)} %collective-permute-done.1.refs_5_), channel_id=1, source_target_pairs={{0,96},{16,112},{32,0},{48,16},{64,32},{80,48},{96,64},{112,80},{1... | collective-permute-start | bytes 1179656 | tf_op jit(solution)/shard_map/ppermute | solution.py:17
  58.4 42.4 %all-to-all-start = ((bf16[16,32,512]{2,1,0:T(8,128)(2,1)}), bf16[16,32,512]{2,1,0:T(8,128)(2,1)S(1)}, u32[]{:S(2)}, u32[]{:S(2)}) async-start(bf16[16,32,512]{2,1,0:T(8,128)(2,1)} %bitcast.29), calls=%async_computation | async-start | bytes 1048576 | tf_op jit(solution)/shard_map/all_to_all | solution.py:292
  66.6 23.4 %collective-permute-start.15 = (bf16[512,256]{1,0:T(8,128)(2,1)S(1)}, bf16[512,256]{1,0:T(8,128)(2,1)S(1)}, u32[]{:S(2)}, u32[]{:S(2)}) collective-permute-start(bf16[512,256]{1,0:T(8,128)(2,1)S(1)} %copy-done.6), channel_id=1, source_target_pairs={{0,2},{1,3},{2,0},{3,1},{4,6},{5,7},{6,4},{7,5},{8,10},{9,11},{10,... | collective-permute-start | bytes 786440 | tf_op jit(solution)/shard_map/ppermute | solution.py:29
  70.1 29.0 %collective-permute-start.14 = (bf16[512,256]{1,0:T(8,128)(2,1)S(1)}, bf16[512,256]{1,0:T(8,128)(2,1)S(1)}, u32[]{:S(2)}, u32[]{:S(2)}) collective-permute-start(bf16[512,256]{1,0:T(8,128)(2,1)S(1)} %copy-done.6), channel_id=1, source_target_pairs={{0,3},{1,0},{2,1},{3,2},{4,7},{5,4},{6,5},{7,6},{8,11},{9,8},{10,9... | collective-permute-start | bytes 786440 | tf_op jit(solution)/shard_map/ppermute | solution.py:29
  71.3 27.8 %collective-permute-start.13 = (bf16[512,256]{1,0:T(8,128)(2,1)S(1)}, bf16[512,256]{1,0:T(8,128)(2,1)S(1)}, u32[]{:S(2)}, u32[]{:S(2)}) collective-permute-start(bf16[512,256]{1,0:T(8,128)(2,1)S(1)} %copy-done.6), channel_id=1, source_target_pairs={{0,1},{1,2},{2,3},{3,0},{4,5},{5,6},{6,7},{7,4},{8,9},{9,10},{10,1... | collective-permute-start | bytes 786440 | tf_op jit(solution)/shard_map/ppermute | solution.py:29
  102.3 5.5 %collective-permute-start.17 = (bf16[2,32,512]{2,1,0:T(8,128)(2,1)S(1)}, bf16[2,32,512]{2,1,0:T(8,128)(2,1)S(1)}, u32[]{:S(2)}, u32[]{:S(2)}) collective-permute-start(bf16[2,32,512]{2,1,0:T(8,128)(2,1)S(1)} %pad_maximum_fusion.2.refs_1_), channel_id=1, source_target_pairs={{0,32},{16,48},{32,64},{48,80},{64,96},{80,112},{96,0},{112,16},{1... | collective-permute-start | bytes 196616 | tf_op jit(solution)/shard_map/ppermute | solution.py:17
  102.3 5.7 %collective-permute-start.18 = (bf16[2,32,512]{2,1,0:T(8,128)(2,1)S(1)}, bf16[2,32,512]{2,1,0:T(8,128)(2,1)S(1)}, u32[]{:S(2)}, u32[]{:S(2)}) collective-permute-start(bf16[2,32,512]{2,1,0:T(8,128)(2,1)S(1)} %pad_maximum_fusion.2.refs_1_), channel_id=1, source_target_pairs={{0,96},{16,112},{32,0},{48,16},{64,32},{80,48},{96,64},{112,80},{1... | collective-permute-start | bytes 196616 | tf_op jit(solution)/shard_map/ppermute | solution.py:17
  105.6 5.8 %collective-permute-start.19 = (bf16[2,32,512]{2,1,0:T(8,128)(2,1)S(1)}, bf16[2,32,512]{2,1,0:T(8,128)(2,1)S(1)}, u32[]{:S(2)}, u32[]{:S(2)}) collective-permute-start(bf16[2,32,512]{2,1,0:T(8,128)(2,1)S(1)} %pad_maximum_fusion.2.refs_1_), channel_id=1, source_target_pairs={{0,64},{16,80},{32,96},{48,112},{64,0},{80,16},{96,32},{112,48},{1... | collective-permute-start | bytes 196616 | tf_op jit(solution)/shard_map/ppermute | solution.py:17
  106.3 66.9 %collective-permute-start.28 = (bf16[4,512,256]{2,1,0:T(8,128)(2,1)S(1)}, bf16[4,512,256]{2,1,0:T(8,128)(2,1)S(1)}, u32[]{:S(2)}, u32[]{:S(2)}) collective-permute-start(bf16[4,512,256]{2,1,0:T(8,128)(2,1)S(1)} %pad_maximum_fusion.refs_0_), channel_id=1, source_target_pairs={{0,4},{1,5},{2,6},{3,7},{4,8},{5,9},{6,10},{7,11},{8,12},{9,13},{1... | collective-permute-start | bytes 3145736 | tf_op jit(solution)/shard_map/ppermute | solution.py:25
  111.3 28.8 %all-to-all-start.1 = ((bf16[16,32,512]{2,1,0:T(8,128)(2,1)}), bf16[16,32,512]{2,1,0:T(8,128)(2,1)}, u32[]{:S(2)}, u32[]{:S(2)}) async-start(bf16[16,32,512]{2,1,0:T(8,128)(2,1)} %bitcast.56), calls=%async_computation.1 | async-start | bytes 1048576 | tf_op jit(solution)/shard_map/all_to_all | solution.py:292
  118.0 58.8 %collective-permute-start.29 = (bf16[4,512,256]{2,1,0:T(8,128)(2,1)S(1)}, bf16[4,512,256]{2,1,0:T(8,128)(2,1)}, u32[]{:S(2)}, u32[]{:S(2)}) collective-permute-start(bf16[4,512,256]{2,1,0:T(8,128)(2,1)S(1)} %pad_maximum_fusion.refs_0_), channel_id=1, source_target_pairs={{0,12},{1,13},{2,14},{3,15},{4,0},{5,1},{6,2},{7,3},{8,4},{9,5},{1... | collective-permute-start | bytes 3145736 | tf_op jit(solution)/shard_map/ppermute | solution.py:25
  121.1 55.7 %collective-permute-start.30 = (bf16[4,512,256]{2,1,0:T(8,128)(2,1)S(1)}, bf16[4,512,256]{2,1,0:T(8,128)(2,1)}, u32[]{:S(2)}, u32[]{:S(2)}) collective-permute-start(bf16[4,512,256]{2,1,0:T(8,128)(2,1)S(1)} %pad_maximum_fusion.refs_0_), channel_id=1, source_target_pairs={{0,8},{1,9},{2,10},{3,11},{4,12},{5,13},{6,14},{7,15},{8,0},{9,1},... | collective-permute-start | bytes 3145736 | tf_op jit(solution)/shard_map/ppermute | solution.py:25
  127.2 5.5 %collective-permute-start.21 = (bf16[2,32,512]{2,1,0:T(8,128)(2,1)S(1)}, bf16[2,32,512]{2,1,0:T(8,128)(2,1)S(1)}, u32[]{:S(2)}, u32[]{:S(2)}) collective-permute-start(bf16[2,32,512]{2,1,0:T(8,128)(2,1)S(1)} %pad_maximum_fusion.3.refs_1_), channel_id=1, source_target_pairs={{0,32},{16,48},{32,64},{48,80},{64,96},{80,112},{96,0},{112,16},{1... | collective-permute-start | bytes 196616 | tf_op jit(solution)/shard_map/ppermute | solution.py:17
  127.3 5.5 %collective-permute-start.22 = (bf16[2,32,512]{2,1,0:T(8,128)(2,1)S(1)}, bf16[2,32,512]{2,1,0:T(8,128)(2,1)S(1)}, u32[]{:S(2)}, u32[]{:S(2)}) collective-permute-start(bf16[2,32,512]{2,1,0:T(8,128)(2,1)S(1)} %pad_maximum_fusion.3.refs_1_), channel_id=1, source_target_pairs={{0,96},{16,112},{32,0},{48,16},{64,32},{80,48},{96,64},{112,80},{1... | collective-permute-start | bytes 196616 | tf_op jit(solution)/shard_map/ppermute | solution.py:17
  132.8 5.8 %collective-permute-start.23 = (bf16[2,32,512]{2,1,0:T(8,128)(2,1)S(1)}, bf16[2,32,512]{2,1,0:T(8,128)(2,1)S(1)}, u32[]{:S(2)}, u32[]{:S(2)}) collective-permute-start(bf16[2,32,512]{2,1,0:T(8,128)(2,1)S(1)} %pad_maximum_fusion.3.refs_1_), channel_id=1, source_target_pairs={{0,64},{16,80},{32,96},{48,112},{64,0},{80,16},{96,32},{112,48},{1... | collective-permute-start | bytes 196616 | tf_op jit(solution)/shard_map/ppermute | solution.py:17
  141.0 40.9 %all-to-all-start.2 = ((bf16[16,32,512]{2,1,0:T(8,128)(2,1)}), bf16[16,32,512]{2,1,0:T(8,128)(2,1)}, u32[]{:S(2)}, u32[]{:S(2)}) async-start(bf16[16,32,512]{2,1,0:T(8,128)(2,1)} %broadcast_in_dim.4), calls=%async_computation.2 | async-start | bytes 1048576 | tf_op jit(solution)/shard_map/all_to_all | solution.py:297
  153.1 23.7 %collective-permute-start.25 = (bf16[2,32,512]{2,1,0:T(8,128)(2,1)S(1)}, bf16[2,32,512]{2,1,0:T(8,128)(2,1)S(1)}, u32[]{:S(2)}, u32[]{:S(2)}) collective-permute-start(bf16[2,32,512]{2,1,0:T(8,128)(2,1)S(1)} %pad_maximum_fusion.4.own), channel_id=1, source_target_pairs={{0,32},{16,48},{32,64},{48,80},{64,96},{80,112},{96,0},{112,16},{1... | collective-permute-start | bytes 196616 | tf_op jit(solution)/shard_map/ppermute | solution.py:17
  173.2 4.8 %collective-permute-start.26 = (bf16[2,32,512]{2,1,0:T(8,128)(2,1)S(1)}, bf16[2,32,512]{2,1,0:T(8,128)(2,1)S(1)}, u32[]{:S(2)}, u32[]{:S(2)}) collective-permute-start(bf16[2,32,512]{2,1,0:T(8,128)(2,1)S(1)} %pad_maximum_fusion.4.own), channel_id=1, source_target_pairs={{0,96},{16,112},{32,0},{48,16},{64,32},{80,48},{96,64},{112,80},{1... | collective-permute-start | bytes 196616 | tf_op jit(solution)/shard_map/ppermute | solution.py:17
  173.2 5.8 %collective-permute-start.27 = (bf16[2,32,512]{2,1,0:T(8,128)(2,1)S(1)}, bf16[2,32,512]{2,1,0:T(8,128)(2,1)S(1)}, u32[]{:S(2)}, u32[]{:S(2)}) collective-permute-start(bf16[2,32,512]{2,1,0:T(8,128)(2,1)S(1)} %pad_maximum_fusion.4.own), channel_id=1, source_target_pairs={{0,64},{16,80},{32,96},{48,112},{64,0},{80,16},{96,32},{112,48},{1... | collective-permute-start | bytes 196616 | tf_op jit(solution)/shard_map/ppermute | solution.py:17
  202.4 6.4 %collective-permute-start.34 = (f32[32,512]{1,0:T(8,128)S(1)}, f32[32,512]{1,0:T(8,128)S(1)}, u32[]{:S(2)}, u32[]{:S(2)}) collective-permute-start(f32[32,512]{1,0:T(8,128)S(1)} %add.281), channel_id=1, source_target_pairs={{0,64},{16,80},{32,96},{48,112},{64,0},{80,16},{96,32},{112,48},{1... | collective-permute-start | bytes 196616 | tf_op jit(solution)/shard_map/ppermute | solution.py:17
  205.7 4.3 %collective-permute-start.33 = (f32[32,512]{1,0:T(8,128)S(1)}, f32[32,512]{1,0:T(8,128)S(1)}, u32[]{:S(2)}, u32[]{:S(2)}) collective-permute-start(f32[32,512]{1,0:T(8,128)S(1)} %add.281), channel_id=1, source_target_pairs={{0,96},{16,112},{32,0},{48,16},{64,32},{80,48},{96,64},{112,80},{1... | collective-permute-start | bytes 196616 | tf_op jit(solution)/shard_map/ppermute | solution.py:17
  206.9 5.5 %collective-permute-start.32 = (f32[32,512]{1,0:T(8,128)S(1)}, f32[32,512]{1,0:T(8,128)S(1)}, u32[]{:S(2)}, u32[]{:S(2)}) collective-permute-start(f32[32,512]{1,0:T(8,128)S(1)} %add.281), channel_id=1, source_target_pairs={{0,32},{16,48},{32,64},{48,80},{64,96},{80,112},{96,0},{112,16},{1... | collective-permute-start | bytes 196616 | tf_op jit(solution)/shard_map/ppermute | solution.py:17
  (17 other events, 207.9 us)
Sparse Core Ops, SparseCore 0:
  10.7 90.1 all-gather.2

commit v7 on v5

--- a/solution.py
+++ b/solution.py
@@ -239,6 +239,10 @@
         cost_estimate=cost(2 * 128 * 1024 * 512, 2 * 1024 * 512),
         compiler_params=ROOMY,
     )(order, *moved, panels)
+    return partial
+
+
+def over_z(partial):
     return z_exchange(partial).astype(F32).sum(axis=0)
 
 
@@ -274,16 +278,15 @@
     before_high, after_low = x_shift(high, 1), x_shift(low, -1)
     sibling = in_hbm(other_core(prev_solution))
     left = split_tiles(in_hbm(left_factor))
-    before_low, after_high, left, lines = lax.optimization_barrier(
-        (before_low, after_high, left, lines)
+    lines = z_exchange(lines)
+    before_low, after_high, before_high, after_low, left, lines = lax.optimization_barrier(
+        (before_low, after_high, before_high, after_low, left, lines)
     )
-    panels = in_hbm(y_gather(z_exchange(lines)))
+    panels = in_hbm(y_gather(lines))
     far_low, far_high = x_shift(before_low, 1), x_shift(after_high, -1)
     pieces = [(prev_solution, 0), (prev_solution, 1), (sibling, 0), (sibling, 1)]
     started = products(order[:2], left, pieces)
-    before_high, after_low, token = lax.optimization_barrier(
-        (before_high, after_low, started[:8, :128])
-    )
+    token = started[:8, :128]
     pieces = []
     for pair in ((before_low, before_high), (after_low, after_high)):
         pieces += [(v, 0) for v in pair] + [(other_core(v), 0) for v in pair]
@@ -300,11 +303,12 @@
     first_rhs = (known[0] - over_sites(first)).astype(BF)
     first_rhs, second = lax.optimization_barrier((first_rhs, second))
     rest = known[1] - over_sites(second)
-    solved_first = stage(order, first_rhs, panels, 0).astype(BF)
+    solved_first = over_z(stage(order, first_rhs, panels, 0)).astype(BF)
     every_first = all_sites(solved_first)
-    second_rhs = (rest - stage(order, solved_first, panels, 1)).astype(BF)
-    second_rhs, every_first = lax.optimization_barrier((second_rhs, every_first))
-    solved_second = stage(order, second_rhs, panels, 2).astype(BF)
+    second_rhs = (rest - over_z(stage(order, solved_first, panels, 1))).astype(BF)
+    partial = stage(order, second_rhs, panels, 2)
+    partial, every_first = lax.optimization_barrier((partial, every_first))
+    solved_second = over_z(partial).astype(BF)
     every_second = all_sites(solved_second)
     outer = outer_part(every_first, col) + outer_part(every_second, col)
     pred_cov = prior_cov - row_sum(outer) / S

time: 211 us -> 197 us (0.934)
  blocking collectives: 44.1 us -> 18.8 us
  starting transfers between devices: 42.4 us -> 55.1 us
  waiting for transfers between devices: 61.6 us -> 59 us
    all_to_all x4 -> x2, blocking collectives: 44.1 us -> 18.8 us  [z_exchange(): return lax.all_to_all(v, 'col', 0, 0, axis_index_groups=groups, tiled=True)]
    all_to_all x2, waiting for transfers between devices: 19.6 us -> 9.69 us  [all_sites(): lax.all_to_all(sent, 'col', 0, 0, tiled=True).reshape(4, 4, 2, 64, 128)]
    all_to_all x0 -> x2, starting transfers between devices: none -> 9.79 us  [z_exchange(): return lax.all_to_all(v, 'col', 0, 0, axis_index_groups=groups, tiled=True)]
    all_to_all x0 -> x2, waiting for transfers between devices: none -> 5.9 us  [z_exchange(): return lax.all_to_all(v, 'col', 0, 0, axis_index_groups=groups, tiled=True)]
    all_to_all x2, starting transfers between devices: 8.75 us -> 11.1 us  [over_sites(): lax.all_to_all(partial, 'col', 0, 0, tiled=True).astype(F32).sum(axis=0)]
  transfers between devices with their start and end apart: 34 -> 36, of which waited for: 21 -> 22; matrix products, arithmetic and copies ran while one was open for 1% -> 1% of each run, Pallas kernels for 15% -> 17%
where the time goes in v7:
time: 197 us; the launch traced here: 196 us
  waiting for transfers between devices  59 us (30%)
  starting transfers between devices  55.1 us (28%)
  Pallas kernels  37.8 us (19%)
  blocking collectives  18.8 us (10%)
  between operations  14.4 us (7%)
  local copies, waits for them, and re-layouts  7.11 us (4%)
  other arithmetic  3.1 us (2%)
    ppermute x18, waiting for transfers between devices, x_shift(): return lax.ppermute(v, 'row', [(r, (r + 2 * step) % 8) for r in range(8)])  24.4 us
    ppermute x18, starting transfers between devices, x_shift(): return lax.ppermute(v, 'row', [(r, (r + 2 * step) % 8) for r in range(8)])  22.1 us
    pallas_call x3, Pallas kernels, products(): pl.pallas_call(kernel, grid_spec=pltpu.PrefetchScalarGridSpec(num_scalar_...  19.1 us
    all_to_all x2, blocking collectives, z_exchange(): return lax.all_to_all(v, 'col', 0, 0, axis_index_groups=groups, tiled=True)  18.8 us
    all_to_all x2, starting transfers between devices, over_sites(): lax.all_to_all(partial, 'col', 0, 0, tiled=True).astype(F32).sum(axis=0)  11.1 us
    all_to_all x2, waiting for transfers between devices, over_sites(): lax.all_to_all(partial, 'col', 0, 0, tiled=True).astype(F32).sum(axis=0)  10.9 us
    pallas_call x1, Pallas kernels, split_tiles(): pl.pallas_call(split_tiles_kernel, grid=(rounds, tile // rows), in_specs=...  10.4 us
    all_to_all x2, starting transfers between devices, all_sites(): lax.all_to_all(sent, 'col', 0, 0, tiled=True).reshape(4, 4, 2, 64, 128)  9.96 us
  transfers between devices with their start and end apart: 36, of which 22 were waited for; matrix products, arithmetic and copies ran while one was open for 1% of the time, Pallas kernels for 17%

profile of v7, /device:TPU:0, one launch (start us, length us, event | category | flops | bytes accessed | tf_op | source)
XLA Modules:
  0.0 195.8 jit_solution(5039837030201067588)
XLA Ops:
  7.2 2.5 %shard_map.77 = (bf16[3,128,512]{2,1,0:T(8,128)(2,1)S(1)}, bf16[3,128,512]{2,1,0:T(8,128)(2,1)S(1)}, bf16[4,3,64,512]{3,2,1,0:T(8,128)(2,1)}) custom-call(bf16[3,256,512]{2,1,0:T(8,128)(2,1)} %refs_1_.1, bf16[2,512,256]{2,1,0:T(8,128)(2,1)} %bitcast.56, bf16[2,512,256]{2,1,0:T(8,128)(2,1)} %bitcast.57, bf16[512,256]{1,0:T(8,128)(2,1)} %bitcast.60), custom_call_target="tpu_custom_call" | custom-call | tf_op jit(solution)/shard_map/pallas_call | solution.py:60
  9.7 5.4 %all-to-all-start = ((bf16[4,3,64,512]{3,2,1,0:T(8,128)(2,1)}), bf16[4,3,64,512]{3,2,1,0:T(8,128)(2,1)}, u32[]{:S(2)}, u32[]{:S(2)}) async-start(bf16[4,3,64,512]{3,2,1,0:T(8,128)(2,1)} %get-tuple-element.22), calls=%async_computation | async-start | bytes 1572864 | tf_op jit(solution)/shard_map/all_to_all | solution.py:25
  16.6 1.7 collective-permute-start.1
  18.6 3.0 %collective-permute-start.3 = (bf16[3,128,512]{2,1,0:T(8,128)(2,1)S(1)}, bf16[3,128,512]{2,1,0:T(8,128)(2,1)S(1)}, u32[]{:S(2)}, u32[]{:S(2)}) collective-permute-start(bf16[3,128,512]{2,1,0:T(8,128)(2,1)S(1)} %get-tuple-element.20), channel_id=1, source_target_pairs={{0,96},{16,112},{32,0},{48,16},{64,32},{80,48},{96,64},{112,80},{1... | collective-permute-start | bytes 1179656 | tf_op jit(solution)/shard_map/ppermute | solution.py:16
  21.6 10.4 %shard_map.78 = bf16[24,4,256,256]{3,2,1,0:T(8,128)(2,1)} custom-call(bf16[4,256,24,256]{3,2,1,0:T(8,128)(2,1)} %src.1), custom_call_target="tpu_custom_call" | custom-call | bytes 25165824 | tf_op jit(solution)/shard_map/pallas_call | solution.py:82
  32.0 3.3 %collective-permute-done.2.refs_1_ = bf16[3,128,512]{2,1,0:T(8,128)(2,1)S(1)} collective-permute-done((bf16[3,128,512]{2,1,0:T(8,128)(2,1)S(1)}, bf16[3,128,512]{2,1,0:T(8,128)(2,1)S(1)}, u32[]{:S(2)}, u32[]{:S(2)}) %collective-permute-start.2) | collective-permute-done | bytes 393248 | tf_op jit(solution)/shard_map/ppermute | solution.py:16
  39.5 2.1 %collective-permute-start.10 = (bf16[3,128,512]{2,1,0:T(8,128)(2,1)S(1)}, bf16[3,128,512]{2,1,0:T(8,128)(2,1)}, u32[]{:S(2)}, u32[]{:S(2)}) collective-permute-start(bf16[3,128,512]{2,1,0:T(8,128)(2,1)S(1)} %collective-permute-done.1.refs_5_), channel_id=1, source_target_pairs={{0,96},{16,112},{32,0},{48,16},{64,32},{80,48},{96,64},{112,80},{1... | collective-permute-start | bytes 1179656 | tf_op jit(solution)/shard_map/ppermute | solution.py:16
  41.6 4.9 %shard_map.79.before = f32[1024,512]{1,0:T(8,128)S(1)} custom-call(s32[2]{0:T(128)S(1)} %pad_add_fusion.2.order, bf16[24,1024,256]{2,1,0:T(8,128)(2,1)} %bitcast.51, bf16[3,256,512]{2,1,0:T(8,128)(2,1)S(1)} %copy-done, bf16[3,256,512]{2,1,0:T(8,128)(2,1)S(1)} %copy-done, bf16[3,256,512]{2,1,0:T(8,128)(2,1)} %collective-permute-done.4.refs_2_.refs_3_, ...), custom_call_target="tpu_custom_call" | custom-call | flops 1610612736 | bytes 6815744 | tf_op jit(solution)/shard_map/pallas_call | solution.py:179
  50.4 8.0 %shard_map.80.before = f32[1024,512]{1,0:T(8,128)S(1)} custom-call(s32[4]{0:T(128)S(1)} %pad_add_fusion.1.order, bf16[24,1024,256]{2,1,0:T(8,128)(2,1)} %bitcast.52, f32[1024,512]{1,0:T(8,128)S(1)} %shard_map.79.before, f32[8,128]{1,0:T(8,128)S(1)} %slice.26.token, bf16[3,128,512]{2,1,0:T(8,128)(2,1)S(1)} %collective-permute-done.refs_0_, ...), custom_call_target="tpu_custom_call" | custom-call | flops 3221225472 | bytes 11534336 | tf_op jit(solution)/shard_map/pallas_call | solution.py:179
  61.0 6.2 %shard_map.81 = (bf16[16,128,128]{2,1,0:T(8,128)(2,1)}, bf16[16,128,128]{2,1,0:T(8,128)(2,1)}) custom-call(s32[2]{0:T(128)S(1)} %pad_add_fusion.order, bf16[24,1024,256]{2,1,0:T(8,128)(2,1)} %bitcast.53, f32[1024,512]{1,0:T(8,128)S(1)} %shard_map.80.before, f32[8,128]{1,0:T(8,128)S(1)} %slice.27.token, bf16[3,128,512]{2,1,0:T(8,128)(2,1)} %collective-permute-done.9.refs_0_, ...), custom_call_target="tpu_custom_call" | custom-call | flops 1610612736 | bytes 6815744 | tf_op jit(solution)/shard_map/pallas_call | solution.py:179
  67.2 7.4 %all-to-all-start.1 = ((bf16[16,128,128]{2,1,0:T(8,128)(2,1)}), bf16[16,128,128]{2,1,0:T(8,128)(2,1)S(1)}, u32[]{:S(2)}, u32[]{:S(2)}) async-start(bf16[16,128,128]{2,1,0:T(8,128)(2,1)} %get-tuple-element.31), calls=%async_computation.1 | async-start | bytes 1048576 | tf_op jit(solution)/shard_map/all_to_all | solution.py:250
  75.5 10.9 %all-to-all-done.1 = bf16[16,128,128]{2,1,0:T(8,128)(2,1)S(1)} async-done(((bf16[16,128,128]{2,1,0:T(8,128)(2,1)}), bf16[16,128,128]{2,1,0:T(8,128)(2,1)S(1)}, u32[]{:S(2)}, u32[]{:S(2)}) %all-to-all-start.1) | async-done | bytes 524320 | tf_op jit(solution)/shard_map/all_to_all | solution.py:250
  87.9 3.2 %collective-permute-start.15 = (bf16[2,128,128]{2,1,0:T(8,128)(2,1)S(1)}, bf16[2,128,128]{2,1,0:T(8,128)(2,1)S(1)}, u32[]{:S(2)}, u32[]{:S(2)}) collective-permute-start(bf16[2,128,128]{2,1,0:T(8,128)(2,1)S(1)} %pad_maximum_fusion.1.own), channel_id=1, source_target_pairs={{0,96},{16,112},{32,0},{48,16},{64,32},{80,48},{96,64},{112,80},{1... | collective-permute-start | bytes 196616 | tf_op jit(solution)/shard_map/ppermute | solution.py:16
  91.2 2.2 %collective-permute-done.14.one = bf16[2,128,128]{2,1,0:T(8,128)(2,1)S(1)} collective-permute-done((bf16[2,128,128]{2,1,0:T(8,128)(2,1)S(1)}, bf16[2,128,128]{2,1,0:T(8,128)(2,1)S(1)}, u32[]{:S(2)}, u32[]{:S(2)}) %collective-permute-start.14) | collective-permute-done | bytes 65568 | tf_op jit(solution)/shard_map/ppermute | solution.py:16
  93.9 3.0 %collective-permute-done.16.three = bf16[2,128,128]{2,1,0:T(8,128)(2,1)S(1)} collective-permute-done((bf16[2,128,128]{2,1,0:T(8,128)(2,1)S(1)}, bf16[2,128,128]{2,1,0:T(8,128)(2,1)S(1)}, u32[]{:S(2)}, u32[]{:S(2)}) %collective-permute-start.16) | collective-permute-done | bytes 65568 | tf_op jit(solution)/shard_map/ppermute | solution.py:16
  98.5 8.4 %all_to_all.40 = bf16[4,128,128]{2,1,0:T(8,128)(2,1)S(1)} all-to-all(bf16[4,128,128]{2,1,0:T(8,128)(2,1)S(1)} %shard_map.82), channel_id=1, replica_groups={{0,1,2,3},{4,5,6,7},{8,9,10,11},{12,13,14,15},{16,17,18,19},{20,21,22,2..., dimensions={0} | all-to-all | bytes 262144 | tf_op jit(solution)/shard_map/all_to_all | solution.py:25
  106.9 3.8 %all-to-all-start.2 = ((bf16[16,128,128]{2,1,0:T(8,128)(2,1)}), bf16[16,128,128]{2,1,0:T(8,128)(2,1)S(1)}, u32[]{:S(2)}, u32[]{:S(2)}) async-start(bf16[16,128,128]{2,1,0:T(8,128)(2,1)} %get-tuple-element.33), calls=%async_computation.2 | async-start | bytes 1048576 | tf_op jit(solution)/shard_map/all_to_all | solution.py:250
  112.1 3.2 %collective-permute-start.19 = (bf16[2,128,128]{2,1,0:T(8,128)(2,1)S(1)}, bf16[2,128,128]{2,1,0:T(8,128)(2,1)S(1)}, u32[]{:S(2)}, u32[]{:S(2)}) collective-permute-start(bf16[2,128,128]{2,1,0:T(8,128)(2,1)S(1)} %pad_maximum_fusion.2.own), channel_id=1, source_target_pairs={{0,96},{16,112},{32,0},{48,16},{64,32},{80,48},{96,64},{112,80},{1... | collective-permute-start | bytes 196616 | tf_op jit(solution)/shard_map/ppermute | solution.py:16
  115.3 2.2 %collective-permute-done.18.one = bf16[2,128,128]{2,1,0:T(8,128)(2,1)S(1)} collective-permute-done((bf16[2,128,128]{2,1,0:T(8,128)(2,1)S(1)}, bf16[2,128,128]{2,1,0:T(8,128)(2,1)S(1)}, u32[]{:S(2)}, u32[]{:S(2)}) %collective-permute-start.18) | collective-permute-done | bytes 65568 | tf_op jit(solution)/shard_map/ppermute | solution.py:16
  118.1 3.0 %collective-permute-done.20.three = bf16[2,128,128]{2,1,0:T(8,128)(2,1)S(1)} collective-permute-done((bf16[2,128,128]{2,1,0:T(8,128)(2,1)S(1)}, bf16[2,128,128]{2,1,0:T(8,128)(2,1)S(1)}, u32[]{:S(2)}, u32[]{:S(2)}) %collective-permute-start.20) | collective-permute-done | bytes 65568 | tf_op jit(solution)/shard_map/ppermute | solution.py:16
  121.1 2.3 %shard_map.83 = bf16[4,128,128]{2,1,0:T(8,128)(2,1)} custom-call(s32[8]{0:T(128)S(1)} %stack.66.order, bf16[2,128,128]{2,1,0:T(8,128)(2,1)S(1)} %pad_maximum_fusion.2.own, bf16[2,128,128]{2,1,0:T(8,128)(2,1)S(1)} %collective-permute-done.18.one, bf16[2,128,128]{2,1,0:T(8,128)(2,1)S(1)} %collective-permute-done.19.two, ...), custom_call_target="tpu_custom_call" | custom-call | flops 134217728 | bytes 1048576 | tf_op jit(solution)/shard_map/pallas_call | solution.py:228
  123.4 4.4 %all-to-all-start.4 = ((bf16[4,128,128]{2,1,0:T(8,128)(2,1)}), bf16[4,128,128]{2,1,0:T(8,128)(2,1)S(1)}, u32[]{:S(2)}, u32[]{:S(2)}) async-start(bf16[4,128,128]{2,1,0:T(8,128)(2,1)} %shard_map.83), calls=%async_computation.4 | async-start | bytes 262144 | tf_op jit(solution)/shard_map/all_to_all | solution.py:25
  127.9 5.9 %all-to-all-done.4 = bf16[4,128,128]{2,1,0:T(8,128)(2,1)S(1)} async-done(((bf16[4,128,128]{2,1,0:T(8,128)(2,1)}), bf16[4,128,128]{2,1,0:T(8,128)(2,1)S(1)}, u32[]{:S(2)}, u32[]{:S(2)}) %all-to-all-start.4) | async-done | bytes 131104 | tf_op jit(solution)/shard_map/all_to_all | solution.py:25
  134.7 5.0 %all-to-all-start.5 = ((bf16[16,128,128]{2,1,0:T(8,128)(2,1)}), bf16[16,128,128]{2,1,0:T(8,128)(2,1)S(1)}, u32[]{:S(2)}, u32[]{:S(2)}) async-start(bf16[16,128,128]{2,1,0:T(8,128)(2,1)} %broadcast_in_dim.4), calls=%async_computation.5 | async-start | bytes 1048576 | tf_op jit(solution)/shard_map/all_to_all | solution.py:255
  141.1 3.2 %collective-permute-start.23 = (bf16[2,128,128]{2,1,0:T(8,128)(2,1)S(1)}, bf16[2,128,128]{2,1,0:T(8,128)(2,1)S(1)}, u32[]{:S(2)}, u32[]{:S(2)}) collective-permute-start(bf16[2,128,128]{2,1,0:T(8,128)(2,1)S(1)} %pad_maximum_fusion.3.own), channel_id=1, source_target_pairs={{0,96},{16,112},{32,0},{48,16},{64,32},{80,48},{96,64},{112,80},{1... | collective-permute-start | bytes 196616 | tf_op jit(solution)/shard_map/ppermute | solution.py:16
  144.4 2.2 %collective-permute-done.22.one = bf16[2,128,128]{2,1,0:T(8,128)(2,1)S(1)} collective-permute-done((bf16[2,128,128]{2,1,0:T(8,128)(2,1)S(1)}, bf16[2,128,128]{2,1,0:T(8,128)(2,1)S(1)}, u32[]{:S(2)}, u32[]{:S(2)}) %collective-permute-start.22) | collective-permute-done | bytes 65568 | tf_op jit(solution)/shard_map/ppermute | solution.py:16
  147.2 3.0 %collective-permute-done.24.three = bf16[2,128,128]{2,1,0:T(8,128)(2,1)S(1)} collective-permute-done((bf16[2,128,128]{2,1,0:T(8,128)(2,1)S(1)}, bf16[2,128,128]{2,1,0:T(8,128)(2,1)S(1)}, u32[]{:S(2)}, u32[]{:S(2)}) %collective-permute-start.24) | collective-permute-done | bytes 65568 | tf_op jit(solution)/shard_map/ppermute | solution.py:16
  150.1 1.7 shard_map.84
  152.5 10.5 %all_to_all.41 = bf16[4,128,128]{2,1,0:T(8,128)(2,1)S(1)} all-to-all(bf16[4,128,128]{2,1,0:T(8,128)(2,1)S(1)} %shard_map.84), channel_id=1, replica_groups={{0,1,2,3},{4,5,6,7},{8,9,10,11},{12,13,14,15},{16,17,18,19},{20,21,22,2..., dimensions={0} | all-to-all | bytes 262144 | tf_op jit(solution)/shard_map/all_to_all | solution.py:25
  163.9 5.0 %all-to-all-start.7 = ((bf16[16,128,128]{2,1,0:T(8,128)(2,1)}), bf16[16,128,128]{2,1,0:T(8,128)(2,1)S(1)}, u32[]{:S(2)}, u32[]{:S(2)}) async-start(bf16[16,128,128]{2,1,0:T(8,128)(2,1)} %broadcast_in_dim.5), calls=%async_computation.7 | async-start | bytes 1048576 | tf_op jit(solution)/shard_map/all_to_all | solution.py:255
  169.2 9.7 %all-to-all-done.7 = bf16[16,128,128]{2,1,0:T(8,128)(2,1)S(1)} async-done(((bf16[16,128,128]{2,1,0:T(8,128)(2,1)}), bf16[16,128,128]{2,1,0:T(8,128)(2,1)S(1)}, u32[]{:S(2)}, u32[]{:S(2)}) %all-to-all-start.7) | async-done | bytes 524320 | tf_op jit(solution)/shard_map/all_to_all | solution.py:255
  184.4 2.7 %collective-permute-done.28 = f32[32,512]{1,0:T(8,128)S(1)} collective-permute-done((f32[32,512]{1,0:T(8,128)S(1)}, f32[32,512]{1,0:T(8,128)S(1)}, u32[]{:S(2)}, u32[]{:S(2)}) %collective-permute-start.28) | collective-permute-done | bytes 65568 | tf_op jit(solution)/shard_map/ppermute | solution.py:16
  (98 shorter events, 31.0 us)
Async XLA Ops:
  9.7 25.6 %all-to-all-start = ((bf16[4,3,64,512]{3,2,1,0:T(8,128)(2,1)}), bf16[4,3,64,512]{3,2,1,0:T(8,128)(2,1)}, u32[]{:S(2)}, u32[]{:S(2)}) async-start(bf16[4,3,64,512]{3,2,1,0:T(8,128)(2,1)} %get-tuple-element.22), calls=%async_computation | async-start | bytes 1572864 | tf_op jit(solution)/shard_map/all_to_all | solution.py:25
  15.1 81.8 %all-gather.2.cloned.1.call-start = ((), (), s32[]{:S(2)}) async-start(), calls=%async_computation.8 | async-start | bytes 3932160 | tf_op jit(solution)/shard_map/all_gather | solution.py:30
  15.1 16.9 %collective-permute-start = (bf16[3,128,512]{2,1,0:T(8,128)(2,1)S(1)}, bf16[3,128,512]{2,1,0:T(8,128)(2,1)S(1)}, u32[]{:S(2)}, u32[]{:S(2)}) collective-permute-start(bf16[3,128,512]{2,1,0:T(8,128)(2,1)S(1)} %get-tuple-element.20), channel_id=1, source_target_pairs={{0,32},{16,48},{32,64},{48,80},{64,96},{80,112},{96,0},{112,16},{1... | collective-permute-start | bytes 1179656 | tf_op jit(solution)/shard_map/ppermute | solution.py:16
  16.6 15.4 %collective-permute-start.1 = (bf16[3,128,512]{2,1,0:T(8,128)(2,1)S(1)}, bf16[3,128,512]{2,1,0:T(8,128)(2,1)S(1)}, u32[]{:S(2)}, u32[]{:S(2)}) collective-permute-start(bf16[3,128,512]{2,1,0:T(8,128)(2,1)S(1)} %get-tuple-element.21), channel_id=1, source_target_pairs={{0,96},{16,112},{32,0},{48,16},{64,32},{80,48},{96,64},{112,80},{1... | collective-permute-start | bytes 1179656 | tf_op jit(solution)/shard_map/ppermute | solution.py:16
  18.3 17.0 %collective-permute-start.2 = (bf16[3,128,512]{2,1,0:T(8,128)(2,1)S(1)}, bf16[3,128,512]{2,1,0:T(8,128)(2,1)S(1)}, u32[]{:S(2)}, u32[]{:S(2)}) collective-permute-start(bf16[3,128,512]{2,1,0:T(8,128)(2,1)S(1)} %get-tuple-element.21), channel_id=1, source_target_pairs={{0,32},{16,48},{32,64},{48,80},{64,96},{80,112},{96,0},{112,16},{1... | collective-permute-start | bytes 1179656 | tf_op jit(solution)/shard_map/ppermute | solution.py:16
  18.6 16.7 %collective-permute-start.3 = (bf16[3,128,512]{2,1,0:T(8,128)(2,1)S(1)}, bf16[3,128,512]{2,1,0:T(8,128)(2,1)S(1)}, u32[]{:S(2)}, u32[]{:S(2)}) collective-permute-start(bf16[3,128,512]{2,1,0:T(8,128)(2,1)S(1)} %get-tuple-element.20), channel_id=1, source_target_pairs={{0,96},{16,112},{32,0},{48,16},{64,32},{80,48},{96,64},{112,80},{1... | collective-permute-start | bytes 1179656 | tf_op jit(solution)/shard_map/ppermute | solution.py:16
  35.4 2.7 %collective-permute-start.4 = (bf16[3,256,512]{2,1,0:T(8,128)(2,1)S(1)}, bf16[3,256,512]{2,1,0:T(8,128)(2,1)}, u32[]{:S(2)}, u32[]{:S(2)}) collective-permute-start(bf16[3,256,512]{2,1,0:T(8,128)(2,1)S(1)} %copy-done), channel_id=1, source_target_pairs={{0,16},{16,0},{32,48},{48,32},{64,80},{80,64},{96,112},{112,96},{1... | collective-permute-start | bytes 2359304 | tf_op jit(solution)/shard_map/ppermute | solution.py:20
  35.5 4.1 %collective-permute-start.5 = (bf16[3,128,512]{2,1,0:T(8,128)(2,1)S(1)}, bf16[3,128,512]{2,1,0:T(8,128)(2,1)S(1)}, u32[]{:S(2)}, u32[]{:S(2)}) collective-permute-start(bf16[3,128,512]{2,1,0:T(8,128)(2,1)S(1)} %collective-permute-done.refs_0_), channel_id=1, source_target_pairs={{0,16},{16,0},{32,48},{48,32},{64,80},{80,64},{96,112},{112,96},{1... | collective-permute-start | bytes 1179656 | tf_op jit(solution)/shard_map/ppermute | solution.py:20
  36.0 10.6 %collective-permute-start.6 = (bf16[3,128,512]{2,1,0:T(8,128)(2,1)S(1)}, bf16[3,128,512]{2,1,0:T(8,128)(2,1)S(1)}, u32[]{:S(2)}, u32[]{:S(2)}) collective-permute-start(bf16[3,128,512]{2,1,0:T(8,128)(2,1)S(1)} %collective-permute-done.2.refs_1_), channel_id=1, source_target_pairs={{0,16},{16,0},{32,48},{48,32},{64,80},{80,64},{96,112},{112,96},{1... | collective-permute-start | bytes 1179656 | tf_op jit(solution)/shard_map/ppermute | solution.py:20
  36.0 11.3 %collective-permute-start.7 = (bf16[3,128,512]{2,1,0:T(8,128)(2,1)S(1)}, bf16[3,128,512]{2,1,0:T(8,128)(2,1)}, u32[]{:S(2)}, u32[]{:S(2)}) collective-permute-start(bf16[3,128,512]{2,1,0:T(8,128)(2,1)S(1)} %collective-permute-done.3.refs_4_), channel_id=1, source_target_pairs={{0,16},{16,0},{32,48},{48,32},{64,80},{80,64},{96,112},{112,96},{1... | collective-permute-start | bytes 1179656 | tf_op jit(solution)/shard_map/ppermute | solution.py:20
  36.5 10.9 %collective-permute-start.8 = (bf16[3,128,512]{2,1,0:T(8,128)(2,1)S(1)}, bf16[3,128,512]{2,1,0:T(8,128)(2,1)}, u32[]{:S(2)}, u32[]{:S(2)}) collective-permute-start(bf16[3,128,512]{2,1,0:T(8,128)(2,1)S(1)} %collective-permute-done.1.refs_5_), channel_id=1, source_target_pairs={{0,16},{16,0},{32,48},{48,32},{64,80},{80,64},{96,112},{112,96},{1... | collective-permute-start | bytes 1179656 | tf_op jit(solution)/shard_map/ppermute | solution.py:20
  38.0 20.4 %collective-permute-start.9 = (bf16[3,128,512]{2,1,0:T(8,128)(2,1)S(1)}, bf16[3,128,512]{2,1,0:T(8,128)(2,1)}, u32[]{:S(2)}, u32[]{:S(2)}) collective-permute-start(bf16[3,128,512]{2,1,0:T(8,128)(2,1)S(1)} %collective-permute-done.refs_0_), channel_id=1, source_target_pairs={{0,32},{16,48},{32,64},{48,80},{64,96},{80,112},{96,0},{112,16},{1... | collective-permute-start | bytes 1179656 | tf_op jit(solution)/shard_map/ppermute | solution.py:16
  39.5 18.9 %collective-permute-start.10 = (bf16[3,128,512]{2,1,0:T(8,128)(2,1)S(1)}, bf16[3,128,512]{2,1,0:T(8,128)(2,1)}, u32[]{:S(2)}, u32[]{:S(2)}) collective-permute-start(bf16[3,128,512]{2,1,0:T(8,128)(2,1)S(1)} %collective-permute-done.1.refs_5_), channel_id=1, source_target_pairs={{0,96},{16,112},{32,0},{48,16},{64,32},{80,48},{96,64},{112,80},{1... | collective-permute-start | bytes 1179656 | tf_op jit(solution)/shard_map/ppermute | solution.py:16
  58.4 2.0 %collective-permute-start.11 = (bf16[3,128,512]{2,1,0:T(8,128)(2,1)}, bf16[3,128,512]{2,1,0:T(8,128)(2,1)S(1)}, u32[]{:S(2)}, u32[]{:S(2)}) collective-permute-start(bf16[3,128,512]{2,1,0:T(8,128)(2,1)} %collective-permute-done.9.refs_0_), channel_id=1, source_target_pairs={{0,16},{16,0},{32,48},{48,32},{64,80},{80,64},{96,112},{112,96},{1... | collective-permute-start | bytes 1179656 | tf_op jit(solution)/shard_map/ppermute | solution.py:20
  58.5 2.5 %collective-permute-start.12 = (bf16[3,128,512]{2,1,0:T(8,128)(2,1)}, bf16[3,128,512]{2,1,0:T(8,128)(2,1)S(1)}, u32[]{:S(2)}, u32[]{:S(2)}) collective-permute-start(bf16[3,128,512]{2,1,0:T(8,128)(2,1)} %collective-permute-done.10.refs_1_), channel_id=1, source_target_pairs={{0,16},{16,0},{32,48},{48,32},{64,80},{80,64},{96,112},{112,96},{1... | collective-permute-start | bytes 1179656 | tf_op jit(solution)/shard_map/ppermute | solution.py:20
  67.2 19.2 %all-to-all-start.1 = ((bf16[16,128,128]{2,1,0:T(8,128)(2,1)}), bf16[16,128,128]{2,1,0:T(8,128)(2,1)S(1)}, u32[]{:S(2)}, u32[]{:S(2)}) async-start(bf16[16,128,128]{2,1,0:T(8,128)(2,1)} %get-tuple-element.31), calls=%async_computation.1 | async-start | bytes 1048576 | tf_op jit(solution)/shard_map/all_to_all | solution.py:250
  87.8 5.5 %collective-permute-start.14 = (bf16[2,128,128]{2,1,0:T(8,128)(2,1)S(1)}, bf16[2,128,128]{2,1,0:T(8,128)(2,1)S(1)}, u32[]{:S(2)}, u32[]{:S(2)}) collective-permute-start(bf16[2,128,128]{2,1,0:T(8,128)(2,1)S(1)} %pad_maximum_fusion.1.own), channel_id=1, source_target_pairs={{0,32},{16,48},{32,64},{48,80},{64,96},{80,112},{96,0},{112,16},{1... | collective-permute-start | bytes 196616 | tf_op jit(solution)/shard_map/ppermute | solution.py:16
  87.9 6.0 %collective-permute-start.15 = (bf16[2,128,128]{2,1,0:T(8,128)(2,1)S(1)}, bf16[2,128,128]{2,1,0:T(8,128)(2,1)S(1)}, u32[]{:S(2)}, u32[]{:S(2)}) collective-permute-start(bf16[2,128,128]{2,1,0:T(8,128)(2,1)S(1)} %pad_maximum_fusion.1.own), channel_id=1, source_target_pairs={{0,96},{16,112},{32,0},{48,16},{64,32},{80,48},{96,64},{112,80},{1... | collective-permute-start | bytes 196616 | tf_op jit(solution)/shard_map/ppermute | solution.py:16
  91.1 5.8 %collective-permute-start.16 = (bf16[2,128,128]{2,1,0:T(8,128)(2,1)S(1)}, bf16[2,128,128]{2,1,0:T(8,128)(2,1)S(1)}, u32[]{:S(2)}, u32[]{:S(2)}) collective-permute-start(bf16[2,128,128]{2,1,0:T(8,128)(2,1)S(1)} %pad_maximum_fusion.1.own), channel_id=1, source_target_pairs={{0,64},{16,80},{32,96},{48,112},{64,0},{80,16},{96,32},{112,48},{1... | collective-permute-start | bytes 196616 | tf_op jit(solution)/shard_map/ppermute | solution.py:16
  106.9 16.5 %all-to-all-start.2 = ((bf16[16,128,128]{2,1,0:T(8,128)(2,1)}), bf16[16,128,128]{2,1,0:T(8,128)(2,1)S(1)}, u32[]{:S(2)}, u32[]{:S(2)}) async-start(bf16[16,128,128]{2,1,0:T(8,128)(2,1)} %get-tuple-element.33), calls=%async_computation.2 | async-start | bytes 1048576 | tf_op jit(solution)/shard_map/all_to_all | solution.py:250
  112.0 5.5 %collective-permute-start.18 = (bf16[2,128,128]{2,1,0:T(8,128)(2,1)S(1)}, bf16[2,128,128]{2,1,0:T(8,128)(2,1)S(1)}, u32[]{:S(2)}, u32[]{:S(2)}) collective-permute-start(bf16[2,128,128]{2,1,0:T(8,128)(2,1)S(1)} %pad_maximum_fusion.2.own), channel_id=1, source_target_pairs={{0,32},{16,48},{32,64},{48,80},{64,96},{80,112},{96,0},{112,16},{1... | collective-permute-start | bytes 196616 | tf_op jit(solution)/shard_map/ppermute | solution.py:16
  112.1 6.0 %collective-permute-start.19 = (bf16[2,128,128]{2,1,0:T(8,128)(2,1)S(1)}, bf16[2,128,128]{2,1,0:T(8,128)(2,1)S(1)}, u32[]{:S(2)}, u32[]{:S(2)}) collective-permute-start(bf16[2,128,128]{2,1,0:T(8,128)(2,1)S(1)} %pad_maximum_fusion.2.own), channel_id=1, source_target_pairs={{0,96},{16,112},{32,0},{48,16},{64,32},{80,48},{96,64},{112,80},{1... | collective-permute-start | bytes 196616 | tf_op jit(solution)/shard_map/ppermute | solution.py:16
  115.3 5.8 %collective-permute-start.20 = (bf16[2,128,128]{2,1,0:T(8,128)(2,1)S(1)}, bf16[2,128,128]{2,1,0:T(8,128)(2,1)S(1)}, u32[]{:S(2)}, u32[]{:S(2)}) collective-permute-start(bf16[2,128,128]{2,1,0:T(8,128)(2,1)S(1)} %pad_maximum_fusion.2.own), channel_id=1, source_target_pairs={{0,64},{16,80},{32,96},{48,112},{64,0},{80,16},{96,32},{112,48},{1... | collective-permute-start | bytes 196616 | tf_op jit(solution)/shard_map/ppermute | solution.py:16
  123.4 10.4 %all-to-all-start.4 = ((bf16[4,128,128]{2,1,0:T(8,128)(2,1)}), bf16[4,128,128]{2,1,0:T(8,128)(2,1)S(1)}, u32[]{:S(2)}, u32[]{:S(2)}) async-start(bf16[4,128,128]{2,1,0:T(8,128)(2,1)} %shard_map.83), calls=%async_computation.4 | async-start | bytes 262144 | tf_op jit(solution)/shard_map/all_to_all | solution.py:25
  134.7 17.1 %all-to-all-start.5 = ((bf16[16,128,128]{2,1,0:T(8,128)(2,1)}), bf16[16,128,128]{2,1,0:T(8,128)(2,1)S(1)}, u32[]{:S(2)}, u32[]{:S(2)}) async-start(bf16[16,128,128]{2,1,0:T(8,128)(2,1)} %broadcast_in_dim.4), calls=%async_computation.5 | async-start | bytes 1048576 | tf_op jit(solution)/shard_map/all_to_all | solution.py:255
  141.1 5.5 %collective-permute-start.22 = (bf16[2,128,128]{2,1,0:T(8,128)(2,1)S(1)}, bf16[2,128,128]{2,1,0:T(8,128)(2,1)S(1)}, u32[]{:S(2)}, u32[]{:S(2)}) collective-permute-start(bf16[2,128,128]{2,1,0:T(8,128)(2,1)S(1)} %pad_maximum_fusion.3.own), channel_id=1, source_target_pairs={{0,32},{16,48},{32,64},{48,80},{64,96},{80,112},{96,0},{112,16},{1... | collective-permute-start | bytes 196616 | tf_op jit(solution)/shard_map/ppermute | solution.py:16
  141.1 6.0 %collective-permute-start.23 = (bf16[2,128,128]{2,1,0:T(8,128)(2,1)S(1)}, bf16[2,128,128]{2,1,0:T(8,128)(2,1)S(1)}, u32[]{:S(2)}, u32[]{:S(2)}) collective-permute-start(bf16[2,128,128]{2,1,0:T(8,128)(2,1)S(1)} %pad_maximum_fusion.3.own), channel_id=1, source_target_pairs={{0,96},{16,112},{32,0},{48,16},{64,32},{80,48},{96,64},{112,80},{1... | collective-permute-start | bytes 196616 | tf_op jit(solution)/shard_map/ppermute | solution.py:16
  144.4 5.8 %collective-permute-start.24 = (bf16[2,128,128]{2,1,0:T(8,128)(2,1)S(1)}, bf16[2,128,128]{2,1,0:T(8,128)(2,1)S(1)}, u32[]{:S(2)}, u32[]{:S(2)}) collective-permute-start(bf16[2,128,128]{2,1,0:T(8,128)(2,1)S(1)} %pad_maximum_fusion.3.own), channel_id=1, source_target_pairs={{0,64},{16,80},{32,96},{48,112},{64,0},{80,16},{96,32},{112,48},{1... | collective-permute-start | bytes 196616 | tf_op jit(solution)/shard_map/ppermute | solution.py:16
  163.9 15.1 %all-to-all-start.7 = ((bf16[16,128,128]{2,1,0:T(8,128)(2,1)}), bf16[16,128,128]{2,1,0:T(8,128)(2,1)S(1)}, u32[]{:S(2)}, u32[]{:S(2)}) async-start(bf16[16,128,128]{2,1,0:T(8,128)(2,1)} %broadcast_in_dim.5), calls=%async_computation.7 | async-start | bytes 1048576 | tf_op jit(solution)/shard_map/all_to_all | solution.py:255
  181.1 6.0 %collective-permute-start.28 = (f32[32,512]{1,0:T(8,128)S(1)}, f32[32,512]{1,0:T(8,128)S(1)}, u32[]{:S(2)}, u32[]{:S(2)}) collective-permute-start(f32[32,512]{1,0:T(8,128)S(1)} %add.128), channel_id=1, source_target_pairs={{0,64},{16,80},{32,96},{48,112},{64,0},{80,16},{96,32},{112,48},{1... | collective-permute-start | bytes 196616 | tf_op jit(solution)/shard_map/ppermute | solution.py:16
  181.2 5.9 %collective-permute-start.27 = (f32[32,512]{1,0:T(8,128)S(1)}, f32[32,512]{1,0:T(8,128)S(1)}, u32[]{:S(2)}, u32[]{:S(2)}) collective-permute-start(f32[32,512]{1,0:T(8,128)S(1)} %add.128), channel_id=1, source_target_pairs={{0,96},{16,112},{32,0},{48,16},{64,32},{80,48},{96,64},{112,80},{1... | collective-permute-start | bytes 196616 | tf_op jit(solution)/shard_map/ppermute | solution.py:16
  182.7 5.5 %collective-permute-start.26 = (f32[32,512]{1,0:T(8,128)S(1)}, f32[32,512]{1,0:T(8,128)S(1)}, u32[]{:S(2)}, u32[]{:S(2)}) collective-permute-start(f32[32,512]{1,0:T(8,128)S(1)} %add.128), channel_id=1, source_target_pairs={{0,32},{16,48},{32,64},{48,80},{64,96},{80,112},{96,0},{112,16},{1... | collective-permute-start | bytes 196616 | tf_op jit(solution)/shard_map/ppermute | solution.py:16
  (12 other events, 65.4 us)
Sparse Core Ops, SparseCore 0:
  35.5 41.1 all-gather.1

commit v8 on v7

--- a/solution.py
+++ b/solution.py
@@ -27,7 +27,9 @@
 
 def y_gather(v):
     groups = [[4 * y + z for y in range(4)] for z in range(4)]
-    return lax.all_gather(v, "col", axis=0, axis_index_groups=groups, tiled=True)
+    sent = jnp.broadcast_to(v[None], (4, *v.shape))
+    gathered = lax.all_to_all(sent, "col", 0, 0, axis_index_groups=groups, tiled=True)
+    return gathered.reshape(16, *v.shape[1:])
 
 
 def whole(array):
@@ -279,9 +281,12 @@
     sibling = in_hbm(other_core(prev_solution))
     left = split_tiles(in_hbm(left_factor))
     lines = z_exchange(lines)
-    before_low, after_high, before_high, after_low, left, lines = lax.optimization_barrier(
-        (before_low, after_high, before_high, after_low, left, lines)
+    before_low, after_high, before_high, after_low, sibling, left, lines = (
+        lax.optimization_barrier(
+            (before_low, after_high, before_high, after_low, sibling, left, lines)
+        )
     )
+    sibling = in_hbm(sibling)
     panels = in_hbm(y_gather(lines))
     far_low, far_high = x_shift(before_low, 1), x_shift(after_high, -1)
     pieces = [(prev_solution, 0), (prev_solution, 1), (sibling, 0), (sibling, 1)]
@@ -289,7 +294,8 @@
     token = started[:8, :128]
     pieces = []
     for pair in ((before_low, before_high), (after_low, after_high)):
-        pieces += [(v, 0) for v in pair] + [(other_core(v), 0) for v in pair]
+        pieces += [(in_hbm(v), 0) for v in pair]
+        pieces += [(in_hbm(other_core(v)), 0) for v in pair]
     started = products(order[2:6], left, pieces, started, token)
     far_low, far_high, token = lax.optimization_barrier(
         (far_low, far_high, started[:8, :128])
@@ -298,6 +304,8 @@
     pieces = [(v, 0) for v in far] + [(other_core(v), 0) for v in far]
     first, second = products(order[6:], left, pieces, started, token, last=True)
 
+    first, second, panels = lax.optimization_barrier((first, second, panels))
+    panels = in_hbm(panels)
     known = lax.dynamic_slice(cross, (0, 64 * z, 128 * y), (4, 64, 128))
     known = known.astype(F32).reshape(2, 128, 128)
     first_rhs = (known[0] - over_sites(first)).astype(BF)
@@ -305,7 +313,9 @@
     rest = known[1] - over_sites(second)
     solved_first = over_z(stage(order, first_rhs, panels, 0)).astype(BF)
     every_first = all_sites(solved_first)
-    second_rhs = (rest - over_z(stage(order, solved_first, panels, 1))).astype(BF)
+    partial = stage(order, solved_first, panels, 1)
+    partial, rest = lax.optimization_barrier((partial, rest))
+    second_rhs = (rest - over_z(partial)).astype(BF)
     partial = stage(order, second_rhs, panels, 2)
     partial, every_first = lax.optimization_barrier((partial, every_first))
     solved_second = over_z(partial).astype(BF)

time: 197 us -> 191 us (0.970)
  between operations: 14.4 us -> 1.06 us
  blocking collectives: 18.8 us -> 28.9 us
    all_to_all x2 -> x3, blocking collectives: 18.8 us -> 28.9 us  [z_exchange(): return lax.all_to_all(v, 'col', 0, 0, axis_index_groups=groups, tiled=True)]
    all_to_all x0 -> x1, waiting for transfers between devices: none -> 8.77 us  [y_gather(): lax.all_to_all(sent, 'col', 0, 0, axis_index_groups=groups, tiled=True)]
    ppermute x18, waiting for transfers between devices: 24.4 us -> 18.2 us  [x_shift(): return lax.ppermute(v, 'row', [(r, (r + 2 * step) % 8) for r in range(8)])]
    all_to_all x2 -> x1, waiting for transfers between devices: 5.9 us -> 0.01 us  [z_exchange(): return lax.all_to_all(v, 'col', 0, 0, axis_index_groups=groups, tiled=True)]
    all_to_all x2, waiting for transfers between devices: 9.69 us -> 15.1 us  [all_sites(): lax.all_to_all(sent, 'col', 0, 0, tiled=True).reshape(4, 4, 2, 64, 128)]
    all_to_all x0 -> x1, starting transfers between devices: none -> 4.8 us  [y_gather(): lax.all_to_all(sent, 'col', 0, 0, axis_index_groups=groups, tiled=True)]
    all_to_all x2 -> x1, starting transfers between devices: 9.79 us -> 5.39 us  [z_exchange(): return lax.all_to_all(v, 'col', 0, 0, axis_index_groups=groups, tiled=True)]
    all_to_all x2, starting transfers between devices: 11.1 us -> 8.66 us  [over_sites(): lax.all_to_all(partial, 'col', 0, 0, tiled=True).astype(F32).sum(axis=0)]
  transfers between devices with their start and end apart: 36 -> 35, of which waited for: 22 -> 19; matrix products, arithmetic and copies ran while one was open for 1% -> 2% of each run, Pallas kernels for 17% -> 18%
where the time goes in v8:
time: 191 us; the launch traced here: 190 us
  waiting for transfers between devices  58 us (30%)
  starting transfers between devices  54.2 us (28%)
  Pallas kernels  37.8 us (20%)
  blocking collectives  28.9 us (15%)
  local copies, waits for them, and re-layouts  6.86 us (4%)
  other arithmetic  3.09 us (2%)
    all_to_all x3, blocking collectives, z_exchange(): return lax.all_to_all(v, 'col', 0, 0, axis_index_groups=groups, tiled=True)  28.9 us
    ppermute x18, starting transfers between devices, x_shift(): return lax.ppermute(v, 'row', [(r, (r + 2 * step) % 8) for r in range(8)])  23.4 us
    pallas_call x3, Pallas kernels, products(): pl.pallas_call(kernel, grid_spec=pltpu.PrefetchScalarGridSpec(num_scalar_...  19.7 us
    ppermute x18, waiting for transfers between devices, x_shift(): return lax.ppermute(v, 'row', [(r, (r + 2 * step) % 8) for r in range(8)])  18.2 us
    all_to_all x2, waiting for transfers between devices, all_sites(): lax.all_to_all(sent, 'col', 0, 0, tiled=True).reshape(4, 4, 2, 64, 128)  15.1 us
    pallas_call x1, Pallas kernels, split_tiles(): pl.pallas_call(split_tiles_kernel, grid=(rounds, tile // rows), in_specs=...  10.4 us
    all_to_all x2, starting transfers between devices, all_sites(): lax.all_to_all(sent, 'col', 0, 0, tiled=True).reshape(4, 4, 2, 64, 128)  9.96 us
    all_to_all x2, waiting for transfers between devices, over_sites(): lax.all_to_all(partial, 'col', 0, 0, tiled=True).astype(F32).sum(axis=0)  9.18 us
  transfers between devices with their start and end apart: 35, of which 19 were waited for; matrix products, arithmetic and copies ran while one was open for 2% of the time, Pallas kernels for 18%

profile of v8, /device:TPU:0, one launch (start us, length us, event | category | flops | bytes accessed | tf_op | source)
XLA Modules:
  0.0 190.3 jit_solution(4396879902930579389)
XLA Ops:
  0.7 2.5 %shard_map.77 = (bf16[3,128,512]{2,1,0:T(8,128)(2,1)S(1)}, bf16[3,128,512]{2,1,0:T(8,128)(2,1)S(1)}, bf16[4,3,64,512]{3,2,1,0:T(8,128)(2,1)}) custom-call(bf16[3,256,512]{2,1,0:T(8,128)(2,1)} %refs_1_.1, bf16[2,512,256]{2,1,0:T(8,128)(2,1)} %bitcast.43, bf16[2,512,256]{2,1,0:T(8,128)(2,1)} %bitcast.44, bf16[512,256]{1,0:T(8,128)(2,1)} %bitcast.46), custom_call_target="tpu_custom_call" | custom-call | tf_op jit(solution)/shard_map/pallas_call | solution.py:62
  3.3 5.4 %all-to-all-start = ((bf16[4,3,64,512]{3,2,1,0:T(8,128)(2,1)}), bf16[4,3,64,512]{3,2,1,0:T(8,128)(2,1)S(1)}, u32[]{:S(2)}, u32[]{:S(2)}) async-start(bf16[4,3,64,512]{3,2,1,0:T(8,128)(2,1)} %get-tuple-element.28), calls=%async_computation | async-start | bytes 1572864 | tf_op jit(solution)/shard_map/all_to_all | solution.py:25
  10.2 1.7 collective-permute-start.1
  12.2 3.0 %collective-permute-start.3 = (bf16[3,128,512]{2,1,0:T(8,128)(2,1)S(1)}, bf16[3,128,512]{2,1,0:T(8,128)(2,1)}, u32[]{:S(2)}, u32[]{:S(2)}) collective-permute-start(bf16[3,128,512]{2,1,0:T(8,128)(2,1)S(1)} %get-tuple-element.26), channel_id=1, source_target_pairs={{0,96},{16,112},{32,0},{48,16},{64,32},{80,48},{96,64},{112,80},{1... | collective-permute-start | bytes 1179656 | tf_op jit(solution)/shard_map/ppermute | solution.py:16
  15.1 10.4 %shard_map.78 = bf16[24,4,256,256]{3,2,1,0:T(8,128)(2,1)} custom-call(bf16[4,256,24,256]{3,2,1,0:T(8,128)(2,1)} %src.1), custom_call_target="tpu_custom_call" | custom-call | bytes 25165824 | tf_op jit(solution)/shard_map/pallas_call | solution.py:84
  25.6 4.1 %collective-permute-done.2.refs_1_ = bf16[3,128,512]{2,1,0:T(8,128)(2,1)} collective-permute-done((bf16[3,128,512]{2,1,0:T(8,128)(2,1)S(1)}, bf16[3,128,512]{2,1,0:T(8,128)(2,1)}, u32[]{:S(2)}, u32[]{:S(2)}) %collective-permute-start.2) | collective-permute-done | bytes 393248 | tf_op jit(solution)/shard_map/ppermute | solution.py:16
  29.7 2.0 %broadcast_in_dim.6 = bf16[4,4,3,64,512]{4,3,2,1,0:T(8,128)(2,1)} broadcast(bf16[4,3,64,512]{3,2,1,0:T(8,128)(2,1)S(1)} %all-to-all-done), dimensions={1,2,3,4} | broadcast | bytes 3932160 | tf_op jit(solution)/shard_map/broadcast_in_dim | solution.py:30
  31.7 4.8 %all-to-all-start.1 = ((bf16[4,4,3,64,512]{4,3,2,1,0:T(8,128)(2,1)}), bf16[4,4,3,64,512]{4,3,2,1,0:T(8,128)(2,1)}, u32[]{:S(2)}, u32[]{:S(2)}) async-start(bf16[4,4,3,64,512]{4,3,2,1,0:T(8,128)(2,1)} %broadcast_in_dim.6), calls=%async_computation.1 | async-start | bytes 6291456 | tf_op jit(solution)/shard_map/all_to_all | solution.py:31
  39.3 2.1 %collective-permute-start.10 = (bf16[3,128,512]{2,1,0:T(8,128)(2,1)}, bf16[3,128,512]{2,1,0:T(8,128)(2,1)S(1)}, u32[]{:S(2)}, u32[]{:S(2)}) collective-permute-start(bf16[3,128,512]{2,1,0:T(8,128)(2,1)} %collective-permute-done.1.refs_5_), channel_id=1, source_target_pairs={{0,96},{16,112},{32,0},{48,16},{64,32},{80,48},{96,64},{112,80},{1... | collective-permute-start | bytes 1179656 | tf_op jit(solution)/shard_map/ppermute | solution.py:16
  41.4 4.9 %shard_map.79.before = f32[1024,512]{1,0:T(8,128)S(1)} custom-call(s32[2]{0:T(128)S(1)} %pad_add_fusion.2.order, bf16[24,1024,256]{2,1,0:T(8,128)(2,1)} %bitcast.38, bf16[3,256,512]{2,1,0:T(8,128)(2,1)S(1)} %copy-done, bf16[3,256,512]{2,1,0:T(8,128)(2,1)S(1)} %copy-done, bf16[3,256,512]{2,1,0:T(8,128)(2,1)} %copy-done.1, bf16[3,256,512]{2,1,0:T(8,128)(2,1)} %copy-done.1), custom_call_target="tpu_custom_call" | custom-call | flops 1610612736 | bytes 6815744 | tf_op jit(solution)/shard_map/pallas_call | solution.py:181
  47.9 8.7 %shard_map.80.before = f32[1024,512]{1,0:T(8,128)S(1)} custom-call(s32[4]{0:T(128)S(1)} %pad_add_fusion.1.order, bf16[24,1024,256]{2,1,0:T(8,128)(2,1)} %bitcast.39, f32[1024,512]{1,0:T(8,128)S(1)} %shard_map.79.before, f32[8,128]{1,0:T(8,128)S(1)} %slice.25.token, bf16[3,128,512]{2,1,0:T(8,128)(2,1)} %copy-done.2, ...), custom_call_target="tpu_custom_call" | custom-call | flops 3221225472 | bytes 11534336 | tf_op jit(solution)/shard_map/pallas_call | solution.py:181
  59.1 6.1 %shard_map.81 = (bf16[16,128,128]{2,1,0:T(8,128)(2,1)}, bf16[16,128,128]{2,1,0:T(8,128)(2,1)}) custom-call(s32[2]{0:T(128)S(1)} %pad_add_fusion.order, bf16[24,1024,256]{2,1,0:T(8,128)(2,1)} %bitcast.40, f32[1024,512]{1,0:T(8,128)S(1)} %shard_map.80.before, f32[8,128]{1,0:T(8,128)S(1)} %slice.26.token, ...), custom_call_target="tpu_custom_call" | custom-call | flops 1610612736 | bytes 6815744 | tf_op jit(solution)/shard_map/pallas_call | solution.py:181
  65.2 8.8 %all-to-all-done.1 = bf16[4,4,3,64,512]{4,3,2,1,0:T(8,128)(2,1)} async-done(((bf16[4,4,3,64,512]{4,3,2,1,0:T(8,128)(2,1)}), bf16[4,4,3,64,512]{4,3,2,1,0:T(8,128)(2,1)}, u32[]{:S(2)}, u32[]{:S(2)}) %all-to-all-start.1) | async-done | bytes 3145760 | tf_op jit(solution)/shard_map/all_to_all | solution.py:31
  74.0 4.9 %all-to-all-start.2 = ((bf16[16,128,128]{2,1,0:T(8,128)(2,1)}), bf16[16,128,128]{2,1,0:T(8,128)(2,1)S(1)}, u32[]{:S(2)}, u32[]{:S(2)}) async-start(bf16[16,128,128]{2,1,0:T(8,128)(2,1)} %get-tuple-element.41), calls=%async_computation.2 | async-start | bytes 1048576 | tf_op jit(solution)/shard_map/all_to_all | solution.py:252
  79.8 9.2 %all-to-all-done.2 = bf16[16,128,128]{2,1,0:T(8,128)(2,1)S(1)} async-done(((bf16[16,128,128]{2,1,0:T(8,128)(2,1)}), bf16[16,128,128]{2,1,0:T(8,128)(2,1)S(1)}, u32[]{:S(2)}, u32[]{:S(2)}) %all-to-all-start.2) | async-done | bytes 524320 | tf_op jit(solution)/shard_map/all_to_all | solution.py:252
  91.6 2.1 %collective-permute-start.15 = (bf16[2,128,128]{2,1,0:T(8,128)(2,1)S(1)}, bf16[2,128,128]{2,1,0:T(8,128)(2,1)S(1)}, u32[]{:S(2)}, u32[]{:S(2)}) collective-permute-start(bf16[2,128,128]{2,1,0:T(8,128)(2,1)S(1)} %pad_maximum_fusion.1.own), channel_id=1, source_target_pairs={{0,96},{16,112},{32,0},{48,16},{64,32},{80,48},{96,64},{112,80},{1... | collective-permute-start | bytes 196616 | tf_op jit(solution)/shard_map/ppermute | solution.py:16
  96.2 3.3 %collective-permute-done.16.three = bf16[2,128,128]{2,1,0:T(8,128)(2,1)S(1)} collective-permute-done((bf16[2,128,128]{2,1,0:T(8,128)(2,1)S(1)}, bf16[2,128,128]{2,1,0:T(8,128)(2,1)S(1)}, u32[]{:S(2)}, u32[]{:S(2)}) %collective-permute-start.16) | collective-permute-done | bytes 65568 | tf_op jit(solution)/shard_map/ppermute | solution.py:16
  101.2 8.4 %all_to_all.45 = bf16[4,128,128]{2,1,0:T(8,128)(2,1)S(1)} all-to-all(bf16[4,128,128]{2,1,0:T(8,128)(2,1)S(1)} %shard_map.82), channel_id=1, replica_groups={{0,1,2,3},{4,5,6,7},{8,9,10,11},{12,13,14,15},{16,17,18,19},{20,21,22,2..., dimensions={0} | all-to-all | bytes 262144 | tf_op jit(solution)/shard_map/all_to_all | solution.py:25
  109.5 3.8 %all-to-all-start.4 = ((bf16[16,128,128]{2,1,0:T(8,128)(2,1)}), bf16[16,128,128]{2,1,0:T(8,128)(2,1)S(1)}, u32[]{:S(2)}, u32[]{:S(2)}) async-start(bf16[16,128,128]{2,1,0:T(8,128)(2,1)} %get-tuple-element.45), calls=%async_computation.4 | async-start | bytes 1048576 | tf_op jit(solution)/shard_map/all_to_all | solution.py:252
  114.7 3.2 %collective-permute-start.19 = (bf16[2,128,128]{2,1,0:T(8,128)(2,1)S(1)}, bf16[2,128,128]{2,1,0:T(8,128)(2,1)S(1)}, u32[]{:S(2)}, u32[]{:S(2)}) collective-permute-start(bf16[2,128,128]{2,1,0:T(8,128)(2,1)S(1)} %pad_maximum_fusion.2.own), channel_id=1, source_target_pairs={{0,96},{16,112},{32,0},{48,16},{64,32},{80,48},{96,64},{112,80},{1... | collective-permute-start | bytes 196616 | tf_op jit(solution)/shard_map/ppermute | solution.py:16
  117.9 2.2 %collective-permute-done.18.one = bf16[2,128,128]{2,1,0:T(8,128)(2,1)S(1)} collective-permute-done((bf16[2,128,128]{2,1,0:T(8,128)(2,1)S(1)}, bf16[2,128,128]{2,1,0:T(8,128)(2,1)S(1)}, u32[]{:S(2)}, u32[]{:S(2)}) %collective-permute-start.18) | collective-permute-done | bytes 65568 | tf_op jit(solution)/shard_map/ppermute | solution.py:16
  120.7 3.0 %collective-permute-done.20.three = bf16[2,128,128]{2,1,0:T(8,128)(2,1)S(1)} collective-permute-done((bf16[2,128,128]{2,1,0:T(8,128)(2,1)S(1)}, bf16[2,128,128]{2,1,0:T(8,128)(2,1)S(1)}, u32[]{:S(2)}, u32[]{:S(2)}) %collective-permute-start.20) | collective-permute-done | bytes 65568 | tf_op jit(solution)/shard_map/ppermute | solution.py:16
  123.7 1.7 shard_map.83
  125.5 10.4 %all_to_all.46 = bf16[4,128,128]{2,1,0:T(8,128)(2,1)S(1)} all-to-all(bf16[4,128,128]{2,1,0:T(8,128)(2,1)S(1)} %shard_map.83), channel_id=1, replica_groups={{0,1,2,3},{4,5,6,7},{8,9,10,11},{12,13,14,15},{16,17,18,19},{20,21,22,2..., dimensions={0} | all-to-all | bytes 262144 | tf_op jit(solution)/shard_map/all_to_all | solution.py:25
  136.7 5.0 %all-to-all-start.6 = ((bf16[16,128,128]{2,1,0:T(8,128)(2,1)}), bf16[16,128,128]{2,1,0:T(8,128)(2,1)S(1)}, u32[]{:S(2)}, u32[]{:S(2)}) async-start(bf16[16,128,128]{2,1,0:T(8,128)(2,1)} %broadcast_in_dim.7), calls=%async_computation.6 | async-start | bytes 1048576 | tf_op jit(solution)/shard_map/all_to_all | solution.py:257
  143.2 3.2 %collective-permute-start.23 = (bf16[2,128,128]{2,1,0:T(8,128)(2,1)S(1)}, bf16[2,128,128]{2,1,0:T(8,128)(2,1)S(1)}, u32[]{:S(2)}, u32[]{:S(2)}) collective-permute-start(bf16[2,128,128]{2,1,0:T(8,128)(2,1)S(1)} %pad_maximum_fusion.3.own), channel_id=1, source_target_pairs={{0,96},{16,112},{32,0},{48,16},{64,32},{80,48},{96,64},{112,80},{1... | collective-permute-start | bytes 196616 | tf_op jit(solution)/shard_map/ppermute | solution.py:16
  146.4 5.4 %all-to-all-done.6 = bf16[16,128,128]{2,1,0:T(8,128)(2,1)S(1)} async-done(((bf16[16,128,128]{2,1,0:T(8,128)(2,1)}), bf16[16,128,128]{2,1,0:T(8,128)(2,1)S(1)}, u32[]{:S(2)}, u32[]{:S(2)}) %all-to-all-start.6) | async-done | bytes 524320 | tf_op jit(solution)/shard_map/all_to_all | solution.py:257
  152.5 1.7 shard_map.84
  154.2 10.1 %all_to_all.47 = bf16[4,128,128]{2,1,0:T(8,128)(2,1)S(1)} all-to-all(bf16[4,128,128]{2,1,0:T(8,128)(2,1)S(1)} %shard_map.84), channel_id=1, replica_groups={{0,1,2,3},{4,5,6,7},{8,9,10,11},{12,13,14,15},{16,17,18,19},{20,21,22,2..., dimensions={0} | all-to-all | bytes 262144 | tf_op jit(solution)/shard_map/all_to_all | solution.py:25
  165.2 5.0 %all-to-all-start.8 = ((bf16[16,128,128]{2,1,0:T(8,128)(2,1)}), bf16[16,128,128]{2,1,0:T(8,128)(2,1)S(1)}, u32[]{:S(2)}, u32[]{:S(2)}) async-start(bf16[16,128,128]{2,1,0:T(8,128)(2,1)} %broadcast_in_dim.8), calls=%async_computation.8 | async-start | bytes 1048576 | tf_op jit(solution)/shard_map/all_to_all | solution.py:257
  170.6 9.7 %all-to-all-done.8 = bf16[16,128,128]{2,1,0:T(8,128)(2,1)S(1)} async-done(((bf16[16,128,128]{2,1,0:T(8,128)(2,1)}), bf16[16,128,128]{2,1,0:T(8,128)(2,1)S(1)}, u32[]{:S(2)}, u32[]{:S(2)}) %all-to-all-start.8) | async-done | bytes 524320 | tf_op jit(solution)/shard_map/all_to_all | solution.py:257
  185.8 2.7 %collective-permute-done.28 = f32[32,512]{1,0:T(8,128)S(1)} collective-permute-done((f32[32,512]{1,0:T(8,128)S(1)}, f32[32,512]{1,0:T(8,128)S(1)}, u32[]{:S(2)}, u32[]{:S(2)}) %collective-permute-start.28) | collective-permute-done | bytes 65568 | tf_op jit(solution)/shard_map/ppermute | solution.py:16
  (93 shorter events, 29.8 us)
Async XLA Ops:
  0.6 29.0 %collective-permute-start.4 = (bf16[3,256,512]{2,1,0:T(8,128)(2,1)}, bf16[3,256,512]{2,1,0:T(8,128)(2,1)S(1)}, u32[]{:S(2)}, u32[]{:S(2)}) collective-permute-start(bf16[3,256,512]{2,1,0:T(8,128)(2,1)} %refs_1_.1), channel_id=1, source_target_pairs={{0,16},{16,0},{32,48},{48,32},{64,80},{80,64},{96,112},{112,96},{1... | collective-permute-start | bytes 2359304 | tf_op jit(solution)/shard_map/ppermute | solution.py:20
  3.3 26.4 %all-to-all-start = ((bf16[4,3,64,512]{3,2,1,0:T(8,128)(2,1)}), bf16[4,3,64,512]{3,2,1,0:T(8,128)(2,1)S(1)}, u32[]{:S(2)}, u32[]{:S(2)}) async-start(bf16[4,3,64,512]{3,2,1,0:T(8,128)(2,1)} %get-tuple-element.28), calls=%async_computation | async-start | bytes 1572864 | tf_op jit(solution)/shard_map/all_to_all | solution.py:25
  8.7 16.9 %collective-permute-start = (bf16[3,128,512]{2,1,0:T(8,128)(2,1)S(1)}, bf16[3,128,512]{2,1,0:T(8,128)(2,1)S(1)}, u32[]{:S(2)}, u32[]{:S(2)}) collective-permute-start(bf16[3,128,512]{2,1,0:T(8,128)(2,1)S(1)} %get-tuple-element.26), channel_id=1, source_target_pairs={{0,32},{16,48},{32,64},{48,80},{64,96},{80,112},{96,0},{112,16},{1... | collective-permute-start | bytes 1179656 | tf_op jit(solution)/shard_map/ppermute | solution.py:16
  10.2 15.4 %collective-permute-start.1 = (bf16[3,128,512]{2,1,0:T(8,128)(2,1)S(1)}, bf16[3,128,512]{2,1,0:T(8,128)(2,1)}, u32[]{:S(2)}, u32[]{:S(2)}) collective-permute-start(bf16[3,128,512]{2,1,0:T(8,128)(2,1)S(1)} %get-tuple-element.27), channel_id=1, source_target_pairs={{0,96},{16,112},{32,0},{48,16},{64,32},{80,48},{96,64},{112,80},{1... | collective-permute-start | bytes 1179656 | tf_op jit(solution)/shard_map/ppermute | solution.py:16
  11.9 17.7 %collective-permute-start.2 = (bf16[3,128,512]{2,1,0:T(8,128)(2,1)S(1)}, bf16[3,128,512]{2,1,0:T(8,128)(2,1)}, u32[]{:S(2)}, u32[]{:S(2)}) collective-permute-start(bf16[3,128,512]{2,1,0:T(8,128)(2,1)S(1)} %get-tuple-element.27), channel_id=1, source_target_pairs={{0,32},{16,48},{32,64},{48,80},{64,96},{80,112},{96,0},{112,16},{1... | collective-permute-start | bytes 1179656 | tf_op jit(solution)/shard_map/ppermute | solution.py:16
  12.2 17.5 %collective-permute-start.3 = (bf16[3,128,512]{2,1,0:T(8,128)(2,1)S(1)}, bf16[3,128,512]{2,1,0:T(8,128)(2,1)}, u32[]{:S(2)}, u32[]{:S(2)}) collective-permute-start(bf16[3,128,512]{2,1,0:T(8,128)(2,1)S(1)} %get-tuple-element.26), channel_id=1, source_target_pairs={{0,96},{16,112},{32,0},{48,16},{64,32},{80,48},{96,64},{112,80},{1... | collective-permute-start | bytes 1179656 | tf_op jit(solution)/shard_map/ppermute | solution.py:16
  31.7 42.3 %all-to-all-start.1 = ((bf16[4,4,3,64,512]{4,3,2,1,0:T(8,128)(2,1)}), bf16[4,4,3,64,512]{4,3,2,1,0:T(8,128)(2,1)}, u32[]{:S(2)}, u32[]{:S(2)}) async-start(bf16[4,4,3,64,512]{4,3,2,1,0:T(8,128)(2,1)} %broadcast_in_dim.6), calls=%async_computation.1 | async-start | bytes 6291456 | tf_op jit(solution)/shard_map/all_to_all | solution.py:31
  36.5 2.8 %collective-permute-start.5 = (bf16[3,128,512]{2,1,0:T(8,128)(2,1)S(1)}, bf16[3,128,512]{2,1,0:T(8,128)(2,1)}, u32[]{:S(2)}, u32[]{:S(2)}) collective-permute-start(bf16[3,128,512]{2,1,0:T(8,128)(2,1)S(1)} %collective-permute-done.refs_0_), channel_id=1, source_target_pairs={{0,16},{16,0},{32,48},{48,32},{64,80},{80,64},{96,112},{112,96},{1... | collective-permute-start | bytes 1179656 | tf_op jit(solution)/shard_map/ppermute | solution.py:20
  36.6 9.7 %collective-permute-start.6 = (bf16[3,128,512]{2,1,0:T(8,128)(2,1)}, bf16[3,128,512]{2,1,0:T(8,128)(2,1)S(1)}, u32[]{:S(2)}, u32[]{:S(2)}) collective-permute-start(bf16[3,128,512]{2,1,0:T(8,128)(2,1)} %collective-permute-done.2.refs_1_), channel_id=1, source_target_pairs={{0,16},{16,0},{32,48},{48,32},{64,80},{80,64},{96,112},{112,96},{1... | collective-permute-start | bytes 1179656 | tf_op jit(solution)/shard_map/ppermute | solution.py:20
  37.1 9.3 %collective-permute-start.7 = (bf16[3,128,512]{2,1,0:T(8,128)(2,1)}, bf16[3,128,512]{2,1,0:T(8,128)(2,1)S(1)}, u32[]{:S(2)}, u32[]{:S(2)}) collective-permute-start(bf16[3,128,512]{2,1,0:T(8,128)(2,1)} %collective-permute-done.3.refs_4_), channel_id=1, source_target_pairs={{0,16},{16,0},{32,48},{48,32},{64,80},{80,64},{96,112},{112,96},{1... | collective-permute-start | bytes 1179656 | tf_op jit(solution)/shard_map/ppermute | solution.py:20
  37.2 10.7 %collective-permute-start.8 = (bf16[3,128,512]{2,1,0:T(8,128)(2,1)}, bf16[3,128,512]{2,1,0:T(8,128)(2,1)}, u32[]{:S(2)}, u32[]{:S(2)}) collective-permute-start(bf16[3,128,512]{2,1,0:T(8,128)(2,1)} %collective-permute-done.1.refs_5_), channel_id=1, source_target_pairs={{0,16},{16,0},{32,48},{48,32},{64,80},{80,64},{96,112},{112,96},{1... | collective-permute-start | bytes 1179656 | tf_op jit(solution)/shard_map/ppermute | solution.py:20
  37.8 18.8 %collective-permute-start.9 = (bf16[3,128,512]{2,1,0:T(8,128)(2,1)S(1)}, bf16[3,128,512]{2,1,0:T(8,128)(2,1)S(1)}, u32[]{:S(2)}, u32[]{:S(2)}) collective-permute-start(bf16[3,128,512]{2,1,0:T(8,128)(2,1)S(1)} %collective-permute-done.refs_0_), channel_id=1, source_target_pairs={{0,32},{16,48},{32,64},{48,80},{64,96},{80,112},{96,0},{112,16},{1... | collective-permute-start | bytes 1179656 | tf_op jit(solution)/shard_map/ppermute | solution.py:16
  39.3 17.3 %collective-permute-start.10 = (bf16[3,128,512]{2,1,0:T(8,128)(2,1)}, bf16[3,128,512]{2,1,0:T(8,128)(2,1)S(1)}, u32[]{:S(2)}, u32[]{:S(2)}) collective-permute-start(bf16[3,128,512]{2,1,0:T(8,128)(2,1)} %collective-permute-done.1.refs_5_), channel_id=1, source_target_pairs={{0,96},{16,112},{32,0},{48,16},{64,32},{80,48},{96,64},{112,80},{1... | collective-permute-start | bytes 1179656 | tf_op jit(solution)/shard_map/ppermute | solution.py:16
  56.6 1.8 collective-permute-start.11
  56.7 2.4 %collective-permute-start.12 = (bf16[3,128,512]{2,1,0:T(8,128)(2,1)S(1)}, bf16[3,128,512]{2,1,0:T(8,128)(2,1)}, u32[]{:S(2)}, u32[]{:S(2)}) collective-permute-start(bf16[3,128,512]{2,1,0:T(8,128)(2,1)S(1)} %collective-permute-done.10.refs_1_), channel_id=1, source_target_pairs={{0,16},{16,0},{32,48},{48,32},{64,80},{80,64},{96,112},{112,96},{1... | collective-permute-start | bytes 1179656 | tf_op jit(solution)/shard_map/ppermute | solution.py:20
  74.0 15.0 %all-to-all-start.2 = ((bf16[16,128,128]{2,1,0:T(8,128)(2,1)}), bf16[16,128,128]{2,1,0:T(8,128)(2,1)S(1)}, u32[]{:S(2)}, u32[]{:S(2)}) async-start(bf16[16,128,128]{2,1,0:T(8,128)(2,1)} %get-tuple-element.41), calls=%async_computation.2 | async-start | bytes 1048576 | tf_op jit(solution)/shard_map/all_to_all | solution.py:252
  89.1 1.3 collective-permute-start.13
  90.4 5.5 %collective-permute-start.14 = (bf16[2,128,128]{2,1,0:T(8,128)(2,1)S(1)}, bf16[2,128,128]{2,1,0:T(8,128)(2,1)S(1)}, u32[]{:S(2)}, u32[]{:S(2)}) collective-permute-start(bf16[2,128,128]{2,1,0:T(8,128)(2,1)S(1)} %pad_maximum_fusion.1.own), channel_id=1, source_target_pairs={{0,32},{16,48},{32,64},{48,80},{64,96},{80,112},{96,0},{112,16},{1... | collective-permute-start | bytes 196616 | tf_op jit(solution)/shard_map/ppermute | solution.py:16
  91.6 4.6 %collective-permute-start.15 = (bf16[2,128,128]{2,1,0:T(8,128)(2,1)S(1)}, bf16[2,128,128]{2,1,0:T(8,128)(2,1)S(1)}, u32[]{:S(2)}, u32[]{:S(2)}) collective-permute-start(bf16[2,128,128]{2,1,0:T(8,128)(2,1)S(1)} %pad_maximum_fusion.1.own), channel_id=1, source_target_pairs={{0,96},{16,112},{32,0},{48,16},{64,32},{80,48},{96,64},{112,80},{1... | collective-permute-start | bytes 196616 | tf_op jit(solution)/shard_map/ppermute | solution.py:16
  93.7 5.8 %collective-permute-start.16 = (bf16[2,128,128]{2,1,0:T(8,128)(2,1)S(1)}, bf16[2,128,128]{2,1,0:T(8,128)(2,1)S(1)}, u32[]{:S(2)}, u32[]{:S(2)}) collective-permute-start(bf16[2,128,128]{2,1,0:T(8,128)(2,1)S(1)} %pad_maximum_fusion.1.own), channel_id=1, source_target_pairs={{0,64},{16,80},{32,96},{48,112},{64,0},{80,16},{96,32},{112,48},{1... | collective-permute-start | bytes 196616 | tf_op jit(solution)/shard_map/ppermute | solution.py:16
  109.5 15.9 %all-to-all-start.4 = ((bf16[16,128,128]{2,1,0:T(8,128)(2,1)}), bf16[16,128,128]{2,1,0:T(8,128)(2,1)S(1)}, u32[]{:S(2)}, u32[]{:S(2)}) async-start(bf16[16,128,128]{2,1,0:T(8,128)(2,1)} %get-tuple-element.45), calls=%async_computation.4 | async-start | bytes 1048576 | tf_op jit(solution)/shard_map/all_to_all | solution.py:252
  114.6 5.5 %collective-permute-start.18 = (bf16[2,128,128]{2,1,0:T(8,128)(2,1)S(1)}, bf16[2,128,128]{2,1,0:T(8,128)(2,1)S(1)}, u32[]{:S(2)}, u32[]{:S(2)}) collective-permute-start(bf16[2,128,128]{2,1,0:T(8,128)(2,1)S(1)} %pad_maximum_fusion.2.own), channel_id=1, source_target_pairs={{0,32},{16,48},{32,64},{48,80},{64,96},{80,112},{96,0},{112,16},{1... | collective-permute-start | bytes 196616 | tf_op jit(solution)/shard_map/ppermute | solution.py:16
  114.7 6.0 %collective-permute-start.19 = (bf16[2,128,128]{2,1,0:T(8,128)(2,1)S(1)}, bf16[2,128,128]{2,1,0:T(8,128)(2,1)S(1)}, u32[]{:S(2)}, u32[]{:S(2)}) collective-permute-start(bf16[2,128,128]{2,1,0:T(8,128)(2,1)S(1)} %pad_maximum_fusion.2.own), channel_id=1, source_target_pairs={{0,96},{16,112},{32,0},{48,16},{64,32},{80,48},{96,64},{112,80},{1... | collective-permute-start | bytes 196616 | tf_op jit(solution)/shard_map/ppermute | solution.py:16
  117.9 5.8 %collective-permute-start.20 = (bf16[2,128,128]{2,1,0:T(8,128)(2,1)S(1)}, bf16[2,128,128]{2,1,0:T(8,128)(2,1)S(1)}, u32[]{:S(2)}, u32[]{:S(2)}) collective-permute-start(bf16[2,128,128]{2,1,0:T(8,128)(2,1)S(1)} %pad_maximum_fusion.2.own), channel_id=1, source_target_pairs={{0,64},{16,80},{32,96},{48,112},{64,0},{80,16},{96,32},{112,48},{1... | collective-permute-start | bytes 196616 | tf_op jit(solution)/shard_map/ppermute | solution.py:16
  136.7 15.1 %all-to-all-start.6 = ((bf16[16,128,128]{2,1,0:T(8,128)(2,1)}), bf16[16,128,128]{2,1,0:T(8,128)(2,1)S(1)}, u32[]{:S(2)}, u32[]{:S(2)}) async-start(bf16[16,128,128]{2,1,0:T(8,128)(2,1)} %broadcast_in_dim.7), calls=%async_computation.6 | async-start | bytes 1048576 | tf_op jit(solution)/shard_map/all_to_all | solution.py:257
  143.1 9.4 %collective-permute-start.22 = (bf16[2,128,128]{2,1,0:T(8,128)(2,1)S(1)}, bf16[2,128,128]{2,1,0:T(8,128)(2,1)S(1)}, u32[]{:S(2)}, u32[]{:S(2)}) collective-permute-start(bf16[2,128,128]{2,1,0:T(8,128)(2,1)S(1)} %pad_maximum_fusion.3.own), channel_id=1, source_target_pairs={{0,32},{16,48},{32,64},{48,80},{64,96},{80,112},{96,0},{112,16},{1... | collective-permute-start | bytes 196616 | tf_op jit(solution)/shard_map/ppermute | solution.py:16
  143.2 9.3 %collective-permute-start.23 = (bf16[2,128,128]{2,1,0:T(8,128)(2,1)S(1)}, bf16[2,128,128]{2,1,0:T(8,128)(2,1)S(1)}, u32[]{:S(2)}, u32[]{:S(2)}) collective-permute-start(bf16[2,128,128]{2,1,0:T(8,128)(2,1)S(1)} %pad_maximum_fusion.3.own), channel_id=1, source_target_pairs={{0,96},{16,112},{32,0},{48,16},{64,32},{80,48},{96,64},{112,80},{1... | collective-permute-start | bytes 196616 | tf_op jit(solution)/shard_map/ppermute | solution.py:16
  146.4 6.1 %collective-permute-start.24 = (bf16[2,128,128]{2,1,0:T(8,128)(2,1)S(1)}, bf16[2,128,128]{2,1,0:T(8,128)(2,1)S(1)}, u32[]{:S(2)}, u32[]{:S(2)}) collective-permute-start(bf16[2,128,128]{2,1,0:T(8,128)(2,1)S(1)} %pad_maximum_fusion.3.own), channel_id=1, source_target_pairs={{0,64},{16,80},{32,96},{48,112},{64,0},{80,16},{96,32},{112,48},{1... | collective-permute-start | bytes 196616 | tf_op jit(solution)/shard_map/ppermute | solution.py:16
  165.2 15.1 %all-to-all-start.8 = ((bf16[16,128,128]{2,1,0:T(8,128)(2,1)}), bf16[16,128,128]{2,1,0:T(8,128)(2,1)S(1)}, u32[]{:S(2)}, u32[]{:S(2)}) async-start(bf16[16,128,128]{2,1,0:T(8,128)(2,1)} %broadcast_in_dim.8), calls=%async_computation.8 | async-start | bytes 1048576 | tf_op jit(solution)/shard_map/all_to_all | solution.py:257
  182.5 5.9 %collective-permute-start.28 = (f32[32,512]{1,0:T(8,128)S(1)}, f32[32,512]{1,0:T(8,128)S(1)}, u32[]{:S(2)}, u32[]{:S(2)}) collective-permute-start(f32[32,512]{1,0:T(8,128)S(1)} %add.128), channel_id=1, source_target_pairs={{0,64},{16,80},{32,96},{48,112},{64,0},{80,16},{96,32},{112,48},{1... | collective-permute-start | bytes 196616 | tf_op jit(solution)/shard_map/ppermute | solution.py:16
  182.6 5.9 %collective-permute-start.27 = (f32[32,512]{1,0:T(8,128)S(1)}, f32[32,512]{1,0:T(8,128)S(1)}, u32[]{:S(2)}, u32[]{:S(2)}) collective-permute-start(f32[32,512]{1,0:T(8,128)S(1)} %add.128), channel_id=1, source_target_pairs={{0,96},{16,112},{32,0},{48,16},{64,32},{80,48},{96,64},{112,80},{1... | collective-permute-start | bytes 196616 | tf_op jit(solution)/shard_map/ppermute | solution.py:16
  184.1 5.5 %collective-permute-start.26 = (f32[32,512]{1,0:T(8,128)S(1)}, f32[32,512]{1,0:T(8,128)S(1)}, u32[]{:S(2)}, u32[]{:S(2)}) collective-permute-start(f32[32,512]{1,0:T(8,128)S(1)} %add.128), channel_id=1, source_target_pairs={{0,32},{16,48},{32,64},{48,80},{64,96},{80,112},{96,0},{112,16},{1... | collective-permute-start | bytes 196616 | tf_op jit(solution)/shard_map/ppermute | solution.py:16
  (9 other events, 48.7 us)

commit v9 on v8

--- a/solution.py
+++ b/solution.py
@@ -23,6 +23,10 @@
 def z_exchange(v):
     groups = [[4 * y + z for z in range(4)] for y in range(4)]
     return lax.all_to_all(v, "col", 0, 0, axis_index_groups=groups, tiled=True)
+
+
+def y_shift(v, step):
+    return lax.ppermute(v, "col", [(c, (c // 4 + step) % 4 * 4 + c % 4) for c in range(16)])
 
 
 def y_gather(v):
@@ -75,30 +79,29 @@
 
 
 def split_tiles_kernel(src, dst):
-    dst[:, 0] = pltpu.einshape("tbu->btu", src[0])
+    tiles = pltpu.einshape("tbu->btu", src[0])
+    for b in range(tiles.shape[0]):
+        dst[b // 3, :, 256 * (b % 3) : 256 * (b % 3 + 1)] = tiles[b]
 
 
 def split_tiles(left):
     rounds, tile, count, width = left.shape
-    rows = 256
-    out = pl.pallas_call(
+    return pl.pallas_call(
         split_tiles_kernel,
-        grid=(rounds, tile // rows),
-        in_specs=[pl.BlockSpec((1, rows, count, width), lambda a, t: (a, t, 0, 0))],
-        out_specs=pl.BlockSpec((count, 1, rows, width), lambda a, t: (0, a, t, 0)),
-        out_shape=pltpu.HBM((count, rounds, tile, width), BF),
+        grid=(rounds,),
+        in_specs=[pl.BlockSpec((1, tile, count, width), lambda a: (a, 0, 0, 0))],
+        out_specs=pl.BlockSpec((count // 3, tile, 3 * width), lambda a: (0, a, 0)),
+        out_shape=pltpu.HBM((count // 3, rounds * tile, 3 * width), BF),
         cost_estimate=cost(0, 2 * left.size * 2),
         compiler_params=ROOMY,
     )(left)
-    return out.reshape(count, rounds * tile, width)
 
 
 def accumulate(acc, left, held, step):
+    values = held[...].reshape(768, 512)
     for base in (0, 512):
         here = slice(base, base + 512)
-        total = jnp.dot(left[0, here, :], held[0], preferred_element_type=F32)
-        for t in range(1, 3):
-            total += jnp.dot(left[t, here, :], held[t], preferred_element_type=F32)
+        total = jnp.dot(left[here, :], values, preferred_element_type=F32)
 
         @pl.when(step == 0)
         def _():
@@ -165,12 +168,12 @@
 def products(order, left, pieces, before=None, token=None, last=False):
     blocks = len(pieces) // 2
     _, rows, width = left.shape
-    left_spec = pl.BlockSpec((3, rows, width), lambda i, order: (order[i], 0, 0))
+    left_spec = pl.BlockSpec((None, rows, width), lambda i, order: (order[i], 0, 0))
     left = pltpu.with_memory_space_constraint(left, pltpu.HBM)
     arrays = [array for array, _ in pieces]
     scratch = [VMEM((3, 256, 512), BF)]
     flops = blocks * 2 * rows * 768 * 512
-    moved = blocks * 3 * 2 * (rows * 256 + 256 * 512) + rows * 512 * 4
+    moved = blocks * 2 * 768 * (rows + 512) + rows * 512 * 4
     starts = [] if before is None else [before, token]
     out = jax.ShapeDtypeStruct((rows, 512), F32)
     kernel = first_products_kernel if before is None else next_products_kernel
@@ -196,21 +199,40 @@
 RELATIVE = (0, -1, 1, 2)
 
 
-def stage_kernel(order, own, one, two, three, weights, out, held):
-    for i, source in enumerate((own, one, two, three)):
+def place_values(order, sources, held):
+    for i, source in enumerate(sources):
         for k in range(2):
             line = order[2 * i + k]
             held[line] = source[k, :64, :]
             held[8 + line] = source[k, 64:, :]
-    values = held[...].reshape(1024, 128).astype(F32)
-    values = jnp.transpose(values).astype(BF)
-    factor = weights[...].reshape(1024, 512)
-    total = jnp.dot(values, factor, preferred_element_type=F32)
+
+
+def put_quarters(total, out):
     total = jnp.transpose(total).astype(BF)
     for q in range(4):
         for a in range(2):
             top = 256 * a + 64 * q
             out[q, 64 * a : 64 * (a + 1), :] = total[top : top + 64, :]
+
+
+def stage_kernel(order, own, one, two, three, weights, out, held):
+    place_values(order, (own, one, two, three), held)
+    values = held[...].reshape(1024, 128).astype(F32)
+    values = jnp.transpose(values).astype(BF)
+    factor = weights[...].reshape(1024, 512)
+    total = jnp.dot(values, factor, preferred_element_type=F32)
+    put_quarters(total, out)
+
+
+def late_stage_kernel(order, ys, own, one, two, three, *refs):
+    *weights, out, held = refs
+    place_values(order, (own, one, two, three), held)
+    total = jnp.zeros((128, 512), F32)
+    for j, ref in enumerate(weights):
+        values = held[pl.ds(4 * ys[j], 4)].reshape(256, 128).astype(F32)
+        values = jnp.transpose(values).astype(BF)
+        total += jnp.dot(values, ref[...].reshape(256, 512), preferred_element_type=F32)
+    put_quarters(total, out)
 
 
 def over_cores(values):
@@ -244,6 +266,21 @@
     return partial
 
 
+def late_stage(order, ys, values, panels):
+    moved = over_chips(over_cores(values))
+    out = jax.ShapeDtypeStruct((4, 128, 128), BF)
+    return pl.pallas_call(
+        late_stage_kernel,
+        grid=(1,),
+        in_specs=[SCALARS, SCALARS, *map(whole, moved), *map(whole, panels)],
+        out_specs=whole(out),
+        scratch_shapes=[VMEM((16, 64, 128), BF)],
+        out_shape=out,
+        cost_estimate=cost(2 * 128 * 1024 * 512, 2 * 1024 * 512),
+        compiler_params=ROOMY,
+    )(order, ys, *moved, *panels)
+
+
 def over_z(partial):
     return z_exchange(partial).astype(F32).sum(axis=0)
 
@@ -273,6 +310,7 @@
     x, k = row // 2, row % 2
     y, z = col // 4, col % 4
     order = jnp.stack([(x + d) % 4 * 2 + (k + e) % 2 for d in RELATIVE for e in range(2)])
+    ys = jnp.stack([(y + d) % 4 for d in RELATIVE]).astype(jnp.int32)
     order = order.astype(jnp.int32)
 
     low, high, lines = prepare(prev_solution, inverses, coupling)
@@ -287,7 +325,7 @@
         )
     )
     sibling = in_hbm(sibling)
-    panels = in_hbm(y_gather(lines))
+    panels, late = in_hbm(y_gather(lines[:, :2])), lines[:, 2]
     far_low, far_high = x_shift(before_low, 1), x_shift(after_high, -1)
     pieces = [(prev_solution, 0), (prev_solution, 1), (sibling, 0), (sibling, 1)]
     started = products(order[:2], left, pieces)
@@ -304,19 +342,23 @@
     pieces = [(v, 0) for v in far] + [(other_core(v), 0) for v in far]
     first, second = products(order[6:], left, pieces, started, token, last=True)
 
-    first, second, panels = lax.optimization_barrier((first, second, panels))
+    first, second, panels, late = lax.optimization_barrier((first, second, panels, late))
+    late_panels = [y_shift(late, -d) if d else late for d in RELATIVE]
     panels = in_hbm(panels)
     known = lax.dynamic_slice(cross, (0, 64 * z, 128 * y), (4, 64, 128))
     known = known.astype(F32).reshape(2, 128, 128)
     first_rhs = (known[0] - over_sites(first)).astype(BF)
-    first_rhs, second = lax.optimization_barrier((first_rhs, second))
+    first_rhs, second, *late_panels = lax.optimization_barrier(
+        (first_rhs, second, *late_panels)
+    )
     rest = known[1] - over_sites(second)
-    solved_first = over_z(stage(order, first_rhs, panels, 0)).astype(BF)
+    partial = stage(order, first_rhs, panels, 0)
+    solved_first = over_z(partial).astype(BF)
     every_first = all_sites(solved_first)
     partial = stage(order, solved_first, panels, 1)
     partial, rest = lax.optimization_barrier((partial, rest))
     second_rhs = (rest - over_z(partial)).astype(BF)
-    partial = stage(order, second_rhs, panels, 2)
+    partial = late_stage(order, ys, second_rhs, late_panels)
     partial, every_first = lax.optimization_barrier((partial, every_first))
     solved_second = over_z(partial).astype(BF)
     every_second = all_sites(solved_second)

time: 191 us -> 197 us (1.031)
  starting transfers between devices: 54.2 us -> 61.2 us
  waiting for transfers between devices: 58 us -> 54.5 us
    all_to_all x1, waiting for transfers between devices: 8.77 us -> 0.01 us  [y_gather(): lax.all_to_all(sent, 'col', 0, 0, axis_index_groups=groups, tiled=True)]
    ppermute x0 -> x3, waiting for transfers between devices: none -> 8.27 us  [y_shift(): lax.ppermute(v, 'col', [(c, (c // 4 + step) % 4 * 4 + c % 4) for c in ran...]
    ppermute x0 -> x3, starting transfers between devices: none -> 5.49 us  [y_shift(): lax.ppermute(v, 'col', [(c, (c // 4 + step) % 4 * 4 + c % 4) for c in ran...]
    all_to_all x2, waiting for transfers between devices: 9.18 us -> 6.14 us  [over_sites(): lax.all_to_all(partial, 'col', 0, 0, tiled=True).astype(F32).sum(axis=0)]
    all_to_all x2, starting transfers between devices: 8.66 us -> 11.6 us  [over_sites(): lax.all_to_all(partial, 'col', 0, 0, tiled=True).astype(F32).sum(axis=0)]
    pallas_call x3 -> x2, Pallas kernels: 5.04 us -> 3.36 us  [stage(): pl.pallas_call(stage_kernel, grid=(1,), in_specs=[SCALARS, *map(whole, mo...]
    pallas_call x1 -> x2, Pallas kernels: 10.4 us -> 11.4 us  [the longest x1 10.4 us: split_tiles(): pl.pallas_call(split_tiles_kernel, grid=(rounds,), in_specs=[pl.BlockSpec...]
  transfers between devices with their start and end apart: 35 -> 38, of which waited for: 19 -> 20; matrix products, arithmetic and copies ran while one was open for 2% -> 2% of each run, Pallas kernels for 18% -> 18%
where the time goes in v9:
time: 197 us; the launch traced here: 196 us
  starting transfers between devices  61.2 us (31%)
  waiting for transfers between devices  54.5 us (28%)
  Pallas kernels  37.1 us (19%)
  blocking collectives  30.5 us (15%)
  local copies, waits for them, and re-layouts  7.59 us (4%)
  other arithmetic  3.17 us (2%)
    all_to_all x3, blocking collectives, z_exchange(): return lax.all_to_all(v, 'col', 0, 0, axis_index_groups=groups, tiled=True)  30.5 us
    ppermute x18, starting transfers between devices, x_shift(): return lax.ppermute(v, 'row', [(r, (r + 2 * step) % 8) for r in range(8)])  22.2 us
    pallas_call x3, Pallas kernels, products(): pl.pallas_call(kernel, grid_spec=pltpu.PrefetchScalarGridSpec(num_scalar_...  19.7 us
    ppermute x18, waiting for transfers between devices, x_shift(): return lax.ppermute(v, 'row', [(r, (r + 2 * step) % 8) for r in range(8)])  19.4 us
    all_to_all x2, waiting for transfers between devices, all_sites(): lax.all_to_all(sent, 'col', 0, 0, tiled=True).reshape(4, 4, 2, 64, 128)  15.1 us
    all_to_all x2, starting transfers between devices, over_sites(): lax.all_to_all(partial, 'col', 0, 0, tiled=True).astype(F32).sum(axis=0)  11.6 us
    pallas_call x1, Pallas kernels, split_tiles(): pl.pallas_call(split_tiles_kernel, grid=(rounds,), in_specs=[pl.BlockSpec...  10.4 us
    all_to_all x2, starting transfers between devices, all_sites(): lax.all_to_all(sent, 'col', 0, 0, tiled=True).reshape(4, 4, 2, 64, 128)  9.96 us
  transfers between devices with their start and end apart: 38, of which 20 were waited for; matrix products, arithmetic and copies ran while one was open for 2% of the time, Pallas kernels for 18%

profile of v9, /device:TPU:0, one launch (start us, length us, event | category | flops | bytes accessed | tf_op | source)
XLA Modules:
  0.0 195.6 jit_solution(14124366353403202810)
XLA Ops:
  0.7 2.5 %shard_map.77 = (bf16[3,128,512]{2,1,0:T(8,128)(2,1)S(1)}, bf16[3,128,512]{2,1,0:T(8,128)(2,1)S(1)}, bf16[4,3,64,512]{3,2,1,0:T(8,128)(2,1)}) custom-call(bf16[3,256,512]{2,1,0:T(8,128)(2,1)} %refs_1_.1, bf16[2,512,256]{2,1,0:T(8,128)(2,1)} %bitcast.45, bf16[2,512,256]{2,1,0:T(8,128)(2,1)} %bitcast.46, bf16[512,256]{1,0:T(8,128)(2,1)} %bitcast.48), custom_call_target="tpu_custom_call" | custom-call | tf_op jit(solution)/shard_map/pallas_call | solution.py:66
  3.3 5.4 %all-to-all-start = ((bf16[4,3,64,512]{3,2,1,0:T(8,128)(2,1)}), bf16[4,3,64,512]{3,2,1,0:T(8,128)(2,1)S(1)}, u32[]{:S(2)}, u32[]{:S(2)}) async-start(bf16[4,3,64,512]{3,2,1,0:T(8,128)(2,1)} %get-tuple-element.33), calls=%async_computation | async-start | bytes 1572864 | tf_op jit(solution)/shard_map/all_to_all | solution.py:25
  12.2 3.0 %collective-permute-start.3 = (bf16[3,128,512]{2,1,0:T(8,128)(2,1)S(1)}, bf16[3,128,512]{2,1,0:T(8,128)(2,1)}, u32[]{:S(2)}, u32[]{:S(2)}) collective-permute-start(bf16[3,128,512]{2,1,0:T(8,128)(2,1)S(1)} %get-tuple-element.31), channel_id=1, source_target_pairs={{0,96},{16,112},{32,0},{48,16},{64,32},{80,48},{96,64},{112,80},{1... | collective-permute-start | bytes 1179656 | tf_op jit(solution)/shard_map/ppermute | solution.py:16
  15.1 10.4 %shard_map.78.left = bf16[8,1024,768]{2,1,0:T(8,128)(2,1)} custom-call(bf16[4,256,24,256]{3,2,1,0:T(8,128)(2,1)} %src.1), custom_call_target="tpu_custom_call" | custom-call | bytes 25165824 | tf_op jit(solution)/shard_map/pallas_call | solution.py:89
  25.6 4.0 %collective-permute-done.2.refs_1_ = bf16[3,128,512]{2,1,0:T(8,128)(2,1)} collective-permute-done((bf16[3,128,512]{2,1,0:T(8,128)(2,1)S(1)}, bf16[3,128,512]{2,1,0:T(8,128)(2,1)}, u32[]{:S(2)}, u32[]{:S(2)}) %collective-permute-start.2) | collective-permute-done | bytes 393248 | tf_op jit(solution)/shard_map/ppermute | solution.py:16
  31.5 4.6 %all-to-all-start.1 = ((bf16[4,4,2,64,512]{4,3,2,1,0:T(8,128)(2,1)}), bf16[4,4,2,64,512]{4,3,2,1,0:T(8,128)(2,1)}, u32[]{:S(2)}, u32[]{:S(2)}) async-start(bf16[4,4,2,64,512]{4,3,2,1,0:T(8,128)(2,1)} %broadcast_in_dim.6), calls=%async_computation.1 | async-start | bytes 4194304 | tf_op jit(solution)/shard_map/all_to_all | solution.py:35
  38.8 2.1 %collective-permute-start.10 = (bf16[3,128,512]{2,1,0:T(8,128)(2,1)}, bf16[3,128,512]{2,1,0:T(8,128)(2,1)S(1)}, u32[]{:S(2)}, u32[]{:S(2)}) collective-permute-start(bf16[3,128,512]{2,1,0:T(8,128)(2,1)} %collective-permute-done.1.refs_5_), channel_id=1, source_target_pairs={{0,96},{16,112},{32,0},{48,16},{64,32},{80,48},{96,64},{112,80},{1... | collective-permute-start | bytes 1179656 | tf_op jit(solution)/shard_map/ppermute | solution.py:16
  41.0 4.9 %shard_map.79.before = f32[1024,512]{1,0:T(8,128)S(1)} custom-call(s32[2]{0:T(128)S(1)} %pad_add_fusion.3.order, bf16[8,1024,768]{2,1,0:T(8,128)(2,1)} %shard_map.78.left, bf16[3,256,512]{2,1,0:T(8,128)(2,1)S(1)} %copy-done, bf16[3,256,512]{2,1,0:T(8,128)(2,1)S(1)} %copy-done, bf16[3,256,512]{2,1,0:T(8,128)(2,1)} %copy-done.1, bf16[3,256,512]{2,1,0:T(8,128)(2,1)} %copy-done.1), custom_call_target="tpu_custom_call" | custom-call | flops 1610612736 | bytes 6815744 | tf_op jit(solution)/shard_map/pallas_call | solution.py:184
  47.4 8.7 %shard_map.80.before = f32[1024,512]{1,0:T(8,128)S(1)} custom-call(s32[4]{0:T(128)S(1)} %pad_add_fusion.2.order, bf16[8,1024,768]{2,1,0:T(8,128)(2,1)} %shard_map.78.left, f32[1024,512]{1,0:T(8,128)S(1)} %shard_map.79.before, f32[8,128]{1,0:T(8,128)S(1)} %slice.33.token, bf16[3,128,512]{2,1,0:T(8,128)(2,1)} %copy-done.3, ...), custom_call_target="tpu_custom_call" | custom-call | flops 3221225472 | bytes 11534336 | tf_op jit(solution)/shard_map/pallas_call | solution.py:184
  58.7 6.1 %shard_map.81 = (bf16[16,128,128]{2,1,0:T(8,128)(2,1)}, bf16[16,128,128]{2,1,0:T(8,128)(2,1)}) custom-call(s32[2]{0:T(128)S(1)} %pad_add_fusion.1.order, bf16[8,1024,768]{2,1,0:T(8,128)(2,1)} %shard_map.78.left, f32[1024,512]{1,0:T(8,128)S(1)} %shard_map.80.before, f32[8,128]{1,0:T(8,128)S(1)} %slice.34.token, ...), custom_call_target="tpu_custom_call" | custom-call | flops 1610612736 | bytes 6815744 | tf_op jit(solution)/shard_map/pallas_call | solution.py:184
  64.8 8.0 %all-to-all-start.2 = ((bf16[16,128,128]{2,1,0:T(8,128)(2,1)}), bf16[16,128,128]{2,1,0:T(8,128)(2,1)S(1)}, u32[]{:S(2)}, u32[]{:S(2)}) async-start(bf16[16,128,128]{2,1,0:T(8,128)(2,1)} %get-tuple-element.46), calls=%async_computation.2 | async-start | bytes 1048576 | tf_op jit(solution)/shard_map/all_to_all | solution.py:289
  73.7 2.0 collective-permute-start.13
  77.0 2.2 %collective-permute-start.15 = (bf16[4,64,512]{2,1,0:T(8,128)(2,1)S(1)}, bf16[4,64,512]{2,1,0:T(8,128)(2,1)S(1)}, u32[]{:S(2)}, u32[]{:S(2)}) collective-permute-start(bf16[4,64,512]{2,1,0:T(8,128)(2,1)S(1)} %slice_bitcast_fusion.refs_0_), channel_id=1, source_target_pairs={{0,8},{1,9},{2,10},{3,11},{4,12},{5,13},{6,14},{7,15},{8,0},{9,1},... | collective-permute-start | bytes 786440 | tf_op jit(solution)/shard_map/ppermute | solution.py:29
  79.2 6.1 %all-to-all-done.2 = bf16[16,128,128]{2,1,0:T(8,128)(2,1)S(1)} async-done(((bf16[16,128,128]{2,1,0:T(8,128)(2,1)}), bf16[16,128,128]{2,1,0:T(8,128)(2,1)S(1)}, u32[]{:S(2)}, u32[]{:S(2)}) %all-to-all-start.2) | async-done | bytes 524320 | tf_op jit(solution)/shard_map/all_to_all | solution.py:289
  85.4 3.2 %collective-permute-done.13.refs_1_ = bf16[4,64,512]{2,1,0:T(8,128)(2,1)S(1)} collective-permute-done((bf16[4,64,512]{2,1,0:T(8,128)(2,1)S(1)}, bf16[4,64,512]{2,1,0:T(8,128)(2,1)S(1)}, u32[]{:S(2)}, u32[]{:S(2)}) %collective-permute-start.13) | collective-permute-done | bytes 262176 | tf_op jit(solution)/shard_map/ppermute | solution.py:29
  88.6 5.1 %collective-permute-done.15.refs_3_ = bf16[4,64,512]{2,1,0:T(8,128)(2,1)S(1)} collective-permute-done((bf16[4,64,512]{2,1,0:T(8,128)(2,1)S(1)}, bf16[4,64,512]{2,1,0:T(8,128)(2,1)S(1)}, u32[]{:S(2)}, u32[]{:S(2)}) %collective-permute-start.15) | collective-permute-done | bytes 262176 | tf_op jit(solution)/shard_map/ppermute | solution.py:29
  95.0 3.2 %collective-permute-start.18 = (bf16[2,128,128]{2,1,0:T(8,128)(2,1)S(1)}, bf16[2,128,128]{2,1,0:T(8,128)(2,1)S(1)}, u32[]{:S(2)}, u32[]{:S(2)}) collective-permute-start(bf16[2,128,128]{2,1,0:T(8,128)(2,1)S(1)} %pad_maximum_fusion.1.own), channel_id=1, source_target_pairs={{0,96},{16,112},{32,0},{48,16},{64,32},{80,48},{96,64},{112,80},{1... | collective-permute-start | bytes 196616 | tf_op jit(solution)/shard_map/ppermute | solution.py:16
  98.3 2.2 %collective-permute-done.17.one = bf16[2,128,128]{2,1,0:T(8,128)(2,1)S(1)} collective-permute-done((bf16[2,128,128]{2,1,0:T(8,128)(2,1)S(1)}, bf16[2,128,128]{2,1,0:T(8,128)(2,1)S(1)}, u32[]{:S(2)}, u32[]{:S(2)}) %collective-permute-start.17) | collective-permute-done | bytes 65568 | tf_op jit(solution)/shard_map/ppermute | solution.py:16
  101.0 3.0 %collective-permute-done.19.three = bf16[2,128,128]{2,1,0:T(8,128)(2,1)S(1)} collective-permute-done((bf16[2,128,128]{2,1,0:T(8,128)(2,1)S(1)}, bf16[2,128,128]{2,1,0:T(8,128)(2,1)S(1)}, u32[]{:S(2)}, u32[]{:S(2)}) %collective-permute-start.19) | collective-permute-done | bytes 65568 | tf_op jit(solution)/shard_map/ppermute | solution.py:16
  105.7 10.0 %all_to_all.45 = bf16[4,128,128]{2,1,0:T(8,128)(2,1)S(1)} all-to-all(bf16[4,128,128]{2,1,0:T(8,128)(2,1)S(1)} %shard_map.82), channel_id=1, replica_groups={{0,1,2,3},{4,5,6,7},{8,9,10,11},{12,13,14,15},{16,17,18,19},{20,21,22,2..., dimensions={0} | all-to-all | bytes 262144 | tf_op jit(solution)/shard_map/all_to_all | solution.py:25
  115.7 3.6 %all-to-all-start.4 = ((bf16[16,128,128]{2,1,0:T(8,128)(2,1)}), bf16[16,128,128]{2,1,0:T(8,128)(2,1)S(1)}, u32[]{:S(2)}, u32[]{:S(2)}) async-start(bf16[16,128,128]{2,1,0:T(8,128)(2,1)} %get-tuple-element.51), calls=%async_computation.4 | async-start | bytes 1048576 | tf_op jit(solution)/shard_map/all_to_all | solution.py:289
  120.7 3.2 %collective-permute-start.22 = (bf16[2,128,128]{2,1,0:T(8,128)(2,1)S(1)}, bf16[2,128,128]{2,1,0:T(8,128)(2,1)S(1)}, u32[]{:S(2)}, u32[]{:S(2)}) collective-permute-start(bf16[2,128,128]{2,1,0:T(8,128)(2,1)S(1)} %pad_maximum_fusion.2.own), channel_id=1, source_target_pairs={{0,96},{16,112},{32,0},{48,16},{64,32},{80,48},{96,64},{112,80},{1... | collective-permute-start | bytes 196616 | tf_op jit(solution)/shard_map/ppermute | solution.py:16
  123.9 2.2 %collective-permute-done.21.one = bf16[2,128,128]{2,1,0:T(8,128)(2,1)S(1)} collective-permute-done((bf16[2,128,128]{2,1,0:T(8,128)(2,1)S(1)}, bf16[2,128,128]{2,1,0:T(8,128)(2,1)S(1)}, u32[]{:S(2)}, u32[]{:S(2)}) %collective-permute-start.21) | collective-permute-done | bytes 65568 | tf_op jit(solution)/shard_map/ppermute | solution.py:16
  126.7 3.0 %collective-permute-done.23.three = bf16[2,128,128]{2,1,0:T(8,128)(2,1)S(1)} collective-permute-done((bf16[2,128,128]{2,1,0:T(8,128)(2,1)S(1)}, bf16[2,128,128]{2,1,0:T(8,128)(2,1)S(1)}, u32[]{:S(2)}, u32[]{:S(2)}) %collective-permute-start.23) | collective-permute-done | bytes 65568 | tf_op jit(solution)/shard_map/ppermute | solution.py:16
  131.5 10.4 %all_to_all.46 = bf16[4,128,128]{2,1,0:T(8,128)(2,1)S(1)} all-to-all(bf16[4,128,128]{2,1,0:T(8,128)(2,1)S(1)} %shard_map.83), channel_id=1, replica_groups={{0,1,2,3},{4,5,6,7},{8,9,10,11},{12,13,14,15},{16,17,18,19},{20,21,22,2..., dimensions={0} | all-to-all | bytes 262144 | tf_op jit(solution)/shard_map/all_to_all | solution.py:25
  142.7 5.0 %all-to-all-start.6 = ((bf16[16,128,128]{2,1,0:T(8,128)(2,1)}), bf16[16,128,128]{2,1,0:T(8,128)(2,1)S(1)}, u32[]{:S(2)}, u32[]{:S(2)}) async-start(bf16[16,128,128]{2,1,0:T(8,128)(2,1)} %broadcast_in_dim.7), calls=%async_computation.6 | async-start | bytes 1048576 | tf_op jit(solution)/shard_map/all_to_all | solution.py:294
  149.2 3.2 %collective-permute-start.26 = (bf16[2,128,128]{2,1,0:T(8,128)(2,1)S(1)}, bf16[2,128,128]{2,1,0:T(8,128)(2,1)S(1)}, u32[]{:S(2)}, u32[]{:S(2)}) collective-permute-start(bf16[2,128,128]{2,1,0:T(8,128)(2,1)S(1)} %pad_maximum_fusion.3.own), channel_id=1, source_target_pairs={{0,96},{16,112},{32,0},{48,16},{64,32},{80,48},{96,64},{112,80},{1... | collective-permute-start | bytes 196616 | tf_op jit(solution)/shard_map/ppermute | solution.py:16
  152.5 5.4 %all-to-all-done.6 = bf16[16,128,128]{2,1,0:T(8,128)(2,1)S(1)} async-done(((bf16[16,128,128]{2,1,0:T(8,128)(2,1)}), bf16[16,128,128]{2,1,0:T(8,128)(2,1)S(1)}, u32[]{:S(2)}, u32[]{:S(2)}) %all-to-all-start.6) | async-done | bytes 524320 | tf_op jit(solution)/shard_map/all_to_all | solution.py:294
  159.5 10.1 %all_to_all.47 = bf16[4,128,128]{2,1,0:T(8,128)(2,1)S(1)} all-to-all(bf16[4,128,128]{2,1,0:T(8,128)(2,1)S(1)} %shard_map.84), channel_id=1, replica_groups={{0,1,2,3},{4,5,6,7},{8,9,10,11},{12,13,14,15},{16,17,18,19},{20,21,22,2..., dimensions={0} | all-to-all | bytes 262144 | tf_op jit(solution)/shard_map/all_to_all | solution.py:25
  170.6 5.0 %all-to-all-start.8 = ((bf16[16,128,128]{2,1,0:T(8,128)(2,1)}), bf16[16,128,128]{2,1,0:T(8,128)(2,1)S(1)}, u32[]{:S(2)}, u32[]{:S(2)}) async-start(bf16[16,128,128]{2,1,0:T(8,128)(2,1)} %broadcast_in_dim.8), calls=%async_computation.8 | async-start | bytes 1048576 | tf_op jit(solution)/shard_map/all_to_all | solution.py:294
  175.9 9.7 %all-to-all-done.8 = bf16[16,128,128]{2,1,0:T(8,128)(2,1)S(1)} async-done(((bf16[16,128,128]{2,1,0:T(8,128)(2,1)}), bf16[16,128,128]{2,1,0:T(8,128)(2,1)S(1)}, u32[]{:S(2)}, u32[]{:S(2)}) %all-to-all-start.8) | async-done | bytes 524320 | tf_op jit(solution)/shard_map/all_to_all | solution.py:294
  191.1 2.7 %collective-permute-done.31 = f32[32,512]{1,0:T(8,128)S(1)} collective-permute-done((f32[32,512]{1,0:T(8,128)S(1)}, f32[32,512]{1,0:T(8,128)S(1)}, u32[]{:S(2)}, u32[]{:S(2)}) %collective-permute-start.31) | collective-permute-done | bytes 65568 | tf_op jit(solution)/shard_map/ppermute | solution.py:16
  (104 shorter events, 34.3 us)
Async XLA Ops:
  0.6 29.0 %collective-permute-start.4 = (bf16[3,256,512]{2,1,0:T(8,128)(2,1)}, bf16[3,256,512]{2,1,0:T(8,128)(2,1)S(1)}, u32[]{:S(2)}, u32[]{:S(2)}) collective-permute-start(bf16[3,256,512]{2,1,0:T(8,128)(2,1)} %refs_1_.1), channel_id=1, source_target_pairs={{0,16},{16,0},{32,48},{48,32},{64,80},{80,64},{96,112},{112,96},{1... | collective-permute-start | bytes 2359304 | tf_op jit(solution)/shard_map/ppermute | solution.py:20
  3.3 26.4 %all-to-all-start = ((bf16[4,3,64,512]{3,2,1,0:T(8,128)(2,1)}), bf16[4,3,64,512]{3,2,1,0:T(8,128)(2,1)S(1)}, u32[]{:S(2)}, u32[]{:S(2)}) async-start(bf16[4,3,64,512]{3,2,1,0:T(8,128)(2,1)} %get-tuple-element.33), calls=%async_computation | async-start | bytes 1572864 | tf_op jit(solution)/shard_map/all_to_all | solution.py:25
  8.7 16.9 %collective-permute-start = (bf16[3,128,512]{2,1,0:T(8,128)(2,1)S(1)}, bf16[3,128,512]{2,1,0:T(8,128)(2,1)S(1)}, u32[]{:S(2)}, u32[]{:S(2)}) collective-permute-start(bf16[3,128,512]{2,1,0:T(8,128)(2,1)S(1)} %get-tuple-element.31), channel_id=1, source_target_pairs={{0,32},{16,48},{32,64},{48,80},{64,96},{80,112},{96,0},{112,16},{1... | collective-permute-start | bytes 1179656 | tf_op jit(solution)/shard_map/ppermute | solution.py:16
  10.2 15.4 %collective-permute-start.1 = (bf16[3,128,512]{2,1,0:T(8,128)(2,1)S(1)}, bf16[3,128,512]{2,1,0:T(8,128)(2,1)}, u32[]{:S(2)}, u32[]{:S(2)}) collective-permute-start(bf16[3,128,512]{2,1,0:T(8,128)(2,1)S(1)} %get-tuple-element.32), channel_id=1, source_target_pairs={{0,96},{16,112},{32,0},{48,16},{64,32},{80,48},{96,64},{112,80},{1... | collective-permute-start | bytes 1179656 | tf_op jit(solution)/shard_map/ppermute | solution.py:16
  11.9 17.7 %collective-permute-start.2 = (bf16[3,128,512]{2,1,0:T(8,128)(2,1)S(1)}, bf16[3,128,512]{2,1,0:T(8,128)(2,1)}, u32[]{:S(2)}, u32[]{:S(2)}) collective-permute-start(bf16[3,128,512]{2,1,0:T(8,128)(2,1)S(1)} %get-tuple-element.32), channel_id=1, source_target_pairs={{0,32},{16,48},{32,64},{48,80},{64,96},{80,112},{96,0},{112,16},{1... | collective-permute-start | bytes 1179656 | tf_op jit(solution)/shard_map/ppermute | solution.py:16
  12.2 17.5 %collective-permute-start.3 = (bf16[3,128,512]{2,1,0:T(8,128)(2,1)S(1)}, bf16[3,128,512]{2,1,0:T(8,128)(2,1)}, u32[]{:S(2)}, u32[]{:S(2)}) collective-permute-start(bf16[3,128,512]{2,1,0:T(8,128)(2,1)S(1)} %get-tuple-element.31), channel_id=1, source_target_pairs={{0,96},{16,112},{32,0},{48,16},{64,32},{80,48},{96,64},{112,80},{1... | collective-permute-start | bytes 1179656 | tf_op jit(solution)/shard_map/ppermute | solution.py:16
  31.5 33.3 %all-to-all-start.1 = ((bf16[4,4,2,64,512]{4,3,2,1,0:T(8,128)(2,1)}), bf16[4,4,2,64,512]{4,3,2,1,0:T(8,128)(2,1)}, u32[]{:S(2)}, u32[]{:S(2)}) async-start(bf16[4,4,2,64,512]{4,3,2,1,0:T(8,128)(2,1)} %broadcast_in_dim.6), calls=%async_computation.1 | async-start | bytes 4194304 | tf_op jit(solution)/shard_map/all_to_all | solution.py:35
  36.1 2.8 %collective-permute-start.5 = (bf16[3,128,512]{2,1,0:T(8,128)(2,1)S(1)}, bf16[3,128,512]{2,1,0:T(8,128)(2,1)}, u32[]{:S(2)}, u32[]{:S(2)}) collective-permute-start(bf16[3,128,512]{2,1,0:T(8,128)(2,1)S(1)} %collective-permute-done.refs_0_), channel_id=1, source_target_pairs={{0,16},{16,0},{32,48},{48,32},{64,80},{80,64},{96,112},{112,96},{1... | collective-permute-start | bytes 1179656 | tf_op jit(solution)/shard_map/ppermute | solution.py:20
  36.2 9.8 %collective-permute-start.6 = (bf16[3,128,512]{2,1,0:T(8,128)(2,1)}, bf16[3,128,512]{2,1,0:T(8,128)(2,1)S(1)}, u32[]{:S(2)}, u32[]{:S(2)}) collective-permute-start(bf16[3,128,512]{2,1,0:T(8,128)(2,1)} %collective-permute-done.2.refs_1_), channel_id=1, source_target_pairs={{0,16},{16,0},{32,48},{48,32},{64,80},{80,64},{96,112},{112,96},{1... | collective-permute-start | bytes 1179656 | tf_op jit(solution)/shard_map/ppermute | solution.py:20
  36.7 9.3 %collective-permute-start.7 = (bf16[3,128,512]{2,1,0:T(8,128)(2,1)}, bf16[3,128,512]{2,1,0:T(8,128)(2,1)S(1)}, u32[]{:S(2)}, u32[]{:S(2)}) collective-permute-start(bf16[3,128,512]{2,1,0:T(8,128)(2,1)} %collective-permute-done.3.refs_4_), channel_id=1, source_target_pairs={{0,16},{16,0},{32,48},{48,32},{64,80},{80,64},{96,112},{112,96},{1... | collective-permute-start | bytes 1179656 | tf_op jit(solution)/shard_map/ppermute | solution.py:20
  36.8 10.7 %collective-permute-start.8 = (bf16[3,128,512]{2,1,0:T(8,128)(2,1)}, bf16[3,128,512]{2,1,0:T(8,128)(2,1)}, u32[]{:S(2)}, u32[]{:S(2)}) collective-permute-start(bf16[3,128,512]{2,1,0:T(8,128)(2,1)} %collective-permute-done.1.refs_5_), channel_id=1, source_target_pairs={{0,16},{16,0},{32,48},{48,32},{64,80},{80,64},{96,112},{112,96},{1... | collective-permute-start | bytes 1179656 | tf_op jit(solution)/shard_map/ppermute | solution.py:20
  37.3 18.8 %collective-permute-start.9 = (bf16[3,128,512]{2,1,0:T(8,128)(2,1)S(1)}, bf16[3,128,512]{2,1,0:T(8,128)(2,1)S(1)}, u32[]{:S(2)}, u32[]{:S(2)}) collective-permute-start(bf16[3,128,512]{2,1,0:T(8,128)(2,1)S(1)} %collective-permute-done.refs_0_), channel_id=1, source_target_pairs={{0,32},{16,48},{32,64},{48,80},{64,96},{80,112},{96,0},{112,16},{1... | collective-permute-start | bytes 1179656 | tf_op jit(solution)/shard_map/ppermute | solution.py:16
  38.8 17.4 %collective-permute-start.10 = (bf16[3,128,512]{2,1,0:T(8,128)(2,1)}, bf16[3,128,512]{2,1,0:T(8,128)(2,1)S(1)}, u32[]{:S(2)}, u32[]{:S(2)}) collective-permute-start(bf16[3,128,512]{2,1,0:T(8,128)(2,1)} %collective-permute-done.1.refs_5_), channel_id=1, source_target_pairs={{0,96},{16,112},{32,0},{48,16},{64,32},{80,48},{96,64},{112,80},{1... | collective-permute-start | bytes 1179656 | tf_op jit(solution)/shard_map/ppermute | solution.py:16
  64.8 20.6 %all-to-all-start.2 = ((bf16[16,128,128]{2,1,0:T(8,128)(2,1)}), bf16[16,128,128]{2,1,0:T(8,128)(2,1)S(1)}, u32[]{:S(2)}, u32[]{:S(2)}) async-start(bf16[16,128,128]{2,1,0:T(8,128)(2,1)} %get-tuple-element.46), calls=%async_computation.2 | async-start | bytes 1048576 | tf_op jit(solution)/shard_map/all_to_all | solution.py:289
  73.7 14.9 %collective-permute-start.13 = (bf16[4,64,512]{2,1,0:T(8,128)(2,1)S(1)}, bf16[4,64,512]{2,1,0:T(8,128)(2,1)S(1)}, u32[]{:S(2)}, u32[]{:S(2)}) collective-permute-start(bf16[4,64,512]{2,1,0:T(8,128)(2,1)S(1)} %slice_bitcast_fusion.refs_0_), channel_id=1, source_target_pairs={{0,4},{1,5},{2,6},{3,7},{4,8},{5,9},{6,10},{7,11},{8,12},{9,13},{1... | collective-permute-start | bytes 786440 | tf_op jit(solution)/shard_map/ppermute | solution.py:29
  75.7 13.0 %collective-permute-start.14 = (bf16[4,64,512]{2,1,0:T(8,128)(2,1)S(1)}, bf16[4,64,512]{2,1,0:T(8,128)(2,1)S(1)}, u32[]{:S(2)}, u32[]{:S(2)}) collective-permute-start(bf16[4,64,512]{2,1,0:T(8,128)(2,1)S(1)} %slice_bitcast_fusion.refs_0_), channel_id=1, source_target_pairs={{0,12},{1,13},{2,14},{3,15},{4,0},{5,1},{6,2},{7,3},{8,4},{9,5},{1... | collective-permute-start | bytes 786440 | tf_op jit(solution)/shard_map/ppermute | solution.py:29
  77.0 16.7 %collective-permute-start.15 = (bf16[4,64,512]{2,1,0:T(8,128)(2,1)S(1)}, bf16[4,64,512]{2,1,0:T(8,128)(2,1)S(1)}, u32[]{:S(2)}, u32[]{:S(2)}) collective-permute-start(bf16[4,64,512]{2,1,0:T(8,128)(2,1)S(1)} %slice_bitcast_fusion.refs_0_), channel_id=1, source_target_pairs={{0,8},{1,9},{2,10},{3,11},{4,12},{5,13},{6,14},{7,15},{8,0},{9,1},... | collective-permute-start | bytes 786440 | tf_op jit(solution)/shard_map/ppermute | solution.py:29
  94.9 5.5 %collective-permute-start.17 = (bf16[2,128,128]{2,1,0:T(8,128)(2,1)S(1)}, bf16[2,128,128]{2,1,0:T(8,128)(2,1)S(1)}, u32[]{:S(2)}, u32[]{:S(2)}) collective-permute-start(bf16[2,128,128]{2,1,0:T(8,128)(2,1)S(1)} %pad_maximum_fusion.1.own), channel_id=1, source_target_pairs={{0,32},{16,48},{32,64},{48,80},{64,96},{80,112},{96,0},{112,16},{1... | collective-permute-start | bytes 196616 | tf_op jit(solution)/shard_map/ppermute | solution.py:16
  95.0 6.0 %collective-permute-start.18 = (bf16[2,128,128]{2,1,0:T(8,128)(2,1)S(1)}, bf16[2,128,128]{2,1,0:T(8,128)(2,1)S(1)}, u32[]{:S(2)}, u32[]{:S(2)}) collective-permute-start(bf16[2,128,128]{2,1,0:T(8,128)(2,1)S(1)} %pad_maximum_fusion.1.own), channel_id=1, source_target_pairs={{0,96},{16,112},{32,0},{48,16},{64,32},{80,48},{96,64},{112,80},{1... | collective-permute-start | bytes 196616 | tf_op jit(solution)/shard_map/ppermute | solution.py:16
  98.2 5.8 %collective-permute-start.19 = (bf16[2,128,128]{2,1,0:T(8,128)(2,1)S(1)}, bf16[2,128,128]{2,1,0:T(8,128)(2,1)S(1)}, u32[]{:S(2)}, u32[]{:S(2)}) collective-permute-start(bf16[2,128,128]{2,1,0:T(8,128)(2,1)S(1)} %pad_maximum_fusion.1.own), channel_id=1, source_target_pairs={{0,64},{16,80},{32,96},{48,112},{64,0},{80,16},{96,32},{112,48},{1... | collective-permute-start | bytes 196616 | tf_op jit(solution)/shard_map/ppermute | solution.py:16
  115.7 15.7 %all-to-all-start.4 = ((bf16[16,128,128]{2,1,0:T(8,128)(2,1)}), bf16[16,128,128]{2,1,0:T(8,128)(2,1)S(1)}, u32[]{:S(2)}, u32[]{:S(2)}) async-start(bf16[16,128,128]{2,1,0:T(8,128)(2,1)} %get-tuple-element.51), calls=%async_computation.4 | async-start | bytes 1048576 | tf_op jit(solution)/shard_map/all_to_all | solution.py:289
  120.6 5.5 %collective-permute-start.21 = (bf16[2,128,128]{2,1,0:T(8,128)(2,1)S(1)}, bf16[2,128,128]{2,1,0:T(8,128)(2,1)S(1)}, u32[]{:S(2)}, u32[]{:S(2)}) collective-permute-start(bf16[2,128,128]{2,1,0:T(8,128)(2,1)S(1)} %pad_maximum_fusion.2.own), channel_id=1, source_target_pairs={{0,32},{16,48},{32,64},{48,80},{64,96},{80,112},{96,0},{112,16},{1... | collective-permute-start | bytes 196616 | tf_op jit(solution)/shard_map/ppermute | solution.py:16
  120.7 6.0 %collective-permute-start.22 = (bf16[2,128,128]{2,1,0:T(8,128)(2,1)S(1)}, bf16[2,128,128]{2,1,0:T(8,128)(2,1)S(1)}, u32[]{:S(2)}, u32[]{:S(2)}) collective-permute-start(bf16[2,128,128]{2,1,0:T(8,128)(2,1)S(1)} %pad_maximum_fusion.2.own), channel_id=1, source_target_pairs={{0,96},{16,112},{32,0},{48,16},{64,32},{80,48},{96,64},{112,80},{1... | collective-permute-start | bytes 196616 | tf_op jit(solution)/shard_map/ppermute | solution.py:16
  123.9 5.8 %collective-permute-start.23 = (bf16[2,128,128]{2,1,0:T(8,128)(2,1)S(1)}, bf16[2,128,128]{2,1,0:T(8,128)(2,1)S(1)}, u32[]{:S(2)}, u32[]{:S(2)}) collective-permute-start(bf16[2,128,128]{2,1,0:T(8,128)(2,1)S(1)} %pad_maximum_fusion.2.own), channel_id=1, source_target_pairs={{0,64},{16,80},{32,96},{48,112},{64,0},{80,16},{96,32},{112,48},{1... | collective-permute-start | bytes 196616 | tf_op jit(solution)/shard_map/ppermute | solution.py:16
  142.7 15.1 %all-to-all-start.6 = ((bf16[16,128,128]{2,1,0:T(8,128)(2,1)}), bf16[16,128,128]{2,1,0:T(8,128)(2,1)S(1)}, u32[]{:S(2)}, u32[]{:S(2)}) async-start(bf16[16,128,128]{2,1,0:T(8,128)(2,1)} %broadcast_in_dim.7), calls=%async_computation.6 | async-start | bytes 1048576 | tf_op jit(solution)/shard_map/all_to_all | solution.py:294
  149.1 9.4 %collective-permute-start.25 = (bf16[2,128,128]{2,1,0:T(8,128)(2,1)S(1)}, bf16[2,128,128]{2,1,0:T(8,128)(2,1)S(1)}, u32[]{:S(2)}, u32[]{:S(2)}) collective-permute-start(bf16[2,128,128]{2,1,0:T(8,128)(2,1)S(1)} %pad_maximum_fusion.3.own), channel_id=1, source_target_pairs={{0,32},{16,48},{32,64},{48,80},{64,96},{80,112},{96,0},{112,16},{1... | collective-permute-start | bytes 196616 | tf_op jit(solution)/shard_map/ppermute | solution.py:16
  149.2 9.3 %collective-permute-start.26 = (bf16[2,128,128]{2,1,0:T(8,128)(2,1)S(1)}, bf16[2,128,128]{2,1,0:T(8,128)(2,1)S(1)}, u32[]{:S(2)}, u32[]{:S(2)}) collective-permute-start(bf16[2,128,128]{2,1,0:T(8,128)(2,1)S(1)} %pad_maximum_fusion.3.own), channel_id=1, source_target_pairs={{0,96},{16,112},{32,0},{48,16},{64,32},{80,48},{96,64},{112,80},{1... | collective-permute-start | bytes 196616 | tf_op jit(solution)/shard_map/ppermute | solution.py:16
  152.4 6.1 %collective-permute-start.27 = (bf16[2,128,128]{2,1,0:T(8,128)(2,1)S(1)}, bf16[2,128,128]{2,1,0:T(8,128)(2,1)S(1)}, u32[]{:S(2)}, u32[]{:S(2)}) collective-permute-start(bf16[2,128,128]{2,1,0:T(8,128)(2,1)S(1)} %pad_maximum_fusion.3.own), channel_id=1, source_target_pairs={{0,64},{16,80},{32,96},{48,112},{64,0},{80,16},{96,32},{112,48},{1... | collective-permute-start | bytes 196616 | tf_op jit(solution)/shard_map/ppermute | solution.py:16
  170.6 15.1 %all-to-all-start.8 = ((bf16[16,128,128]{2,1,0:T(8,128)(2,1)}), bf16[16,128,128]{2,1,0:T(8,128)(2,1)S(1)}, u32[]{:S(2)}, u32[]{:S(2)}) async-start(bf16[16,128,128]{2,1,0:T(8,128)(2,1)} %broadcast_in_dim.8), calls=%async_computation.8 | async-start | bytes 1048576 | tf_op jit(solution)/shard_map/all_to_all | solution.py:294
  187.8 6.0 %collective-permute-start.31 = (f32[32,512]{1,0:T(8,128)S(1)}, f32[32,512]{1,0:T(8,128)S(1)}, u32[]{:S(2)}, u32[]{:S(2)}) collective-permute-start(f32[32,512]{1,0:T(8,128)S(1)} %add.156), channel_id=1, source_target_pairs={{0,64},{16,80},{32,96},{48,112},{64,0},{80,16},{96,32},{112,48},{1... | collective-permute-start | bytes 196616 | tf_op jit(solution)/shard_map/ppermute | solution.py:16
  187.9 5.9 %collective-permute-start.30 = (f32[32,512]{1,0:T(8,128)S(1)}, f32[32,512]{1,0:T(8,128)S(1)}, u32[]{:S(2)}, u32[]{:S(2)}) collective-permute-start(f32[32,512]{1,0:T(8,128)S(1)} %add.156), channel_id=1, source_target_pairs={{0,96},{16,112},{32,0},{48,16},{64,32},{80,48},{96,64},{112,80},{1... | collective-permute-start | bytes 196616 | tf_op jit(solution)/shard_map/ppermute | solution.py:16
  189.5 5.5 %collective-permute-start.29 = (f32[32,512]{1,0:T(8,128)S(1)}, f32[32,512]{1,0:T(8,128)S(1)}, u32[]{:S(2)}, u32[]{:S(2)}) collective-permute-start(f32[32,512]{1,0:T(8,128)S(1)} %add.156), channel_id=1, source_target_pairs={{0,32},{16,48},{32,64},{48,80},{64,96},{80,112},{96,0},{112,16},{1... | collective-permute-start | bytes 196616 | tf_op jit(solution)/shard_map/ppermute | solution.py:16
  (13 other events, 50.3 us)

commit v10 on v8

--- a/solution.py
+++ b/solution.py
@@ -32,6 +32,10 @@
     return gathered.reshape(16, *v.shape[1:])
 
 
+def z_shift(v, step):
+    return lax.ppermute(v, "col", [(c, c // 4 * 4 + (c + step) % 4) for c in range(16)])
+
+
 def whole(array):
     rank = len(array.shape)
     return pl.BlockSpec(array.shape, lambda i, *_: (0,) * rank)
@@ -45,33 +49,29 @@
     return pltpu.with_memory_space_constraint(array, pltpu.HBM)
 
 
-def prepare_kernel(values, first, second, linking, low, high, lines):
-    low[...] = values[:, :128, :]
-    high[...] = values[:, 128:, :]
+def prepare_kernel(first, second, linking, lines):
     for m, source in enumerate((first, linking, second)):
         turned = jnp.transpose(source[...].astype(F32)).astype(BF)
         for q in range(4):
             lines[q, m] = turned[64 * q : 64 * (q + 1), :]
 
 
-def prepare(values, inverses, coupling):
+def prepare(inverses, coupling):
     inverses = in_hbm(inverses.reshape(2, 512, 256))
     coupling = in_hbm(coupling.reshape(512, 256))
-    half = jax.ShapeDtypeStruct((3, 128, 512), BF)
-    out = [half, half, jax.ShapeDtypeStruct((4, 3, 64, 512), BF)]
+    out = jax.ShapeDtypeStruct((4, 3, 64, 512), BF)
     return pl.pallas_call(
         prepare_kernel,
         grid=(1,),
         in_specs=[
-            whole(values),
             pl.BlockSpec((None, 512, 256), lambda i: (0, 0, 0)),
             pl.BlockSpec((None, 512, 256), lambda i: (1, 0, 0)),
             whole(coupling),
         ],
-        out_specs=list(map(whole, out)),
+        out_specs=whole(out),
         out_shape=out,
         compiler_params=ROOMY,
-    )(in_hbm(values), inverses, inverses, coupling)
+    )(inverses, inverses, coupling)
 
 
 def split_tiles_kernel(src, dst):
@@ -196,7 +196,8 @@
 RELATIVE = (0, -1, 1, 2)
 
 
-def stage_kernel(order, own, one, two, three, weights, out, held):
+def stage_kernel(order, targets, own, one, two, three, weights, *refs):
+    *parts, held, result = refs
     for i, source in enumerate((own, one, two, three)):
         for k in range(2):
             line = order[2 * i + k]
@@ -206,11 +207,11 @@
     values = jnp.transpose(values).astype(BF)
     factor = weights[...].reshape(1024, 512)
     total = jnp.dot(values, factor, preferred_element_type=F32)
-    total = jnp.transpose(total).astype(BF)
-    for q in range(4):
+    result[...] = jnp.transpose(total)
+    for d, part in enumerate(parts):
         for a in range(2):
-            top = 256 * a + 64 * q
-            out[q, 64 * a : 64 * (a + 1), :] = total[top : top + 64, :]
+            top = pl.multiple_of(256 * a + 64 * targets[d], 64)
+            part[64 * a : 64 * (a + 1), :] = result[pl.ds(top, 64), :].astype(BF)
 
 
 def over_cores(values):
@@ -224,28 +225,29 @@
 SCALARS = pl.BlockSpec(memory_space=pltpu.SMEM)
 
 
-def stage(order, values, panels, which):
+def stage(order, targets, values, panels, which):
     moved = over_chips(over_cores(values))
-    out = jax.ShapeDtypeStruct((4, 128, 128), BF)
-    partial = pl.pallas_call(
+    out = [jax.ShapeDtypeStruct((128, 128), BF)] * 4
+    return pl.pallas_call(
         stage_kernel,
         grid=(1,),
         in_specs=[
             SCALARS,
+            SCALARS,
             *map(whole, moved),
             pl.BlockSpec((16, None, 64, 512), lambda i: (0, which, 0, 0)),
         ],
-        out_specs=whole(out),
-        scratch_shapes=[VMEM((16, 64, 128), BF)],
+        out_specs=list(map(whole, out)),
+        scratch_shapes=[VMEM((16, 64, 128), BF), VMEM((512, 128), F32)],
         out_shape=out,
         cost_estimate=cost(2 * 128 * 1024 * 512, 2 * 1024 * 512),
         compiler_params=ROOMY,
-    )(order, *moved, panels)
-    return partial
-
-
-def over_z(partial):
-    return z_exchange(partial).astype(F32).sum(axis=0)
+    )(order, targets, *moved, panels)
+
+
+def over_z(parts):
+    moved = [z_shift(part, d) if d else part for d, part in enumerate(parts)]
+    return sum(part.astype(F32) for part in moved)
 
 
 def over_sites(partial):
@@ -274,28 +276,25 @@
     y, z = col // 4, col % 4
     order = jnp.stack([(x + d) % 4 * 2 + (k + e) % 2 for d in RELATIVE for e in range(2)])
     order = order.astype(jnp.int32)
-
-    low, high, lines = prepare(prev_solution, inverses, coupling)
-    before_low, after_high = x_shift(low, 1), x_shift(high, -1)
-    before_high, after_low = x_shift(high, 1), x_shift(low, -1)
-    sibling = in_hbm(other_core(prev_solution))
+    targets = jnp.stack([(z + d) % 4 for d in range(4)]).astype(jnp.int32)
+
+    lines = prepare(inverses, coupling)
+    before, after = x_shift(prev_solution, 1), x_shift(prev_solution, -1)
+    sibling = other_core(prev_solution)
     left = split_tiles(in_hbm(left_factor))
     lines = z_exchange(lines)
-    before_low, after_high, before_high, after_low, sibling, left, lines = (
-        lax.optimization_barrier(
-            (before_low, after_high, before_high, after_low, sibling, left, lines)
-        )
-    )
-    sibling = in_hbm(sibling)
+    before, after, sibling, left, lines = lax.optimization_barrier(
+        (before, after, sibling, left, lines)
+    )
     panels = in_hbm(y_gather(lines))
-    far_low, far_high = x_shift(before_low, 1), x_shift(after_high, -1)
-    pieces = [(prev_solution, 0), (prev_solution, 1), (sibling, 0), (sibling, 1)]
+    far_low, far_high = x_shift(before[:, :128, :], 1), x_shift(after[:, 128:, :], -1)
+    halves = lambda v: [(in_hbm(v), 0), (in_hbm(v), 1)]
+    pieces = halves(prev_solution) + halves(sibling)
     started = products(order[:2], left, pieces)
     token = started[:8, :128]
     pieces = []
-    for pair in ((before_low, before_high), (after_low, after_high)):
-        pieces += [(in_hbm(v), 0) for v in pair]
-        pieces += [(in_hbm(other_core(v)), 0) for v in pair]
+    for block in (before, after):
+        pieces += halves(block) + halves(other_core(block))
     started = products(order[2:6], left, pieces, started, token)
     far_low, far_high, token = lax.optimization_barrier(
         (far_low, far_high, started[:8, :128])
@@ -311,14 +310,16 @@
     first_rhs = (known[0] - over_sites(first)).astype(BF)
     first_rhs, second = lax.optimization_barrier((first_rhs, second))
     rest = known[1] - over_sites(second)
-    solved_first = over_z(stage(order, first_rhs, panels, 0)).astype(BF)
+    solved_first = over_z(stage(order, targets, first_rhs, panels, 0)).astype(BF)
     every_first = all_sites(solved_first)
-    partial = stage(order, solved_first, panels, 1)
-    partial, rest = lax.optimization_barrier((partial, rest))
-    second_rhs = (rest - over_z(partial)).astype(BF)
-    partial = stage(order, second_rhs, panels, 2)
-    partial, every_first = lax.optimization_barrier((partial, every_first))
-    solved_second = over_z(partial).astype(BF)
+    *parts, rest = lax.optimization_barrier(
+        (*stage(order, targets, solved_first, panels, 1), rest)
+    )
+    second_rhs = (rest - over_z(parts)).astype(BF)
+    *parts, every_first = lax.optimization_barrier(
+        (*stage(order, targets, second_rhs, panels, 2), every_first)
+    )
+    solved_second = over_z(parts).astype(BF)
     every_second = all_sites(solved_second)
     outer = outer_part(every_first, col) + outer_part(every_second, col)
     pred_cov = prior_cov - row_sum(outer) / S

time: 191 us -> 178 us (0.932)
  blocking collectives: 28.9 us -> 0 us
  waiting for transfers between devices: 58 us -> 68.4 us
  starting transfers between devices: 54.2 us -> 60 us
    all_to_all x3 -> x0, blocking collectives: 28.9 us -> none  [z_exchange(): return lax.all_to_all(v, 'col', 0, 0, axis_index_groups=groups, tiled=True)]
    ppermute x0 -> x9, waiting for transfers between devices: none -> 15.9 us  [z_shift(): lax.ppermute(v, 'col', [(c, c // 4 * 4 + (c + step) % 4) for c in range(1...]
    ppermute x0 -> x9, starting transfers between devices: none -> 10.5 us  [z_shift(): lax.ppermute(v, 'col', [(c, c // 4 * 4 + (c + step) % 4) for c in range(1...]
    all_to_all x2, waiting for transfers between devices: 15.1 us -> 9.69 us  [all_sites(): lax.all_to_all(sent, 'col', 0, 0, tiled=True).reshape(4, 4, 2, 64, 128)]
    ppermute x18 -> x16, waiting for transfers between devices: 18.2 us -> 13.2 us  [x_shift(): return lax.ppermute(v, 'row', [(r, (r + 2 * step) % 8) for r in range(8)])]
    all_to_all x1, waiting for transfers between devices: 0.01 us -> 2.53 us  [z_exchange(): return lax.all_to_all(v, 'col', 0, 0, axis_index_groups=groups, tiled=True)]
    ppermute x18 -> x16, starting transfers between devices: 23.4 us -> 22.4 us  [x_shift(): return lax.ppermute(v, 'row', [(r, (r + 2 * step) % 8) for r in range(8)])]
    ppermute x11 -> x9, waiting for transfers between devices: 6.68 us -> 6.58 us  [other_core(): return lax.ppermute(v, 'row', [(r, r ^ 1) for r in range(8)])]
  transfers between devices with their start and end apart: 35 -> 40, of which waited for: 19 -> 27; matrix products, arithmetic and copies ran while one was open for 2% -> 2% of each run, Pallas kernels for 18% -> 21%
where the time goes in v10:
time: 178 us; the launch traced here: 177 us
  waiting for transfers between devices  68.4 us (38%)
  starting transfers between devices  60 us (34%)
  Pallas kernels  38 us (21%)
  local copies, waits for them, and re-layouts  5.7 us (3%)
  other arithmetic  3.16 us (2%)
    ppermute x16, starting transfers between devices, x_shift(): return lax.ppermute(v, 'row', [(r, (r + 2 * step) % 8) for r in range(8)])  22.4 us
    pallas_call x3, Pallas kernels, products(): pl.pallas_call(kernel, grid_spec=pltpu.PrefetchScalarGridSpec(num_scalar_...  20.1 us
    ppermute x9, waiting for transfers between devices, z_shift(): lax.ppermute(v, 'col', [(c, c // 4 * 4 + (c + step) % 4) for c in range(1...  15.9 us
    ppermute x16, waiting for transfers between devices, x_shift(): return lax.ppermute(v, 'row', [(r, (r + 2 * step) % 8) for r in range(8)])  13.2 us
    all_to_all x1, waiting for transfers between devices, y_gather(): lax.all_to_all(sent, 'col', 0, 0, axis_index_groups=groups, tiled=True)  10.7 us
    ppermute x9, starting transfers between devices, z_shift(): lax.ppermute(v, 'col', [(c, c // 4 * 4 + (c + step) % 4) for c in range(1...  10.5 us
    pallas_call x1, Pallas kernels, split_tiles(): pl.pallas_call(split_tiles_kernel, grid=(rounds, tile // rows), in_specs=...  10.4 us
    all_to_all x2, waiting for transfers between devices, over_sites(): lax.all_to_all(partial, 'col', 0, 0, tiled=True).astype(F32).sum(axis=0)  9.78 us
  transfers between devices with their start and end apart: 40, of which 27 were waited for; matrix products, arithmetic and copies ran while one was open for 2% of the time, Pallas kernels for 21%

profile of v10, /device:TPU:0, one launch (start us, length us, event | category | flops | bytes accessed | tf_op | source)
XLA Modules:
  0.0 176.7 jit_solution(12448761776941508421)
XLA Ops:
  3.9 2.3 %shard_map.78 = bf16[4,3,64,512]{3,2,1,0:T(8,128)(2,1)} custom-call(bf16[2,512,256]{2,1,0:T(8,128)(2,1)} %bitcast.47, bf16[2,512,256]{2,1,0:T(8,128)(2,1)} %bitcast.48, bf16[512,256]{1,0:T(8,128)(2,1)} %bitcast.50), custom_call_target="tpu_custom_call" | custom-call | tf_op jit(solution)/shard_map/pallas_call | solution.py:63
  6.2 5.4 %all-to-all-start = ((bf16[4,3,64,512]{3,2,1,0:T(8,128)(2,1)}), bf16[4,3,64,512]{3,2,1,0:T(8,128)(2,1)S(1)}, u32[]{:S(2)}, u32[]{:S(2)}) async-start(bf16[4,3,64,512]{3,2,1,0:T(8,128)(2,1)} %shard_map.78), calls=%async_computation | async-start | bytes 1572864 | tf_op jit(solution)/shard_map/all_to_all | solution.py:25
  11.6 10.4 %shard_map.77 = bf16[24,4,256,256]{3,2,1,0:T(8,128)(2,1)} custom-call(bf16[4,256,24,256]{3,2,1,0:T(8,128)(2,1)} %src.1), custom_call_target="tpu_custom_call" | custom-call | bytes 25165824 | tf_op jit(solution)/shard_map/pallas_call | solution.py:84
  22.0 2.5 %all-to-all-done = bf16[4,3,64,512]{3,2,1,0:T(8,128)(2,1)S(1)} async-done(((bf16[4,3,64,512]{3,2,1,0:T(8,128)(2,1)}), bf16[4,3,64,512]{3,2,1,0:T(8,128)(2,1)S(1)}, u32[]{:S(2)}, u32[]{:S(2)}) %all-to-all-start) | async-done | bytes 786464 | tf_op jit(solution)/shard_map/all_to_all | solution.py:25
  24.6 2.3 %broadcast_in_dim.6 = bf16[4,4,3,64,512]{4,3,2,1,0:T(8,128)(2,1)} broadcast(bf16[4,3,64,512]{3,2,1,0:T(8,128)(2,1)S(1)} %all-to-all-done), dimensions={1,2,3,4} | broadcast | bytes 3932160 | tf_op jit(solution)/shard_map/broadcast_in_dim | solution.py:30
  26.9 4.7 %all-to-all-start.1 = ((bf16[4,4,3,64,512]{4,3,2,1,0:T(8,128)(2,1)}), bf16[4,4,3,64,512]{4,3,2,1,0:T(8,128)(2,1)}, u32[]{:S(2)}, u32[]{:S(2)}) async-start(bf16[4,4,3,64,512]{4,3,2,1,0:T(8,128)(2,1)} %broadcast_in_dim.6), calls=%async_computation.1 | async-start | bytes 6291456 | tf_op jit(solution)/shard_map/all_to_all | solution.py:31
  32.7 3.0 %collective-permute-start.6 = (bf16[3,128,512]{2,1,0:T(8,128)(2,1)S(1)}, bf16[3,128,512]{2,1,0:T(8,128)(2,1)S(1)}, u32[]{:S(2)}, u32[]{:S(2)}) collective-permute-start(bf16[3,128,512]{2,1,0:T(8,128)(2,1)S(1)} %slice.29), channel_id=1, source_target_pairs={{0,96},{16,112},{32,0},{48,16},{64,32},{80,48},{96,64},{112,80},{1... | collective-permute-start | bytes 1179656 | tf_op jit(solution)/shard_map/ppermute | solution.py:16
  35.7 5.2 %shard_map.79.before = f32[1024,512]{1,0:T(8,128)S(1)} custom-call(s32[2]{0:T(128)S(1)} %pad_add_fusion.3.order, bf16[24,1024,256]{2,1,0:T(8,128)(2,1)} %bitcast.42, bf16[3,256,512]{2,1,0:T(8,128)(2,1)} %refs_1_.1, bf16[3,256,512]{2,1,0:T(8,128)(2,1)} %refs_1_.1, bf16[3,256,512]{2,1,0:T(8,128)(2,1)} %copy-done.2, bf16[3,256,512]{2,1,0:T(8,128)(2,1)} %copy-done.2), custom_call_target="tpu_custom_call" | custom-call | flops 1610612736 | bytes 6815744 | tf_op jit(solution)/shard_map/pallas_call | solution.py:181
  40.9 8.9 %shard_map.80.before = f32[1024,512]{1,0:T(8,128)S(1)} custom-call(s32[4]{0:T(128)S(1)} %pad_add_fusion.2.order, bf16[24,1024,256]{2,1,0:T(8,128)(2,1)} %bitcast.43, f32[1024,512]{1,0:T(8,128)S(1)} %shard_map.79.before, f32[8,128]{1,0:T(8,128)S(1)} %slice.33.token, bf16[3,256,512]{2,1,0:T(8,128)(2,1)} %copy-done, bf16[3,256,512]{2,1,0:T(8,128)(2,1)} %copy-done, ...), custom_call_target="tpu_custom_call" | custom-call | flops 3221225472 | bytes 11534336 | tf_op jit(solution)/shard_map/pallas_call | solution.py:181
  52.3 6.1 %shard_map.81 = (bf16[16,128,128]{2,1,0:T(8,128)(2,1)}, bf16[16,128,128]{2,1,0:T(8,128)(2,1)}) custom-call(s32[2]{0:T(128)S(1)} %pad_add_fusion.1.order, bf16[24,1024,256]{2,1,0:T(8,128)(2,1)} %bitcast.44, f32[1024,512]{1,0:T(8,128)S(1)} %shard_map.80.before, f32[8,128]{1,0:T(8,128)S(1)} %slice.34.token, ...), custom_call_target="tpu_custom_call" | custom-call | flops 1610612736 | bytes 6815744 | tf_op jit(solution)/shard_map/pallas_call | solution.py:181
  58.4 10.7 %all-to-all-done.1 = bf16[4,4,3,64,512]{4,3,2,1,0:T(8,128)(2,1)} async-done(((bf16[4,4,3,64,512]{4,3,2,1,0:T(8,128)(2,1)}), bf16[4,4,3,64,512]{4,3,2,1,0:T(8,128)(2,1)}, u32[]{:S(2)}, u32[]{:S(2)}) %all-to-all-start.1) | async-done | bytes 3145760 | tf_op jit(solution)/shard_map/all_to_all | solution.py:31
  69.0 3.6 %all-to-all-start.2 = ((bf16[16,128,128]{2,1,0:T(8,128)(2,1)}), bf16[16,128,128]{2,1,0:T(8,128)(2,1)S(1)}, u32[]{:S(2)}, u32[]{:S(2)}) async-start(bf16[16,128,128]{2,1,0:T(8,128)(2,1)} %get-tuple-element.49), calls=%async_computation.2 | async-start | bytes 1048576 | tf_op jit(solution)/shard_map/all_to_all | solution.py:254
  73.5 9.8 %all-to-all-done.2 = bf16[16,128,128]{2,1,0:T(8,128)(2,1)S(1)} async-done(((bf16[16,128,128]{2,1,0:T(8,128)(2,1)}), bf16[16,128,128]{2,1,0:T(8,128)(2,1)S(1)}, u32[]{:S(2)}, u32[]{:S(2)}) %all-to-all-start.2) | async-done | bytes 524320 | tf_op jit(solution)/shard_map/all_to_all | solution.py:254
  84.8 3.2 %collective-permute-start.11 = (bf16[2,128,128]{2,1,0:T(8,128)(2,1)S(1)}, bf16[2,128,128]{2,1,0:T(8,128)(2,1)S(1)}, u32[]{:S(2)}, u32[]{:S(2)}) collective-permute-start(bf16[2,128,128]{2,1,0:T(8,128)(2,1)S(1)} %pad_maximum_fusion.1.own), channel_id=1, source_target_pairs={{0,96},{16,112},{32,0},{48,16},{64,32},{80,48},{96,64},{112,80},{1... | collective-permute-start | bytes 196616 | tf_op jit(solution)/shard_map/ppermute | solution.py:16
  88.4 3.6 %all-to-all-start.3 = ((bf16[16,128,128]{2,1,0:T(8,128)(2,1)}), bf16[16,128,128]{2,1,0:T(8,128)(2,1)S(1)}, u32[]{:S(2)}, u32[]{:S(2)}) async-start(bf16[16,128,128]{2,1,0:T(8,128)(2,1)} %get-tuple-element.61), calls=%async_computation.3 | async-start | bytes 1048576 | tf_op jit(solution)/shard_map/all_to_all | solution.py:254
  92.0 1.8 %collective-permute-done.12.three = bf16[2,128,128]{2,1,0:T(8,128)(2,1)S(1)} collective-permute-done((bf16[2,128,128]{2,1,0:T(8,128)(2,1)S(1)}, bf16[2,128,128]{2,1,0:T(8,128)(2,1)S(1)}, u32[]{:S(2)}, u32[]{:S(2)}) %collective-permute-start.12) | collective-permute-done | bytes 65568 | tf_op jit(solution)/shard_map/ppermute | solution.py:16
  98.5 2.6 %collective-permute-done.15 = bf16[128,128]{1,0:T(8,128)(2,1)S(1)} collective-permute-done((bf16[128,128]{1,0:T(8,128)(2,1)S(1)}, bf16[128,128]{1,0:T(8,128)(2,1)S(1)}, u32[]{:S(2)}, u32[]{:S(2)}) %collective-permute-start.15) | collective-permute-done | bytes 32800 | tf_op jit(solution)/shard_map/ppermute | solution.py:36
  101.1 2.4 %collective-permute-done.14 = bf16[128,128]{1,0:T(8,128)(2,1)S(1)} collective-permute-done((bf16[128,128]{1,0:T(8,128)(2,1)S(1)}, bf16[128,128]{1,0:T(8,128)(2,1)S(1)}, u32[]{:S(2)}, u32[]{:S(2)}) %collective-permute-start.14) | collective-permute-done | bytes 32800 | tf_op jit(solution)/shard_map/ppermute | solution.py:36
  106.0 2.5 %collective-permute-start.18 = (bf16[2,128,128]{2,1,0:T(8,128)(2,1)S(1)}, bf16[2,128,128]{2,1,0:T(8,128)(2,1)S(1)}, u32[]{:S(2)}, u32[]{:S(2)}) collective-permute-start(bf16[2,128,128]{2,1,0:T(8,128)(2,1)S(1)} %pad_maximum_fusion.2.own), channel_id=1, source_target_pairs={{0,96},{16,112},{32,0},{48,16},{64,32},{80,48},{96,64},{112,80},{1... | collective-permute-start | bytes 196616 | tf_op jit(solution)/shard_map/ppermute | solution.py:16
  108.5 1.9 %collective-permute-start.19 = (bf16[2,128,128]{2,1,0:T(8,128)(2,1)S(1)}, bf16[2,128,128]{2,1,0:T(8,128)(2,1)S(1)}, u32[]{:S(2)}, u32[]{:S(2)}) collective-permute-start(bf16[2,128,128]{2,1,0:T(8,128)(2,1)S(1)} %pad_maximum_fusion.2.own), channel_id=1, source_target_pairs={{0,64},{16,80},{32,96},{48,112},{64,0},{80,16},{96,32},{112,48},{1... | collective-permute-start | bytes 196616 | tf_op jit(solution)/shard_map/ppermute | solution.py:16
  111.5 2.8 %collective-permute-done.19.three = bf16[2,128,128]{2,1,0:T(8,128)(2,1)S(1)} collective-permute-done((bf16[2,128,128]{2,1,0:T(8,128)(2,1)S(1)}, bf16[2,128,128]{2,1,0:T(8,128)(2,1)S(1)}, u32[]{:S(2)}, u32[]{:S(2)}) %collective-permute-start.19) | collective-permute-done | bytes 65568 | tf_op jit(solution)/shard_map/ppermute | solution.py:16
  116.9 4.4 %all-to-all-start.4 = ((bf16[16,128,128]{2,1,0:T(8,128)(2,1)}), bf16[16,128,128]{2,1,0:T(8,128)(2,1)S(1)}, u32[]{:S(2)}, u32[]{:S(2)}) async-start(bf16[16,128,128]{2,1,0:T(8,128)(2,1)} %broadcast_in_dim.7), calls=%async_computation.4 | async-start | bytes 1048576 | tf_op jit(solution)/shard_map/all_to_all | solution.py:259
  121.4 3.2 %collective-permute-start.22 = (bf16[128,128]{1,0:T(8,128)(2,1)S(1)}, bf16[128,128]{1,0:T(8,128)(2,1)S(1)}, u32[]{:S(2)}, u32[]{:S(2)}) collective-permute-start(bf16[128,128]{1,0:T(8,128)(2,1)S(1)} %get-tuple-element.66), channel_id=1, source_target_pairs={{0,3},{1,0},{2,1},{3,2},{4,7},{5,4},{6,5},{7,6},{8,11},{9,8},{10,9... | collective-permute-start | bytes 98312 | tf_op jit(solution)/shard_map/ppermute | solution.py:36
  126.4 3.0 %collective-permute-done.22 = bf16[128,128]{1,0:T(8,128)(2,1)S(1)} collective-permute-done((bf16[128,128]{1,0:T(8,128)(2,1)S(1)}, bf16[128,128]{1,0:T(8,128)(2,1)S(1)}, u32[]{:S(2)}, u32[]{:S(2)}) %collective-permute-start.22) | collective-permute-done | bytes 32800 | tf_op jit(solution)/shard_map/ppermute | solution.py:36
  129.4 2.5 %collective-permute-done.21 = bf16[128,128]{1,0:T(8,128)(2,1)S(1)} collective-permute-done((bf16[128,128]{1,0:T(8,128)(2,1)S(1)}, bf16[128,128]{1,0:T(8,128)(2,1)S(1)}, u32[]{:S(2)}, u32[]{:S(2)}) %collective-permute-start.21) | collective-permute-done | bytes 32800 | tf_op jit(solution)/shard_map/ppermute | solution.py:36
  133.6 3.0 %collective-permute-start.25 = (bf16[2,128,128]{2,1,0:T(8,128)(2,1)S(1)}, bf16[2,128,128]{2,1,0:T(8,128)(2,1)S(1)}, u32[]{:S(2)}, u32[]{:S(2)}) collective-permute-start(bf16[2,128,128]{2,1,0:T(8,128)(2,1)S(1)} %pad_maximum_fusion.3.own), channel_id=1, source_target_pairs={{0,96},{16,112},{32,0},{48,16},{64,32},{80,48},{96,64},{112,80},{1... | collective-permute-start | bytes 196616 | tf_op jit(solution)/shard_map/ppermute | solution.py:16
  139.4 3.0 %collective-permute-done.26.three = bf16[2,128,128]{2,1,0:T(8,128)(2,1)S(1)} collective-permute-done((bf16[2,128,128]{2,1,0:T(8,128)(2,1)S(1)}, bf16[2,128,128]{2,1,0:T(8,128)(2,1)S(1)}, u32[]{:S(2)}, u32[]{:S(2)}) %collective-permute-start.26) | collective-permute-done | bytes 65568 | tf_op jit(solution)/shard_map/ppermute | solution.py:16
  142.3 1.7 shard_map.84
  148.1 2.4 %collective-permute-done.28 = bf16[128,128]{1,0:T(8,128)(2,1)S(1)} collective-permute-done((bf16[128,128]{1,0:T(8,128)(2,1)S(1)}, bf16[128,128]{1,0:T(8,128)(2,1)S(1)}, u32[]{:S(2)}, u32[]{:S(2)}) %collective-permute-start.28) | collective-permute-done | bytes 32800 | tf_op jit(solution)/shard_map/ppermute | solution.py:36
  152.6 3.9 %all-to-all-start.5 = ((bf16[16,128,128]{2,1,0:T(8,128)(2,1)}), bf16[16,128,128]{2,1,0:T(8,128)(2,1)S(1)}, u32[]{:S(2)}, u32[]{:S(2)}) async-start(bf16[16,128,128]{2,1,0:T(8,128)(2,1)} %broadcast_in_dim.8), calls=%async_computation.5 | async-start | bytes 1048576 | tf_op jit(solution)/shard_map/all_to_all | solution.py:259
  156.9 9.7 %all-to-all-done.5 = bf16[16,128,128]{2,1,0:T(8,128)(2,1)S(1)} async-done(((bf16[16,128,128]{2,1,0:T(8,128)(2,1)}), bf16[16,128,128]{2,1,0:T(8,128)(2,1)S(1)}, u32[]{:S(2)}, u32[]{:S(2)}) %all-to-all-start.5) | async-done | bytes 524320 | tf_op jit(solution)/shard_map/all_to_all | solution.py:259
  172.8 2.0 %collective-permute-done.33 = f32[32,512]{1,0:T(8,128)S(1)} collective-permute-done((f32[32,512]{1,0:T(8,128)S(1)}, f32[32,512]{1,0:T(8,128)S(1)}, u32[]{:S(2)}, u32[]{:S(2)}) %collective-permute-start.33) | collective-permute-done | bytes 65568 | tf_op jit(solution)/shard_map/ppermute | solution.py:16
  (98 shorter events, 41.4 us)
Async XLA Ops:
  0.6 23.9 %collective-permute-start = (bf16[3,256,512]{2,1,0:T(8,128)(2,1)}, bf16[3,256,512]{2,1,0:T(8,128)(2,1)S(1)}, u32[]{:S(2)}, u32[]{:S(2)}) collective-permute-start(bf16[3,256,512]{2,1,0:T(8,128)(2,1)} %refs_1_.1), channel_id=1, source_target_pairs={{0,32},{16,48},{32,64},{48,80},{64,96},{80,112},{96,0},{112,16},{1... | collective-permute-start | bytes 2359304 | tf_op jit(solution)/shard_map/ppermute | solution.py:16
  2.3 22.3 %collective-permute-start.1 = (bf16[3,256,512]{2,1,0:T(8,128)(2,1)}, bf16[3,256,512]{2,1,0:T(8,128)(2,1)S(1)}, u32[]{:S(2)}, u32[]{:S(2)}) collective-permute-start(bf16[3,256,512]{2,1,0:T(8,128)(2,1)} %refs_1_.1), channel_id=1, source_target_pairs={{0,96},{16,112},{32,0},{48,16},{64,32},{80,48},{96,64},{112,80},{1... | collective-permute-start | bytes 2359304 | tf_op jit(solution)/shard_map/ppermute | solution.py:16
  3.9 20.6 %collective-permute-start.2 = (bf16[3,256,512]{2,1,0:T(8,128)(2,1)}, bf16[3,256,512]{2,1,0:T(8,128)(2,1)S(1)}, u32[]{:S(2)}, u32[]{:S(2)}) collective-permute-start(bf16[3,256,512]{2,1,0:T(8,128)(2,1)} %refs_1_.1), channel_id=1, source_target_pairs={{0,16},{16,0},{32,48},{48,32},{64,80},{80,64},{96,112},{112,96},{1... | collective-permute-start | bytes 2359304 | tf_op jit(solution)/shard_map/ppermute | solution.py:20
  6.2 18.3 %all-to-all-start = ((bf16[4,3,64,512]{3,2,1,0:T(8,128)(2,1)}), bf16[4,3,64,512]{3,2,1,0:T(8,128)(2,1)S(1)}, u32[]{:S(2)}, u32[]{:S(2)}) async-start(bf16[4,3,64,512]{3,2,1,0:T(8,128)(2,1)} %shard_map.78), calls=%async_computation | async-start | bytes 1572864 | tf_op jit(solution)/shard_map/all_to_all | solution.py:25
  26.9 42.1 %all-to-all-start.1 = ((bf16[4,4,3,64,512]{4,3,2,1,0:T(8,128)(2,1)}), bf16[4,4,3,64,512]{4,3,2,1,0:T(8,128)(2,1)}, u32[]{:S(2)}, u32[]{:S(2)}) async-start(bf16[4,4,3,64,512]{4,3,2,1,0:T(8,128)(2,1)} %broadcast_in_dim.6), calls=%async_computation.1 | async-start | bytes 6291456 | tf_op jit(solution)/shard_map/all_to_all | solution.py:31
  31.6 9.3 %collective-permute-start.3 = (bf16[3,256,512]{2,1,0:T(8,128)(2,1)S(1)}, bf16[3,256,512]{2,1,0:T(8,128)(2,1)}, u32[]{:S(2)}, u32[]{:S(2)}) collective-permute-start(bf16[3,256,512]{2,1,0:T(8,128)(2,1)S(1)} %collective-permute-done.refs_0_.refs_1_), channel_id=1, source_target_pairs={{0,16},{16,0},{32,48},{48,32},{64,80},{80,64},{96,112},{112,96},{1... | collective-permute-start | bytes 2359304 | tf_op jit(solution)/shard_map/ppermute | solution.py:20
  31.6 9.2 %collective-permute-start.4 = (bf16[3,256,512]{2,1,0:T(8,128)(2,1)S(1)}, bf16[3,256,512]{2,1,0:T(8,128)(2,1)}, u32[]{:S(2)}, u32[]{:S(2)}) collective-permute-start(bf16[3,256,512]{2,1,0:T(8,128)(2,1)S(1)} %collective-permute-done.1.refs_4_.refs_5_), channel_id=1, source_target_pairs={{0,16},{16,0},{32,48},{48,32},{64,80},{80,64},{96,112},{112,96},{1... | collective-permute-start | bytes 2359304 | tf_op jit(solution)/shard_map/ppermute | solution.py:20
  32.4 17.4 %collective-permute-start.5 = (bf16[3,128,512]{2,1,0:T(8,128)(2,1)S(1)}, bf16[3,128,512]{2,1,0:T(8,128)(2,1)S(1)}, u32[]{:S(2)}, u32[]{:S(2)}) collective-permute-start(bf16[3,128,512]{2,1,0:T(8,128)(2,1)S(1)} %slice.28), channel_id=1, source_target_pairs={{0,32},{16,48},{32,64},{48,80},{64,96},{80,112},{96,0},{112,16},{1... | collective-permute-start | bytes 1179656 | tf_op jit(solution)/shard_map/ppermute | solution.py:16
  32.7 17.1 %collective-permute-start.6 = (bf16[3,128,512]{2,1,0:T(8,128)(2,1)S(1)}, bf16[3,128,512]{2,1,0:T(8,128)(2,1)S(1)}, u32[]{:S(2)}, u32[]{:S(2)}) collective-permute-start(bf16[3,128,512]{2,1,0:T(8,128)(2,1)S(1)} %slice.29), channel_id=1, source_target_pairs={{0,96},{16,112},{32,0},{48,16},{64,32},{80,48},{96,64},{112,80},{1... | collective-permute-start | bytes 1179656 | tf_op jit(solution)/shard_map/ppermute | solution.py:16
  69.0 14.3 %all-to-all-start.2 = ((bf16[16,128,128]{2,1,0:T(8,128)(2,1)}), bf16[16,128,128]{2,1,0:T(8,128)(2,1)S(1)}, u32[]{:S(2)}, u32[]{:S(2)}) async-start(bf16[16,128,128]{2,1,0:T(8,128)(2,1)} %get-tuple-element.49), calls=%async_computation.2 | async-start | bytes 1048576 | tf_op jit(solution)/shard_map/all_to_all | solution.py:254
  84.7 7.3 %collective-permute-start.10 = (bf16[2,128,128]{2,1,0:T(8,128)(2,1)S(1)}, bf16[2,128,128]{2,1,0:T(8,128)(2,1)S(1)}, u32[]{:S(2)}, u32[]{:S(2)}) collective-permute-start(bf16[2,128,128]{2,1,0:T(8,128)(2,1)S(1)} %pad_maximum_fusion.1.own), channel_id=1, source_target_pairs={{0,32},{16,48},{32,64},{48,80},{64,96},{80,112},{96,0},{112,16},{1... | collective-permute-start | bytes 196616 | tf_op jit(solution)/shard_map/ppermute | solution.py:16
  84.8 7.2 %collective-permute-start.11 = (bf16[2,128,128]{2,1,0:T(8,128)(2,1)S(1)}, bf16[2,128,128]{2,1,0:T(8,128)(2,1)S(1)}, u32[]{:S(2)}, u32[]{:S(2)}) collective-permute-start(bf16[2,128,128]{2,1,0:T(8,128)(2,1)S(1)} %pad_maximum_fusion.1.own), channel_id=1, source_target_pairs={{0,96},{16,112},{32,0},{48,16},{64,32},{80,48},{96,64},{112,80},{1... | collective-permute-start | bytes 196616 | tf_op jit(solution)/shard_map/ppermute | solution.py:16
  88.0 5.8 %collective-permute-start.12 = (bf16[2,128,128]{2,1,0:T(8,128)(2,1)S(1)}, bf16[2,128,128]{2,1,0:T(8,128)(2,1)S(1)}, u32[]{:S(2)}, u32[]{:S(2)}) collective-permute-start(bf16[2,128,128]{2,1,0:T(8,128)(2,1)S(1)} %pad_maximum_fusion.1.own), channel_id=1, source_target_pairs={{0,64},{16,80},{32,96},{48,112},{64,0},{80,16},{96,32},{112,48},{1... | collective-permute-start | bytes 196616 | tf_op jit(solution)/shard_map/ppermute | solution.py:16
  88.4 27.7 %all-to-all-start.3 = ((bf16[16,128,128]{2,1,0:T(8,128)(2,1)}), bf16[16,128,128]{2,1,0:T(8,128)(2,1)S(1)}, u32[]{:S(2)}, u32[]{:S(2)}) async-start(bf16[16,128,128]{2,1,0:T(8,128)(2,1)} %get-tuple-element.61), calls=%async_computation.3 | async-start | bytes 1048576 | tf_op jit(solution)/shard_map/all_to_all | solution.py:254
  95.5 5.6 %collective-permute-start.15 = (bf16[128,128]{1,0:T(8,128)(2,1)S(1)}, bf16[128,128]{1,0:T(8,128)(2,1)S(1)}, u32[]{:S(2)}, u32[]{:S(2)}) collective-permute-start(bf16[128,128]{1,0:T(8,128)(2,1)S(1)} %get-tuple-element.56), channel_id=1, source_target_pairs={{0,3},{1,0},{2,1},{3,2},{4,7},{5,4},{6,5},{7,6},{8,11},{9,8},{10,9... | collective-permute-start | bytes 98312 | tf_op jit(solution)/shard_map/ppermute | solution.py:36
  96.8 6.7 %collective-permute-start.14 = (bf16[128,128]{1,0:T(8,128)(2,1)S(1)}, bf16[128,128]{1,0:T(8,128)(2,1)S(1)}, u32[]{:S(2)}, u32[]{:S(2)}) collective-permute-start(bf16[128,128]{1,0:T(8,128)(2,1)S(1)} %get-tuple-element.55), channel_id=1, source_target_pairs={{0,2},{1,3},{2,0},{3,1},{4,6},{5,7},{6,4},{7,5},{8,10},{9,11},{10,... | collective-permute-start | bytes 98312 | tf_op jit(solution)/shard_map/ppermute | solution.py:36
  98.2 5.5 %collective-permute-start.13 = (bf16[128,128]{1,0:T(8,128)(2,1)S(1)}, bf16[128,128]{1,0:T(8,128)(2,1)S(1)}, u32[]{:S(2)}, u32[]{:S(2)}) collective-permute-start(bf16[128,128]{1,0:T(8,128)(2,1)S(1)} %get-tuple-element.54), channel_id=1, source_target_pairs={{0,1},{1,2},{2,3},{3,0},{4,5},{5,6},{6,7},{7,4},{8,9},{9,10},{10,1... | collective-permute-start | bytes 98312 | tf_op jit(solution)/shard_map/ppermute | solution.py:36
  105.2 5.5 %collective-permute-start.17 = (bf16[2,128,128]{2,1,0:T(8,128)(2,1)S(1)}, bf16[2,128,128]{2,1,0:T(8,128)(2,1)S(1)}, u32[]{:S(2)}, u32[]{:S(2)}) collective-permute-start(bf16[2,128,128]{2,1,0:T(8,128)(2,1)S(1)} %pad_maximum_fusion.2.own), channel_id=1, source_target_pairs={{0,32},{16,48},{32,64},{48,80},{64,96},{80,112},{96,0},{112,16},{1... | collective-permute-start | bytes 196616 | tf_op jit(solution)/shard_map/ppermute | solution.py:16
  106.0 5.5 %collective-permute-start.18 = (bf16[2,128,128]{2,1,0:T(8,128)(2,1)S(1)}, bf16[2,128,128]{2,1,0:T(8,128)(2,1)S(1)}, u32[]{:S(2)}, u32[]{:S(2)}) collective-permute-start(bf16[2,128,128]{2,1,0:T(8,128)(2,1)S(1)} %pad_maximum_fusion.2.own), channel_id=1, source_target_pairs={{0,96},{16,112},{32,0},{48,16},{64,32},{80,48},{96,64},{112,80},{1... | collective-permute-start | bytes 196616 | tf_op jit(solution)/shard_map/ppermute | solution.py:16
  108.5 5.8 %collective-permute-start.19 = (bf16[2,128,128]{2,1,0:T(8,128)(2,1)S(1)}, bf16[2,128,128]{2,1,0:T(8,128)(2,1)S(1)}, u32[]{:S(2)}, u32[]{:S(2)}) collective-permute-start(bf16[2,128,128]{2,1,0:T(8,128)(2,1)S(1)} %pad_maximum_fusion.2.own), channel_id=1, source_target_pairs={{0,64},{16,80},{32,96},{48,112},{64,0},{80,16},{96,32},{112,48},{1... | collective-permute-start | bytes 196616 | tf_op jit(solution)/shard_map/ppermute | solution.py:16
  116.9 20.5 %all-to-all-start.4 = ((bf16[16,128,128]{2,1,0:T(8,128)(2,1)}), bf16[16,128,128]{2,1,0:T(8,128)(2,1)S(1)}, u32[]{:S(2)}, u32[]{:S(2)}) async-start(bf16[16,128,128]{2,1,0:T(8,128)(2,1)} %broadcast_in_dim.7), calls=%async_computation.4 | async-start | bytes 1048576 | tf_op jit(solution)/shard_map/all_to_all | solution.py:259
  121.4 8.0 %collective-permute-start.22 = (bf16[128,128]{1,0:T(8,128)(2,1)S(1)}, bf16[128,128]{1,0:T(8,128)(2,1)S(1)}, u32[]{:S(2)}, u32[]{:S(2)}) collective-permute-start(bf16[128,128]{1,0:T(8,128)(2,1)S(1)} %get-tuple-element.66), channel_id=1, source_target_pairs={{0,3},{1,0},{2,1},{3,2},{4,7},{5,4},{6,5},{7,6},{8,11},{9,8},{10,9... | collective-permute-start | bytes 98312 | tf_op jit(solution)/shard_map/ppermute | solution.py:36
  124.6 7.3 %collective-permute-start.21 = (bf16[128,128]{1,0:T(8,128)(2,1)S(1)}, bf16[128,128]{1,0:T(8,128)(2,1)S(1)}, u32[]{:S(2)}, u32[]{:S(2)}) collective-permute-start(bf16[128,128]{1,0:T(8,128)(2,1)S(1)} %get-tuple-element.65), channel_id=1, source_target_pairs={{0,2},{1,3},{2,0},{3,1},{4,6},{5,7},{6,4},{7,5},{8,10},{9,11},{10,... | collective-permute-start | bytes 98312 | tf_op jit(solution)/shard_map/ppermute | solution.py:36
  125.5 6.4 %collective-permute-start.20 = (bf16[128,128]{1,0:T(8,128)(2,1)S(1)}, bf16[128,128]{1,0:T(8,128)(2,1)S(1)}, u32[]{:S(2)}, u32[]{:S(2)}) collective-permute-start(bf16[128,128]{1,0:T(8,128)(2,1)S(1)} %get-tuple-element.64), channel_id=1, source_target_pairs={{0,1},{1,2},{2,3},{3,0},{4,5},{5,6},{6,7},{7,4},{8,9},{9,10},{10,1... | collective-permute-start | bytes 98312 | tf_op jit(solution)/shard_map/ppermute | solution.py:36
  133.3 5.5 %collective-permute-start.24 = (bf16[2,128,128]{2,1,0:T(8,128)(2,1)S(1)}, bf16[2,128,128]{2,1,0:T(8,128)(2,1)S(1)}, u32[]{:S(2)}, u32[]{:S(2)}) collective-permute-start(bf16[2,128,128]{2,1,0:T(8,128)(2,1)S(1)} %pad_maximum_fusion.3.own), channel_id=1, source_target_pairs={{0,32},{16,48},{32,64},{48,80},{64,96},{80,112},{96,0},{112,16},{1... | collective-permute-start | bytes 196616 | tf_op jit(solution)/shard_map/ppermute | solution.py:16
  133.6 5.8 %collective-permute-start.25 = (bf16[2,128,128]{2,1,0:T(8,128)(2,1)S(1)}, bf16[2,128,128]{2,1,0:T(8,128)(2,1)S(1)}, u32[]{:S(2)}, u32[]{:S(2)}) collective-permute-start(bf16[2,128,128]{2,1,0:T(8,128)(2,1)S(1)} %pad_maximum_fusion.3.own), channel_id=1, source_target_pairs={{0,96},{16,112},{32,0},{48,16},{64,32},{80,48},{96,64},{112,80},{1... | collective-permute-start | bytes 196616 | tf_op jit(solution)/shard_map/ppermute | solution.py:16
  136.6 5.8 %collective-permute-start.26 = (bf16[2,128,128]{2,1,0:T(8,128)(2,1)S(1)}, bf16[2,128,128]{2,1,0:T(8,128)(2,1)S(1)}, u32[]{:S(2)}, u32[]{:S(2)}) collective-permute-start(bf16[2,128,128]{2,1,0:T(8,128)(2,1)S(1)} %pad_maximum_fusion.3.own), channel_id=1, source_target_pairs={{0,64},{16,80},{32,96},{48,112},{64,0},{80,16},{96,32},{112,48},{1... | collective-permute-start | bytes 196616 | tf_op jit(solution)/shard_map/ppermute | solution.py:16
  145.1 5.4 %collective-permute-start.28 = (bf16[128,128]{1,0:T(8,128)(2,1)S(1)}, bf16[128,128]{1,0:T(8,128)(2,1)S(1)}, u32[]{:S(2)}, u32[]{:S(2)}) collective-permute-start(bf16[128,128]{1,0:T(8,128)(2,1)S(1)} %get-tuple-element.74), channel_id=1, source_target_pairs={{0,2},{1,3},{2,0},{3,1},{4,6},{5,7},{6,4},{7,5},{8,10},{9,11},{10,... | collective-permute-start | bytes 98312 | tf_op jit(solution)/shard_map/ppermute | solution.py:36
  146.6 5.1 %collective-permute-start.27 = (bf16[128,128]{1,0:T(8,128)(2,1)S(1)}, bf16[128,128]{1,0:T(8,128)(2,1)S(1)}, u32[]{:S(2)}, u32[]{:S(2)}) collective-permute-start(bf16[128,128]{1,0:T(8,128)(2,1)S(1)} %get-tuple-element.73), channel_id=1, source_target_pairs={{0,1},{1,2},{2,3},{3,0},{4,5},{5,6},{6,7},{7,4},{8,9},{9,10},{10,1... | collective-permute-start | bytes 98312 | tf_op jit(solution)/shard_map/ppermute | solution.py:36
  152.6 14.0 %all-to-all-start.5 = ((bf16[16,128,128]{2,1,0:T(8,128)(2,1)}), bf16[16,128,128]{2,1,0:T(8,128)(2,1)S(1)}, u32[]{:S(2)}, u32[]{:S(2)}) async-start(bf16[16,128,128]{2,1,0:T(8,128)(2,1)} %broadcast_in_dim.8), calls=%async_computation.5 | async-start | bytes 1048576 | tf_op jit(solution)/shard_map/all_to_all | solution.py:259
  168.8 6.0 %collective-permute-start.33 = (f32[32,512]{1,0:T(8,128)S(1)}, f32[32,512]{1,0:T(8,128)S(1)}, u32[]{:S(2)}, u32[]{:S(2)}) collective-permute-start(f32[32,512]{1,0:T(8,128)S(1)} %add.192), channel_id=1, source_target_pairs={{0,64},{16,80},{32,96},{48,112},{64,0},{80,16},{96,32},{112,48},{1... | collective-permute-start | bytes 196616 | tf_op jit(solution)/shard_map/ppermute | solution.py:16
  170.5 5.5 %collective-permute-start.31 = (f32[32,512]{1,0:T(8,128)S(1)}, f32[32,512]{1,0:T(8,128)S(1)}, u32[]{:S(2)}, u32[]{:S(2)}) collective-permute-start(f32[32,512]{1,0:T(8,128)S(1)} %add.192), channel_id=1, source_target_pairs={{0,32},{16,48},{32,64},{48,80},{64,96},{80,112},{96,0},{112,16},{1... | collective-permute-start | bytes 196616 | tf_op jit(solution)/shard_map/ppermute | solution.py:16
  (12 other events, 55.9 us)

commit v11 on v10

--- a/solution.py
+++ b/solution.py
@@ -74,31 +74,34 @@
     )(inverses, inverses, coupling)
 
 
-def split_tiles_kernel(src, dst):
-    dst[:, 0] = pltpu.einshape("tbu->btu", src[0])
-
-
-def split_tiles(left):
-    rounds, tile, count, width = left.shape
-    rows = 256
-    out = pl.pallas_call(
+def split_tiles_kernel(src, token, dst):
+    del token
+    tiles = pltpu.einshape("tbu->btu", src[0])
+    for b in range(tiles.shape[0]):
+        dst[b // 3, :, 256 * (b % 3) : 256 * (b % 3 + 1)] = tiles[b]
+
+
+def split_tiles(left, half, token):
+    _, tile, count, width = left.shape
+    return pl.pallas_call(
         split_tiles_kernel,
-        grid=(rounds, tile // rows),
-        in_specs=[pl.BlockSpec((1, rows, count, width), lambda a, t: (a, t, 0, 0))],
-        out_specs=pl.BlockSpec((count, 1, rows, width), lambda a, t: (0, a, t, 0)),
-        out_shape=pltpu.HBM((count, rounds, tile, width), BF),
-        cost_estimate=cost(0, 2 * left.size * 2),
+        grid=(2,),
+        in_specs=[
+            pl.BlockSpec((1, tile, count, width), lambda a: (2 * half + a, 0, 0, 0)),
+            whole(token),
+        ],
+        out_specs=pl.BlockSpec((count // 3, tile, 3 * width), lambda a: (0, a, 0)),
+        out_shape=pltpu.HBM((count // 3, 2 * tile, 3 * width), BF),
+        cost_estimate=cost(0, left.size * 2),
         compiler_params=ROOMY,
-    )(left)
-    return out.reshape(count, rounds * tile, width)
-
-
-def accumulate(acc, left, held, step):
-    for base in (0, 512):
-        here = slice(base, base + 512)
-        total = jnp.dot(left[0, here, :], held[0], preferred_element_type=F32)
-        for t in range(1, 3):
-            total += jnp.dot(left[t, here, :], held[t], preferred_element_type=F32)
+    )(left, token)
+
+
+def accumulate(acc, halves, held, step):
+    values = held[...].reshape(768, 512)
+    for half, left in enumerate(halves):
+        here = slice(512 * half, 512 * (half + 1))
+        total = jnp.dot(left[...], values, preferred_element_type=F32)
 
         @pl.when(step == 0)
         def _():
@@ -119,15 +122,15 @@
             held[:, half:, :] = pieces[2 * j + 1][...]
 
 
-def first_products_kernel(order, left, *refs):
+def first_products_kernel(order, upper, lower, *refs):
     del order
     *pieces, acc, held = refs
     step = pl.program_id(0)
     take_pieces(step, pieces, held)
-    accumulate(acc, left, held, step)
-
-
-def next_products_kernel(order, left, before, token, *refs):
+    accumulate(acc, (upper, lower), held, step)
+
+
+def next_products_kernel(order, upper, lower, before, token, *refs):
     del order, token
     *pieces, acc, held = refs
     step = pl.program_id(0)
@@ -137,12 +140,12 @@
         acc[...] = before[...]
 
     take_pieces(step, pieces, held)
-    accumulate(acc, left, held, step + 1)
-
-
-def last_products_kernel(order, left, before, token, *refs):
+    accumulate(acc, (upper, lower), held, step + 1)
+
+
+def last_products_kernel(order, upper, lower, before, token, *refs):
     *pieces, first, second, acc, held = refs
-    next_products_kernel(order, left, before, token, *pieces, acc, held)
+    next_products_kernel(order, upper, lower, before, token, *pieces, acc, held)
 
     @pl.when(pl.program_id(0) == pl.num_programs(0) - 1)
     def _():
@@ -164,13 +167,13 @@
 
 def products(order, left, pieces, before=None, token=None, last=False):
     blocks = len(pieces) // 2
-    _, rows, width = left.shape
-    left_spec = pl.BlockSpec((3, rows, width), lambda i, order: (order[i], 0, 0))
-    left = pltpu.with_memory_space_constraint(left, pltpu.HBM)
+    rows = 1024
+    left_spec = pl.BlockSpec((None, 512, 768), lambda i, order: (order[i], 0, 0))
+    left = [in_hbm(half) for half in left]
     arrays = [array for array, _ in pieces]
     scratch = [VMEM((3, 256, 512), BF)]
     flops = blocks * 2 * rows * 768 * 512
-    moved = blocks * 3 * 2 * (rows * 256 + 256 * 512) + rows * 512 * 4
+    moved = blocks * 2 * 768 * (rows + 512) + rows * 512 * 4
     starts = [] if before is None else [before, token]
     out = jax.ShapeDtypeStruct((rows, 512), F32)
     kernel = first_products_kernel if before is None else next_products_kernel
@@ -183,14 +186,14 @@
         grid_spec=pltpu.PrefetchScalarGridSpec(
             num_scalar_prefetch=1,
             grid=(blocks,),
-            in_specs=[left_spec, *map(whole, starts), *piece_specs(pieces)],
+            in_specs=[left_spec, left_spec, *map(whole, starts), *piece_specs(pieces)],
             out_specs=jax.tree.map(whole, out),
             scratch_shapes=scratch,
         ),
         out_shape=out,
         cost_estimate=cost(flops, moved),
         compiler_params=ROOMY,
-    )(order, left, *starts, *arrays)
+    )(order, *left, *starts, *arrays)
 
 
 RELATIVE = (0, -1, 1, 2)
@@ -281,11 +284,14 @@
     lines = prepare(inverses, coupling)
     before, after = x_shift(prev_solution, 1), x_shift(prev_solution, -1)
     sibling = other_core(prev_solution)
-    left = split_tiles(in_hbm(left_factor))
-    lines = z_exchange(lines)
-    before, after, sibling, left, lines = lax.optimization_barrier(
-        (before, after, sibling, left, lines)
-    )
+    tiles = in_hbm(left_factor)
+    upper = split_tiles(tiles, 0, lines[0, 0, :16, :128])
+    lines, token = lax.optimization_barrier((z_exchange(lines), upper[0, :16, :128]))
+    lower = split_tiles(tiles, 1, token)
+    before, after, sibling, upper, lower = lax.optimization_barrier(
+        (before, after, sibling, upper, lower)
+    )
+    left = (upper, lower)
     panels = in_hbm(y_gather(lines))
     far_low, far_high = x_shift(before[:, :128, :], 1), x_shift(after[:, 128:, :], -1)
     halves = lambda v: [(in_hbm(v), 0), (in_hbm(v), 1)]

time: 178 us -> 176 us (0.989)
  waiting for transfers between devices: 68.4 us -> 62.8 us
  local copies, waits for them, and re-layouts: 5.7 us -> 7.94 us
    all_to_all x1, waiting for transfers between devices: 10.7 us -> 4.29 us  [y_gather(): lax.all_to_all(sent, 'col', 0, 0, axis_index_groups=groups, tiled=True)]
    pallas_call x1 -> x2, Pallas kernels: 10.4 us -> 10.8 us  [split_tiles(): pl.pallas_call(split_tiles_kernel, grid=(2,), in_specs=[pl.BlockSpec((1,...]
  transfers between devices with their start and end apart: 40 -> 40, of which waited for: 27 -> 27; matrix products, arithmetic and copies ran while one was open for 2% -> 5% of each run, Pallas kernels for 21% -> 20%
where the time goes in v11:
time: 176 us; the launch traced here: 175 us
  waiting for transfers between devices  62.8 us (36%)
  starting transfers between devices  61 us (35%)
  Pallas kernels  38.4 us (22%)
  local copies, waits for them, and re-layouts  7.94 us (5%)
  other arithmetic  3.16 us (2%)
    ppermute x16, starting transfers between devices, x_shift(): return lax.ppermute(v, 'row', [(r, (r + 2 * step) % 8) for r in range(8)])  22.5 us
    pallas_call x3, Pallas kernels, products(): pl.pallas_call(kernel, grid_spec=pltpu.PrefetchScalarGridSpec(num_scalar_...  20.2 us
    ppermute x9, waiting for transfers between devices, z_shift(): lax.ppermute(v, 'col', [(c, c // 4 * 4 + (c + step) % 4) for c in range(1...  16 us
    ppermute x16, waiting for transfers between devices, x_shift(): return lax.ppermute(v, 'row', [(r, (r + 2 * step) % 8) for r in range(8)])  13.3 us
    pallas_call x2, Pallas kernels, split_tiles(): pl.pallas_call(split_tiles_kernel, grid=(2,), in_specs=[pl.BlockSpec((1,...  10.8 us
    all_to_all x2, waiting for transfers between devices, over_sites(): lax.all_to_all(partial, 'col', 0, 0, tiled=True).astype(F32).sum(axis=0)  10.5 us
    ppermute x9, starting transfers between devices, z_shift(): lax.ppermute(v, 'col', [(c, c // 4 * 4 + (c + step) % 4) for c in range(1...  10.4 us
    all_to_all x2, waiting for transfers between devices, all_sites(): lax.all_to_all(sent, 'col', 0, 0, tiled=True).reshape(4, 4, 2, 64, 128)  9.7 us
  transfers between devices with their start and end apart: 40, of which 27 were waited for; matrix products, arithmetic and copies ran while one was open for 5% of the time, Pallas kernels for 20%

profile of v11, /device:TPU:0, one launch (start us, length us, event | category | flops | bytes accessed | tf_op | source)
XLA Modules:
  0.0 174.8 jit_solution(6931147941140036499)
XLA Ops:
  0.6 2.3 %shard_map.77 = bf16[4,3,64,512]{3,2,1,0:T(8,128)(2,1)} custom-call(bf16[2,512,256]{2,1,0:T(8,128)(2,1)} %bitcast.47, bf16[2,512,256]{2,1,0:T(8,128)(2,1)} %bitcast.48, bf16[512,256]{1,0:T(8,128)(2,1)} %bitcast.50), custom_call_target="tpu_custom_call" | custom-call | tf_op jit(solution)/shard_map/pallas_call | solution.py:63
  2.9 5.4 %all-to-all-start = ((bf16[4,3,64,512]{3,2,1,0:T(8,128)(2,1)}), bf16[4,3,64,512]{3,2,1,0:T(8,128)(2,1)}, u32[]{:S(2)}, u32[]{:S(2)}) async-start(bf16[4,3,64,512]{3,2,1,0:T(8,128)(2,1)} %shard_map.77), calls=%async_computation | async-start | bytes 1572864 | tf_op jit(solution)/shard_map/all_to_all | solution.py:25
  9.8 1.7 collective-permute-start.1
  12.2 5.3 %shard_map.78.upper = bf16[8,512,768]{2,1,0:T(8,128)(2,1)} custom-call(bf16[4,256,24,256]{3,2,1,0:T(8,128)(2,1)} %src.3, bf16[16,128]{1,0:T(8,128)(2,1)S(1)} %slice_bitcast_fusion.1.token), custom_call_target="tpu_custom_call" | custom-call | bytes 12582912 | tf_op jit(solution)/shard_map/pallas_call | solution.py:86
  18.2 2.4 %all-to-all-done = bf16[4,3,64,512]{3,2,1,0:T(8,128)(2,1)} async-done(((bf16[4,3,64,512]{3,2,1,0:T(8,128)(2,1)}), bf16[4,3,64,512]{3,2,1,0:T(8,128)(2,1)}, u32[]{:S(2)}, u32[]{:S(2)}) %all-to-all-start) | async-done | bytes 786464 | tf_op jit(solution)/shard_map/all_to_all | solution.py:25
  20.7 3.2 %broadcast_in_dim.6 = bf16[4,4,3,64,512]{4,3,2,1,0:T(8,128)(2,1)} broadcast(bf16[4,3,64,512]{3,2,1,0:T(8,128)(2,1)} %all-to-all-done), dimensions={1,2,3,4} | broadcast | bytes 3932160 | tf_op jit(solution)/shard_map/broadcast_in_dim | solution.py:30
  23.9 4.6 %all-to-all-start.1 = ((bf16[4,4,3,64,512]{4,3,2,1,0:T(8,128)(2,1)}), bf16[4,4,3,64,512]{4,3,2,1,0:T(8,128)(2,1)}, u32[]{:S(2)}, u32[]{:S(2)}) async-start(bf16[4,4,3,64,512]{4,3,2,1,0:T(8,128)(2,1)} %broadcast_in_dim.6), calls=%async_computation.1 | async-start | bytes 6291456 | tf_op jit(solution)/shard_map/all_to_all | solution.py:31
  28.5 5.4 %shard_map.79.lower = bf16[8,512,768]{2,1,0:T(8,128)(2,1)} custom-call(bf16[4,256,24,256]{3,2,1,0:T(8,128)(2,1)} %src.3, bf16[16,128]{1,0:T(8,128)(2,1)S(1)} %slice_bitcast_fusion.token), custom_call_target="tpu_custom_call" | custom-call | bytes 12582912 | tf_op jit(solution)/shard_map/pallas_call | solution.py:86
  36.3 1.7 collective-permute-start.6
  38.1 5.2 %shard_map.80.before = f32[1024,512]{1,0:T(8,128)S(1)} custom-call(s32[2]{0:T(128)S(1)} %pad_add_fusion.3.order, bf16[8,512,768]{2,1,0:T(8,128)(2,1)} %shard_map.78.upper, bf16[8,512,768]{2,1,0:T(8,128)(2,1)} %shard_map.79.lower, bf16[3,256,512]{2,1,0:T(8,128)(2,1)} %refs_1_.1, bf16[3,256,512]{2,1,0:T(8,128)(2,1)} %refs_1_.1, ...), custom_call_target="tpu_custom_call" | custom-call | flops 1610612736 | bytes 6815744 | tf_op jit(solution)/shard_map/pallas_call | solution.py:184
  43.4 8.9 %shard_map.81.before = f32[1024,512]{1,0:T(8,128)S(1)} custom-call(s32[4]{0:T(128)S(1)} %pad_add_fusion.2.order, bf16[8,512,768]{2,1,0:T(8,128)(2,1)} %shard_map.78.upper, bf16[8,512,768]{2,1,0:T(8,128)(2,1)} %shard_map.79.lower, f32[1024,512]{1,0:T(8,128)S(1)} %shard_map.80.before, f32[8,128]{1,0:T(8,128)S(1)} %slice.43.token, ...), custom_call_target="tpu_custom_call" | custom-call | flops 3221225472 | bytes 11534336 | tf_op jit(solution)/shard_map/pallas_call | solution.py:184
  54.8 6.1 %shard_map.82 = (bf16[16,128,128]{2,1,0:T(8,128)(2,1)}, bf16[16,128,128]{2,1,0:T(8,128)(2,1)}) custom-call(s32[2]{0:T(128)S(1)} %pad_add_fusion.1.order, bf16[8,512,768]{2,1,0:T(8,128)(2,1)} %shard_map.78.upper, bf16[8,512,768]{2,1,0:T(8,128)(2,1)} %shard_map.79.lower, f32[1024,512]{1,0:T(8,128)S(1)} %shard_map.81.before, f32[8,128]{1,0:T(8,128)S(1)} %slice.44.token, ...), custom_call_target="tpu_custom_call" | custom-call | flops 1610612736 | bytes 6815744 | tf_op jit(solution)/shard_map/pallas_call | solution.py:184
  60.9 4.3 %all-to-all-done.1 = bf16[4,4,3,64,512]{4,3,2,1,0:T(8,128)(2,1)} async-done(((bf16[4,4,3,64,512]{4,3,2,1,0:T(8,128)(2,1)}), bf16[4,4,3,64,512]{4,3,2,1,0:T(8,128)(2,1)}, u32[]{:S(2)}, u32[]{:S(2)}) %all-to-all-start.1) | async-done | bytes 3145760 | tf_op jit(solution)/shard_map/all_to_all | solution.py:31
  65.2 4.9 %all-to-all-start.2 = ((bf16[16,128,128]{2,1,0:T(8,128)(2,1)}), bf16[16,128,128]{2,1,0:T(8,128)(2,1)S(1)}, u32[]{:S(2)}, u32[]{:S(2)}) async-start(bf16[16,128,128]{2,1,0:T(8,128)(2,1)} %get-tuple-element.53), calls=%async_computation.2 | async-start | bytes 1048576 | tf_op jit(solution)/shard_map/all_to_all | solution.py:257
  71.1 10.5 %all-to-all-done.2 = bf16[16,128,128]{2,1,0:T(8,128)(2,1)S(1)} async-done(((bf16[16,128,128]{2,1,0:T(8,128)(2,1)}), bf16[16,128,128]{2,1,0:T(8,128)(2,1)S(1)}, u32[]{:S(2)}, u32[]{:S(2)}) %all-to-all-start.2) | async-done | bytes 524320 | tf_op jit(solution)/shard_map/all_to_all | solution.py:257
  83.0 3.2 %collective-permute-start.11 = (bf16[2,128,128]{2,1,0:T(8,128)(2,1)S(1)}, bf16[2,128,128]{2,1,0:T(8,128)(2,1)S(1)}, u32[]{:S(2)}, u32[]{:S(2)}) collective-permute-start(bf16[2,128,128]{2,1,0:T(8,128)(2,1)S(1)} %pad_maximum_fusion.1.own), channel_id=1, source_target_pairs={{0,96},{16,112},{32,0},{48,16},{64,32},{80,48},{96,64},{112,80},{1... | collective-permute-start | bytes 196616 | tf_op jit(solution)/shard_map/ppermute | solution.py:16
  86.3 3.6 %all-to-all-start.3 = ((bf16[16,128,128]{2,1,0:T(8,128)(2,1)}), bf16[16,128,128]{2,1,0:T(8,128)(2,1)S(1)}, u32[]{:S(2)}, u32[]{:S(2)}) async-start(bf16[16,128,128]{2,1,0:T(8,128)(2,1)} %get-tuple-element.65), calls=%async_computation.3 | async-start | bytes 1048576 | tf_op jit(solution)/shard_map/all_to_all | solution.py:257
  89.9 2.1 %collective-permute-done.12.three = bf16[2,128,128]{2,1,0:T(8,128)(2,1)S(1)} collective-permute-done((bf16[2,128,128]{2,1,0:T(8,128)(2,1)S(1)}, bf16[2,128,128]{2,1,0:T(8,128)(2,1)S(1)}, u32[]{:S(2)}, u32[]{:S(2)}) %collective-permute-start.12) | collective-permute-done | bytes 65568 | tf_op jit(solution)/shard_map/ppermute | solution.py:16
  96.7 2.5 %collective-permute-done.15 = bf16[128,128]{1,0:T(8,128)(2,1)S(1)} collective-permute-done((bf16[128,128]{1,0:T(8,128)(2,1)S(1)}, bf16[128,128]{1,0:T(8,128)(2,1)S(1)}, u32[]{:S(2)}, u32[]{:S(2)}) %collective-permute-start.15) | collective-permute-done | bytes 32800 | tf_op jit(solution)/shard_map/ppermute | solution.py:36
  99.2 2.6 %collective-permute-done.14 = bf16[128,128]{1,0:T(8,128)(2,1)S(1)} collective-permute-done((bf16[128,128]{1,0:T(8,128)(2,1)S(1)}, bf16[128,128]{1,0:T(8,128)(2,1)S(1)}, u32[]{:S(2)}, u32[]{:S(2)}) %collective-permute-start.14) | collective-permute-done | bytes 32800 | tf_op jit(solution)/shard_map/ppermute | solution.py:36
  104.0 2.6 %collective-permute-start.18 = (bf16[2,128,128]{2,1,0:T(8,128)(2,1)S(1)}, bf16[2,128,128]{2,1,0:T(8,128)(2,1)S(1)}, u32[]{:S(2)}, u32[]{:S(2)}) collective-permute-start(bf16[2,128,128]{2,1,0:T(8,128)(2,1)S(1)} %pad_maximum_fusion.2.own), channel_id=1, source_target_pairs={{0,96},{16,112},{32,0},{48,16},{64,32},{80,48},{96,64},{112,80},{1... | collective-permute-start | bytes 196616 | tf_op jit(solution)/shard_map/ppermute | solution.py:16
  106.7 1.8 %collective-permute-start.19 = (bf16[2,128,128]{2,1,0:T(8,128)(2,1)S(1)}, bf16[2,128,128]{2,1,0:T(8,128)(2,1)S(1)}, u32[]{:S(2)}, u32[]{:S(2)}) collective-permute-start(bf16[2,128,128]{2,1,0:T(8,128)(2,1)S(1)} %pad_maximum_fusion.2.own), channel_id=1, source_target_pairs={{0,64},{16,80},{32,96},{48,112},{64,0},{80,16},{96,32},{112,48},{1... | collective-permute-start | bytes 196616 | tf_op jit(solution)/shard_map/ppermute | solution.py:16
  109.6 2.8 %collective-permute-done.19.three = bf16[2,128,128]{2,1,0:T(8,128)(2,1)S(1)} collective-permute-done((bf16[2,128,128]{2,1,0:T(8,128)(2,1)S(1)}, bf16[2,128,128]{2,1,0:T(8,128)(2,1)S(1)}, u32[]{:S(2)}, u32[]{:S(2)}) %collective-permute-start.19) | collective-permute-done | bytes 65568 | tf_op jit(solution)/shard_map/ppermute | solution.py:16
  115.1 4.2 %all-to-all-start.4 = ((bf16[16,128,128]{2,1,0:T(8,128)(2,1)}), bf16[16,128,128]{2,1,0:T(8,128)(2,1)S(1)}, u32[]{:S(2)}, u32[]{:S(2)}) async-start(bf16[16,128,128]{2,1,0:T(8,128)(2,1)} %broadcast_in_dim.7), calls=%async_computation.4 | async-start | bytes 1048576 | tf_op jit(solution)/shard_map/all_to_all | solution.py:262
  119.4 3.2 %collective-permute-start.22 = (bf16[128,128]{1,0:T(8,128)(2,1)S(1)}, bf16[128,128]{1,0:T(8,128)(2,1)S(1)}, u32[]{:S(2)}, u32[]{:S(2)}) collective-permute-start(bf16[128,128]{1,0:T(8,128)(2,1)S(1)} %get-tuple-element.70), channel_id=1, source_target_pairs={{0,3},{1,0},{2,1},{3,2},{4,7},{5,4},{6,5},{7,6},{8,11},{9,8},{10,9... | collective-permute-start | bytes 98312 | tf_op jit(solution)/shard_map/ppermute | solution.py:36
  124.3 3.0 %collective-permute-done.22 = bf16[128,128]{1,0:T(8,128)(2,1)S(1)} collective-permute-done((bf16[128,128]{1,0:T(8,128)(2,1)S(1)}, bf16[128,128]{1,0:T(8,128)(2,1)S(1)}, u32[]{:S(2)}, u32[]{:S(2)}) %collective-permute-start.22) | collective-permute-done | bytes 32800 | tf_op jit(solution)/shard_map/ppermute | solution.py:36
  127.4 2.5 %collective-permute-done.21 = bf16[128,128]{1,0:T(8,128)(2,1)S(1)} collective-permute-done((bf16[128,128]{1,0:T(8,128)(2,1)S(1)}, bf16[128,128]{1,0:T(8,128)(2,1)S(1)}, u32[]{:S(2)}, u32[]{:S(2)}) %collective-permute-start.21) | collective-permute-done | bytes 32800 | tf_op jit(solution)/shard_map/ppermute | solution.py:36
  131.8 2.7 %collective-permute-start.25 = (bf16[2,128,128]{2,1,0:T(8,128)(2,1)S(1)}, bf16[2,128,128]{2,1,0:T(8,128)(2,1)S(1)}, u32[]{:S(2)}, u32[]{:S(2)}) collective-permute-start(bf16[2,128,128]{2,1,0:T(8,128)(2,1)S(1)} %pad_maximum_fusion.3.own), channel_id=1, source_target_pairs={{0,96},{16,112},{32,0},{48,16},{64,32},{80,48},{96,64},{112,80},{1... | collective-permute-start | bytes 196616 | tf_op jit(solution)/shard_map/ppermute | solution.py:16
  137.3 3.0 %collective-permute-done.26.three = bf16[2,128,128]{2,1,0:T(8,128)(2,1)S(1)} collective-permute-done((bf16[2,128,128]{2,1,0:T(8,128)(2,1)S(1)}, bf16[2,128,128]{2,1,0:T(8,128)(2,1)S(1)}, u32[]{:S(2)}, u32[]{:S(2)}) %collective-permute-start.26) | collective-permute-done | bytes 65568 | tf_op jit(solution)/shard_map/ppermute | solution.py:16
  146.0 2.4 %collective-permute-done.28 = bf16[128,128]{1,0:T(8,128)(2,1)S(1)} collective-permute-done((bf16[128,128]{1,0:T(8,128)(2,1)S(1)}, bf16[128,128]{1,0:T(8,128)(2,1)S(1)}, u32[]{:S(2)}, u32[]{:S(2)}) %collective-permute-start.28) | collective-permute-done | bytes 32800 | tf_op jit(solution)/shard_map/ppermute | solution.py:36
  150.6 3.9 %all-to-all-start.5 = ((bf16[16,128,128]{2,1,0:T(8,128)(2,1)}), bf16[16,128,128]{2,1,0:T(8,128)(2,1)S(1)}, u32[]{:S(2)}, u32[]{:S(2)}) async-start(bf16[16,128,128]{2,1,0:T(8,128)(2,1)} %broadcast_in_dim.8), calls=%async_computation.5 | async-start | bytes 1048576 | tf_op jit(solution)/shard_map/all_to_all | solution.py:262
  154.9 9.7 %all-to-all-done.5 = bf16[16,128,128]{2,1,0:T(8,128)(2,1)S(1)} async-done(((bf16[16,128,128]{2,1,0:T(8,128)(2,1)}), bf16[16,128,128]{2,1,0:T(8,128)(2,1)S(1)}, u32[]{:S(2)}, u32[]{:S(2)}) %all-to-all-start.5) | async-done | bytes 524320 | tf_op jit(solution)/shard_map/all_to_all | solution.py:262
  (101 shorter events, 45.9 us)
Async XLA Ops:
  2.9 17.8 %all-to-all-start = ((bf16[4,3,64,512]{3,2,1,0:T(8,128)(2,1)}), bf16[4,3,64,512]{3,2,1,0:T(8,128)(2,1)}, u32[]{:S(2)}, u32[]{:S(2)}) async-start(bf16[4,3,64,512]{3,2,1,0:T(8,128)(2,1)} %shard_map.77), calls=%async_computation | async-start | bytes 1572864 | tf_op jit(solution)/shard_map/all_to_all | solution.py:25
  8.3 25.6 %collective-permute-start = (bf16[3,256,512]{2,1,0:T(8,128)(2,1)}, bf16[3,256,512]{2,1,0:T(8,128)(2,1)S(1)}, u32[]{:S(2)}, u32[]{:S(2)}) collective-permute-start(bf16[3,256,512]{2,1,0:T(8,128)(2,1)} %refs_1_.1), channel_id=1, source_target_pairs={{0,32},{16,48},{32,64},{48,80},{64,96},{80,112},{96,0},{112,16},{1... | collective-permute-start | bytes 2359304 | tf_op jit(solution)/shard_map/ppermute | solution.py:16
  9.8 24.2 %collective-permute-start.1 = (bf16[3,256,512]{2,1,0:T(8,128)(2,1)}, bf16[3,256,512]{2,1,0:T(8,128)(2,1)S(1)}, u32[]{:S(2)}, u32[]{:S(2)}) collective-permute-start(bf16[3,256,512]{2,1,0:T(8,128)(2,1)} %refs_1_.1), channel_id=1, source_target_pairs={{0,96},{16,112},{32,0},{48,16},{64,32},{80,48},{96,64},{112,80},{1... | collective-permute-start | bytes 2359304 | tf_op jit(solution)/shard_map/ppermute | solution.py:16
  11.5 22.4 %collective-permute-start.2 = (bf16[3,256,512]{2,1,0:T(8,128)(2,1)}, bf16[3,256,512]{2,1,0:T(8,128)(2,1)S(1)}, u32[]{:S(2)}, u32[]{:S(2)}) collective-permute-start(bf16[3,256,512]{2,1,0:T(8,128)(2,1)} %refs_1_.1), channel_id=1, source_target_pairs={{0,16},{16,0},{32,48},{48,32},{64,80},{80,64},{96,112},{112,96},{1... | collective-permute-start | bytes 2359304 | tf_op jit(solution)/shard_map/ppermute | solution.py:20
  23.9 41.4 %all-to-all-start.1 = ((bf16[4,4,3,64,512]{4,3,2,1,0:T(8,128)(2,1)}), bf16[4,4,3,64,512]{4,3,2,1,0:T(8,128)(2,1)}, u32[]{:S(2)}, u32[]{:S(2)}) async-start(bf16[4,4,3,64,512]{4,3,2,1,0:T(8,128)(2,1)} %broadcast_in_dim.6), calls=%async_computation.1 | async-start | bytes 6291456 | tf_op jit(solution)/shard_map/all_to_all | solution.py:31
  34.0 9.4 %collective-permute-start.3 = (bf16[3,256,512]{2,1,0:T(8,128)(2,1)S(1)}, bf16[3,256,512]{2,1,0:T(8,128)(2,1)}, u32[]{:S(2)}, u32[]{:S(2)}) collective-permute-start(bf16[3,256,512]{2,1,0:T(8,128)(2,1)S(1)} %collective-permute-done.refs_0_.refs_1_), channel_id=1, source_target_pairs={{0,16},{16,0},{32,48},{48,32},{64,80},{80,64},{96,112},{112,96},{1... | collective-permute-start | bytes 2359304 | tf_op jit(solution)/shard_map/ppermute | solution.py:20
  34.1 9.3 %collective-permute-start.4 = (bf16[3,256,512]{2,1,0:T(8,128)(2,1)S(1)}, bf16[3,256,512]{2,1,0:T(8,128)(2,1)}, u32[]{:S(2)}, u32[]{:S(2)}) collective-permute-start(bf16[3,256,512]{2,1,0:T(8,128)(2,1)S(1)} %collective-permute-done.1.refs_4_.refs_5_), channel_id=1, source_target_pairs={{0,16},{16,0},{32,48},{48,32},{64,80},{80,64},{96,112},{112,96},{1... | collective-permute-start | bytes 2359304 | tf_op jit(solution)/shard_map/ppermute | solution.py:20
  34.8 17.5 %collective-permute-start.5 = (bf16[3,128,512]{2,1,0:T(8,128)(2,1)S(1)}, bf16[3,128,512]{2,1,0:T(8,128)(2,1)S(1)}, u32[]{:S(2)}, u32[]{:S(2)}) collective-permute-start(bf16[3,128,512]{2,1,0:T(8,128)(2,1)S(1)} %slice.36), channel_id=1, source_target_pairs={{0,32},{16,48},{32,64},{48,80},{64,96},{80,112},{96,0},{112,16},{1... | collective-permute-start | bytes 1179656 | tf_op jit(solution)/shard_map/ppermute | solution.py:16
  36.3 16.0 %collective-permute-start.6 = (bf16[3,128,512]{2,1,0:T(8,128)(2,1)S(1)}, bf16[3,128,512]{2,1,0:T(8,128)(2,1)S(1)}, u32[]{:S(2)}, u32[]{:S(2)}) collective-permute-start(bf16[3,128,512]{2,1,0:T(8,128)(2,1)S(1)} %slice.37), channel_id=1, source_target_pairs={{0,96},{16,112},{32,0},{48,16},{64,32},{80,48},{96,64},{112,80},{1... | collective-permute-start | bytes 1179656 | tf_op jit(solution)/shard_map/ppermute | solution.py:16
  65.2 16.3 %all-to-all-start.2 = ((bf16[16,128,128]{2,1,0:T(8,128)(2,1)}), bf16[16,128,128]{2,1,0:T(8,128)(2,1)S(1)}, u32[]{:S(2)}, u32[]{:S(2)}) async-start(bf16[16,128,128]{2,1,0:T(8,128)(2,1)} %get-tuple-element.53), calls=%async_computation.2 | async-start | bytes 1048576 | tf_op jit(solution)/shard_map/all_to_all | solution.py:257
  82.9 7.0 %collective-permute-start.10 = (bf16[2,128,128]{2,1,0:T(8,128)(2,1)S(1)}, bf16[2,128,128]{2,1,0:T(8,128)(2,1)S(1)}, u32[]{:S(2)}, u32[]{:S(2)}) collective-permute-start(bf16[2,128,128]{2,1,0:T(8,128)(2,1)S(1)} %pad_maximum_fusion.1.own), channel_id=1, source_target_pairs={{0,32},{16,48},{32,64},{48,80},{64,96},{80,112},{96,0},{112,16},{1... | collective-permute-start | bytes 196616 | tf_op jit(solution)/shard_map/ppermute | solution.py:16
  83.0 6.9 %collective-permute-start.11 = (bf16[2,128,128]{2,1,0:T(8,128)(2,1)S(1)}, bf16[2,128,128]{2,1,0:T(8,128)(2,1)S(1)}, u32[]{:S(2)}, u32[]{:S(2)}) collective-permute-start(bf16[2,128,128]{2,1,0:T(8,128)(2,1)S(1)} %pad_maximum_fusion.1.own), channel_id=1, source_target_pairs={{0,96},{16,112},{32,0},{48,16},{64,32},{80,48},{96,64},{112,80},{1... | collective-permute-start | bytes 196616 | tf_op jit(solution)/shard_map/ppermute | solution.py:16
  86.2 5.8 %collective-permute-start.12 = (bf16[2,128,128]{2,1,0:T(8,128)(2,1)S(1)}, bf16[2,128,128]{2,1,0:T(8,128)(2,1)S(1)}, u32[]{:S(2)}, u32[]{:S(2)}) collective-permute-start(bf16[2,128,128]{2,1,0:T(8,128)(2,1)S(1)} %pad_maximum_fusion.1.own), channel_id=1, source_target_pairs={{0,64},{16,80},{32,96},{48,112},{64,0},{80,16},{96,32},{112,48},{1... | collective-permute-start | bytes 196616 | tf_op jit(solution)/shard_map/ppermute | solution.py:16
  86.3 27.9 %all-to-all-start.3 = ((bf16[16,128,128]{2,1,0:T(8,128)(2,1)}), bf16[16,128,128]{2,1,0:T(8,128)(2,1)S(1)}, u32[]{:S(2)}, u32[]{:S(2)}) async-start(bf16[16,128,128]{2,1,0:T(8,128)(2,1)} %get-tuple-element.65), calls=%async_computation.3 | async-start | bytes 1048576 | tf_op jit(solution)/shard_map/all_to_all | solution.py:257
  93.7 5.4 %collective-permute-start.15 = (bf16[128,128]{1,0:T(8,128)(2,1)S(1)}, bf16[128,128]{1,0:T(8,128)(2,1)S(1)}, u32[]{:S(2)}, u32[]{:S(2)}) collective-permute-start(bf16[128,128]{1,0:T(8,128)(2,1)S(1)} %get-tuple-element.60), channel_id=1, source_target_pairs={{0,3},{1,0},{2,1},{3,2},{4,7},{5,4},{6,5},{7,6},{8,11},{9,8},{10,9... | collective-permute-start | bytes 98312 | tf_op jit(solution)/shard_map/ppermute | solution.py:36
  95.0 6.8 %collective-permute-start.14 = (bf16[128,128]{1,0:T(8,128)(2,1)S(1)}, bf16[128,128]{1,0:T(8,128)(2,1)S(1)}, u32[]{:S(2)}, u32[]{:S(2)}) collective-permute-start(bf16[128,128]{1,0:T(8,128)(2,1)S(1)} %get-tuple-element.59), channel_id=1, source_target_pairs={{0,2},{1,3},{2,0},{3,1},{4,6},{5,7},{6,4},{7,5},{8,10},{9,11},{10,... | collective-permute-start | bytes 98312 | tf_op jit(solution)/shard_map/ppermute | solution.py:36
  96.6 5.4 %collective-permute-start.13 = (bf16[128,128]{1,0:T(8,128)(2,1)S(1)}, bf16[128,128]{1,0:T(8,128)(2,1)S(1)}, u32[]{:S(2)}, u32[]{:S(2)}) collective-permute-start(bf16[128,128]{1,0:T(8,128)(2,1)S(1)} %get-tuple-element.58), channel_id=1, source_target_pairs={{0,1},{1,2},{2,3},{3,0},{4,5},{5,6},{6,7},{7,4},{8,9},{9,10},{10,1... | collective-permute-start | bytes 98312 | tf_op jit(solution)/shard_map/ppermute | solution.py:36
  103.4 5.5 %collective-permute-start.17 = (bf16[2,128,128]{2,1,0:T(8,128)(2,1)S(1)}, bf16[2,128,128]{2,1,0:T(8,128)(2,1)S(1)}, u32[]{:S(2)}, u32[]{:S(2)}) collective-permute-start(bf16[2,128,128]{2,1,0:T(8,128)(2,1)S(1)} %pad_maximum_fusion.2.own), channel_id=1, source_target_pairs={{0,32},{16,48},{32,64},{48,80},{64,96},{80,112},{96,0},{112,16},{1... | collective-permute-start | bytes 196616 | tf_op jit(solution)/shard_map/ppermute | solution.py:16
  104.0 5.6 %collective-permute-start.18 = (bf16[2,128,128]{2,1,0:T(8,128)(2,1)S(1)}, bf16[2,128,128]{2,1,0:T(8,128)(2,1)S(1)}, u32[]{:S(2)}, u32[]{:S(2)}) collective-permute-start(bf16[2,128,128]{2,1,0:T(8,128)(2,1)S(1)} %pad_maximum_fusion.2.own), channel_id=1, source_target_pairs={{0,96},{16,112},{32,0},{48,16},{64,32},{80,48},{96,64},{112,80},{1... | collective-permute-start | bytes 196616 | tf_op jit(solution)/shard_map/ppermute | solution.py:16
  106.7 5.8 %collective-permute-start.19 = (bf16[2,128,128]{2,1,0:T(8,128)(2,1)S(1)}, bf16[2,128,128]{2,1,0:T(8,128)(2,1)S(1)}, u32[]{:S(2)}, u32[]{:S(2)}) collective-permute-start(bf16[2,128,128]{2,1,0:T(8,128)(2,1)S(1)} %pad_maximum_fusion.2.own), channel_id=1, source_target_pairs={{0,64},{16,80},{32,96},{48,112},{64,0},{80,16},{96,32},{112,48},{1... | collective-permute-start | bytes 196616 | tf_op jit(solution)/shard_map/ppermute | solution.py:16
  115.1 20.5 %all-to-all-start.4 = ((bf16[16,128,128]{2,1,0:T(8,128)(2,1)}), bf16[16,128,128]{2,1,0:T(8,128)(2,1)S(1)}, u32[]{:S(2)}, u32[]{:S(2)}) async-start(bf16[16,128,128]{2,1,0:T(8,128)(2,1)} %broadcast_in_dim.7), calls=%async_computation.4 | async-start | bytes 1048576 | tf_op jit(solution)/shard_map/all_to_all | solution.py:262
  119.4 8.0 %collective-permute-start.22 = (bf16[128,128]{1,0:T(8,128)(2,1)S(1)}, bf16[128,128]{1,0:T(8,128)(2,1)S(1)}, u32[]{:S(2)}, u32[]{:S(2)}) collective-permute-start(bf16[128,128]{1,0:T(8,128)(2,1)S(1)} %get-tuple-element.70), channel_id=1, source_target_pairs={{0,3},{1,0},{2,1},{3,2},{4,7},{5,4},{6,5},{7,6},{8,11},{9,8},{10,9... | collective-permute-start | bytes 98312 | tf_op jit(solution)/shard_map/ppermute | solution.py:36
  122.6 7.3 %collective-permute-start.21 = (bf16[128,128]{1,0:T(8,128)(2,1)S(1)}, bf16[128,128]{1,0:T(8,128)(2,1)S(1)}, u32[]{:S(2)}, u32[]{:S(2)}) collective-permute-start(bf16[128,128]{1,0:T(8,128)(2,1)S(1)} %get-tuple-element.69), channel_id=1, source_target_pairs={{0,2},{1,3},{2,0},{3,1},{4,6},{5,7},{6,4},{7,5},{8,10},{9,11},{10,... | collective-permute-start | bytes 98312 | tf_op jit(solution)/shard_map/ppermute | solution.py:36
  123.4 6.4 %collective-permute-start.20 = (bf16[128,128]{1,0:T(8,128)(2,1)S(1)}, bf16[128,128]{1,0:T(8,128)(2,1)S(1)}, u32[]{:S(2)}, u32[]{:S(2)}) collective-permute-start(bf16[128,128]{1,0:T(8,128)(2,1)S(1)} %get-tuple-element.68), channel_id=1, source_target_pairs={{0,1},{1,2},{2,3},{3,0},{4,5},{5,6},{6,7},{7,4},{8,9},{9,10},{10,1... | collective-permute-start | bytes 98312 | tf_op jit(solution)/shard_map/ppermute | solution.py:36
  131.2 5.5 %collective-permute-start.24 = (bf16[2,128,128]{2,1,0:T(8,128)(2,1)S(1)}, bf16[2,128,128]{2,1,0:T(8,128)(2,1)S(1)}, u32[]{:S(2)}, u32[]{:S(2)}) collective-permute-start(bf16[2,128,128]{2,1,0:T(8,128)(2,1)S(1)} %pad_maximum_fusion.3.own), channel_id=1, source_target_pairs={{0,32},{16,48},{32,64},{48,80},{64,96},{80,112},{96,0},{112,16},{1... | collective-permute-start | bytes 196616 | tf_op jit(solution)/shard_map/ppermute | solution.py:16
  131.8 5.5 %collective-permute-start.25 = (bf16[2,128,128]{2,1,0:T(8,128)(2,1)S(1)}, bf16[2,128,128]{2,1,0:T(8,128)(2,1)S(1)}, u32[]{:S(2)}, u32[]{:S(2)}) collective-permute-start(bf16[2,128,128]{2,1,0:T(8,128)(2,1)S(1)} %pad_maximum_fusion.3.own), channel_id=1, source_target_pairs={{0,96},{16,112},{32,0},{48,16},{64,32},{80,48},{96,64},{112,80},{1... | collective-permute-start | bytes 196616 | tf_op jit(solution)/shard_map/ppermute | solution.py:16
  134.5 5.8 %collective-permute-start.26 = (bf16[2,128,128]{2,1,0:T(8,128)(2,1)S(1)}, bf16[2,128,128]{2,1,0:T(8,128)(2,1)S(1)}, u32[]{:S(2)}, u32[]{:S(2)}) collective-permute-start(bf16[2,128,128]{2,1,0:T(8,128)(2,1)S(1)} %pad_maximum_fusion.3.own), channel_id=1, source_target_pairs={{0,64},{16,80},{32,96},{48,112},{64,0},{80,16},{96,32},{112,48},{1... | collective-permute-start | bytes 196616 | tf_op jit(solution)/shard_map/ppermute | solution.py:16
  143.0 5.4 %collective-permute-start.28 = (bf16[128,128]{1,0:T(8,128)(2,1)S(1)}, bf16[128,128]{1,0:T(8,128)(2,1)S(1)}, u32[]{:S(2)}, u32[]{:S(2)}) collective-permute-start(bf16[128,128]{1,0:T(8,128)(2,1)S(1)} %get-tuple-element.78), channel_id=1, source_target_pairs={{0,2},{1,3},{2,0},{3,1},{4,6},{5,7},{6,4},{7,5},{8,10},{9,11},{10,... | collective-permute-start | bytes 98312 | tf_op jit(solution)/shard_map/ppermute | solution.py:36
  144.5 5.1 %collective-permute-start.27 = (bf16[128,128]{1,0:T(8,128)(2,1)S(1)}, bf16[128,128]{1,0:T(8,128)(2,1)S(1)}, u32[]{:S(2)}, u32[]{:S(2)}) collective-permute-start(bf16[128,128]{1,0:T(8,128)(2,1)S(1)} %get-tuple-element.77), channel_id=1, source_target_pairs={{0,1},{1,2},{2,3},{3,0},{4,5},{5,6},{6,7},{7,4},{8,9},{9,10},{10,1... | collective-permute-start | bytes 98312 | tf_op jit(solution)/shard_map/ppermute | solution.py:36
  150.6 14.0 %all-to-all-start.5 = ((bf16[16,128,128]{2,1,0:T(8,128)(2,1)}), bf16[16,128,128]{2,1,0:T(8,128)(2,1)S(1)}, u32[]{:S(2)}, u32[]{:S(2)}) async-start(bf16[16,128,128]{2,1,0:T(8,128)(2,1)} %broadcast_in_dim.8), calls=%async_computation.5 | async-start | bytes 1048576 | tf_op jit(solution)/shard_map/all_to_all | solution.py:262
  166.8 5.9 %collective-permute-start.33 = (f32[32,512]{1,0:T(8,128)S(1)}, f32[32,512]{1,0:T(8,128)S(1)}, u32[]{:S(2)}, u32[]{:S(2)}) collective-permute-start(f32[32,512]{1,0:T(8,128)S(1)} %add.192), channel_id=1, source_target_pairs={{0,64},{16,80},{32,96},{48,112},{64,0},{80,16},{96,32},{112,48},{1... | collective-permute-start | bytes 196616 | tf_op jit(solution)/shard_map/ppermute | solution.py:16
  168.7 5.5 %collective-permute-start.31 = (f32[32,512]{1,0:T(8,128)S(1)}, f32[32,512]{1,0:T(8,128)S(1)}, u32[]{:S(2)}, u32[]{:S(2)}) collective-permute-start(f32[32,512]{1,0:T(8,128)S(1)} %add.192), channel_id=1, source_target_pairs={{0,32},{16,48},{32,64},{48,80},{64,96},{80,112},{96,0},{112,16},{1... | collective-permute-start | bytes 196616 | tf_op jit(solution)/shard_map/ppermute | solution.py:16
  (12 other events, 79.1 us)

commit v12 on v11

--- a/solution.py
+++ b/solution.py
@@ -228,8 +228,8 @@
 SCALARS = pl.BlockSpec(memory_space=pltpu.SMEM)
 
 
-def stage(order, targets, values, panels, which):
-    moved = over_chips(over_cores(values))
+def stage(order, targets, pair, panels, which):
+    moved = over_chips(pair)
     out = [jax.ShapeDtypeStruct((128, 128), BF)] * 4
     return pl.pallas_call(
         stage_kernel,
@@ -296,12 +296,9 @@
     far_low, far_high = x_shift(before[:, :128, :], 1), x_shift(after[:, 128:, :], -1)
     halves = lambda v: [(in_hbm(v), 0), (in_hbm(v), 1)]
     pieces = halves(prev_solution) + halves(sibling)
-    started = products(order[:2], left, pieces)
-    token = started[:8, :128]
-    pieces = []
     for block in (before, after):
         pieces += halves(block) + halves(other_core(block))
-    started = products(order[2:6], left, pieces, started, token)
+    started = products(order[:6], left, pieces)
     far_low, far_high, token = lax.optimization_barrier(
         (far_low, far_high, started[:8, :128])
     )
@@ -316,14 +313,13 @@
     first_rhs = (known[0] - over_sites(first)).astype(BF)
     first_rhs, second = lax.optimization_barrier((first_rhs, second))
     rest = known[1] - over_sites(second)
-    solved_first = over_z(stage(order, targets, first_rhs, panels, 0)).astype(BF)
+    solved_first = over_z(stage(order, targets, over_cores(first_rhs), panels, 0)).astype(BF)
+    pair, rest = lax.optimization_barrier((over_cores(solved_first), rest))
     every_first = all_sites(solved_first)
-    *parts, rest = lax.optimization_barrier(
-        (*stage(order, targets, solved_first, panels, 1), rest)
-    )
+    parts = stage(order, targets, pair, panels, 1)
     second_rhs = (rest - over_z(parts)).astype(BF)
     *parts, every_first = lax.optimization_barrier(
-        (*stage(order, targets, second_rhs, panels, 2), every_first)
+        (*stage(order, targets, over_cores(second_rhs), panels, 2), every_first)
     )
     solved_second = over_z(parts).astype(BF)
     every_second = all_sites(solved_second)

time: 176 us -> 174 us (0.989)
  starting transfers between devices: 61 us -> 64.7 us
  waiting for transfers between devices: 62.8 us -> 60.4 us
    all_to_all x1, waiting for transfers between devices: 4.29 us -> 6.17 us  [y_gather(): lax.all_to_all(sent, 'col', 0, 0, axis_index_groups=groups, tiled=True)]
    ppermute x9, starting transfers between devices: 10.4 us -> 12.2 us  [z_shift(): lax.ppermute(v, 'col', [(c, c // 4 * 4 + (c + step) % 4) for c in range(1...]
    pallas_call x3 -> x2, Pallas kernels: 20.2 us -> 18.5 us  [products(): pl.pallas_call(kernel, grid_spec=pltpu.PrefetchScalarGridSpec(num_scalar_...]
  transfers between devices with their start and end apart: 40 -> 40, of which waited for: 27 -> 24; matrix products, arithmetic and copies ran while one was open for 5% -> 4% of each run, Pallas kernels for 20% -> 19%
where the time goes in v12:
time: 174 us; the launch traced here: 173 us
  starting transfers between devices  64.7 us (37%)
  waiting for transfers between devices  60.4 us (35%)
  Pallas kernels  36.7 us (21%)
  local copies, waits for them, and re-layouts  6.87 us (4%)
  other arithmetic  3.01 us (2%)
    ppermute x16, starting transfers between devices, x_shift(): return lax.ppermute(v, 'row', [(r, (r + 2 * step) % 8) for r in range(8)])  22.8 us
    pallas_call x2, Pallas kernels, products(): pl.pallas_call(kernel, grid_spec=pltpu.PrefetchScalarGridSpec(num_scalar_...  18.5 us
    ppermute x9, waiting for transfers between devices, z_shift(): lax.ppermute(v, 'col', [(c, c // 4 * 4 + (c + step) % 4) for c in range(1...  14.4 us
    ppermute x9, starting transfers between devices, z_shift(): lax.ppermute(v, 'col', [(c, c // 4 * 4 + (c + step) % 4) for c in range(1...  12.2 us
    ppermute x16, waiting for transfers between devices, x_shift(): return lax.ppermute(v, 'row', [(r, (r + 2 * step) % 8) for r in range(8)])  11.9 us
    pallas_call x2, Pallas kernels, split_tiles(): pl.pallas_call(split_tiles_kernel, grid=(2,), in_specs=[pl.BlockSpec((1,...  10.8 us
    all_to_all x2, waiting for transfers between devices, over_sites(): lax.all_to_all(partial, 'col', 0, 0, tiled=True).astype(F32).sum(axis=0)  10.5 us
    all_to_all x2, waiting for transfers between devices, all_sites(): lax.all_to_all(sent, 'col', 0, 0, tiled=True).reshape(4, 4, 2, 64, 128)  9.7 us
  transfers between devices with their start and end apart: 40, of which 24 were waited for; matrix products, arithmetic and copies ran while one was open for 4% of the time, Pallas kernels for 19%

profile of v12, /device:TPU:0, one launch (start us, length us, event | category | flops | bytes accessed | tf_op | source)
XLA Modules:
  0.0 173.3 jit_solution(7963584677559654419)
XLA Ops:
  0.6 2.3 %shard_map.77 = bf16[4,3,64,512]{3,2,1,0:T(8,128)(2,1)} custom-call(bf16[2,512,256]{2,1,0:T(8,128)(2,1)} %bitcast.47, bf16[2,512,256]{2,1,0:T(8,128)(2,1)} %bitcast.48, bf16[512,256]{1,0:T(8,128)(2,1)} %bitcast.50), custom_call_target="tpu_custom_call" | custom-call | tf_op jit(solution)/shard_map/pallas_call | solution.py:63
  2.9 5.4 %all-to-all-start = ((bf16[4,3,64,512]{3,2,1,0:T(8,128)(2,1)}), bf16[4,3,64,512]{3,2,1,0:T(8,128)(2,1)S(1)}, u32[]{:S(2)}, u32[]{:S(2)}) async-start(bf16[4,3,64,512]{3,2,1,0:T(8,128)(2,1)} %shard_map.77), calls=%async_computation | async-start | bytes 1572864 | tf_op jit(solution)/shard_map/all_to_all | solution.py:25
  9.8 1.7 %collective-permute-start.1 = (bf16[3,256,512]{2,1,0:T(8,128)(2,1)}, bf16[3,256,512]{2,1,0:T(8,128)(2,1)S(1)}, u32[]{:S(2)}, u32[]{:S(2)}) collective-permute-start(bf16[3,256,512]{2,1,0:T(8,128)(2,1)} %refs_1_.1), channel_id=1, source_target_pairs={{0,96},{16,112},{32,0},{48,16},{64,32},{80,48},{96,64},{112,80},{1... | collective-permute-start | bytes 2359304 | tf_op jit(solution)/shard_map/ppermute | solution.py:16
  12.2 5.4 %shard_map.78.upper = bf16[8,512,768]{2,1,0:T(8,128)(2,1)} custom-call(bf16[4,256,24,256]{3,2,1,0:T(8,128)(2,1)} %src.3, bf16[16,128]{1,0:T(8,128)(2,1)S(1)} %slice_bitcast_fusion.1.token), custom_call_target="tpu_custom_call" | custom-call | bytes 12582912 | tf_op jit(solution)/shard_map/pallas_call | solution.py:86
  18.3 2.3 %all-to-all-done = bf16[4,3,64,512]{3,2,1,0:T(8,128)(2,1)S(1)} async-done(((bf16[4,3,64,512]{3,2,1,0:T(8,128)(2,1)}), bf16[4,3,64,512]{3,2,1,0:T(8,128)(2,1)S(1)}, u32[]{:S(2)}, u32[]{:S(2)}) %all-to-all-start) | async-done | bytes 786464 | tf_op jit(solution)/shard_map/all_to_all | solution.py:25
  20.6 2.0 %broadcast_in_dim.6 = bf16[4,4,3,64,512]{4,3,2,1,0:T(8,128)(2,1)} broadcast(bf16[4,3,64,512]{3,2,1,0:T(8,128)(2,1)S(1)} %all-to-all-done), dimensions={1,2,3,4} | broadcast | bytes 3932160 | tf_op jit(solution)/shard_map/broadcast_in_dim | solution.py:30
  22.6 4.6 %all-to-all-start.1 = ((bf16[4,4,3,64,512]{4,3,2,1,0:T(8,128)(2,1)}), bf16[4,4,3,64,512]{4,3,2,1,0:T(8,128)(2,1)}, u32[]{:S(2)}, u32[]{:S(2)}) async-start(bf16[4,4,3,64,512]{4,3,2,1,0:T(8,128)(2,1)} %broadcast_in_dim.6), calls=%async_computation.1 | async-start | bytes 6291456 | tf_op jit(solution)/shard_map/all_to_all | solution.py:31
  27.2 5.4 %shard_map.79.lower = bf16[8,512,768]{2,1,0:T(8,128)(2,1)} custom-call(bf16[4,256,24,256]{3,2,1,0:T(8,128)(2,1)} %src.3, bf16[16,128]{1,0:T(8,128)(2,1)S(1)} %slice_bitcast_fusion.token), custom_call_target="tpu_custom_call" | custom-call | bytes 12582912 | tf_op jit(solution)/shard_map/pallas_call | solution.py:86
  36.8 12.4 %shard_map.80.before = f32[1024,512]{1,0:T(8,128)S(1)} custom-call(s32[6]{0:T(128)S(1)} %stack.88.order, bf16[8,512,768]{2,1,0:T(8,128)(2,1)} %shard_map.78.upper, bf16[8,512,768]{2,1,0:T(8,128)(2,1)} %shard_map.79.lower, bf16[3,256,512]{2,1,0:T(8,128)(2,1)} %refs_1_.1, bf16[3,256,512]{2,1,0:T(8,128)(2,1)} %refs_1_.1, ...), custom_call_target="tpu_custom_call" | custom-call | flops 4831838208 | bytes 16252928 | tf_op jit(solution)/shard_map/pallas_call | solution.py:184
  51.7 6.1 %shard_map.81 = (bf16[16,128,128]{2,1,0:T(8,128)(2,1)}, bf16[16,128,128]{2,1,0:T(8,128)(2,1)}) custom-call(s32[2]{0:T(128)S(1)} %pad_add_fusion.1.order, bf16[8,512,768]{2,1,0:T(8,128)(2,1)} %shard_map.78.upper, bf16[8,512,768]{2,1,0:T(8,128)(2,1)} %shard_map.79.lower, f32[1024,512]{1,0:T(8,128)S(1)} %shard_map.80.before, f32[8,128]{1,0:T(8,128)S(1)} %slice.37.token, ...), custom_call_target="tpu_custom_call" | custom-call | flops 1610612736 | bytes 6815744 | tf_op jit(solution)/shard_map/pallas_call | solution.py:184
  57.8 6.2 %all-to-all-done.1 = bf16[4,4,3,64,512]{4,3,2,1,0:T(8,128)(2,1)} async-done(((bf16[4,4,3,64,512]{4,3,2,1,0:T(8,128)(2,1)}), bf16[4,4,3,64,512]{4,3,2,1,0:T(8,128)(2,1)}, u32[]{:S(2)}, u32[]{:S(2)}) %all-to-all-start.1) | async-done | bytes 3145760 | tf_op jit(solution)/shard_map/all_to_all | solution.py:31
  64.0 5.1 %all-to-all-start.2 = ((bf16[16,128,128]{2,1,0:T(8,128)(2,1)}), bf16[16,128,128]{2,1,0:T(8,128)(2,1)S(1)}, u32[]{:S(2)}, u32[]{:S(2)}) async-start(bf16[16,128,128]{2,1,0:T(8,128)(2,1)} %get-tuple-element.50), calls=%async_computation.2 | async-start | bytes 1048576 | tf_op jit(solution)/shard_map/all_to_all | solution.py:257
  70.0 10.5 %all-to-all-done.2 = bf16[16,128,128]{2,1,0:T(8,128)(2,1)S(1)} async-done(((bf16[16,128,128]{2,1,0:T(8,128)(2,1)}), bf16[16,128,128]{2,1,0:T(8,128)(2,1)S(1)}, u32[]{:S(2)}, u32[]{:S(2)}) %all-to-all-start.2) | async-done | bytes 524320 | tf_op jit(solution)/shard_map/all_to_all | solution.py:257
  80.7 3.6 %all-to-all-start.3 = ((bf16[16,128,128]{2,1,0:T(8,128)(2,1)}), bf16[16,128,128]{2,1,0:T(8,128)(2,1)S(1)}, u32[]{:S(2)}, u32[]{:S(2)}) async-start(bf16[16,128,128]{2,1,0:T(8,128)(2,1)} %get-tuple-element.58), calls=%async_computation.3 | async-start | bytes 1048576 | tf_op jit(solution)/shard_map/all_to_all | solution.py:257
  84.4 3.2 %collective-permute-start.11 = (bf16[2,128,128]{2,1,0:T(8,128)(2,1)S(1)}, bf16[2,128,128]{2,1,0:T(8,128)(2,1)S(1)}, u32[]{:S(2)}, u32[]{:S(2)}) collective-permute-start(bf16[2,128,128]{2,1,0:T(8,128)(2,1)S(1)} %pad_maximum_fusion.1.own), channel_id=1, source_target_pairs={{0,96},{16,112},{32,0},{48,16},{64,32},{80,48},{96,64},{112,80},{1... | collective-permute-start | bytes 196616 | tf_op jit(solution)/shard_map/ppermute | solution.py:16
  87.7 2.4 %collective-permute-done.10.one = bf16[2,128,128]{2,1,0:T(8,128)(2,1)S(1)} collective-permute-done((bf16[2,128,128]{2,1,0:T(8,128)(2,1)S(1)}, bf16[2,128,128]{2,1,0:T(8,128)(2,1)S(1)}, u32[]{:S(2)}, u32[]{:S(2)}) %collective-permute-start.10) | collective-permute-done | bytes 65568 | tf_op jit(solution)/shard_map/ppermute | solution.py:16
  90.8 2.6 %collective-permute-done.12.three = bf16[2,128,128]{2,1,0:T(8,128)(2,1)S(1)} collective-permute-done((bf16[2,128,128]{2,1,0:T(8,128)(2,1)S(1)}, bf16[2,128,128]{2,1,0:T(8,128)(2,1)S(1)}, u32[]{:S(2)}, u32[]{:S(2)}) %collective-permute-start.12) | collective-permute-done | bytes 65568 | tf_op jit(solution)/shard_map/ppermute | solution.py:16
  95.1 3.1 %collective-permute-start.15 = (bf16[128,128]{1,0:T(8,128)(2,1)S(1)}, bf16[128,128]{1,0:T(8,128)(2,1)S(1)}, u32[]{:S(2)}, u32[]{:S(2)}) collective-permute-start(bf16[128,128]{1,0:T(8,128)(2,1)S(1)} %get-tuple-element.57), channel_id=1, source_target_pairs={{0,3},{1,0},{2,1},{3,2},{4,7},{5,4},{6,5},{7,6},{8,11},{9,8},{10,9... | collective-permute-start | bytes 98312 | tf_op jit(solution)/shard_map/ppermute | solution.py:36
  100.0 3.7 %collective-permute-done.14 = bf16[128,128]{1,0:T(8,128)(2,1)S(1)} collective-permute-done((bf16[128,128]{1,0:T(8,128)(2,1)S(1)}, bf16[128,128]{1,0:T(8,128)(2,1)S(1)}, u32[]{:S(2)}, u32[]{:S(2)}) %collective-permute-start.14) | collective-permute-done | bytes 32800 | tf_op jit(solution)/shard_map/ppermute | solution.py:36
  105.9 3.2 %collective-permute-start.18 = (bf16[2,128,128]{2,1,0:T(8,128)(2,1)S(1)}, bf16[2,128,128]{2,1,0:T(8,128)(2,1)S(1)}, u32[]{:S(2)}, u32[]{:S(2)}) collective-permute-start(bf16[2,128,128]{2,1,0:T(8,128)(2,1)S(1)} %pad_maximum_fusion.2.own), channel_id=1, source_target_pairs={{0,96},{16,112},{32,0},{48,16},{64,32},{80,48},{96,64},{112,80},{1... | collective-permute-start | bytes 196616 | tf_op jit(solution)/shard_map/ppermute | solution.py:16
  110.0 5.3 %all-to-all-start.4 = ((bf16[16,128,128]{2,1,0:T(8,128)(2,1)}), bf16[16,128,128]{2,1,0:T(8,128)(2,1)S(1)}, u32[]{:S(2)}, u32[]{:S(2)}) async-start(bf16[16,128,128]{2,1,0:T(8,128)(2,1)} %broadcast_in_dim.7), calls=%async_computation.4 | async-start | bytes 1048576 | tf_op jit(solution)/shard_map/all_to_all | solution.py:262
  117.1 3.2 %collective-permute-start.22 = (bf16[128,128]{1,0:T(8,128)(2,1)S(1)}, bf16[128,128]{1,0:T(8,128)(2,1)S(1)}, u32[]{:S(2)}, u32[]{:S(2)}) collective-permute-start(bf16[128,128]{1,0:T(8,128)(2,1)S(1)} %get-tuple-element.64), channel_id=1, source_target_pairs={{0,3},{1,0},{2,1},{3,2},{4,7},{5,4},{6,5},{7,6},{8,11},{9,8},{10,9... | collective-permute-start | bytes 98312 | tf_op jit(solution)/shard_map/ppermute | solution.py:36
  122.0 2.6 %collective-permute-done.22 = bf16[128,128]{1,0:T(8,128)(2,1)S(1)} collective-permute-done((bf16[128,128]{1,0:T(8,128)(2,1)S(1)}, bf16[128,128]{1,0:T(8,128)(2,1)S(1)}, u32[]{:S(2)}, u32[]{:S(2)}) %collective-permute-start.22) | collective-permute-done | bytes 32800 | tf_op jit(solution)/shard_map/ppermute | solution.py:36
  124.6 2.4 %collective-permute-done.21 = bf16[128,128]{1,0:T(8,128)(2,1)S(1)} collective-permute-done((bf16[128,128]{1,0:T(8,128)(2,1)S(1)}, bf16[128,128]{1,0:T(8,128)(2,1)S(1)}, u32[]{:S(2)}, u32[]{:S(2)}) %collective-permute-start.21) | collective-permute-done | bytes 32800 | tf_op jit(solution)/shard_map/ppermute | solution.py:36
  129.3 2.4 %collective-permute-start.25 = (bf16[2,128,128]{2,1,0:T(8,128)(2,1)S(1)}, bf16[2,128,128]{2,1,0:T(8,128)(2,1)S(1)}, u32[]{:S(2)}, u32[]{:S(2)}) collective-permute-start(bf16[2,128,128]{2,1,0:T(8,128)(2,1)S(1)} %pad_maximum_fusion.3.own), channel_id=1, source_target_pairs={{0,96},{16,112},{32,0},{48,16},{64,32},{80,48},{96,64},{112,80},{1... | collective-permute-start | bytes 196616 | tf_op jit(solution)/shard_map/ppermute | solution.py:16
  131.7 1.9 %collective-permute-start.26 = (bf16[2,128,128]{2,1,0:T(8,128)(2,1)S(1)}, bf16[2,128,128]{2,1,0:T(8,128)(2,1)S(1)}, u32[]{:S(2)}, u32[]{:S(2)}) collective-permute-start(bf16[2,128,128]{2,1,0:T(8,128)(2,1)S(1)} %pad_maximum_fusion.3.own), channel_id=1, source_target_pairs={{0,64},{16,80},{32,96},{48,112},{64,0},{80,16},{96,32},{112,48},{1... | collective-permute-start | bytes 196616 | tf_op jit(solution)/shard_map/ppermute | solution.py:16
  134.7 2.7 %collective-permute-done.26.three = bf16[2,128,128]{2,1,0:T(8,128)(2,1)S(1)} collective-permute-done((bf16[2,128,128]{2,1,0:T(8,128)(2,1)S(1)}, bf16[2,128,128]{2,1,0:T(8,128)(2,1)S(1)}, u32[]{:S(2)}, u32[]{:S(2)}) %collective-permute-start.26) | collective-permute-done | bytes 65568 | tf_op jit(solution)/shard_map/ppermute | solution.py:16
  143.2 2.8 %collective-permute-done.28 = bf16[128,128]{1,0:T(8,128)(2,1)S(1)} collective-permute-done((bf16[128,128]{1,0:T(8,128)(2,1)S(1)}, bf16[128,128]{1,0:T(8,128)(2,1)S(1)}, u32[]{:S(2)}, u32[]{:S(2)}) %collective-permute-start.28) | collective-permute-done | bytes 32800 | tf_op jit(solution)/shard_map/ppermute | solution.py:36
  147.7 4.2 %all-to-all-start.5 = ((bf16[16,128,128]{2,1,0:T(8,128)(2,1)}), bf16[16,128,128]{2,1,0:T(8,128)(2,1)S(1)}, u32[]{:S(2)}, u32[]{:S(2)}) async-start(bf16[16,128,128]{2,1,0:T(8,128)(2,1)} %broadcast_in_dim.8), calls=%async_computation.5 | async-start | bytes 1048576 | tf_op jit(solution)/shard_map/all_to_all | solution.py:262
  152.2 9.7 %all-to-all-done.5 = bf16[16,128,128]{2,1,0:T(8,128)(2,1)S(1)} async-done(((bf16[16,128,128]{2,1,0:T(8,128)(2,1)}), bf16[16,128,128]{2,1,0:T(8,128)(2,1)S(1)}, u32[]{:S(2)}, u32[]{:S(2)}) %all-to-all-start.5) | async-done | bytes 524320 | tf_op jit(solution)/shard_map/all_to_all | solution.py:262
  164.1 2.4 %collective-permute-start.33 = (f32[32,512]{1,0:T(8,128)S(1)}, f32[32,512]{1,0:T(8,128)S(1)}, u32[]{:S(2)}, u32[]{:S(2)}) collective-permute-start(f32[32,512]{1,0:T(8,128)S(1)} %add.192), channel_id=1, source_target_pairs={{0,64},{16,80},{32,96},{48,112},{64,0},{80,16},{96,32},{112,48},{1... | collective-permute-start | bytes 196616 | tf_op jit(solution)/shard_map/ppermute | solution.py:16
  170.8 1.8 %collective-permute-done.31 = f32[32,512]{1,0:T(8,128)S(1)} collective-permute-done((f32[32,512]{1,0:T(8,128)S(1)}, f32[32,512]{1,0:T(8,128)S(1)}, u32[]{:S(2)}, u32[]{:S(2)}) %collective-permute-start.31) | collective-permute-done | bytes 65568 | tf_op jit(solution)/shard_map/ppermute | solution.py:16
  (96 shorter events, 39.7 us)
Async XLA Ops:
  2.9 17.7 %all-to-all-start = ((bf16[4,3,64,512]{3,2,1,0:T(8,128)(2,1)}), bf16[4,3,64,512]{3,2,1,0:T(8,128)(2,1)S(1)}, u32[]{:S(2)}, u32[]{:S(2)}) async-start(bf16[4,3,64,512]{3,2,1,0:T(8,128)(2,1)} %shard_map.77), calls=%async_computation | async-start | bytes 1572864 | tf_op jit(solution)/shard_map/all_to_all | solution.py:25
  8.3 24.4 %collective-permute-start = (bf16[3,256,512]{2,1,0:T(8,128)(2,1)}, bf16[3,256,512]{2,1,0:T(8,128)(2,1)S(1)}, u32[]{:S(2)}, u32[]{:S(2)}) collective-permute-start(bf16[3,256,512]{2,1,0:T(8,128)(2,1)} %refs_1_.1), channel_id=1, source_target_pairs={{0,32},{16,48},{32,64},{48,80},{64,96},{80,112},{96,0},{112,16},{1... | collective-permute-start | bytes 2359304 | tf_op jit(solution)/shard_map/ppermute | solution.py:16
  9.8 22.9 %collective-permute-start.1 = (bf16[3,256,512]{2,1,0:T(8,128)(2,1)}, bf16[3,256,512]{2,1,0:T(8,128)(2,1)S(1)}, u32[]{:S(2)}, u32[]{:S(2)}) collective-permute-start(bf16[3,256,512]{2,1,0:T(8,128)(2,1)} %refs_1_.1), channel_id=1, source_target_pairs={{0,96},{16,112},{32,0},{48,16},{64,32},{80,48},{96,64},{112,80},{1... | collective-permute-start | bytes 2359304 | tf_op jit(solution)/shard_map/ppermute | solution.py:16
  11.5 21.2 %collective-permute-start.2 = (bf16[3,256,512]{2,1,0:T(8,128)(2,1)}, bf16[3,256,512]{2,1,0:T(8,128)(2,1)}, u32[]{:S(2)}, u32[]{:S(2)}) collective-permute-start(bf16[3,256,512]{2,1,0:T(8,128)(2,1)} %refs_1_.1), channel_id=1, source_target_pairs={{0,16},{16,0},{32,48},{48,32},{64,80},{80,64},{96,112},{112,96},{1... | collective-permute-start | bytes 2359304 | tf_op jit(solution)/shard_map/ppermute | solution.py:20
  22.6 41.4 %all-to-all-start.1 = ((bf16[4,4,3,64,512]{4,3,2,1,0:T(8,128)(2,1)}), bf16[4,4,3,64,512]{4,3,2,1,0:T(8,128)(2,1)}, u32[]{:S(2)}, u32[]{:S(2)}) async-start(bf16[4,4,3,64,512]{4,3,2,1,0:T(8,128)(2,1)} %broadcast_in_dim.6), calls=%async_computation.1 | async-start | bytes 6291456 | tf_op jit(solution)/shard_map/all_to_all | solution.py:31
  32.7 4.0 %collective-permute-start.3 = (bf16[3,256,512]{2,1,0:T(8,128)(2,1)S(1)}, bf16[3,256,512]{2,1,0:T(8,128)(2,1)}, u32[]{:S(2)}, u32[]{:S(2)}) collective-permute-start(bf16[3,256,512]{2,1,0:T(8,128)(2,1)S(1)} %collective-permute-done.refs_4_.refs_5_), channel_id=1, source_target_pairs={{0,16},{16,0},{32,48},{48,32},{64,80},{80,64},{96,112},{112,96},{1... | collective-permute-start | bytes 2359304 | tf_op jit(solution)/shard_map/ppermute | solution.py:20
  33.5 15.7 %collective-permute-start.5 = (bf16[3,128,512]{2,1,0:T(8,128)(2,1)S(1)}, bf16[3,128,512]{2,1,0:T(8,128)(2,1)S(1)}, u32[]{:S(2)}, u32[]{:S(2)}) collective-permute-start(bf16[3,128,512]{2,1,0:T(8,128)(2,1)S(1)} %slice.30), channel_id=1, source_target_pairs={{0,32},{16,48},{32,64},{48,80},{64,96},{80,112},{96,0},{112,16},{1... | collective-permute-start | bytes 1179656 | tf_op jit(solution)/shard_map/ppermute | solution.py:16
  35.0 14.2 %collective-permute-start.6 = (bf16[3,128,512]{2,1,0:T(8,128)(2,1)S(1)}, bf16[3,128,512]{2,1,0:T(8,128)(2,1)S(1)}, u32[]{:S(2)}, u32[]{:S(2)}) collective-permute-start(bf16[3,128,512]{2,1,0:T(8,128)(2,1)S(1)} %slice.31), channel_id=1, source_target_pairs={{0,96},{16,112},{32,0},{48,16},{64,32},{80,48},{96,64},{112,80},{1... | collective-permute-start | bytes 1179656 | tf_op jit(solution)/shard_map/ppermute | solution.py:16
  64.0 16.5 %all-to-all-start.2 = ((bf16[16,128,128]{2,1,0:T(8,128)(2,1)}), bf16[16,128,128]{2,1,0:T(8,128)(2,1)S(1)}, u32[]{:S(2)}, u32[]{:S(2)}) async-start(bf16[16,128,128]{2,1,0:T(8,128)(2,1)} %get-tuple-element.50), calls=%async_computation.2 | async-start | bytes 1048576 | tf_op jit(solution)/shard_map/all_to_all | solution.py:257
  80.7 25.0 %all-to-all-start.3 = ((bf16[16,128,128]{2,1,0:T(8,128)(2,1)}), bf16[16,128,128]{2,1,0:T(8,128)(2,1)S(1)}, u32[]{:S(2)}, u32[]{:S(2)}) async-start(bf16[16,128,128]{2,1,0:T(8,128)(2,1)} %get-tuple-element.58), calls=%async_computation.3 | async-start | bytes 1048576 | tf_op jit(solution)/shard_map/all_to_all | solution.py:257
  84.3 5.8 %collective-permute-start.10 = (bf16[2,128,128]{2,1,0:T(8,128)(2,1)S(1)}, bf16[2,128,128]{2,1,0:T(8,128)(2,1)S(1)}, u32[]{:S(2)}, u32[]{:S(2)}) collective-permute-start(bf16[2,128,128]{2,1,0:T(8,128)(2,1)S(1)} %pad_maximum_fusion.1.own), channel_id=1, source_target_pairs={{0,32},{16,48},{32,64},{48,80},{64,96},{80,112},{96,0},{112,16},{1... | collective-permute-start | bytes 196616 | tf_op jit(solution)/shard_map/ppermute | solution.py:16
  84.4 6.4 %collective-permute-start.11 = (bf16[2,128,128]{2,1,0:T(8,128)(2,1)S(1)}, bf16[2,128,128]{2,1,0:T(8,128)(2,1)S(1)}, u32[]{:S(2)}, u32[]{:S(2)}) collective-permute-start(bf16[2,128,128]{2,1,0:T(8,128)(2,1)S(1)} %pad_maximum_fusion.1.own), channel_id=1, source_target_pairs={{0,96},{16,112},{32,0},{48,16},{64,32},{80,48},{96,64},{112,80},{1... | collective-permute-start | bytes 196616 | tf_op jit(solution)/shard_map/ppermute | solution.py:16
  87.6 5.8 %collective-permute-start.12 = (bf16[2,128,128]{2,1,0:T(8,128)(2,1)S(1)}, bf16[2,128,128]{2,1,0:T(8,128)(2,1)S(1)}, u32[]{:S(2)}, u32[]{:S(2)}) collective-permute-start(bf16[2,128,128]{2,1,0:T(8,128)(2,1)S(1)} %pad_maximum_fusion.1.own), channel_id=1, source_target_pairs={{0,64},{16,80},{32,96},{48,112},{64,0},{80,16},{96,32},{112,48},{1... | collective-permute-start | bytes 196616 | tf_op jit(solution)/shard_map/ppermute | solution.py:16
  95.1 4.8 %collective-permute-start.15 = (bf16[128,128]{1,0:T(8,128)(2,1)S(1)}, bf16[128,128]{1,0:T(8,128)(2,1)S(1)}, u32[]{:S(2)}, u32[]{:S(2)}) collective-permute-start(bf16[128,128]{1,0:T(8,128)(2,1)S(1)} %get-tuple-element.57), channel_id=1, source_target_pairs={{0,3},{1,0},{2,1},{3,2},{4,7},{5,4},{6,5},{7,6},{8,11},{9,8},{10,9... | collective-permute-start | bytes 98312 | tf_op jit(solution)/shard_map/ppermute | solution.py:36
  98.2 5.4 %collective-permute-start.14 = (bf16[128,128]{1,0:T(8,128)(2,1)S(1)}, bf16[128,128]{1,0:T(8,128)(2,1)S(1)}, u32[]{:S(2)}, u32[]{:S(2)}) collective-permute-start(bf16[128,128]{1,0:T(8,128)(2,1)S(1)} %get-tuple-element.56), channel_id=1, source_target_pairs={{0,2},{1,3},{2,0},{3,1},{4,6},{5,7},{6,4},{7,5},{8,10},{9,11},{10,... | collective-permute-start | bytes 98312 | tf_op jit(solution)/shard_map/ppermute | solution.py:36
  99.1 5.1 %collective-permute-start.13 = (bf16[128,128]{1,0:T(8,128)(2,1)S(1)}, bf16[128,128]{1,0:T(8,128)(2,1)S(1)}, u32[]{:S(2)}, u32[]{:S(2)}) collective-permute-start(bf16[128,128]{1,0:T(8,128)(2,1)S(1)} %get-tuple-element.55), channel_id=1, source_target_pairs={{0,1},{1,2},{2,3},{3,0},{4,5},{5,6},{6,7},{7,4},{8,9},{9,10},{10,1... | collective-permute-start | bytes 98312 | tf_op jit(solution)/shard_map/ppermute | solution.py:36
  105.8 9.5 %collective-permute-start.17 = (bf16[2,128,128]{2,1,0:T(8,128)(2,1)S(1)}, bf16[2,128,128]{2,1,0:T(8,128)(2,1)S(1)}, u32[]{:S(2)}, u32[]{:S(2)}) collective-permute-start(bf16[2,128,128]{2,1,0:T(8,128)(2,1)S(1)} %pad_maximum_fusion.2.own), channel_id=1, source_target_pairs={{0,32},{16,48},{32,64},{48,80},{64,96},{80,112},{96,0},{112,16},{1... | collective-permute-start | bytes 196616 | tf_op jit(solution)/shard_map/ppermute | solution.py:16
  105.9 9.4 %collective-permute-start.18 = (bf16[2,128,128]{2,1,0:T(8,128)(2,1)S(1)}, bf16[2,128,128]{2,1,0:T(8,128)(2,1)S(1)}, u32[]{:S(2)}, u32[]{:S(2)}) collective-permute-start(bf16[2,128,128]{2,1,0:T(8,128)(2,1)S(1)} %pad_maximum_fusion.2.own), channel_id=1, source_target_pairs={{0,96},{16,112},{32,0},{48,16},{64,32},{80,48},{96,64},{112,80},{1... | collective-permute-start | bytes 196616 | tf_op jit(solution)/shard_map/ppermute | solution.py:16
  109.2 6.2 %collective-permute-start.19 = (bf16[2,128,128]{2,1,0:T(8,128)(2,1)S(1)}, bf16[2,128,128]{2,1,0:T(8,128)(2,1)S(1)}, u32[]{:S(2)}, u32[]{:S(2)}) collective-permute-start(bf16[2,128,128]{2,1,0:T(8,128)(2,1)S(1)} %pad_maximum_fusion.2.own), channel_id=1, source_target_pairs={{0,64},{16,80},{32,96},{48,112},{64,0},{80,16},{96,32},{112,48},{1... | collective-permute-start | bytes 196616 | tf_op jit(solution)/shard_map/ppermute | solution.py:16
  110.0 23.6 %all-to-all-start.4 = ((bf16[16,128,128]{2,1,0:T(8,128)(2,1)}), bf16[16,128,128]{2,1,0:T(8,128)(2,1)S(1)}, u32[]{:S(2)}, u32[]{:S(2)}) async-start(bf16[16,128,128]{2,1,0:T(8,128)(2,1)} %broadcast_in_dim.7), calls=%async_computation.4 | async-start | bytes 1048576 | tf_op jit(solution)/shard_map/all_to_all | solution.py:262
  117.1 7.5 %collective-permute-start.22 = (bf16[128,128]{1,0:T(8,128)(2,1)S(1)}, bf16[128,128]{1,0:T(8,128)(2,1)S(1)}, u32[]{:S(2)}, u32[]{:S(2)}) collective-permute-start(bf16[128,128]{1,0:T(8,128)(2,1)S(1)} %get-tuple-element.64), channel_id=1, source_target_pairs={{0,3},{1,0},{2,1},{3,2},{4,7},{5,4},{6,5},{7,6},{8,11},{9,8},{10,9... | collective-permute-start | bytes 98312 | tf_op jit(solution)/shard_map/ppermute | solution.py:36
  120.3 6.7 %collective-permute-start.21 = (bf16[128,128]{1,0:T(8,128)(2,1)S(1)}, bf16[128,128]{1,0:T(8,128)(2,1)S(1)}, u32[]{:S(2)}, u32[]{:S(2)}) collective-permute-start(bf16[128,128]{1,0:T(8,128)(2,1)S(1)} %get-tuple-element.63), channel_id=1, source_target_pairs={{0,2},{1,3},{2,0},{3,1},{4,6},{5,7},{6,4},{7,5},{8,10},{9,11},{10,... | collective-permute-start | bytes 98312 | tf_op jit(solution)/shard_map/ppermute | solution.py:36
  121.2 5.9 %collective-permute-start.20 = (bf16[128,128]{1,0:T(8,128)(2,1)S(1)}, bf16[128,128]{1,0:T(8,128)(2,1)S(1)}, u32[]{:S(2)}, u32[]{:S(2)}) collective-permute-start(bf16[128,128]{1,0:T(8,128)(2,1)S(1)} %get-tuple-element.62), channel_id=1, source_target_pairs={{0,1},{1,2},{2,3},{3,0},{4,5},{5,6},{6,7},{7,4},{8,9},{9,10},{10,1... | collective-permute-start | bytes 98312 | tf_op jit(solution)/shard_map/ppermute | solution.py:36
  128.4 5.9 %collective-permute-start.24 = (bf16[2,128,128]{2,1,0:T(8,128)(2,1)S(1)}, bf16[2,128,128]{2,1,0:T(8,128)(2,1)S(1)}, u32[]{:S(2)}, u32[]{:S(2)}) collective-permute-start(bf16[2,128,128]{2,1,0:T(8,128)(2,1)S(1)} %pad_maximum_fusion.3.own), channel_id=1, source_target_pairs={{0,32},{16,48},{32,64},{48,80},{64,96},{80,112},{96,0},{112,16},{1... | collective-permute-start | bytes 196616 | tf_op jit(solution)/shard_map/ppermute | solution.py:16
  129.3 5.4 %collective-permute-start.25 = (bf16[2,128,128]{2,1,0:T(8,128)(2,1)S(1)}, bf16[2,128,128]{2,1,0:T(8,128)(2,1)S(1)}, u32[]{:S(2)}, u32[]{:S(2)}) collective-permute-start(bf16[2,128,128]{2,1,0:T(8,128)(2,1)S(1)} %pad_maximum_fusion.3.own), channel_id=1, source_target_pairs={{0,96},{16,112},{32,0},{48,16},{64,32},{80,48},{96,64},{112,80},{1... | collective-permute-start | bytes 196616 | tf_op jit(solution)/shard_map/ppermute | solution.py:16
  131.7 5.8 %collective-permute-start.26 = (bf16[2,128,128]{2,1,0:T(8,128)(2,1)S(1)}, bf16[2,128,128]{2,1,0:T(8,128)(2,1)S(1)}, u32[]{:S(2)}, u32[]{:S(2)}) collective-permute-start(bf16[2,128,128]{2,1,0:T(8,128)(2,1)S(1)} %pad_maximum_fusion.3.own), channel_id=1, source_target_pairs={{0,64},{16,80},{32,96},{48,112},{64,0},{80,16},{96,32},{112,48},{1... | collective-permute-start | bytes 196616 | tf_op jit(solution)/shard_map/ppermute | solution.py:16
  140.5 5.4 %collective-permute-start.28 = (bf16[128,128]{1,0:T(8,128)(2,1)S(1)}, bf16[128,128]{1,0:T(8,128)(2,1)S(1)}, u32[]{:S(2)}, u32[]{:S(2)}) collective-permute-start(bf16[128,128]{1,0:T(8,128)(2,1)S(1)} %get-tuple-element.72), channel_id=1, source_target_pairs={{0,2},{1,3},{2,0},{3,1},{4,6},{5,7},{6,4},{7,5},{8,10},{9,11},{10,... | collective-permute-start | bytes 98312 | tf_op jit(solution)/shard_map/ppermute | solution.py:36
  141.6 5.1 %collective-permute-start.27 = (bf16[128,128]{1,0:T(8,128)(2,1)S(1)}, bf16[128,128]{1,0:T(8,128)(2,1)S(1)}, u32[]{:S(2)}, u32[]{:S(2)}) collective-permute-start(bf16[128,128]{1,0:T(8,128)(2,1)S(1)} %get-tuple-element.71), channel_id=1, source_target_pairs={{0,1},{1,2},{2,3},{3,0},{4,5},{5,6},{6,7},{7,4},{8,9},{9,10},{10,1... | collective-permute-start | bytes 98312 | tf_op jit(solution)/shard_map/ppermute | solution.py:36
  147.7 14.3 %all-to-all-start.5 = ((bf16[16,128,128]{2,1,0:T(8,128)(2,1)}), bf16[16,128,128]{2,1,0:T(8,128)(2,1)S(1)}, u32[]{:S(2)}, u32[]{:S(2)}) async-start(bf16[16,128,128]{2,1,0:T(8,128)(2,1)} %broadcast_in_dim.8), calls=%async_computation.5 | async-start | bytes 1048576 | tf_op jit(solution)/shard_map/all_to_all | solution.py:262
  164.1 5.9 %collective-permute-start.33 = (f32[32,512]{1,0:T(8,128)S(1)}, f32[32,512]{1,0:T(8,128)S(1)}, u32[]{:S(2)}, u32[]{:S(2)}) collective-permute-start(f32[32,512]{1,0:T(8,128)S(1)} %add.192), channel_id=1, source_target_pairs={{0,64},{16,80},{32,96},{48,112},{64,0},{80,16},{96,32},{112,48},{1... | collective-permute-start | bytes 196616 | tf_op jit(solution)/shard_map/ppermute | solution.py:16
  166.5 4.3 %collective-permute-start.32 = (f32[32,512]{1,0:T(8,128)S(1)}, f32[32,512]{1,0:T(8,128)S(1)}, u32[]{:S(2)}, u32[]{:S(2)}) collective-permute-start(f32[32,512]{1,0:T(8,128)S(1)} %add.192), channel_id=1, source_target_pairs={{0,96},{16,112},{32,0},{48,16},{64,32},{80,48},{96,64},{112,80},{1... | collective-permute-start | bytes 196616 | tf_op jit(solution)/shard_map/ppermute | solution.py:16
  167.1 5.5 %collective-permute-start.31 = (f32[32,512]{1,0:T(8,128)S(1)}, f32[32,512]{1,0:T(8,128)S(1)}, u32[]{:S(2)}, u32[]{:S(2)}) collective-permute-start(f32[32,512]{1,0:T(8,128)S(1)} %add.192), channel_id=1, source_target_pairs={{0,32},{16,48},{32,64},{48,80},{64,96},{80,112},{96,0},{112,16},{1... | collective-permute-start | bytes 196616 | tf_op jit(solution)/shard_map/ppermute | solution.py:16
  (11 other events, 66.7 us)

commit v13 on v12

--- a/solution.py
+++ b/solution.py
@@ -88,7 +88,7 @@
         grid=(2,),
         in_specs=[
             pl.BlockSpec((1, tile, count, width), lambda a: (2 * half + a, 0, 0, 0)),
-            whole(token),
+            pl.BlockSpec(memory_space=pltpu.HBM),
         ],
         out_specs=pl.BlockSpec((count // 3, tile, 3 * width), lambda a: (0, a, 0)),
         out_shape=pltpu.HBM((count // 3, 2 * tile, 3 * width), BF),
@@ -285,9 +285,9 @@
     before, after = x_shift(prev_solution, 1), x_shift(prev_solution, -1)
     sibling = other_core(prev_solution)
     tiles = in_hbm(left_factor)
-    upper = split_tiles(tiles, 0, lines[0, 0, :16, :128])
-    lines, token = lax.optimization_barrier((z_exchange(lines), upper[0, :16, :128]))
-    lower = split_tiles(tiles, 1, token)
+    upper = split_tiles(tiles, 0, in_hbm(lines))
+    lines, upper = lax.optimization_barrier((z_exchange(lines), upper))
+    lower = split_tiles(tiles, 1, in_hbm(upper))
     before, after, sibling, upper, lower = lax.optimization_barrier(
         (before, after, sibling, upper, lower)
     )

time: 174 us -> 172 us (0.989)
  no operation moved by 1% of the time
where the time goes in v13:
time: 172 us; the launch traced here: 171 us
  starting transfers between devices  64.6 us (38%)
  waiting for transfers between devices  59.3 us (34%)
  Pallas kernels  36.7 us (21%)
  local copies, waits for them, and re-layouts  5.87 us (3%)
  other arithmetic  3.01 us (2%)
    ppermute x16, starting transfers between devices, x_shift(): return lax.ppermute(v, 'row', [(r, (r + 2 * step) % 8) for r in range(8)])  24.1 us
    pallas_call x2, Pallas kernels, products(): pl.pallas_call(kernel, grid_spec=pltpu.PrefetchScalarGridSpec(num_scalar_...  18.5 us
    ppermute x9, waiting for transfers between devices, z_shift(): lax.ppermute(v, 'col', [(c, c // 4 * 4 + (c + step) % 4) for c in range(1...  14.3 us
    ppermute x9, starting transfers between devices, z_shift(): lax.ppermute(v, 'col', [(c, c // 4 * 4 + (c + step) % 4) for c in range(1...  12.2 us
    pallas_call x2, Pallas kernels, split_tiles(): pl.pallas_call(split_tiles_kernel, grid=(2,), in_specs=[pl.BlockSpec((1,...  10.8 us
    ppermute x16, waiting for transfers between devices, x_shift(): return lax.ppermute(v, 'row', [(r, (r + 2 * step) % 8) for r in range(8)])  10.7 us
    all_to_all x2, waiting for transfers between devices, all_sites(): lax.all_to_all(sent, 'col', 0, 0, tiled=True).reshape(4, 4, 2, 64, 128)  9.7 us
    all_to_all x2, waiting for transfers between devices, over_sites(): lax.all_to_all(partial, 'col', 0, 0, tiled=True).astype(F32).sum(axis=0)  9.63 us
  transfers between devices with their start and end apart: 40, of which 24 were waited for; matrix products, arithmetic and copies ran while one was open for 4% of the time, Pallas kernels for 19%

profile of v13, /device:TPU:0, one launch (start us, length us, event | category | flops | bytes accessed | tf_op | source)
XLA Modules:
  0.0 171.1 jit_solution(6401948597747488481)
XLA Ops:
  0.6 2.3 %shard_map.77.token = bf16[4,3,64,512]{3,2,1,0:T(8,128)(2,1)} custom-call(bf16[2,512,256]{2,1,0:T(8,128)(2,1)} %bitcast.43, bf16[2,512,256]{2,1,0:T(8,128)(2,1)} %bitcast.44, bf16[512,256]{1,0:T(8,128)(2,1)} %bitcast.46), custom_call_target="tpu_custom_call" | custom-call | tf_op jit(solution)/shard_map/pallas_call | solution.py:63
  2.9 5.4 %all-to-all-start = ((bf16[4,3,64,512]{3,2,1,0:T(8,128)(2,1)}), bf16[4,3,64,512]{3,2,1,0:T(8,128)(2,1)S(1)}, u32[]{:S(2)}, u32[]{:S(2)}) async-start(bf16[4,3,64,512]{3,2,1,0:T(8,128)(2,1)} %shard_map.77.token), calls=%async_computation | async-start | bytes 1572864 | tf_op jit(solution)/shard_map/all_to_all | solution.py:25
  9.8 1.7 %collective-permute-start.1 = (bf16[3,256,512]{2,1,0:T(8,128)(2,1)}, bf16[3,256,512]{2,1,0:T(8,128)(2,1)S(1)}, u32[]{:S(2)}, u32[]{:S(2)}) collective-permute-start(bf16[3,256,512]{2,1,0:T(8,128)(2,1)} %refs_1_.1), channel_id=1, source_target_pairs={{0,96},{16,112},{32,0},{48,16},{64,32},{80,48},{96,64},{112,80},{1... | collective-permute-start | bytes 2359304 | tf_op jit(solution)/shard_map/ppermute | solution.py:16
  11.5 5.3 %shard_map.78.token.upper = bf16[8,512,768]{2,1,0:T(8,128)(2,1)} custom-call(bf16[4,256,24,256]{3,2,1,0:T(8,128)(2,1)} %src.3, bf16[4,3,64,512]{3,2,1,0:T(8,128)(2,1)} %shard_map.77.token), custom_call_target="tpu_custom_call" | custom-call | bytes 12582912 | tf_op jit(solution)/shard_map/pallas_call | solution.py:86
  16.9 3.7 %all-to-all-done = bf16[4,3,64,512]{3,2,1,0:T(8,128)(2,1)S(1)} async-done(((bf16[4,3,64,512]{3,2,1,0:T(8,128)(2,1)}), bf16[4,3,64,512]{3,2,1,0:T(8,128)(2,1)S(1)}, u32[]{:S(2)}, u32[]{:S(2)}) %all-to-all-start) | async-done | bytes 786464 | tf_op jit(solution)/shard_map/all_to_all | solution.py:25
  20.6 2.1 %broadcast_in_dim.6 = bf16[4,4,3,64,512]{4,3,2,1,0:T(8,128)(2,1)} broadcast(bf16[4,3,64,512]{3,2,1,0:T(8,128)(2,1)S(1)} %all-to-all-done), dimensions={1,2,3,4} | broadcast | bytes 3932160 | tf_op jit(solution)/shard_map/broadcast_in_dim | solution.py:30
  22.6 4.6 %all-to-all-start.1 = ((bf16[4,4,3,64,512]{4,3,2,1,0:T(8,128)(2,1)}), bf16[4,4,3,64,512]{4,3,2,1,0:T(8,128)(2,1)}, u32[]{:S(2)}, u32[]{:S(2)}) async-start(bf16[4,4,3,64,512]{4,3,2,1,0:T(8,128)(2,1)} %broadcast_in_dim.6), calls=%async_computation.1 | async-start | bytes 6291456 | tf_op jit(solution)/shard_map/all_to_all | solution.py:31
  27.3 5.4 %shard_map.79.lower = bf16[8,512,768]{2,1,0:T(8,128)(2,1)} custom-call(bf16[4,256,24,256]{3,2,1,0:T(8,128)(2,1)} %src.3, bf16[8,512,768]{2,1,0:T(8,128)(2,1)} %shard_map.78.token.upper), custom_call_target="tpu_custom_call" | custom-call | bytes 12582912 | tf_op jit(solution)/shard_map/pallas_call | solution.py:86
  35.4 1.7 %collective-permute-start.6 = (bf16[3,128,512]{2,1,0:T(8,128)(2,1)S(1)}, bf16[3,128,512]{2,1,0:T(8,128)(2,1)S(1)}, u32[]{:S(2)}, u32[]{:S(2)}) collective-permute-start(bf16[3,128,512]{2,1,0:T(8,128)(2,1)S(1)} %slice.23), channel_id=1, source_target_pairs={{0,96},{16,112},{32,0},{48,16},{64,32},{80,48},{96,64},{112,80},{1... | collective-permute-start | bytes 1179656 | tf_op jit(solution)/shard_map/ppermute | solution.py:16
  37.1 12.4 %shard_map.80.before = f32[1024,512]{1,0:T(8,128)S(1)} custom-call(s32[6]{0:T(128)S(1)} %stack.88.order, bf16[8,512,768]{2,1,0:T(8,128)(2,1)} %shard_map.78.token.upper, bf16[8,512,768]{2,1,0:T(8,128)(2,1)} %shard_map.79.lower, bf16[3,256,512]{2,1,0:T(8,128)(2,1)} %refs_1_.1, bf16[3,256,512]{2,1,0:T(8,128)(2,1)} %refs_1_.1, bf16[3,256,512]{2,1,0:T(8,128)(2,1)} %copy-done.2, ...), custom_call_target="tpu_custom_call" | custom-call | flops 4831838208 | bytes 16252928 | tf_op jit(solution)/shard_map/pallas_call | solution.py:184
  52.1 6.1 %shard_map.81 = (bf16[16,128,128]{2,1,0:T(8,128)(2,1)}, bf16[16,128,128]{2,1,0:T(8,128)(2,1)}) custom-call(s32[2]{0:T(128)S(1)} %pad_add_fusion.1.order, bf16[8,512,768]{2,1,0:T(8,128)(2,1)} %shard_map.78.token.upper, bf16[8,512,768]{2,1,0:T(8,128)(2,1)} %shard_map.79.lower, f32[1024,512]{1,0:T(8,128)S(1)} %shard_map.80.before, f32[8,128]{1,0:T(8,128)S(1)} %slice.27.token, ...), custom_call_target="tpu_custom_call" | custom-call | flops 1610612736 | bytes 6815744 | tf_op jit(solution)/shard_map/pallas_call | solution.py:184
  58.2 5.8 %all-to-all-done.1 = bf16[4,4,3,64,512]{4,3,2,1,0:T(8,128)(2,1)} async-done(((bf16[4,4,3,64,512]{4,3,2,1,0:T(8,128)(2,1)}), bf16[4,4,3,64,512]{4,3,2,1,0:T(8,128)(2,1)}, u32[]{:S(2)}, u32[]{:S(2)}) %all-to-all-start.1) | async-done | bytes 3145760 | tf_op jit(solution)/shard_map/all_to_all | solution.py:31
  64.0 3.7 %all-to-all-start.2 = ((bf16[16,128,128]{2,1,0:T(8,128)(2,1)}), bf16[16,128,128]{2,1,0:T(8,128)(2,1)S(1)}, u32[]{:S(2)}, u32[]{:S(2)}) async-start(bf16[16,128,128]{2,1,0:T(8,128)(2,1)} %get-tuple-element.50), calls=%async_computation.2 | async-start | bytes 1048576 | tf_op jit(solution)/shard_map/all_to_all | solution.py:257
  68.6 9.6 %all-to-all-done.2 = bf16[16,128,128]{2,1,0:T(8,128)(2,1)S(1)} async-done(((bf16[16,128,128]{2,1,0:T(8,128)(2,1)}), bf16[16,128,128]{2,1,0:T(8,128)(2,1)S(1)}, u32[]{:S(2)}, u32[]{:S(2)}) %all-to-all-start.2) | async-done | bytes 524320 | tf_op jit(solution)/shard_map/all_to_all | solution.py:257
  78.5 3.6 %all-to-all-start.3 = ((bf16[16,128,128]{2,1,0:T(8,128)(2,1)}), bf16[16,128,128]{2,1,0:T(8,128)(2,1)S(1)}, u32[]{:S(2)}, u32[]{:S(2)}) async-start(bf16[16,128,128]{2,1,0:T(8,128)(2,1)} %get-tuple-element.58), calls=%async_computation.3 | async-start | bytes 1048576 | tf_op jit(solution)/shard_map/all_to_all | solution.py:257
  83.1 2.3 %collective-permute-start.11 = (bf16[2,128,128]{2,1,0:T(8,128)(2,1)S(1)}, bf16[2,128,128]{2,1,0:T(8,128)(2,1)S(1)}, u32[]{:S(2)}, u32[]{:S(2)}) collective-permute-start(bf16[2,128,128]{2,1,0:T(8,128)(2,1)S(1)} %pad_maximum_fusion.1.own), channel_id=1, source_target_pairs={{0,96},{16,112},{32,0},{48,16},{64,32},{80,48},{96,64},{112,80},{1... | collective-permute-start | bytes 196616 | tf_op jit(solution)/shard_map/ppermute | solution.py:16
  87.9 3.3 %collective-permute-done.12.three = bf16[2,128,128]{2,1,0:T(8,128)(2,1)S(1)} collective-permute-done((bf16[2,128,128]{2,1,0:T(8,128)(2,1)S(1)}, bf16[2,128,128]{2,1,0:T(8,128)(2,1)S(1)}, u32[]{:S(2)}, u32[]{:S(2)}) %collective-permute-start.12) | collective-permute-done | bytes 65568 | tf_op jit(solution)/shard_map/ppermute | solution.py:16
  92.9 3.1 %collective-permute-start.15 = (bf16[128,128]{1,0:T(8,128)(2,1)S(1)}, bf16[128,128]{1,0:T(8,128)(2,1)S(1)}, u32[]{:S(2)}, u32[]{:S(2)}) collective-permute-start(bf16[128,128]{1,0:T(8,128)(2,1)S(1)} %get-tuple-element.57), channel_id=1, source_target_pairs={{0,3},{1,0},{2,1},{3,2},{4,7},{5,4},{6,5},{7,6},{8,11},{9,8},{10,9... | collective-permute-start | bytes 98312 | tf_op jit(solution)/shard_map/ppermute | solution.py:36
  97.7 3.7 %collective-permute-done.14 = bf16[128,128]{1,0:T(8,128)(2,1)S(1)} collective-permute-done((bf16[128,128]{1,0:T(8,128)(2,1)S(1)}, bf16[128,128]{1,0:T(8,128)(2,1)S(1)}, u32[]{:S(2)}, u32[]{:S(2)}) %collective-permute-start.14) | collective-permute-done | bytes 32800 | tf_op jit(solution)/shard_map/ppermute | solution.py:36
  103.7 3.2 %collective-permute-start.18 = (bf16[2,128,128]{2,1,0:T(8,128)(2,1)S(1)}, bf16[2,128,128]{2,1,0:T(8,128)(2,1)S(1)}, u32[]{:S(2)}, u32[]{:S(2)}) collective-permute-start(bf16[2,128,128]{2,1,0:T(8,128)(2,1)S(1)} %pad_maximum_fusion.2.own), channel_id=1, source_target_pairs={{0,96},{16,112},{32,0},{48,16},{64,32},{80,48},{96,64},{112,80},{1... | collective-permute-start | bytes 196616 | tf_op jit(solution)/shard_map/ppermute | solution.py:16
  107.8 5.3 %all-to-all-start.4 = ((bf16[16,128,128]{2,1,0:T(8,128)(2,1)}), bf16[16,128,128]{2,1,0:T(8,128)(2,1)S(1)}, u32[]{:S(2)}, u32[]{:S(2)}) async-start(bf16[16,128,128]{2,1,0:T(8,128)(2,1)} %broadcast_in_dim.7), calls=%async_computation.4 | async-start | bytes 1048576 | tf_op jit(solution)/shard_map/all_to_all | solution.py:262
  114.9 3.2 %collective-permute-start.22 = (bf16[128,128]{1,0:T(8,128)(2,1)S(1)}, bf16[128,128]{1,0:T(8,128)(2,1)S(1)}, u32[]{:S(2)}, u32[]{:S(2)}) collective-permute-start(bf16[128,128]{1,0:T(8,128)(2,1)S(1)} %get-tuple-element.64), channel_id=1, source_target_pairs={{0,3},{1,0},{2,1},{3,2},{4,7},{5,4},{6,5},{7,6},{8,11},{9,8},{10,9... | collective-permute-start | bytes 98312 | tf_op jit(solution)/shard_map/ppermute | solution.py:36
  119.8 2.6 %collective-permute-done.22 = bf16[128,128]{1,0:T(8,128)(2,1)S(1)} collective-permute-done((bf16[128,128]{1,0:T(8,128)(2,1)S(1)}, bf16[128,128]{1,0:T(8,128)(2,1)S(1)}, u32[]{:S(2)}, u32[]{:S(2)}) %collective-permute-start.22) | collective-permute-done | bytes 32800 | tf_op jit(solution)/shard_map/ppermute | solution.py:36
  122.4 2.4 %collective-permute-done.21 = bf16[128,128]{1,0:T(8,128)(2,1)S(1)} collective-permute-done((bf16[128,128]{1,0:T(8,128)(2,1)S(1)}, bf16[128,128]{1,0:T(8,128)(2,1)S(1)}, u32[]{:S(2)}, u32[]{:S(2)}) %collective-permute-start.21) | collective-permute-done | bytes 32800 | tf_op jit(solution)/shard_map/ppermute | solution.py:36
  127.1 2.4 %collective-permute-start.25 = (bf16[2,128,128]{2,1,0:T(8,128)(2,1)S(1)}, bf16[2,128,128]{2,1,0:T(8,128)(2,1)S(1)}, u32[]{:S(2)}, u32[]{:S(2)}) collective-permute-start(bf16[2,128,128]{2,1,0:T(8,128)(2,1)S(1)} %pad_maximum_fusion.3.own), channel_id=1, source_target_pairs={{0,96},{16,112},{32,0},{48,16},{64,32},{80,48},{96,64},{112,80},{1... | collective-permute-start | bytes 196616 | tf_op jit(solution)/shard_map/ppermute | solution.py:16
  129.5 1.9 %collective-permute-start.26 = (bf16[2,128,128]{2,1,0:T(8,128)(2,1)S(1)}, bf16[2,128,128]{2,1,0:T(8,128)(2,1)S(1)}, u32[]{:S(2)}, u32[]{:S(2)}) collective-permute-start(bf16[2,128,128]{2,1,0:T(8,128)(2,1)S(1)} %pad_maximum_fusion.3.own), channel_id=1, source_target_pairs={{0,64},{16,80},{32,96},{48,112},{64,0},{80,16},{96,32},{112,48},{1... | collective-permute-start | bytes 196616 | tf_op jit(solution)/shard_map/ppermute | solution.py:16
  132.5 2.7 %collective-permute-done.26.three = bf16[2,128,128]{2,1,0:T(8,128)(2,1)S(1)} collective-permute-done((bf16[2,128,128]{2,1,0:T(8,128)(2,1)S(1)}, bf16[2,128,128]{2,1,0:T(8,128)(2,1)S(1)}, u32[]{:S(2)}, u32[]{:S(2)}) %collective-permute-start.26) | collective-permute-done | bytes 65568 | tf_op jit(solution)/shard_map/ppermute | solution.py:16
  141.0 2.8 %collective-permute-done.28 = bf16[128,128]{1,0:T(8,128)(2,1)S(1)} collective-permute-done((bf16[128,128]{1,0:T(8,128)(2,1)S(1)}, bf16[128,128]{1,0:T(8,128)(2,1)S(1)}, u32[]{:S(2)}, u32[]{:S(2)}) %collective-permute-start.28) | collective-permute-done | bytes 32800 | tf_op jit(solution)/shard_map/ppermute | solution.py:36
  145.5 4.2 %all-to-all-start.5 = ((bf16[16,128,128]{2,1,0:T(8,128)(2,1)}), bf16[16,128,128]{2,1,0:T(8,128)(2,1)S(1)}, u32[]{:S(2)}, u32[]{:S(2)}) async-start(bf16[16,128,128]{2,1,0:T(8,128)(2,1)} %broadcast_in_dim.8), calls=%async_computation.5 | async-start | bytes 1048576 | tf_op jit(solution)/shard_map/all_to_all | solution.py:262
  150.0 9.7 %all-to-all-done.5 = bf16[16,128,128]{2,1,0:T(8,128)(2,1)S(1)} async-done(((bf16[16,128,128]{2,1,0:T(8,128)(2,1)}), bf16[16,128,128]{2,1,0:T(8,128)(2,1)S(1)}, u32[]{:S(2)}, u32[]{:S(2)}) %all-to-all-start.5) | async-done | bytes 524320 | tf_op jit(solution)/shard_map/all_to_all | solution.py:262
  161.9 2.4 %collective-permute-start.33 = (f32[32,512]{1,0:T(8,128)S(1)}, f32[32,512]{1,0:T(8,128)S(1)}, u32[]{:S(2)}, u32[]{:S(2)}) collective-permute-start(f32[32,512]{1,0:T(8,128)S(1)} %add.192), channel_id=1, source_target_pairs={{0,64},{16,80},{32,96},{48,112},{64,0},{80,16},{96,32},{112,48},{1... | collective-permute-start | bytes 196616 | tf_op jit(solution)/shard_map/ppermute | solution.py:16
  168.6 1.8 %collective-permute-done.31 = f32[32,512]{1,0:T(8,128)S(1)} collective-permute-done((f32[32,512]{1,0:T(8,128)S(1)}, f32[32,512]{1,0:T(8,128)S(1)}, u32[]{:S(2)}, u32[]{:S(2)}) %collective-permute-start.31) | collective-permute-done | bytes 65568 | tf_op jit(solution)/shard_map/ppermute | solution.py:16
  (96 shorter events, 39.5 us)
Async XLA Ops:
  2.9 17.7 %all-to-all-start = ((bf16[4,3,64,512]{3,2,1,0:T(8,128)(2,1)}), bf16[4,3,64,512]{3,2,1,0:T(8,128)(2,1)S(1)}, u32[]{:S(2)}, u32[]{:S(2)}) async-start(bf16[4,3,64,512]{3,2,1,0:T(8,128)(2,1)} %shard_map.77.token), calls=%async_computation | async-start | bytes 1572864 | tf_op jit(solution)/shard_map/all_to_all | solution.py:25
  8.3 24.4 %collective-permute-start = (bf16[3,256,512]{2,1,0:T(8,128)(2,1)}, bf16[3,256,512]{2,1,0:T(8,128)(2,1)S(1)}, u32[]{:S(2)}, u32[]{:S(2)}) collective-permute-start(bf16[3,256,512]{2,1,0:T(8,128)(2,1)} %refs_1_.1), channel_id=1, source_target_pairs={{0,32},{16,48},{32,64},{48,80},{64,96},{80,112},{96,0},{112,16},{1... | collective-permute-start | bytes 2359304 | tf_op jit(solution)/shard_map/ppermute | solution.py:16
  9.8 22.9 %collective-permute-start.1 = (bf16[3,256,512]{2,1,0:T(8,128)(2,1)}, bf16[3,256,512]{2,1,0:T(8,128)(2,1)S(1)}, u32[]{:S(2)}, u32[]{:S(2)}) collective-permute-start(bf16[3,256,512]{2,1,0:T(8,128)(2,1)} %refs_1_.1), channel_id=1, source_target_pairs={{0,96},{16,112},{32,0},{48,16},{64,32},{80,48},{96,64},{112,80},{1... | collective-permute-start | bytes 2359304 | tf_op jit(solution)/shard_map/ppermute | solution.py:16
  11.5 21.2 %collective-permute-start.2 = (bf16[3,256,512]{2,1,0:T(8,128)(2,1)}, bf16[3,256,512]{2,1,0:T(8,128)(2,1)S(1)}, u32[]{:S(2)}, u32[]{:S(2)}) collective-permute-start(bf16[3,256,512]{2,1,0:T(8,128)(2,1)} %refs_1_.1), channel_id=1, source_target_pairs={{0,16},{16,0},{32,48},{48,32},{64,80},{80,64},{96,112},{112,96},{1... | collective-permute-start | bytes 2359304 | tf_op jit(solution)/shard_map/ppermute | solution.py:20
  22.6 41.4 %all-to-all-start.1 = ((bf16[4,4,3,64,512]{4,3,2,1,0:T(8,128)(2,1)}), bf16[4,4,3,64,512]{4,3,2,1,0:T(8,128)(2,1)}, u32[]{:S(2)}, u32[]{:S(2)}) async-start(bf16[4,4,3,64,512]{4,3,2,1,0:T(8,128)(2,1)} %broadcast_in_dim.6), calls=%async_computation.1 | async-start | bytes 6291456 | tf_op jit(solution)/shard_map/all_to_all | solution.py:31
  32.7 4.4 %collective-permute-start.3 = (bf16[3,256,512]{2,1,0:T(8,128)(2,1)S(1)}, bf16[3,256,512]{2,1,0:T(8,128)(2,1)}, u32[]{:S(2)}, u32[]{:S(2)}) collective-permute-start(bf16[3,256,512]{2,1,0:T(8,128)(2,1)S(1)} %collective-permute-done.refs_4_.refs_5_), channel_id=1, source_target_pairs={{0,16},{16,0},{32,48},{48,32},{64,80},{80,64},{96,112},{112,96},{1... | collective-permute-start | bytes 2359304 | tf_op jit(solution)/shard_map/ppermute | solution.py:20
  32.8 4.3 %collective-permute-start.4 = (bf16[3,256,512]{2,1,0:T(8,128)(2,1)S(1)}, bf16[3,256,512]{2,1,0:T(8,128)(2,1)}, u32[]{:S(2)}, u32[]{:S(2)}) collective-permute-start(bf16[3,256,512]{2,1,0:T(8,128)(2,1)S(1)} %collective-permute-done.1.refs_8_.refs_9_), channel_id=1, source_target_pairs={{0,16},{16,0},{32,48},{48,32},{64,80},{80,64},{96,112},{112,96},{1... | collective-permute-start | bytes 2359304 | tf_op jit(solution)/shard_map/ppermute | solution.py:20
  33.8 15.7 %collective-permute-start.5 = (bf16[3,128,512]{2,1,0:T(8,128)(2,1)S(1)}, bf16[3,128,512]{2,1,0:T(8,128)(2,1)S(1)}, u32[]{:S(2)}, u32[]{:S(2)}) collective-permute-start(bf16[3,128,512]{2,1,0:T(8,128)(2,1)S(1)} %slice.22), channel_id=1, source_target_pairs={{0,32},{16,48},{32,64},{48,80},{64,96},{80,112},{96,0},{112,16},{1... | collective-permute-start | bytes 1179656 | tf_op jit(solution)/shard_map/ppermute | solution.py:16
  35.4 14.2 %collective-permute-start.6 = (bf16[3,128,512]{2,1,0:T(8,128)(2,1)S(1)}, bf16[3,128,512]{2,1,0:T(8,128)(2,1)S(1)}, u32[]{:S(2)}, u32[]{:S(2)}) collective-permute-start(bf16[3,128,512]{2,1,0:T(8,128)(2,1)S(1)} %slice.23), channel_id=1, source_target_pairs={{0,96},{16,112},{32,0},{48,16},{64,32},{80,48},{96,64},{112,80},{1... | collective-permute-start | bytes 1179656 | tf_op jit(solution)/shard_map/ppermute | solution.py:16
  64.0 14.2 %all-to-all-start.2 = ((bf16[16,128,128]{2,1,0:T(8,128)(2,1)}), bf16[16,128,128]{2,1,0:T(8,128)(2,1)S(1)}, u32[]{:S(2)}, u32[]{:S(2)}) async-start(bf16[16,128,128]{2,1,0:T(8,128)(2,1)} %get-tuple-element.50), calls=%async_computation.2 | async-start | bytes 1048576 | tf_op jit(solution)/shard_map/all_to_all | solution.py:257
  78.5 25.0 %all-to-all-start.3 = ((bf16[16,128,128]{2,1,0:T(8,128)(2,1)}), bf16[16,128,128]{2,1,0:T(8,128)(2,1)S(1)}, u32[]{:S(2)}, u32[]{:S(2)}) async-start(bf16[16,128,128]{2,1,0:T(8,128)(2,1)} %get-tuple-element.58), calls=%async_computation.3 | async-start | bytes 1048576 | tf_op jit(solution)/shard_map/all_to_all | solution.py:257
  82.1 5.8 %collective-permute-start.10 = (bf16[2,128,128]{2,1,0:T(8,128)(2,1)S(1)}, bf16[2,128,128]{2,1,0:T(8,128)(2,1)S(1)}, u32[]{:S(2)}, u32[]{:S(2)}) collective-permute-start(bf16[2,128,128]{2,1,0:T(8,128)(2,1)S(1)} %pad_maximum_fusion.1.own), channel_id=1, source_target_pairs={{0,32},{16,48},{32,64},{48,80},{64,96},{80,112},{96,0},{112,16},{1... | collective-permute-start | bytes 196616 | tf_op jit(solution)/shard_map/ppermute | solution.py:16
  83.1 4.8 %collective-permute-start.11 = (bf16[2,128,128]{2,1,0:T(8,128)(2,1)S(1)}, bf16[2,128,128]{2,1,0:T(8,128)(2,1)S(1)}, u32[]{:S(2)}, u32[]{:S(2)}) collective-permute-start(bf16[2,128,128]{2,1,0:T(8,128)(2,1)S(1)} %pad_maximum_fusion.1.own), channel_id=1, source_target_pairs={{0,96},{16,112},{32,0},{48,16},{64,32},{80,48},{96,64},{112,80},{1... | collective-permute-start | bytes 196616 | tf_op jit(solution)/shard_map/ppermute | solution.py:16
  85.4 5.8 %collective-permute-start.12 = (bf16[2,128,128]{2,1,0:T(8,128)(2,1)S(1)}, bf16[2,128,128]{2,1,0:T(8,128)(2,1)S(1)}, u32[]{:S(2)}, u32[]{:S(2)}) collective-permute-start(bf16[2,128,128]{2,1,0:T(8,128)(2,1)S(1)} %pad_maximum_fusion.1.own), channel_id=1, source_target_pairs={{0,64},{16,80},{32,96},{48,112},{64,0},{80,16},{96,32},{112,48},{1... | collective-permute-start | bytes 196616 | tf_op jit(solution)/shard_map/ppermute | solution.py:16
  92.9 4.8 %collective-permute-start.15 = (bf16[128,128]{1,0:T(8,128)(2,1)S(1)}, bf16[128,128]{1,0:T(8,128)(2,1)S(1)}, u32[]{:S(2)}, u32[]{:S(2)}) collective-permute-start(bf16[128,128]{1,0:T(8,128)(2,1)S(1)} %get-tuple-element.57), channel_id=1, source_target_pairs={{0,3},{1,0},{2,1},{3,2},{4,7},{5,4},{6,5},{7,6},{8,11},{9,8},{10,9... | collective-permute-start | bytes 98312 | tf_op jit(solution)/shard_map/ppermute | solution.py:36
  96.0 5.4 %collective-permute-start.14 = (bf16[128,128]{1,0:T(8,128)(2,1)S(1)}, bf16[128,128]{1,0:T(8,128)(2,1)S(1)}, u32[]{:S(2)}, u32[]{:S(2)}) collective-permute-start(bf16[128,128]{1,0:T(8,128)(2,1)S(1)} %get-tuple-element.56), channel_id=1, source_target_pairs={{0,2},{1,3},{2,0},{3,1},{4,6},{5,7},{6,4},{7,5},{8,10},{9,11},{10,... | collective-permute-start | bytes 98312 | tf_op jit(solution)/shard_map/ppermute | solution.py:36
  96.9 5.1 %collective-permute-start.13 = (bf16[128,128]{1,0:T(8,128)(2,1)S(1)}, bf16[128,128]{1,0:T(8,128)(2,1)S(1)}, u32[]{:S(2)}, u32[]{:S(2)}) collective-permute-start(bf16[128,128]{1,0:T(8,128)(2,1)S(1)} %get-tuple-element.55), channel_id=1, source_target_pairs={{0,1},{1,2},{2,3},{3,0},{4,5},{5,6},{6,7},{7,4},{8,9},{9,10},{10,1... | collective-permute-start | bytes 98312 | tf_op jit(solution)/shard_map/ppermute | solution.py:36
  103.6 9.5 %collective-permute-start.17 = (bf16[2,128,128]{2,1,0:T(8,128)(2,1)S(1)}, bf16[2,128,128]{2,1,0:T(8,128)(2,1)S(1)}, u32[]{:S(2)}, u32[]{:S(2)}) collective-permute-start(bf16[2,128,128]{2,1,0:T(8,128)(2,1)S(1)} %pad_maximum_fusion.2.own), channel_id=1, source_target_pairs={{0,32},{16,48},{32,64},{48,80},{64,96},{80,112},{96,0},{112,16},{1... | collective-permute-start | bytes 196616 | tf_op jit(solution)/shard_map/ppermute | solution.py:16
  103.7 9.5 %collective-permute-start.18 = (bf16[2,128,128]{2,1,0:T(8,128)(2,1)S(1)}, bf16[2,128,128]{2,1,0:T(8,128)(2,1)S(1)}, u32[]{:S(2)}, u32[]{:S(2)}) collective-permute-start(bf16[2,128,128]{2,1,0:T(8,128)(2,1)S(1)} %pad_maximum_fusion.2.own), channel_id=1, source_target_pairs={{0,96},{16,112},{32,0},{48,16},{64,32},{80,48},{96,64},{112,80},{1... | collective-permute-start | bytes 196616 | tf_op jit(solution)/shard_map/ppermute | solution.py:16
  106.9 6.3 %collective-permute-start.19 = (bf16[2,128,128]{2,1,0:T(8,128)(2,1)S(1)}, bf16[2,128,128]{2,1,0:T(8,128)(2,1)S(1)}, u32[]{:S(2)}, u32[]{:S(2)}) collective-permute-start(bf16[2,128,128]{2,1,0:T(8,128)(2,1)S(1)} %pad_maximum_fusion.2.own), channel_id=1, source_target_pairs={{0,64},{16,80},{32,96},{48,112},{64,0},{80,16},{96,32},{112,48},{1... | collective-permute-start | bytes 196616 | tf_op jit(solution)/shard_map/ppermute | solution.py:16
  107.8 23.6 %all-to-all-start.4 = ((bf16[16,128,128]{2,1,0:T(8,128)(2,1)}), bf16[16,128,128]{2,1,0:T(8,128)(2,1)S(1)}, u32[]{:S(2)}, u32[]{:S(2)}) async-start(bf16[16,128,128]{2,1,0:T(8,128)(2,1)} %broadcast_in_dim.7), calls=%async_computation.4 | async-start | bytes 1048576 | tf_op jit(solution)/shard_map/all_to_all | solution.py:262
  114.9 7.5 %collective-permute-start.22 = (bf16[128,128]{1,0:T(8,128)(2,1)S(1)}, bf16[128,128]{1,0:T(8,128)(2,1)S(1)}, u32[]{:S(2)}, u32[]{:S(2)}) collective-permute-start(bf16[128,128]{1,0:T(8,128)(2,1)S(1)} %get-tuple-element.64), channel_id=1, source_target_pairs={{0,3},{1,0},{2,1},{3,2},{4,7},{5,4},{6,5},{7,6},{8,11},{9,8},{10,9... | collective-permute-start | bytes 98312 | tf_op jit(solution)/shard_map/ppermute | solution.py:36
  118.1 6.7 %collective-permute-start.21 = (bf16[128,128]{1,0:T(8,128)(2,1)S(1)}, bf16[128,128]{1,0:T(8,128)(2,1)S(1)}, u32[]{:S(2)}, u32[]{:S(2)}) collective-permute-start(bf16[128,128]{1,0:T(8,128)(2,1)S(1)} %get-tuple-element.63), channel_id=1, source_target_pairs={{0,2},{1,3},{2,0},{3,1},{4,6},{5,7},{6,4},{7,5},{8,10},{9,11},{10,... | collective-permute-start | bytes 98312 | tf_op jit(solution)/shard_map/ppermute | solution.py:36
  119.0 5.8 %collective-permute-start.20 = (bf16[128,128]{1,0:T(8,128)(2,1)S(1)}, bf16[128,128]{1,0:T(8,128)(2,1)S(1)}, u32[]{:S(2)}, u32[]{:S(2)}) collective-permute-start(bf16[128,128]{1,0:T(8,128)(2,1)S(1)} %get-tuple-element.62), channel_id=1, source_target_pairs={{0,1},{1,2},{2,3},{3,0},{4,5},{5,6},{6,7},{7,4},{8,9},{9,10},{10,1... | collective-permute-start | bytes 98312 | tf_op jit(solution)/shard_map/ppermute | solution.py:36
  126.2 5.9 %collective-permute-start.24 = (bf16[2,128,128]{2,1,0:T(8,128)(2,1)S(1)}, bf16[2,128,128]{2,1,0:T(8,128)(2,1)S(1)}, u32[]{:S(2)}, u32[]{:S(2)}) collective-permute-start(bf16[2,128,128]{2,1,0:T(8,128)(2,1)S(1)} %pad_maximum_fusion.3.own), channel_id=1, source_target_pairs={{0,32},{16,48},{32,64},{48,80},{64,96},{80,112},{96,0},{112,16},{1... | collective-permute-start | bytes 196616 | tf_op jit(solution)/shard_map/ppermute | solution.py:16
  127.1 5.4 %collective-permute-start.25 = (bf16[2,128,128]{2,1,0:T(8,128)(2,1)S(1)}, bf16[2,128,128]{2,1,0:T(8,128)(2,1)S(1)}, u32[]{:S(2)}, u32[]{:S(2)}) collective-permute-start(bf16[2,128,128]{2,1,0:T(8,128)(2,1)S(1)} %pad_maximum_fusion.3.own), channel_id=1, source_target_pairs={{0,96},{16,112},{32,0},{48,16},{64,32},{80,48},{96,64},{112,80},{1... | collective-permute-start | bytes 196616 | tf_op jit(solution)/shard_map/ppermute | solution.py:16
  129.5 5.8 %collective-permute-start.26 = (bf16[2,128,128]{2,1,0:T(8,128)(2,1)S(1)}, bf16[2,128,128]{2,1,0:T(8,128)(2,1)S(1)}, u32[]{:S(2)}, u32[]{:S(2)}) collective-permute-start(bf16[2,128,128]{2,1,0:T(8,128)(2,1)S(1)} %pad_maximum_fusion.3.own), channel_id=1, source_target_pairs={{0,64},{16,80},{32,96},{48,112},{64,0},{80,16},{96,32},{112,48},{1... | collective-permute-start | bytes 196616 | tf_op jit(solution)/shard_map/ppermute | solution.py:16
  138.3 5.4 %collective-permute-start.28 = (bf16[128,128]{1,0:T(8,128)(2,1)S(1)}, bf16[128,128]{1,0:T(8,128)(2,1)S(1)}, u32[]{:S(2)}, u32[]{:S(2)}) collective-permute-start(bf16[128,128]{1,0:T(8,128)(2,1)S(1)} %get-tuple-element.72), channel_id=1, source_target_pairs={{0,2},{1,3},{2,0},{3,1},{4,6},{5,7},{6,4},{7,5},{8,10},{9,11},{10,... | collective-permute-start | bytes 98312 | tf_op jit(solution)/shard_map/ppermute | solution.py:36
  139.4 5.1 %collective-permute-start.27 = (bf16[128,128]{1,0:T(8,128)(2,1)S(1)}, bf16[128,128]{1,0:T(8,128)(2,1)S(1)}, u32[]{:S(2)}, u32[]{:S(2)}) collective-permute-start(bf16[128,128]{1,0:T(8,128)(2,1)S(1)} %get-tuple-element.71), channel_id=1, source_target_pairs={{0,1},{1,2},{2,3},{3,0},{4,5},{5,6},{6,7},{7,4},{8,9},{9,10},{10,1... | collective-permute-start | bytes 98312 | tf_op jit(solution)/shard_map/ppermute | solution.py:36
  145.5 14.3 %all-to-all-start.5 = ((bf16[16,128,128]{2,1,0:T(8,128)(2,1)}), bf16[16,128,128]{2,1,0:T(8,128)(2,1)S(1)}, u32[]{:S(2)}, u32[]{:S(2)}) async-start(bf16[16,128,128]{2,1,0:T(8,128)(2,1)} %broadcast_in_dim.8), calls=%async_computation.5 | async-start | bytes 1048576 | tf_op jit(solution)/shard_map/all_to_all | solution.py:262
  161.9 5.9 %collective-permute-start.33 = (f32[32,512]{1,0:T(8,128)S(1)}, f32[32,512]{1,0:T(8,128)S(1)}, u32[]{:S(2)}, u32[]{:S(2)}) collective-permute-start(f32[32,512]{1,0:T(8,128)S(1)} %add.192), channel_id=1, source_target_pairs={{0,64},{16,80},{32,96},{48,112},{64,0},{80,16},{96,32},{112,48},{1... | collective-permute-start | bytes 196616 | tf_op jit(solution)/shard_map/ppermute | solution.py:16
  164.9 5.5 %collective-permute-start.31 = (f32[32,512]{1,0:T(8,128)S(1)}, f32[32,512]{1,0:T(8,128)S(1)}, u32[]{:S(2)}, u32[]{:S(2)}) collective-permute-start(f32[32,512]{1,0:T(8,128)S(1)} %add.192), channel_id=1, source_target_pairs={{0,32},{16,48},{32,64},{48,80},{64,96},{80,112},{96,0},{112,16},{1... | collective-permute-start | bytes 196616 | tf_op jit(solution)/shard_map/ppermute | solution.py:16
  (12 other events, 68.6 us)

commit v14 on v13

--- a/solution.py
+++ b/solution.py
@@ -292,21 +292,21 @@
         (before, after, sibling, upper, lower)
     )
     left = (upper, lower)
-    panels = in_hbm(y_gather(lines))
+    panels, late = in_hbm(y_gather(lines[:, :2])), lines[:, 2:]
     far_low, far_high = x_shift(before[:, :128, :], 1), x_shift(after[:, 128:, :], -1)
     halves = lambda v: [(in_hbm(v), 0), (in_hbm(v), 1)]
     pieces = halves(prev_solution) + halves(sibling)
     for block in (before, after):
         pieces += halves(block) + halves(other_core(block))
     started = products(order[:6], left, pieces)
-    far_low, far_high, token = lax.optimization_barrier(
-        (far_low, far_high, started[:8, :128])
+    far_low, far_high, token, panels = lax.optimization_barrier(
+        (far_low, far_high, started[:8, :128], panels)
     )
     far = (far_low, far_high)
     pieces = [(v, 0) for v in far] + [(other_core(v), 0) for v in far]
     first, second = products(order[6:], left, pieces, started, token, last=True)
 
-    first, second, panels = lax.optimization_barrier((first, second, panels))
+    first, second, late = lax.optimization_barrier((first, second, late))
     panels = in_hbm(panels)
     known = lax.dynamic_slice(cross, (0, 64 * z, 128 * y), (4, 64, 128))
     known = known.astype(F32).reshape(2, 128, 128)
@@ -315,13 +315,15 @@
     rest = known[1] - over_sites(second)
     solved_first = over_z(stage(order, targets, over_cores(first_rhs), panels, 0)).astype(BF)
     pair, rest = lax.optimization_barrier((over_cores(solved_first), rest))
-    every_first = all_sites(solved_first)
+    sent, late = lax.optimization_barrier((solved_first, late))
+    late = in_hbm(y_gather(late))
     parts = stage(order, targets, pair, panels, 1)
     second_rhs = (rest - over_z(parts)).astype(BF)
-    *parts, every_first = lax.optimization_barrier(
-        (*stage(order, targets, over_cores(second_rhs), panels, 2), every_first)
-    )
+    pair, late = lax.optimization_barrier((over_cores(second_rhs), late))
+    every_first = all_sites(sent)
+    parts = stage(order, targets, pair, in_hbm(late), 0)
     solved_second = over_z(parts).astype(BF)
+    solved_second, every_first = lax.optimization_barrier((solved_second, every_first))
     every_second = all_sites(solved_second)
     outer = outer_part(every_first, col) + outer_part(every_second, col)
     pred_cov = prior_cov - row_sum(outer) / S

time: 172 us -> 178 us (1.035)
  starting transfers between devices: 64.6 us -> 69.5 us
    ppermute x16, waiting for transfers between devices: 10.7 us -> 18.7 us  [x_shift(): return lax.ppermute(v, 'row', [(r, (r + 2 * step) % 8) for r in range(8)])]
    ppermute x9, waiting for transfers between devices: 14.3 us -> 7.9 us  [z_shift(): lax.ppermute(v, 'col', [(c, c // 4 * 4 + (c + step) % 4) for c in range(1...]
    all_to_all x1 -> x2, starting transfers between devices: 4.65 us -> 8.75 us  [y_gather(): lax.all_to_all(sent, 'col', 0, 0, axis_index_groups=groups, tiled=True)]
    all_to_all x2, starting transfers between devices: 9.49 us -> 12.9 us  [all_sites(): lax.all_to_all(sent, 'col', 0, 0, tiled=True).reshape(4, 4, 2, 64, 128)]
    ppermute x16, starting transfers between devices: 24.1 us -> 21.1 us  [x_shift(): return lax.ppermute(v, 'row', [(r, (r + 2 * step) % 8) for r in range(8)])]
    all_to_all x1 -> x2, waiting for transfers between devices: 5.83 us -> 3.19 us  [y_gather(): lax.all_to_all(sent, 'col', 0, 0, axis_index_groups=groups, tiled=True)]
  transfers between devices with their start and end apart: 40 -> 41, of which waited for: 24 -> 24; matrix products, arithmetic and copies ran while one was open for 4% -> 3% of each run, Pallas kernels for 19% -> 16%
where the time goes in v14:
time: 178 us; the launch traced here: 177 us
  starting transfers between devices  69.5 us (39%)
  waiting for transfers between devices  59.6 us (33%)
  Pallas kernels  36.7 us (21%)
  local copies, waits for them, and re-layouts  6.6 us (4%)
  other arithmetic  3.01 us (2%)
    ppermute x16, starting transfers between devices, x_shift(): return lax.ppermute(v, 'row', [(r, (r + 2 * step) % 8) for r in range(8)])  21.1 us
    ppermute x16, waiting for transfers between devices, x_shift(): return lax.ppermute(v, 'row', [(r, (r + 2 * step) % 8) for r in range(8)])  18.7 us
    pallas_call x2, Pallas kernels, products(): pl.pallas_call(kernel, grid_spec=pltpu.PrefetchScalarGridSpec(num_scalar_...  18.5 us
    all_to_all x2, starting transfers between devices, all_sites(): lax.all_to_all(sent, 'col', 0, 0, tiled=True).reshape(4, 4, 2, 64, 128)  12.9 us
    ppermute x9, starting transfers between devices, z_shift(): lax.ppermute(v, 'col', [(c, c // 4 * 4 + (c + step) % 4) for c in range(1...  12.7 us
    all_to_all x2, waiting for transfers between devices, over_sites(): lax.all_to_all(partial, 'col', 0, 0, tiled=True).astype(F32).sum(axis=0)  11 us
    pallas_call x2, Pallas kernels, split_tiles(): pl.pallas_call(split_tiles_kernel, grid=(2,), in_specs=[pl.BlockSpec((1,...  10.8 us
    all_to_all x2, waiting for transfers between devices, all_sites(): lax.all_to_all(sent, 'col', 0, 0, tiled=True).reshape(4, 4, 2, 64, 128)  9.7 us
  transfers between devices with their start and end apart: 41, of which 24 were waited for; matrix products, arithmetic and copies ran while one was open for 3% of the time, Pallas kernels for 16%

profile of v14, /device:TPU:0, one launch (start us, length us, event | category | flops | bytes accessed | tf_op | source)
XLA Modules:
  0.0 176.9 jit_solution(17004350560936842271)
XLA Ops:
  0.6 2.3 %shard_map.77.token = bf16[4,3,64,512]{3,2,1,0:T(8,128)(2,1)} custom-call(bf16[2,512,256]{2,1,0:T(8,128)(2,1)} %bitcast.47, bf16[2,512,256]{2,1,0:T(8,128)(2,1)} %bitcast.48, bf16[512,256]{1,0:T(8,128)(2,1)} %bitcast.50), custom_call_target="tpu_custom_call" | custom-call | tf_op jit(solution)/shard_map/pallas_call | solution.py:63
  2.9 5.4 %all-to-all-start = ((bf16[4,3,64,512]{3,2,1,0:T(8,128)(2,1)}), bf16[4,3,64,512]{3,2,1,0:T(8,128)(2,1)S(1)}, u32[]{:S(2)}, u32[]{:S(2)}) async-start(bf16[4,3,64,512]{3,2,1,0:T(8,128)(2,1)} %shard_map.77.token), calls=%async_computation | async-start | bytes 1572864 | tf_op jit(solution)/shard_map/all_to_all | solution.py:25
  9.8 1.7 collective-permute-start.1
  11.5 5.4 %shard_map.78.token.upper = bf16[8,512,768]{2,1,0:T(8,128)(2,1)} custom-call(bf16[4,256,24,256]{3,2,1,0:T(8,128)(2,1)} %src.3, bf16[4,3,64,512]{3,2,1,0:T(8,128)(2,1)} %shard_map.77.token), custom_call_target="tpu_custom_call" | custom-call | bytes 12582912 | tf_op jit(solution)/shard_map/pallas_call | solution.py:86
  16.9 3.6 %all-to-all-done = bf16[4,3,64,512]{3,2,1,0:T(8,128)(2,1)S(1)} async-done(((bf16[4,3,64,512]{3,2,1,0:T(8,128)(2,1)}), bf16[4,3,64,512]{3,2,1,0:T(8,128)(2,1)S(1)}, u32[]{:S(2)}, u32[]{:S(2)}) %all-to-all-start) | async-done | bytes 786464 | tf_op jit(solution)/shard_map/all_to_all | solution.py:25
  22.2 4.5 %all-to-all-start.1 = ((bf16[4,4,2,64,512]{4,3,2,1,0:T(8,128)(2,1)}), bf16[4,4,2,64,512]{4,3,2,1,0:T(8,128)(2,1)}, u32[]{:S(2)}, u32[]{:S(2)}) async-start(bf16[4,4,2,64,512]{4,3,2,1,0:T(8,128)(2,1)} %broadcast_in_dim.10), calls=%async_computation.1 | async-start | bytes 4194304 | tf_op jit(solution)/shard_map/all_to_all | solution.py:31
  26.6 5.4 %shard_map.79.lower = bf16[8,512,768]{2,1,0:T(8,128)(2,1)} custom-call(bf16[4,256,24,256]{3,2,1,0:T(8,128)(2,1)} %src.3, bf16[8,512,768]{2,1,0:T(8,128)(2,1)} %shard_map.78.token.upper), custom_call_target="tpu_custom_call" | custom-call | bytes 12582912 | tf_op jit(solution)/shard_map/pallas_call | solution.py:86
  34.7 1.7 collective-permute-start.6
  36.5 12.4 %shard_map.80.before = f32[1024,512]{1,0:T(8,128)S(1)} custom-call(s32[6]{0:T(128)S(1)} %stack.88.order, bf16[8,512,768]{2,1,0:T(8,128)(2,1)} %shard_map.78.token.upper, bf16[8,512,768]{2,1,0:T(8,128)(2,1)} %shard_map.79.lower, bf16[3,256,512]{2,1,0:T(8,128)(2,1)} %refs_1_.1, bf16[3,256,512]{2,1,0:T(8,128)(2,1)} %refs_1_.1, bf16[3,256,512]{2,1,0:T(8,128)(2,1)} %copy-done.4, ...), custom_call_target="tpu_custom_call" | custom-call | flops 4831838208 | bytes 16252928 | tf_op jit(solution)/shard_map/pallas_call | solution.py:184
  48.9 3.2 %all-to-all-done.1 = bf16[4,4,2,64,512]{4,3,2,1,0:T(8,128)(2,1)} async-done(((bf16[4,4,2,64,512]{4,3,2,1,0:T(8,128)(2,1)}), bf16[4,4,2,64,512]{4,3,2,1,0:T(8,128)(2,1)}, u32[]{:S(2)}, u32[]{:S(2)}) %all-to-all-start.1) | async-done | bytes 2097184 | tf_op jit(solution)/shard_map/all_to_all | solution.py:31
  54.5 6.1 %shard_map.81 = (bf16[16,128,128]{2,1,0:T(8,128)(2,1)}, bf16[16,128,128]{2,1,0:T(8,128)(2,1)}) custom-call(s32[2]{0:T(128)S(1)} %pad_add_fusion.1.order, bf16[8,512,768]{2,1,0:T(8,128)(2,1)} %shard_map.78.token.upper, bf16[8,512,768]{2,1,0:T(8,128)(2,1)} %shard_map.79.lower, f32[1024,512]{1,0:T(8,128)S(1)} %shard_map.80.before, f32[8,128]{1,0:T(8,128)S(1)} %slice.35.token, ...), custom_call_target="tpu_custom_call" | custom-call | flops 1610612736 | bytes 6815744 | tf_op jit(solution)/shard_map/pallas_call | solution.py:184
  60.6 3.9 %all-to-all-start.2 = ((bf16[16,128,128]{2,1,0:T(8,128)(2,1)}), bf16[16,128,128]{2,1,0:T(8,128)(2,1)S(1)}, u32[]{:S(2)}, u32[]{:S(2)}) async-start(bf16[16,128,128]{2,1,0:T(8,128)(2,1)} %get-tuple-element.52), calls=%async_computation.2 | async-start | bytes 1048576 | tf_op jit(solution)/shard_map/all_to_all | solution.py:257
  65.4 11.0 %all-to-all-done.2 = bf16[16,128,128]{2,1,0:T(8,128)(2,1)S(1)} async-done(((bf16[16,128,128]{2,1,0:T(8,128)(2,1)}), bf16[16,128,128]{2,1,0:T(8,128)(2,1)S(1)}, u32[]{:S(2)}, u32[]{:S(2)}) %all-to-all-start.2) | async-done | bytes 524320 | tf_op jit(solution)/shard_map/all_to_all | solution.py:257
  76.7 3.6 %all-to-all-start.3 = ((bf16[16,128,128]{2,1,0:T(8,128)(2,1)}), bf16[16,128,128]{2,1,0:T(8,128)(2,1)S(1)}, u32[]{:S(2)}, u32[]{:S(2)}) async-start(bf16[16,128,128]{2,1,0:T(8,128)(2,1)} %get-tuple-element.60), calls=%async_computation.3 | async-start | bytes 1048576 | tf_op jit(solution)/shard_map/all_to_all | solution.py:257
  81.8 1.7 collective-permute-start.11
  83.6 1.8 %collective-permute-start.12 = (bf16[2,128,128]{2,1,0:T(8,128)(2,1)S(1)}, bf16[2,128,128]{2,1,0:T(8,128)(2,1)S(1)}, u32[]{:S(2)}, u32[]{:S(2)}) collective-permute-start(bf16[2,128,128]{2,1,0:T(8,128)(2,1)S(1)} %pad_maximum_fusion.1.own), channel_id=1, source_target_pairs={{0,64},{16,80},{32,96},{48,112},{64,0},{80,16},{96,32},{112,48},{1... | collective-permute-start | bytes 196616 | tf_op jit(solution)/shard_map/ppermute | solution.py:16
  86.1 3.2 %collective-permute-done.12.three = bf16[2,128,128]{2,1,0:T(8,128)(2,1)S(1)} collective-permute-done((bf16[2,128,128]{2,1,0:T(8,128)(2,1)S(1)}, bf16[2,128,128]{2,1,0:T(8,128)(2,1)S(1)}, u32[]{:S(2)}, u32[]{:S(2)}) %collective-permute-start.12) | collective-permute-done | bytes 65568 | tf_op jit(solution)/shard_map/ppermute | solution.py:16
  89.4 1.7 shard_map.82
  91.1 3.1 %collective-permute-start.15 = (bf16[128,128]{1,0:T(8,128)(2,1)S(1)}, bf16[128,128]{1,0:T(8,128)(2,1)S(1)}, u32[]{:S(2)}, u32[]{:S(2)}) collective-permute-start(bf16[128,128]{1,0:T(8,128)(2,1)S(1)} %get-tuple-element.59), channel_id=1, source_target_pairs={{0,3},{1,0},{2,1},{3,2},{4,7},{5,4},{6,5},{7,6},{8,11},{9,8},{10,9... | collective-permute-start | bytes 98312 | tf_op jit(solution)/shard_map/ppermute | solution.py:36
  95.9 3.7 %collective-permute-done.14 = bf16[128,128]{1,0:T(8,128)(2,1)S(1)} collective-permute-done((bf16[128,128]{1,0:T(8,128)(2,1)S(1)}, bf16[128,128]{1,0:T(8,128)(2,1)S(1)}, u32[]{:S(2)}, u32[]{:S(2)}) %collective-permute-start.14) | collective-permute-done | bytes 32800 | tf_op jit(solution)/shard_map/ppermute | solution.py:36
  101.3 4.3 %all-to-all-start.4 = ((bf16[4,4,1,64,512]{4,3,1,2,0:T(8,128)(2,1)}), bf16[4,4,1,64,512]{4,3,1,2,0:T(8,128)(2,1)S(1)}, u32[]{:S(2)}, u32[]{:S(2)}) async-start(bf16[4,4,1,64,512]{4,3,1,2,0:T(8,128)(2,1)} %broadcast_in_dim.12), calls=%async_computation.4 | async-start | bytes 2097152 | tf_op jit(solution)/shard_map/all_to_all | solution.py:31
  107.2 2.9 %collective-permute-start.18 = (bf16[2,128,128]{2,1,0:T(8,128)(2,1)S(1)}, bf16[2,128,128]{2,1,0:T(8,128)(2,1)S(1)}, u32[]{:S(2)}, u32[]{:S(2)}) collective-permute-start(bf16[2,128,128]{2,1,0:T(8,128)(2,1)S(1)} %pad_maximum_fusion.2.own), channel_id=1, source_target_pairs={{0,96},{16,112},{32,0},{48,16},{64,32},{80,48},{96,64},{112,80},{1... | collective-permute-start | bytes 196616 | tf_op jit(solution)/shard_map/ppermute | solution.py:16
  113.0 2.9 %collective-permute-done.19.three = bf16[2,128,128]{2,1,0:T(8,128)(2,1)S(1)} collective-permute-done((bf16[2,128,128]{2,1,0:T(8,128)(2,1)S(1)}, bf16[2,128,128]{2,1,0:T(8,128)(2,1)S(1)}, u32[]{:S(2)}, u32[]{:S(2)}) %collective-permute-start.19) | collective-permute-done | bytes 65568 | tf_op jit(solution)/shard_map/ppermute | solution.py:16
  121.7 7.6 %all-to-all-start.5 = ((bf16[16,128,128]{2,1,0:T(8,128)(2,1)}), bf16[16,128,128]{2,1,0:T(8,128)(2,1)S(1)}, u32[]{:S(2)}, u32[]{:S(2)}) async-start(bf16[16,128,128]{2,1,0:T(8,128)(2,1)} %broadcast_in_dim.13), calls=%async_computation.5 | async-start | bytes 1048576 | tf_op jit(solution)/shard_map/all_to_all | solution.py:262
  130.7 3.2 %collective-permute-start.25 = (bf16[2,128,128]{2,1,0:T(8,128)(2,1)S(1)}, bf16[2,128,128]{2,1,0:T(8,128)(2,1)S(1)}, u32[]{:S(2)}, u32[]{:S(2)}) collective-permute-start(bf16[2,128,128]{2,1,0:T(8,128)(2,1)S(1)} %pad_maximum_fusion.3.own), channel_id=1, source_target_pairs={{0,96},{16,112},{32,0},{48,16},{64,32},{80,48},{96,64},{112,80},{1... | collective-permute-start | bytes 196616 | tf_op jit(solution)/shard_map/ppermute | solution.py:16
  134.0 2.2 %collective-permute-done.24.one = bf16[2,128,128]{2,1,0:T(8,128)(2,1)S(1)} collective-permute-done((bf16[2,128,128]{2,1,0:T(8,128)(2,1)S(1)}, bf16[2,128,128]{2,1,0:T(8,128)(2,1)S(1)}, u32[]{:S(2)}, u32[]{:S(2)}) %collective-permute-start.24) | collective-permute-done | bytes 65568 | tf_op jit(solution)/shard_map/ppermute | solution.py:16
  136.8 3.0 %collective-permute-done.26.three = bf16[2,128,128]{2,1,0:T(8,128)(2,1)S(1)} collective-permute-done((bf16[2,128,128]{2,1,0:T(8,128)(2,1)S(1)}, bf16[2,128,128]{2,1,0:T(8,128)(2,1)S(1)}, u32[]{:S(2)}, u32[]{:S(2)}) %collective-permute-start.26) | collective-permute-done | bytes 65568 | tf_op jit(solution)/shard_map/ppermute | solution.py:16
  141.5 3.2 %collective-permute-start.29 = (bf16[128,128]{1,0:T(8,128)(2,1)S(1)}, bf16[128,128]{1,0:T(8,128)(2,1)S(1)}, u32[]{:S(2)}, u32[]{:S(2)}) collective-permute-start(bf16[128,128]{1,0:T(8,128)(2,1)S(1)} %get-tuple-element.74), channel_id=1, source_target_pairs={{0,3},{1,0},{2,1},{3,2},{4,7},{5,4},{6,5},{7,6},{8,11},{9,8},{10,9... | collective-permute-start | bytes 98312 | tf_op jit(solution)/shard_map/ppermute | solution.py:36
  147.0 3.1 %collective-permute-done.28 = bf16[128,128]{1,0:T(8,128)(2,1)S(1)} collective-permute-done((bf16[128,128]{1,0:T(8,128)(2,1)S(1)}, bf16[128,128]{1,0:T(8,128)(2,1)S(1)}, u32[]{:S(2)}, u32[]{:S(2)}) %collective-permute-start.28) | collective-permute-done | bytes 32800 | tf_op jit(solution)/shard_map/ppermute | solution.py:36
  151.6 5.3 %all-to-all-start.6 = ((bf16[16,128,128]{2,1,0:T(8,128)(2,1)}), bf16[16,128,128]{2,1,0:T(8,128)(2,1)S(1)}, u32[]{:S(2)}, u32[]{:S(2)}) async-start(bf16[16,128,128]{2,1,0:T(8,128)(2,1)} %broadcast_in_dim.14), calls=%async_computation.6 | async-start | bytes 1048576 | tf_op jit(solution)/shard_map/all_to_all | solution.py:262
  157.2 9.7 %all-to-all-done.6 = bf16[16,128,128]{2,1,0:T(8,128)(2,1)S(1)} async-done(((bf16[16,128,128]{2,1,0:T(8,128)(2,1)}), bf16[16,128,128]{2,1,0:T(8,128)(2,1)S(1)}, u32[]{:S(2)}, u32[]{:S(2)}) %all-to-all-start.6) | async-done | bytes 524320 | tf_op jit(solution)/shard_map/all_to_all | solution.py:262
  172.4 2.7 %collective-permute-done.33 = f32[32,512]{1,0:T(8,128)S(1)} collective-permute-done((f32[32,512]{1,0:T(8,128)S(1)}, f32[32,512]{1,0:T(8,128)S(1)}, u32[]{:S(2)}, u32[]{:S(2)}) %collective-permute-start.33) | collective-permute-done | bytes 65568 | tf_op jit(solution)/shard_map/ppermute | solution.py:16
  (106 shorter events, 40.3 us)
Async XLA Ops:
  2.9 17.7 %all-to-all-start = ((bf16[4,3,64,512]{3,2,1,0:T(8,128)(2,1)}), bf16[4,3,64,512]{3,2,1,0:T(8,128)(2,1)S(1)}, u32[]{:S(2)}, u32[]{:S(2)}) async-start(bf16[4,3,64,512]{3,2,1,0:T(8,128)(2,1)} %shard_map.77.token), calls=%async_computation | async-start | bytes 1572864 | tf_op jit(solution)/shard_map/all_to_all | solution.py:25
  8.3 23.8 %collective-permute-start = (bf16[3,256,512]{2,1,0:T(8,128)(2,1)}, bf16[3,256,512]{2,1,0:T(8,128)(2,1)S(1)}, u32[]{:S(2)}, u32[]{:S(2)}) collective-permute-start(bf16[3,256,512]{2,1,0:T(8,128)(2,1)} %refs_1_.1), channel_id=1, source_target_pairs={{0,32},{16,48},{32,64},{48,80},{64,96},{80,112},{96,0},{112,16},{1... | collective-permute-start | bytes 2359304 | tf_op jit(solution)/shard_map/ppermute | solution.py:16
  9.8 22.3 %collective-permute-start.1 = (bf16[3,256,512]{2,1,0:T(8,128)(2,1)}, bf16[3,256,512]{2,1,0:T(8,128)(2,1)S(1)}, u32[]{:S(2)}, u32[]{:S(2)}) collective-permute-start(bf16[3,256,512]{2,1,0:T(8,128)(2,1)} %refs_1_.1), channel_id=1, source_target_pairs={{0,96},{16,112},{32,0},{48,16},{64,32},{80,48},{96,64},{112,80},{1... | collective-permute-start | bytes 2359304 | tf_op jit(solution)/shard_map/ppermute | solution.py:16
  11.5 20.6 %collective-permute-start.2 = (bf16[3,256,512]{2,1,0:T(8,128)(2,1)}, bf16[3,256,512]{2,1,0:T(8,128)(2,1)S(1)}, u32[]{:S(2)}, u32[]{:S(2)}) collective-permute-start(bf16[3,256,512]{2,1,0:T(8,128)(2,1)} %refs_1_.1), channel_id=1, source_target_pairs={{0,16},{16,0},{32,48},{48,32},{64,80},{80,64},{96,112},{112,96},{1... | collective-permute-start | bytes 2359304 | tf_op jit(solution)/shard_map/ppermute | solution.py:20
  22.2 29.9 %all-to-all-start.1 = ((bf16[4,4,2,64,512]{4,3,2,1,0:T(8,128)(2,1)}), bf16[4,4,2,64,512]{4,3,2,1,0:T(8,128)(2,1)}, u32[]{:S(2)}, u32[]{:S(2)}) async-start(bf16[4,4,2,64,512]{4,3,2,1,0:T(8,128)(2,1)} %broadcast_in_dim.10), calls=%async_computation.1 | async-start | bytes 4194304 | tf_op jit(solution)/shard_map/all_to_all | solution.py:31
  33.2 15.7 %collective-permute-start.5 = (bf16[3,128,512]{2,1,0:T(8,128)(2,1)S(1)}, bf16[3,128,512]{2,1,0:T(8,128)(2,1)S(1)}, u32[]{:S(2)}, u32[]{:S(2)}) collective-permute-start(bf16[3,128,512]{2,1,0:T(8,128)(2,1)S(1)} %slice.28), channel_id=1, source_target_pairs={{0,32},{16,48},{32,64},{48,80},{64,96},{80,112},{96,0},{112,16},{1... | collective-permute-start | bytes 1179656 | tf_op jit(solution)/shard_map/ppermute | solution.py:16
  34.7 14.2 %collective-permute-start.6 = (bf16[3,128,512]{2,1,0:T(8,128)(2,1)S(1)}, bf16[3,128,512]{2,1,0:T(8,128)(2,1)S(1)}, u32[]{:S(2)}, u32[]{:S(2)}) collective-permute-start(bf16[3,128,512]{2,1,0:T(8,128)(2,1)S(1)} %slice.29), channel_id=1, source_target_pairs={{0,96},{16,112},{32,0},{48,16},{64,32},{80,48},{96,64},{112,80},{1... | collective-permute-start | bytes 1179656 | tf_op jit(solution)/shard_map/ppermute | solution.py:16
  60.6 15.7 %all-to-all-start.2 = ((bf16[16,128,128]{2,1,0:T(8,128)(2,1)}), bf16[16,128,128]{2,1,0:T(8,128)(2,1)S(1)}, u32[]{:S(2)}, u32[]{:S(2)}) async-start(bf16[16,128,128]{2,1,0:T(8,128)(2,1)} %get-tuple-element.52), calls=%async_computation.2 | async-start | bytes 1048576 | tf_op jit(solution)/shard_map/all_to_all | solution.py:257
  76.7 23.5 %all-to-all-start.3 = ((bf16[16,128,128]{2,1,0:T(8,128)(2,1)}), bf16[16,128,128]{2,1,0:T(8,128)(2,1)S(1)}, u32[]{:S(2)}, u32[]{:S(2)}) async-start(bf16[16,128,128]{2,1,0:T(8,128)(2,1)} %get-tuple-element.60), calls=%async_computation.3 | async-start | bytes 1048576 | tf_op jit(solution)/shard_map/all_to_all | solution.py:257
  80.3 5.8 %collective-permute-start.10 = (bf16[2,128,128]{2,1,0:T(8,128)(2,1)S(1)}, bf16[2,128,128]{2,1,0:T(8,128)(2,1)S(1)}, u32[]{:S(2)}, u32[]{:S(2)}) collective-permute-start(bf16[2,128,128]{2,1,0:T(8,128)(2,1)S(1)} %pad_maximum_fusion.1.own), channel_id=1, source_target_pairs={{0,32},{16,48},{32,64},{48,80},{64,96},{80,112},{96,0},{112,16},{1... | collective-permute-start | bytes 196616 | tf_op jit(solution)/shard_map/ppermute | solution.py:16
  83.6 5.8 %collective-permute-start.12 = (bf16[2,128,128]{2,1,0:T(8,128)(2,1)S(1)}, bf16[2,128,128]{2,1,0:T(8,128)(2,1)S(1)}, u32[]{:S(2)}, u32[]{:S(2)}) collective-permute-start(bf16[2,128,128]{2,1,0:T(8,128)(2,1)S(1)} %pad_maximum_fusion.1.own), channel_id=1, source_target_pairs={{0,64},{16,80},{32,96},{48,112},{64,0},{80,16},{96,32},{112,48},{1... | collective-permute-start | bytes 196616 | tf_op jit(solution)/shard_map/ppermute | solution.py:16
  91.1 4.8 %collective-permute-start.15 = (bf16[128,128]{1,0:T(8,128)(2,1)S(1)}, bf16[128,128]{1,0:T(8,128)(2,1)S(1)}, u32[]{:S(2)}, u32[]{:S(2)}) collective-permute-start(bf16[128,128]{1,0:T(8,128)(2,1)S(1)} %get-tuple-element.59), channel_id=1, source_target_pairs={{0,3},{1,0},{2,1},{3,2},{4,7},{5,4},{6,5},{7,6},{8,11},{9,8},{10,9... | collective-permute-start | bytes 98312 | tf_op jit(solution)/shard_map/ppermute | solution.py:36
  94.2 5.4 %collective-permute-start.14 = (bf16[128,128]{1,0:T(8,128)(2,1)S(1)}, bf16[128,128]{1,0:T(8,128)(2,1)S(1)}, u32[]{:S(2)}, u32[]{:S(2)}) collective-permute-start(bf16[128,128]{1,0:T(8,128)(2,1)S(1)} %get-tuple-element.58), channel_id=1, source_target_pairs={{0,2},{1,3},{2,0},{3,1},{4,6},{5,7},{6,4},{7,5},{8,10},{9,11},{10,... | collective-permute-start | bytes 98312 | tf_op jit(solution)/shard_map/ppermute | solution.py:36
  95.0 5.1 %collective-permute-start.13 = (bf16[128,128]{1,0:T(8,128)(2,1)S(1)}, bf16[128,128]{1,0:T(8,128)(2,1)S(1)}, u32[]{:S(2)}, u32[]{:S(2)}) collective-permute-start(bf16[128,128]{1,0:T(8,128)(2,1)S(1)} %get-tuple-element.57), channel_id=1, source_target_pairs={{0,1},{1,2},{2,3},{3,0},{4,5},{5,6},{6,7},{7,4},{8,9},{9,10},{10,1... | collective-permute-start | bytes 98312 | tf_op jit(solution)/shard_map/ppermute | solution.py:36
  101.3 19.4 %all-to-all-start.4 = ((bf16[4,4,1,64,512]{4,3,1,2,0:T(8,128)(2,1)}), bf16[4,4,1,64,512]{4,3,1,2,0:T(8,128)(2,1)S(1)}, u32[]{:S(2)}, u32[]{:S(2)}) async-start(bf16[4,4,1,64,512]{4,3,1,2,0:T(8,128)(2,1)} %broadcast_in_dim.12), calls=%async_computation.4 | async-start | bytes 2097152 | tf_op jit(solution)/shard_map/all_to_all | solution.py:31
  106.9 5.5 %collective-permute-start.17 = (bf16[2,128,128]{2,1,0:T(8,128)(2,1)S(1)}, bf16[2,128,128]{2,1,0:T(8,128)(2,1)S(1)}, u32[]{:S(2)}, u32[]{:S(2)}) collective-permute-start(bf16[2,128,128]{2,1,0:T(8,128)(2,1)S(1)} %pad_maximum_fusion.2.own), channel_id=1, source_target_pairs={{0,32},{16,48},{32,64},{48,80},{64,96},{80,112},{96,0},{112,16},{1... | collective-permute-start | bytes 196616 | tf_op jit(solution)/shard_map/ppermute | solution.py:16
  107.2 5.8 %collective-permute-start.18 = (bf16[2,128,128]{2,1,0:T(8,128)(2,1)S(1)}, bf16[2,128,128]{2,1,0:T(8,128)(2,1)S(1)}, u32[]{:S(2)}, u32[]{:S(2)}) collective-permute-start(bf16[2,128,128]{2,1,0:T(8,128)(2,1)S(1)} %pad_maximum_fusion.2.own), channel_id=1, source_target_pairs={{0,96},{16,112},{32,0},{48,16},{64,32},{80,48},{96,64},{112,80},{1... | collective-permute-start | bytes 196616 | tf_op jit(solution)/shard_map/ppermute | solution.py:16
  110.2 5.8 %collective-permute-start.19 = (bf16[2,128,128]{2,1,0:T(8,128)(2,1)S(1)}, bf16[2,128,128]{2,1,0:T(8,128)(2,1)S(1)}, u32[]{:S(2)}, u32[]{:S(2)}) collective-permute-start(bf16[2,128,128]{2,1,0:T(8,128)(2,1)S(1)} %pad_maximum_fusion.2.own), channel_id=1, source_target_pairs={{0,64},{16,80},{32,96},{48,112},{64,0},{80,16},{96,32},{112,48},{1... | collective-permute-start | bytes 196616 | tf_op jit(solution)/shard_map/ppermute | solution.py:16
  117.7 11.6 %collective-permute-start.22 = (bf16[128,128]{1,0:T(8,128)(2,1)S(1)}, bf16[128,128]{1,0:T(8,128)(2,1)S(1)}, u32[]{:S(2)}, u32[]{:S(2)}) collective-permute-start(bf16[128,128]{1,0:T(8,128)(2,1)S(1)} %get-tuple-element.66), channel_id=1, source_target_pairs={{0,3},{1,0},{2,1},{3,2},{4,7},{5,4},{6,5},{7,6},{8,11},{9,8},{10,9... | collective-permute-start | bytes 98312 | tf_op jit(solution)/shard_map/ppermute | solution.py:36
  118.1 11.2 %collective-permute-start.21 = (bf16[128,128]{1,0:T(8,128)(2,1)S(1)}, bf16[128,128]{1,0:T(8,128)(2,1)S(1)}, u32[]{:S(2)}, u32[]{:S(2)}) collective-permute-start(bf16[128,128]{1,0:T(8,128)(2,1)S(1)} %get-tuple-element.65), channel_id=1, source_target_pairs={{0,2},{1,3},{2,0},{3,1},{4,6},{5,7},{6,4},{7,5},{8,10},{9,11},{10,... | collective-permute-start | bytes 98312 | tf_op jit(solution)/shard_map/ppermute | solution.py:36
  119.5 9.8 %collective-permute-start.20 = (bf16[128,128]{1,0:T(8,128)(2,1)S(1)}, bf16[128,128]{1,0:T(8,128)(2,1)S(1)}, u32[]{:S(2)}, u32[]{:S(2)}) collective-permute-start(bf16[128,128]{1,0:T(8,128)(2,1)S(1)} %get-tuple-element.64), channel_id=1, source_target_pairs={{0,1},{1,2},{2,3},{3,0},{4,5},{5,6},{6,7},{7,4},{8,9},{9,10},{10,1... | collective-permute-start | bytes 98312 | tf_op jit(solution)/shard_map/ppermute | solution.py:36
  121.7 24.7 %all-to-all-start.5 = ((bf16[16,128,128]{2,1,0:T(8,128)(2,1)}), bf16[16,128,128]{2,1,0:T(8,128)(2,1)S(1)}, u32[]{:S(2)}, u32[]{:S(2)}) async-start(bf16[16,128,128]{2,1,0:T(8,128)(2,1)} %broadcast_in_dim.13), calls=%async_computation.5 | async-start | bytes 1048576 | tf_op jit(solution)/shard_map/all_to_all | solution.py:262
  130.7 5.5 %collective-permute-start.24 = (bf16[2,128,128]{2,1,0:T(8,128)(2,1)S(1)}, bf16[2,128,128]{2,1,0:T(8,128)(2,1)S(1)}, u32[]{:S(2)}, u32[]{:S(2)}) collective-permute-start(bf16[2,128,128]{2,1,0:T(8,128)(2,1)S(1)} %pad_maximum_fusion.3.own), channel_id=1, source_target_pairs={{0,32},{16,48},{32,64},{48,80},{64,96},{80,112},{96,0},{112,16},{1... | collective-permute-start | bytes 196616 | tf_op jit(solution)/shard_map/ppermute | solution.py:16
  130.7 6.0 %collective-permute-start.25 = (bf16[2,128,128]{2,1,0:T(8,128)(2,1)S(1)}, bf16[2,128,128]{2,1,0:T(8,128)(2,1)S(1)}, u32[]{:S(2)}, u32[]{:S(2)}) collective-permute-start(bf16[2,128,128]{2,1,0:T(8,128)(2,1)S(1)} %pad_maximum_fusion.3.own), channel_id=1, source_target_pairs={{0,96},{16,112},{32,0},{48,16},{64,32},{80,48},{96,64},{112,80},{1... | collective-permute-start | bytes 196616 | tf_op jit(solution)/shard_map/ppermute | solution.py:16
  134.0 5.8 %collective-permute-start.26 = (bf16[2,128,128]{2,1,0:T(8,128)(2,1)S(1)}, bf16[2,128,128]{2,1,0:T(8,128)(2,1)S(1)}, u32[]{:S(2)}, u32[]{:S(2)}) collective-permute-start(bf16[2,128,128]{2,1,0:T(8,128)(2,1)S(1)} %pad_maximum_fusion.3.own), channel_id=1, source_target_pairs={{0,64},{16,80},{32,96},{48,112},{64,0},{80,16},{96,32},{112,48},{1... | collective-permute-start | bytes 196616 | tf_op jit(solution)/shard_map/ppermute | solution.py:16
  141.5 5.5 %collective-permute-start.29 = (bf16[128,128]{1,0:T(8,128)(2,1)S(1)}, bf16[128,128]{1,0:T(8,128)(2,1)S(1)}, u32[]{:S(2)}, u32[]{:S(2)}) collective-permute-start(bf16[128,128]{1,0:T(8,128)(2,1)S(1)} %get-tuple-element.74), channel_id=1, source_target_pairs={{0,3},{1,0},{2,1},{3,2},{4,7},{5,4},{6,5},{7,6},{8,11},{9,8},{10,9... | collective-permute-start | bytes 98312 | tf_op jit(solution)/shard_map/ppermute | solution.py:36
  144.7 5.4 %collective-permute-start.28 = (bf16[128,128]{1,0:T(8,128)(2,1)S(1)}, bf16[128,128]{1,0:T(8,128)(2,1)S(1)}, u32[]{:S(2)}, u32[]{:S(2)}) collective-permute-start(bf16[128,128]{1,0:T(8,128)(2,1)S(1)} %get-tuple-element.73), channel_id=1, source_target_pairs={{0,2},{1,3},{2,0},{3,1},{4,6},{5,7},{6,4},{7,5},{8,10},{9,11},{10,... | collective-permute-start | bytes 98312 | tf_op jit(solution)/shard_map/ppermute | solution.py:36
  145.5 5.1 %collective-permute-start.27 = (bf16[128,128]{1,0:T(8,128)(2,1)S(1)}, bf16[128,128]{1,0:T(8,128)(2,1)S(1)}, u32[]{:S(2)}, u32[]{:S(2)}) collective-permute-start(bf16[128,128]{1,0:T(8,128)(2,1)S(1)} %get-tuple-element.72), channel_id=1, source_target_pairs={{0,1},{1,2},{2,3},{3,0},{4,5},{5,6},{6,7},{7,4},{8,9},{9,10},{10,1... | collective-permute-start | bytes 98312 | tf_op jit(solution)/shard_map/ppermute | solution.py:36
  151.6 15.4 %all-to-all-start.6 = ((bf16[16,128,128]{2,1,0:T(8,128)(2,1)}), bf16[16,128,128]{2,1,0:T(8,128)(2,1)S(1)}, u32[]{:S(2)}, u32[]{:S(2)}) async-start(bf16[16,128,128]{2,1,0:T(8,128)(2,1)} %broadcast_in_dim.14), calls=%async_computation.6 | async-start | bytes 1048576 | tf_op jit(solution)/shard_map/all_to_all | solution.py:262
  169.1 5.9 %collective-permute-start.33 = (f32[32,512]{1,0:T(8,128)S(1)}, f32[32,512]{1,0:T(8,128)S(1)}, u32[]{:S(2)}, u32[]{:S(2)}) collective-permute-start(f32[32,512]{1,0:T(8,128)S(1)} %add.192), channel_id=1, source_target_pairs={{0,64},{16,80},{32,96},{48,112},{64,0},{80,16},{96,32},{112,48},{1... | collective-permute-start | bytes 196616 | tf_op jit(solution)/shard_map/ppermute | solution.py:16
  169.2 5.9 %collective-permute-start.32 = (f32[32,512]{1,0:T(8,128)S(1)}, f32[32,512]{1,0:T(8,128)S(1)}, u32[]{:S(2)}, u32[]{:S(2)}) collective-permute-start(f32[32,512]{1,0:T(8,128)S(1)} %add.192), channel_id=1, source_target_pairs={{0,96},{16,112},{32,0},{48,16},{64,32},{80,48},{96,64},{112,80},{1... | collective-permute-start | bytes 196616 | tf_op jit(solution)/shard_map/ppermute | solution.py:16
  170.8 5.5 %collective-permute-start.31 = (f32[32,512]{1,0:T(8,128)S(1)}, f32[32,512]{1,0:T(8,128)S(1)}, u32[]{:S(2)}, u32[]{:S(2)}) collective-permute-start(f32[32,512]{1,0:T(8,128)S(1)} %add.192), channel_id=1, source_target_pairs={{0,32},{16,48},{32,64},{48,80},{64,96},{80,112},{96,0},{112,16},{1... | collective-permute-start | bytes 196616 | tf_op jit(solution)/shard_map/ppermute | solution.py:16
  (16 other events, 153.2 us)

commit v15 on v13

--- a/solution.py
+++ b/solution.py
@@ -314,7 +314,7 @@
     first_rhs, second = lax.optimization_barrier((first_rhs, second))
     rest = known[1] - over_sites(second)
     solved_first = over_z(stage(order, targets, over_cores(first_rhs), panels, 0)).astype(BF)
-    pair, rest = lax.optimization_barrier((over_cores(solved_first), rest))
+    pair = over_cores(solved_first)
     every_first = all_sites(solved_first)
     parts = stage(order, targets, pair, panels, 1)
     second_rhs = (rest - over_z(parts)).astype(BF)

time: 172 us -> 171 us (level)
    ppermute x9, waiting for transfers between devices: 14.3 us -> 9.29 us  [z_shift(): lax.ppermute(v, 'col', [(c, c // 4 * 4 + (c + step) % 4) for c in range(1...]
    ppermute x16, waiting for transfers between devices: 10.7 us -> 15.2 us  [x_shift(): return lax.ppermute(v, 'row', [(r, (r + 2 * step) % 8) for r in range(8)])]
    ppermute x16, starting transfers between devices: 24.1 us -> 21 us  [x_shift(): return lax.ppermute(v, 'row', [(r, (r + 2 * step) % 8) for r in range(8)])]
    all_to_all x2, starting transfers between devices: 9.49 us -> 12.1 us  [all_sites(): lax.all_to_all(sent, 'col', 0, 0, tiled=True).reshape(4, 4, 2, 64, 128)]
  transfers between devices with their start and end apart: 40 -> 40, of which waited for: 24 -> 23; matrix products, arithmetic and copies ran while one was open for 4% -> 3% of each run, Pallas kernels for 19% -> 20%
where the time goes in v15:
time: 171 us; the launch traced here: 170 us
  starting transfers between devices  63.3 us (37%)
  waiting for transfers between devices  59.9 us (35%)
  Pallas kernels  36.7 us (21%)
  local copies, waits for them, and re-layouts  5.87 us (3%)
  other arithmetic  3.01 us (2%)
    ppermute x16, starting transfers between devices, x_shift(): return lax.ppermute(v, 'row', [(r, (r + 2 * step) % 8) for r in range(8)])  21 us
    pallas_call x2, Pallas kernels, products(): pl.pallas_call(kernel, grid_spec=pltpu.PrefetchScalarGridSpec(num_scalar_...  18.5 us
    ppermute x16, waiting for transfers between devices, x_shift(): return lax.ppermute(v, 'row', [(r, (r + 2 * step) % 8) for r in range(8)])  15.2 us
    all_to_all x2, starting transfers between devices, all_sites(): lax.all_to_all(sent, 'col', 0, 0, tiled=True).reshape(4, 4, 2, 64, 128)  12.1 us
    ppermute x9, starting transfers between devices, z_shift(): lax.ppermute(v, 'col', [(c, c // 4 * 4 + (c + step) % 4) for c in range(1...  11.3 us
    pallas_call x2, Pallas kernels, split_tiles(): pl.pallas_call(split_tiles_kernel, grid=(2,), in_specs=[pl.BlockSpec((1,...  10.8 us
    all_to_all x2, waiting for transfers between devices, all_sites(): lax.all_to_all(sent, 'col', 0, 0, tiled=True).reshape(4, 4, 2, 64, 128)  9.7 us
    all_to_all x2, waiting for transfers between devices, over_sites(): lax.all_to_all(partial, 'col', 0, 0, tiled=True).astype(F32).sum(axis=0)  9.63 us
  transfers between devices with their start and end apart: 40, of which 23 were waited for; matrix products, arithmetic and copies ran while one was open for 3% of the time, Pallas kernels for 20%

profile of v15, /device:TPU:0, one launch (start us, length us, event | category | flops | bytes accessed | tf_op | source)
XLA Modules:
  0.0 170.3 jit_solution(2768703774082164781)
XLA Ops:
  0.6 2.3 %shard_map.77.token = bf16[4,3,64,512]{3,2,1,0:T(8,128)(2,1)} custom-call(bf16[2,512,256]{2,1,0:T(8,128)(2,1)} %bitcast.47, bf16[2,512,256]{2,1,0:T(8,128)(2,1)} %bitcast.48, bf16[512,256]{1,0:T(8,128)(2,1)} %bitcast.50), custom_call_target="tpu_custom_call" | custom-call | tf_op jit(solution)/shard_map/pallas_call | solution.py:63
  2.9 5.4 %all-to-all-start = ((bf16[4,3,64,512]{3,2,1,0:T(8,128)(2,1)}), bf16[4,3,64,512]{3,2,1,0:T(8,128)(2,1)S(1)}, u32[]{:S(2)}, u32[]{:S(2)}) async-start(bf16[4,3,64,512]{3,2,1,0:T(8,128)(2,1)} %shard_map.77.token), calls=%async_computation | async-start | bytes 1572864 | tf_op jit(solution)/shard_map/all_to_all | solution.py:25
  9.8 1.7 %collective-permute-start.1 = (bf16[3,256,512]{2,1,0:T(8,128)(2,1)}, bf16[3,256,512]{2,1,0:T(8,128)(2,1)S(1)}, u32[]{:S(2)}, u32[]{:S(2)}) collective-permute-start(bf16[3,256,512]{2,1,0:T(8,128)(2,1)} %refs_1_.1), channel_id=1, source_target_pairs={{0,96},{16,112},{32,0},{48,16},{64,32},{80,48},{96,64},{112,80},{1... | collective-permute-start | bytes 2359304 | tf_op jit(solution)/shard_map/ppermute | solution.py:16
  11.5 5.3 %shard_map.78.token.upper = bf16[8,512,768]{2,1,0:T(8,128)(2,1)} custom-call(bf16[4,256,24,256]{3,2,1,0:T(8,128)(2,1)} %src.3, bf16[4,3,64,512]{3,2,1,0:T(8,128)(2,1)} %shard_map.77.token), custom_call_target="tpu_custom_call" | custom-call | bytes 12582912 | tf_op jit(solution)/shard_map/pallas_call | solution.py:86
  16.9 3.7 %all-to-all-done = bf16[4,3,64,512]{3,2,1,0:T(8,128)(2,1)S(1)} async-done(((bf16[4,3,64,512]{3,2,1,0:T(8,128)(2,1)}), bf16[4,3,64,512]{3,2,1,0:T(8,128)(2,1)S(1)}, u32[]{:S(2)}, u32[]{:S(2)}) %all-to-all-start) | async-done | bytes 786464 | tf_op jit(solution)/shard_map/all_to_all | solution.py:25
  20.6 2.1 %broadcast_in_dim.6 = bf16[4,4,3,64,512]{4,3,2,1,0:T(8,128)(2,1)} broadcast(bf16[4,3,64,512]{3,2,1,0:T(8,128)(2,1)S(1)} %all-to-all-done), dimensions={1,2,3,4} | broadcast | bytes 3932160 | tf_op jit(solution)/shard_map/broadcast_in_dim | solution.py:30
  22.6 4.6 %all-to-all-start.1 = ((bf16[4,4,3,64,512]{4,3,2,1,0:T(8,128)(2,1)}), bf16[4,4,3,64,512]{4,3,2,1,0:T(8,128)(2,1)}, u32[]{:S(2)}, u32[]{:S(2)}) async-start(bf16[4,4,3,64,512]{4,3,2,1,0:T(8,128)(2,1)} %broadcast_in_dim.6), calls=%async_computation.1 | async-start | bytes 6291456 | tf_op jit(solution)/shard_map/all_to_all | solution.py:31
  27.3 5.4 %shard_map.79.lower = bf16[8,512,768]{2,1,0:T(8,128)(2,1)} custom-call(bf16[4,256,24,256]{3,2,1,0:T(8,128)(2,1)} %src.3, bf16[8,512,768]{2,1,0:T(8,128)(2,1)} %shard_map.78.token.upper), custom_call_target="tpu_custom_call" | custom-call | bytes 12582912 | tf_op jit(solution)/shard_map/pallas_call | solution.py:86
  35.4 1.7 %collective-permute-start.6 = (bf16[3,128,512]{2,1,0:T(8,128)(2,1)S(1)}, bf16[3,128,512]{2,1,0:T(8,128)(2,1)S(1)}, u32[]{:S(2)}, u32[]{:S(2)}) collective-permute-start(bf16[3,128,512]{2,1,0:T(8,128)(2,1)S(1)} %slice.24), channel_id=1, source_target_pairs={{0,96},{16,112},{32,0},{48,16},{64,32},{80,48},{96,64},{112,80},{1... | collective-permute-start | bytes 1179656 | tf_op jit(solution)/shard_map/ppermute | solution.py:16
  37.1 12.4 %shard_map.80.before = f32[1024,512]{1,0:T(8,128)S(1)} custom-call(s32[6]{0:T(128)S(1)} %stack.88.order, bf16[8,512,768]{2,1,0:T(8,128)(2,1)} %shard_map.78.token.upper, bf16[8,512,768]{2,1,0:T(8,128)(2,1)} %shard_map.79.lower, bf16[3,256,512]{2,1,0:T(8,128)(2,1)} %refs_1_.1, bf16[3,256,512]{2,1,0:T(8,128)(2,1)} %refs_1_.1, bf16[3,256,512]{2,1,0:T(8,128)(2,1)} %copy-done.2, ...), custom_call_target="tpu_custom_call" | custom-call | flops 4831838208 | bytes 16252928 | tf_op jit(solution)/shard_map/pallas_call | solution.py:184
  52.1 6.1 %shard_map.81 = (bf16[16,128,128]{2,1,0:T(8,128)(2,1)}, bf16[16,128,128]{2,1,0:T(8,128)(2,1)}) custom-call(s32[2]{0:T(128)S(1)} %pad_add_fusion.1.order, bf16[8,512,768]{2,1,0:T(8,128)(2,1)} %shard_map.78.token.upper, bf16[8,512,768]{2,1,0:T(8,128)(2,1)} %shard_map.79.lower, f32[1024,512]{1,0:T(8,128)S(1)} %shard_map.80.before, f32[8,128]{1,0:T(8,128)S(1)} %slice.28.token, ...), custom_call_target="tpu_custom_call" | custom-call | flops 1610612736 | bytes 6815744 | tf_op jit(solution)/shard_map/pallas_call | solution.py:184
  58.2 5.8 %all-to-all-done.1 = bf16[4,4,3,64,512]{4,3,2,1,0:T(8,128)(2,1)} async-done(((bf16[4,4,3,64,512]{4,3,2,1,0:T(8,128)(2,1)}), bf16[4,4,3,64,512]{4,3,2,1,0:T(8,128)(2,1)}, u32[]{:S(2)}, u32[]{:S(2)}) %all-to-all-start.1) | async-done | bytes 3145760 | tf_op jit(solution)/shard_map/all_to_all | solution.py:31
  64.0 3.7 %all-to-all-start.2 = ((bf16[16,128,128]{2,1,0:T(8,128)(2,1)}), bf16[16,128,128]{2,1,0:T(8,128)(2,1)S(1)}, u32[]{:S(2)}, u32[]{:S(2)}) async-start(bf16[16,128,128]{2,1,0:T(8,128)(2,1)} %get-tuple-element.48), calls=%async_computation.2 | async-start | bytes 1048576 | tf_op jit(solution)/shard_map/all_to_all | solution.py:257
  68.6 9.6 %all-to-all-done.2 = bf16[16,128,128]{2,1,0:T(8,128)(2,1)S(1)} async-done(((bf16[16,128,128]{2,1,0:T(8,128)(2,1)}), bf16[16,128,128]{2,1,0:T(8,128)(2,1)S(1)}, u32[]{:S(2)}, u32[]{:S(2)}) %all-to-all-start.2) | async-done | bytes 524320 | tf_op jit(solution)/shard_map/all_to_all | solution.py:257
  80.6 2.3 %collective-permute-start.11 = (bf16[2,128,128]{2,1,0:T(8,128)(2,1)S(1)}, bf16[2,128,128]{2,1,0:T(8,128)(2,1)S(1)}, u32[]{:S(2)}, u32[]{:S(2)}) collective-permute-start(bf16[2,128,128]{2,1,0:T(8,128)(2,1)S(1)} %pad_maximum_fusion.1.own), channel_id=1, source_target_pairs={{0,96},{16,112},{32,0},{48,16},{64,32},{80,48},{96,64},{112,80},{1... | collective-permute-start | bytes 196616 | tf_op jit(solution)/shard_map/ppermute | solution.py:16
  84.2 3.6 %all-to-all-start.3 = ((bf16[16,128,128]{2,1,0:T(8,128)(2,1)}), bf16[16,128,128]{2,1,0:T(8,128)(2,1)S(1)}, u32[]{:S(2)}, u32[]{:S(2)}) async-start(bf16[16,128,128]{2,1,0:T(8,128)(2,1)} %get-tuple-element.50), calls=%async_computation.3 | async-start | bytes 1048576 | tf_op jit(solution)/shard_map/all_to_all | solution.py:257
  88.7 1.7 %shard_map.82 = (bf16[128,128]{1,0:T(8,128)(2,1)S(1)}, bf16[128,128]{1,0:T(8,128)(2,1)S(1)}, bf16[128,128]{1,0:T(8,128)(2,1)S(1)}, bf16[128,128]{1,0:T(8,128)(2,1)S(1)}) custom-call(s32[8]{0:T(128)S(1)} %stack.81.order, s32[4]{0:T(128)S(1)} %pad_add_fusion.targets, bf16[2,128,128]{2,1,0:T(8,128)(2,1)S(1)} %pad_maximum_fusion.1.own, ...), custom_call_target="tpu_custom_call" | custom-call | flops 134217728 | bytes 1048576 | tf_op jit(solution)/shard_map/pallas_call | solution.py:234
  90.4 2.3 %collective-permute-start.15 = (bf16[128,128]{1,0:T(8,128)(2,1)S(1)}, bf16[128,128]{1,0:T(8,128)(2,1)S(1)}, u32[]{:S(2)}, u32[]{:S(2)}) collective-permute-start(bf16[128,128]{1,0:T(8,128)(2,1)S(1)} %get-tuple-element.56), channel_id=1, source_target_pairs={{0,3},{1,0},{2,1},{3,2},{4,7},{5,4},{6,5},{7,6},{8,11},{9,8},{10,9... | collective-permute-start | bytes 98312 | tf_op jit(solution)/shard_map/ppermute | solution.py:36
  94.4 2.6 %collective-permute-done.15 = bf16[128,128]{1,0:T(8,128)(2,1)S(1)} collective-permute-done((bf16[128,128]{1,0:T(8,128)(2,1)S(1)}, bf16[128,128]{1,0:T(8,128)(2,1)S(1)}, u32[]{:S(2)}, u32[]{:S(2)}) %collective-permute-start.15) | collective-permute-done | bytes 32800 | tf_op jit(solution)/shard_map/ppermute | solution.py:36
  97.0 2.4 %collective-permute-done.14 = bf16[128,128]{1,0:T(8,128)(2,1)S(1)} collective-permute-done((bf16[128,128]{1,0:T(8,128)(2,1)S(1)}, bf16[128,128]{1,0:T(8,128)(2,1)S(1)}, u32[]{:S(2)}, u32[]{:S(2)}) %collective-permute-start.14) | collective-permute-done | bytes 32800 | tf_op jit(solution)/shard_map/ppermute | solution.py:36
  101.6 2.6 %collective-permute-start.18 = (bf16[2,128,128]{2,1,0:T(8,128)(2,1)S(1)}, bf16[2,128,128]{2,1,0:T(8,128)(2,1)S(1)}, u32[]{:S(2)}, u32[]{:S(2)}) collective-permute-start(bf16[2,128,128]{2,1,0:T(8,128)(2,1)S(1)} %pad_maximum_fusion.2.own), channel_id=1, source_target_pairs={{0,96},{16,112},{32,0},{48,16},{64,32},{80,48},{96,64},{112,80},{1... | collective-permute-start | bytes 196616 | tf_op jit(solution)/shard_map/ppermute | solution.py:16
  107.0 3.0 %collective-permute-done.19.three = bf16[2,128,128]{2,1,0:T(8,128)(2,1)S(1)} collective-permute-done((bf16[2,128,128]{2,1,0:T(8,128)(2,1)S(1)}, bf16[2,128,128]{2,1,0:T(8,128)(2,1)S(1)}, u32[]{:S(2)}, u32[]{:S(2)}) %collective-permute-start.19) | collective-permute-done | bytes 65568 | tf_op jit(solution)/shard_map/ppermute | solution.py:16
  110.0 1.7 %shard_map.83 = (bf16[128,128]{1,0:T(8,128)(2,1)S(1)}, bf16[128,128]{1,0:T(8,128)(2,1)S(1)}, bf16[128,128]{1,0:T(8,128)(2,1)S(1)}, bf16[128,128]{1,0:T(8,128)(2,1)S(1)}) custom-call(s32[8]{0:T(128)S(1)} %stack.81.order, s32[4]{0:T(128)S(1)} %pad_add_fusion.targets, bf16[2,128,128]{2,1,0:T(8,128)(2,1)S(1)} %pad_maximum_fusion.2.own, ...), custom_call_target="tpu_custom_call" | custom-call | flops 134217728 | bytes 1048576 | tf_op jit(solution)/shard_map/pallas_call | solution.py:234
  115.1 6.9 %all-to-all-start.4 = ((bf16[16,128,128]{2,1,0:T(8,128)(2,1)}), bf16[16,128,128]{2,1,0:T(8,128)(2,1)S(1)}, u32[]{:S(2)}, u32[]{:S(2)}) async-start(bf16[16,128,128]{2,1,0:T(8,128)(2,1)} %broadcast_in_dim.7), calls=%async_computation.4 | async-start | bytes 1048576 | tf_op jit(solution)/shard_map/all_to_all | solution.py:262
  123.5 3.2 %collective-permute-start.25 = (bf16[2,128,128]{2,1,0:T(8,128)(2,1)S(1)}, bf16[2,128,128]{2,1,0:T(8,128)(2,1)S(1)}, u32[]{:S(2)}, u32[]{:S(2)}) collective-permute-start(bf16[2,128,128]{2,1,0:T(8,128)(2,1)S(1)} %pad_maximum_fusion.3.own), channel_id=1, source_target_pairs={{0,96},{16,112},{32,0},{48,16},{64,32},{80,48},{96,64},{112,80},{1... | collective-permute-start | bytes 196616 | tf_op jit(solution)/shard_map/ppermute | solution.py:16
  126.7 2.2 %collective-permute-done.24.one = bf16[2,128,128]{2,1,0:T(8,128)(2,1)S(1)} collective-permute-done((bf16[2,128,128]{2,1,0:T(8,128)(2,1)S(1)}, bf16[2,128,128]{2,1,0:T(8,128)(2,1)S(1)}, u32[]{:S(2)}, u32[]{:S(2)}) %collective-permute-start.24) | collective-permute-done | bytes 65568 | tf_op jit(solution)/shard_map/ppermute | solution.py:16
  129.5 2.9 %collective-permute-done.26.three = bf16[2,128,128]{2,1,0:T(8,128)(2,1)S(1)} collective-permute-done((bf16[2,128,128]{2,1,0:T(8,128)(2,1)S(1)}, bf16[2,128,128]{2,1,0:T(8,128)(2,1)S(1)}, u32[]{:S(2)}, u32[]{:S(2)}) %collective-permute-start.26) | collective-permute-done | bytes 65568 | tf_op jit(solution)/shard_map/ppermute | solution.py:16
  134.8 3.2 %collective-permute-start.29 = (bf16[128,128]{1,0:T(8,128)(2,1)S(1)}, bf16[128,128]{1,0:T(8,128)(2,1)S(1)}, u32[]{:S(2)}, u32[]{:S(2)}) collective-permute-start(bf16[128,128]{1,0:T(8,128)(2,1)S(1)} %get-tuple-element.69), channel_id=1, source_target_pairs={{0,3},{1,0},{2,1},{3,2},{4,7},{5,4},{6,5},{7,6},{8,11},{9,8},{10,9... | collective-permute-start | bytes 98312 | tf_op jit(solution)/shard_map/ppermute | solution.py:36
  139.8 3.7 %collective-permute-done.28 = bf16[128,128]{1,0:T(8,128)(2,1)S(1)} collective-permute-done((bf16[128,128]{1,0:T(8,128)(2,1)S(1)}, bf16[128,128]{1,0:T(8,128)(2,1)S(1)}, u32[]{:S(2)}, u32[]{:S(2)}) %collective-permute-start.28) | collective-permute-done | bytes 32800 | tf_op jit(solution)/shard_map/ppermute | solution.py:36
  145.0 5.3 %all-to-all-start.5 = ((bf16[16,128,128]{2,1,0:T(8,128)(2,1)}), bf16[16,128,128]{2,1,0:T(8,128)(2,1)S(1)}, u32[]{:S(2)}, u32[]{:S(2)}) async-start(bf16[16,128,128]{2,1,0:T(8,128)(2,1)} %broadcast_in_dim.8), calls=%async_computation.5 | async-start | bytes 1048576 | tf_op jit(solution)/shard_map/all_to_all | solution.py:262
  150.6 9.7 %all-to-all-done.5 = bf16[16,128,128]{2,1,0:T(8,128)(2,1)S(1)} async-done(((bf16[16,128,128]{2,1,0:T(8,128)(2,1)}), bf16[16,128,128]{2,1,0:T(8,128)(2,1)S(1)}, u32[]{:S(2)}, u32[]{:S(2)}) %all-to-all-start.5) | async-done | bytes 524320 | tf_op jit(solution)/shard_map/all_to_all | solution.py:262
  165.8 2.7 %collective-permute-done.33 = f32[32,512]{1,0:T(8,128)S(1)} collective-permute-done((f32[32,512]{1,0:T(8,128)S(1)}, f32[32,512]{1,0:T(8,128)S(1)}, u32[]{:S(2)}, u32[]{:S(2)}) %collective-permute-start.33) | collective-permute-done | bytes 65568 | tf_op jit(solution)/shard_map/ppermute | solution.py:16
  (95 shorter events, 37.3 us)
Async XLA Ops:
  2.9 17.7 %all-to-all-start = ((bf16[4,3,64,512]{3,2,1,0:T(8,128)(2,1)}), bf16[4,3,64,512]{3,2,1,0:T(8,128)(2,1)S(1)}, u32[]{:S(2)}, u32[]{:S(2)}) async-start(bf16[4,3,64,512]{3,2,1,0:T(8,128)(2,1)} %shard_map.77.token), calls=%async_computation | async-start | bytes 1572864 | tf_op jit(solution)/shard_map/all_to_all | solution.py:25
  8.3 24.4 %collective-permute-start = (bf16[3,256,512]{2,1,0:T(8,128)(2,1)}, bf16[3,256,512]{2,1,0:T(8,128)(2,1)S(1)}, u32[]{:S(2)}, u32[]{:S(2)}) collective-permute-start(bf16[3,256,512]{2,1,0:T(8,128)(2,1)} %refs_1_.1), channel_id=1, source_target_pairs={{0,32},{16,48},{32,64},{48,80},{64,96},{80,112},{96,0},{112,16},{1... | collective-permute-start | bytes 2359304 | tf_op jit(solution)/shard_map/ppermute | solution.py:16
  9.8 22.9 %collective-permute-start.1 = (bf16[3,256,512]{2,1,0:T(8,128)(2,1)}, bf16[3,256,512]{2,1,0:T(8,128)(2,1)S(1)}, u32[]{:S(2)}, u32[]{:S(2)}) collective-permute-start(bf16[3,256,512]{2,1,0:T(8,128)(2,1)} %refs_1_.1), channel_id=1, source_target_pairs={{0,96},{16,112},{32,0},{48,16},{64,32},{80,48},{96,64},{112,80},{1... | collective-permute-start | bytes 2359304 | tf_op jit(solution)/shard_map/ppermute | solution.py:16
  11.5 21.2 %collective-permute-start.2 = (bf16[3,256,512]{2,1,0:T(8,128)(2,1)}, bf16[3,256,512]{2,1,0:T(8,128)(2,1)S(1)}, u32[]{:S(2)}, u32[]{:S(2)}) collective-permute-start(bf16[3,256,512]{2,1,0:T(8,128)(2,1)} %refs_1_.1), channel_id=1, source_target_pairs={{0,16},{16,0},{32,48},{48,32},{64,80},{80,64},{96,112},{112,96},{1... | collective-permute-start | bytes 2359304 | tf_op jit(solution)/shard_map/ppermute | solution.py:20
  22.6 41.4 %all-to-all-start.1 = ((bf16[4,4,3,64,512]{4,3,2,1,0:T(8,128)(2,1)}), bf16[4,4,3,64,512]{4,3,2,1,0:T(8,128)(2,1)}, u32[]{:S(2)}, u32[]{:S(2)}) async-start(bf16[4,4,3,64,512]{4,3,2,1,0:T(8,128)(2,1)} %broadcast_in_dim.6), calls=%async_computation.1 | async-start | bytes 6291456 | tf_op jit(solution)/shard_map/all_to_all | solution.py:31
  33.8 15.7 %collective-permute-start.5 = (bf16[3,128,512]{2,1,0:T(8,128)(2,1)S(1)}, bf16[3,128,512]{2,1,0:T(8,128)(2,1)S(1)}, u32[]{:S(2)}, u32[]{:S(2)}) collective-permute-start(bf16[3,128,512]{2,1,0:T(8,128)(2,1)S(1)} %slice.23), channel_id=1, source_target_pairs={{0,32},{16,48},{32,64},{48,80},{64,96},{80,112},{96,0},{112,16},{1... | collective-permute-start | bytes 1179656 | tf_op jit(solution)/shard_map/ppermute | solution.py:16
  35.4 14.2 %collective-permute-start.6 = (bf16[3,128,512]{2,1,0:T(8,128)(2,1)S(1)}, bf16[3,128,512]{2,1,0:T(8,128)(2,1)S(1)}, u32[]{:S(2)}, u32[]{:S(2)}) collective-permute-start(bf16[3,128,512]{2,1,0:T(8,128)(2,1)S(1)} %slice.24), channel_id=1, source_target_pairs={{0,96},{16,112},{32,0},{48,16},{64,32},{80,48},{96,64},{112,80},{1... | collective-permute-start | bytes 1179656 | tf_op jit(solution)/shard_map/ppermute | solution.py:16
  64.0 14.2 %all-to-all-start.2 = ((bf16[16,128,128]{2,1,0:T(8,128)(2,1)}), bf16[16,128,128]{2,1,0:T(8,128)(2,1)S(1)}, u32[]{:S(2)}, u32[]{:S(2)}) async-start(bf16[16,128,128]{2,1,0:T(8,128)(2,1)} %get-tuple-element.48), calls=%async_computation.2 | async-start | bytes 1048576 | tf_op jit(solution)/shard_map/all_to_all | solution.py:257
  79.6 8.2 %collective-permute-start.10 = (bf16[2,128,128]{2,1,0:T(8,128)(2,1)S(1)}, bf16[2,128,128]{2,1,0:T(8,128)(2,1)S(1)}, u32[]{:S(2)}, u32[]{:S(2)}) collective-permute-start(bf16[2,128,128]{2,1,0:T(8,128)(2,1)S(1)} %pad_maximum_fusion.1.own), channel_id=1, source_target_pairs={{0,32},{16,48},{32,64},{48,80},{64,96},{80,112},{96,0},{112,16},{1... | collective-permute-start | bytes 196616 | tf_op jit(solution)/shard_map/ppermute | solution.py:16
  80.6 7.2 %collective-permute-start.11 = (bf16[2,128,128]{2,1,0:T(8,128)(2,1)S(1)}, bf16[2,128,128]{2,1,0:T(8,128)(2,1)S(1)}, u32[]{:S(2)}, u32[]{:S(2)}) collective-permute-start(bf16[2,128,128]{2,1,0:T(8,128)(2,1)S(1)} %pad_maximum_fusion.1.own), channel_id=1, source_target_pairs={{0,96},{16,112},{32,0},{48,16},{64,32},{80,48},{96,64},{112,80},{1... | collective-permute-start | bytes 196616 | tf_op jit(solution)/shard_map/ppermute | solution.py:16
  82.9 5.8 %collective-permute-start.12 = (bf16[2,128,128]{2,1,0:T(8,128)(2,1)S(1)}, bf16[2,128,128]{2,1,0:T(8,128)(2,1)S(1)}, u32[]{:S(2)}, u32[]{:S(2)}) collective-permute-start(bf16[2,128,128]{2,1,0:T(8,128)(2,1)S(1)} %pad_maximum_fusion.1.own), channel_id=1, source_target_pairs={{0,64},{16,80},{32,96},{48,112},{64,0},{80,16},{96,32},{112,48},{1... | collective-permute-start | bytes 196616 | tf_op jit(solution)/shard_map/ppermute | solution.py:16
  84.2 29.9 %all-to-all-start.3 = ((bf16[16,128,128]{2,1,0:T(8,128)(2,1)}), bf16[16,128,128]{2,1,0:T(8,128)(2,1)S(1)}, u32[]{:S(2)}, u32[]{:S(2)}) async-start(bf16[16,128,128]{2,1,0:T(8,128)(2,1)} %get-tuple-element.50), calls=%async_computation.3 | async-start | bytes 1048576 | tf_op jit(solution)/shard_map/all_to_all | solution.py:257
  90.4 6.6 %collective-permute-start.15 = (bf16[128,128]{1,0:T(8,128)(2,1)S(1)}, bf16[128,128]{1,0:T(8,128)(2,1)S(1)}, u32[]{:S(2)}, u32[]{:S(2)}) collective-permute-start(bf16[128,128]{1,0:T(8,128)(2,1)S(1)} %get-tuple-element.56), channel_id=1, source_target_pairs={{0,3},{1,0},{2,1},{3,2},{4,7},{5,4},{6,5},{7,6},{8,11},{9,8},{10,9... | collective-permute-start | bytes 98312 | tf_op jit(solution)/shard_map/ppermute | solution.py:36
  92.7 6.7 %collective-permute-start.14 = (bf16[128,128]{1,0:T(8,128)(2,1)S(1)}, bf16[128,128]{1,0:T(8,128)(2,1)S(1)}, u32[]{:S(2)}, u32[]{:S(2)}) collective-permute-start(bf16[128,128]{1,0:T(8,128)(2,1)S(1)} %get-tuple-element.55), channel_id=1, source_target_pairs={{0,2},{1,3},{2,0},{3,1},{4,6},{5,7},{6,4},{7,5},{8,10},{9,11},{10,... | collective-permute-start | bytes 98312 | tf_op jit(solution)/shard_map/ppermute | solution.py:36
  93.5 5.9 %collective-permute-start.13 = (bf16[128,128]{1,0:T(8,128)(2,1)S(1)}, bf16[128,128]{1,0:T(8,128)(2,1)S(1)}, u32[]{:S(2)}, u32[]{:S(2)}) collective-permute-start(bf16[128,128]{1,0:T(8,128)(2,1)S(1)} %get-tuple-element.54), channel_id=1, source_target_pairs={{0,1},{1,2},{2,3},{3,0},{4,5},{5,6},{6,7},{7,4},{8,9},{9,10},{10,1... | collective-permute-start | bytes 98312 | tf_op jit(solution)/shard_map/ppermute | solution.py:36
  100.9 5.5 %collective-permute-start.17 = (bf16[2,128,128]{2,1,0:T(8,128)(2,1)S(1)}, bf16[2,128,128]{2,1,0:T(8,128)(2,1)S(1)}, u32[]{:S(2)}, u32[]{:S(2)}) collective-permute-start(bf16[2,128,128]{2,1,0:T(8,128)(2,1)S(1)} %pad_maximum_fusion.2.own), channel_id=1, source_target_pairs={{0,32},{16,48},{32,64},{48,80},{64,96},{80,112},{96,0},{112,16},{1... | collective-permute-start | bytes 196616 | tf_op jit(solution)/shard_map/ppermute | solution.py:16
  101.6 5.4 %collective-permute-start.18 = (bf16[2,128,128]{2,1,0:T(8,128)(2,1)S(1)}, bf16[2,128,128]{2,1,0:T(8,128)(2,1)S(1)}, u32[]{:S(2)}, u32[]{:S(2)}) collective-permute-start(bf16[2,128,128]{2,1,0:T(8,128)(2,1)S(1)} %pad_maximum_fusion.2.own), channel_id=1, source_target_pairs={{0,96},{16,112},{32,0},{48,16},{64,32},{80,48},{96,64},{112,80},{1... | collective-permute-start | bytes 196616 | tf_op jit(solution)/shard_map/ppermute | solution.py:16
  104.2 5.8 %collective-permute-start.19 = (bf16[2,128,128]{2,1,0:T(8,128)(2,1)S(1)}, bf16[2,128,128]{2,1,0:T(8,128)(2,1)S(1)}, u32[]{:S(2)}, u32[]{:S(2)}) collective-permute-start(bf16[2,128,128]{2,1,0:T(8,128)(2,1)S(1)} %pad_maximum_fusion.2.own), channel_id=1, source_target_pairs={{0,64},{16,80},{32,96},{48,112},{64,0},{80,16},{96,32},{112,48},{1... | collective-permute-start | bytes 196616 | tf_op jit(solution)/shard_map/ppermute | solution.py:16
  111.7 10.3 %collective-permute-start.22 = (bf16[128,128]{1,0:T(8,128)(2,1)S(1)}, bf16[128,128]{1,0:T(8,128)(2,1)S(1)}, u32[]{:S(2)}, u32[]{:S(2)}) collective-permute-start(bf16[128,128]{1,0:T(8,128)(2,1)S(1)} %get-tuple-element.60), channel_id=1, source_target_pairs={{0,3},{1,0},{2,1},{3,2},{4,7},{5,4},{6,5},{7,6},{8,11},{9,8},{10,9... | collective-permute-start | bytes 98312 | tf_op jit(solution)/shard_map/ppermute | solution.py:36
  113.0 9.0 %collective-permute-start.21 = (bf16[128,128]{1,0:T(8,128)(2,1)S(1)}, bf16[128,128]{1,0:T(8,128)(2,1)S(1)}, u32[]{:S(2)}, u32[]{:S(2)}) collective-permute-start(bf16[128,128]{1,0:T(8,128)(2,1)S(1)} %get-tuple-element.59), channel_id=1, source_target_pairs={{0,2},{1,3},{2,0},{3,1},{4,6},{5,7},{6,4},{7,5},{8,10},{9,11},{10,... | collective-permute-start | bytes 98312 | tf_op jit(solution)/shard_map/ppermute | solution.py:36
  114.1 7.9 %collective-permute-start.20 = (bf16[128,128]{1,0:T(8,128)(2,1)S(1)}, bf16[128,128]{1,0:T(8,128)(2,1)S(1)}, u32[]{:S(2)}, u32[]{:S(2)}) collective-permute-start(bf16[128,128]{1,0:T(8,128)(2,1)S(1)} %get-tuple-element.58), channel_id=1, source_target_pairs={{0,1},{1,2},{2,3},{3,0},{4,5},{5,6},{6,7},{7,4},{8,9},{9,10},{10,1... | collective-permute-start | bytes 98312 | tf_op jit(solution)/shard_map/ppermute | solution.py:36
  115.1 19.2 %all-to-all-start.4 = ((bf16[16,128,128]{2,1,0:T(8,128)(2,1)}), bf16[16,128,128]{2,1,0:T(8,128)(2,1)S(1)}, u32[]{:S(2)}, u32[]{:S(2)}) async-start(bf16[16,128,128]{2,1,0:T(8,128)(2,1)} %broadcast_in_dim.7), calls=%async_computation.4 | async-start | bytes 1048576 | tf_op jit(solution)/shard_map/all_to_all | solution.py:262
  123.4 5.5 %collective-permute-start.24 = (bf16[2,128,128]{2,1,0:T(8,128)(2,1)S(1)}, bf16[2,128,128]{2,1,0:T(8,128)(2,1)S(1)}, u32[]{:S(2)}, u32[]{:S(2)}) collective-permute-start(bf16[2,128,128]{2,1,0:T(8,128)(2,1)S(1)} %pad_maximum_fusion.3.own), channel_id=1, source_target_pairs={{0,32},{16,48},{32,64},{48,80},{64,96},{80,112},{96,0},{112,16},{1... | collective-permute-start | bytes 196616 | tf_op jit(solution)/shard_map/ppermute | solution.py:16
  123.5 6.1 %collective-permute-start.25 = (bf16[2,128,128]{2,1,0:T(8,128)(2,1)S(1)}, bf16[2,128,128]{2,1,0:T(8,128)(2,1)S(1)}, u32[]{:S(2)}, u32[]{:S(2)}) collective-permute-start(bf16[2,128,128]{2,1,0:T(8,128)(2,1)S(1)} %pad_maximum_fusion.3.own), channel_id=1, source_target_pairs={{0,96},{16,112},{32,0},{48,16},{64,32},{80,48},{96,64},{112,80},{1... | collective-permute-start | bytes 196616 | tf_op jit(solution)/shard_map/ppermute | solution.py:16
  126.7 5.8 %collective-permute-start.26 = (bf16[2,128,128]{2,1,0:T(8,128)(2,1)S(1)}, bf16[2,128,128]{2,1,0:T(8,128)(2,1)S(1)}, u32[]{:S(2)}, u32[]{:S(2)}) collective-permute-start(bf16[2,128,128]{2,1,0:T(8,128)(2,1)S(1)} %pad_maximum_fusion.3.own), channel_id=1, source_target_pairs={{0,64},{16,80},{32,96},{48,112},{64,0},{80,16},{96,32},{112,48},{1... | collective-permute-start | bytes 196616 | tf_op jit(solution)/shard_map/ppermute | solution.py:16
  134.8 4.9 %collective-permute-start.29 = (bf16[128,128]{1,0:T(8,128)(2,1)S(1)}, bf16[128,128]{1,0:T(8,128)(2,1)S(1)}, u32[]{:S(2)}, u32[]{:S(2)}) collective-permute-start(bf16[128,128]{1,0:T(8,128)(2,1)S(1)} %get-tuple-element.69), channel_id=1, source_target_pairs={{0,3},{1,0},{2,1},{3,2},{4,7},{5,4},{6,5},{7,6},{8,11},{9,8},{10,9... | collective-permute-start | bytes 98312 | tf_op jit(solution)/shard_map/ppermute | solution.py:36
  138.1 5.4 %collective-permute-start.28 = (bf16[128,128]{1,0:T(8,128)(2,1)S(1)}, bf16[128,128]{1,0:T(8,128)(2,1)S(1)}, u32[]{:S(2)}, u32[]{:S(2)}) collective-permute-start(bf16[128,128]{1,0:T(8,128)(2,1)S(1)} %get-tuple-element.68), channel_id=1, source_target_pairs={{0,2},{1,3},{2,0},{3,1},{4,6},{5,7},{6,4},{7,5},{8,10},{9,11},{10,... | collective-permute-start | bytes 98312 | tf_op jit(solution)/shard_map/ppermute | solution.py:36
  138.9 5.1 %collective-permute-start.27 = (bf16[128,128]{1,0:T(8,128)(2,1)S(1)}, bf16[128,128]{1,0:T(8,128)(2,1)S(1)}, u32[]{:S(2)}, u32[]{:S(2)}) collective-permute-start(bf16[128,128]{1,0:T(8,128)(2,1)S(1)} %get-tuple-element.67), channel_id=1, source_target_pairs={{0,1},{1,2},{2,3},{3,0},{4,5},{5,6},{6,7},{7,4},{8,9},{9,10},{10,1... | collective-permute-start | bytes 98312 | tf_op jit(solution)/shard_map/ppermute | solution.py:36
  145.0 15.4 %all-to-all-start.5 = ((bf16[16,128,128]{2,1,0:T(8,128)(2,1)}), bf16[16,128,128]{2,1,0:T(8,128)(2,1)S(1)}, u32[]{:S(2)}, u32[]{:S(2)}) async-start(bf16[16,128,128]{2,1,0:T(8,128)(2,1)} %broadcast_in_dim.8), calls=%async_computation.5 | async-start | bytes 1048576 | tf_op jit(solution)/shard_map/all_to_all | solution.py:262
  162.5 5.9 %collective-permute-start.33 = (f32[32,512]{1,0:T(8,128)S(1)}, f32[32,512]{1,0:T(8,128)S(1)}, u32[]{:S(2)}, u32[]{:S(2)}) collective-permute-start(f32[32,512]{1,0:T(8,128)S(1)} %add.192), channel_id=1, source_target_pairs={{0,64},{16,80},{32,96},{48,112},{64,0},{80,16},{96,32},{112,48},{1... | collective-permute-start | bytes 196616 | tf_op jit(solution)/shard_map/ppermute | solution.py:16
  162.6 5.9 %collective-permute-start.32 = (f32[32,512]{1,0:T(8,128)S(1)}, f32[32,512]{1,0:T(8,128)S(1)}, u32[]{:S(2)}, u32[]{:S(2)}) collective-permute-start(f32[32,512]{1,0:T(8,128)S(1)} %add.192), channel_id=1, source_target_pairs={{0,96},{16,112},{32,0},{48,16},{64,32},{80,48},{96,64},{112,80},{1... | collective-permute-start | bytes 196616 | tf_op jit(solution)/shard_map/ppermute | solution.py:16
  164.1 5.5 %collective-permute-start.31 = (f32[32,512]{1,0:T(8,128)S(1)}, f32[32,512]{1,0:T(8,128)S(1)}, u32[]{:S(2)}, u32[]{:S(2)}) collective-permute-start(f32[32,512]{1,0:T(8,128)S(1)} %add.192), channel_id=1, source_target_pairs={{0,32},{16,48},{32,64},{48,80},{64,96},{80,112},{96,0},{112,16},{1... | collective-permute-start | bytes 196616 | tf_op jit(solution)/shard_map/ppermute | solution.py:16
  (12 other events, 74.3 us)

commit v16 on v15

--- a/solution.py
+++ b/solution.py
@@ -265,7 +265,8 @@
 
 def row_sum(values):
     values = values + other_core(values)
-    return values + x_shift(values, 1) + x_shift(values, -1) + x_shift(values, 2)
+    sent = values.astype(BF)
+    return values + sum(x_shift(sent, d).astype(F32) for d in (1, -1, 2))
 
 
 def outer_part(every, col):

time: 171 us -> 171 us (level)
  no operation moved by 1% of the time
where the time goes in v16:
time: 171 us; the launch traced here: 170 us
  starting transfers between devices  63.3 us (37%)
  waiting for transfers between devices  59.5 us (35%)
  Pallas kernels  36.7 us (21%)
  local copies, waits for them, and re-layouts  5.87 us (3%)
  other arithmetic  3.01 us (2%)
    ppermute x16, starting transfers between devices, x_shift(): return lax.ppermute(v, 'row', [(r, (r + 2 * step) % 8) for r in range(8)])  21 us
    pallas_call x2, Pallas kernels, products(): pl.pallas_call(kernel, grid_spec=pltpu.PrefetchScalarGridSpec(num_scalar_...  18.5 us
    ppermute x16, waiting for transfers between devices, x_shift(): return lax.ppermute(v, 'row', [(r, (r + 2 * step) % 8) for r in range(8)])  14.8 us
    all_to_all x2, starting transfers between devices, all_sites(): lax.all_to_all(sent, 'col', 0, 0, tiled=True).reshape(4, 4, 2, 64, 128)  12.1 us
    ppermute x9, starting transfers between devices, z_shift(): lax.ppermute(v, 'col', [(c, c // 4 * 4 + (c + step) % 4) for c in range(1...  11.3 us
    pallas_call x2, Pallas kernels, split_tiles(): pl.pallas_call(split_tiles_kernel, grid=(2,), in_specs=[pl.BlockSpec((1,...  10.8 us
    all_to_all x2, waiting for transfers between devices, all_sites(): lax.all_to_all(sent, 'col', 0, 0, tiled=True).reshape(4, 4, 2, 64, 128)  9.7 us
    all_to_all x2, waiting for transfers between devices, over_sites(): lax.all_to_all(partial, 'col', 0, 0, tiled=True).astype(F32).sum(axis=0)  9.63 us
  transfers between devices with their start and end apart: 40, of which 23 were waited for; matrix products, arithmetic and copies ran while one was open for 3% of the time, Pallas kernels for 20%

profile of v16, /device:TPU:0, one launch (start us, length us, event | category | flops | bytes accessed | tf_op | source)
XLA Modules:
  0.0 169.9 jit_solution(9029813453467532392)
XLA Ops:
  0.6 2.3 %shard_map.77.token = bf16[4,3,64,512]{3,2,1,0:T(8,128)(2,1)} custom-call(bf16[2,512,256]{2,1,0:T(8,128)(2,1)} %bitcast.47, bf16[2,512,256]{2,1,0:T(8,128)(2,1)} %bitcast.48, bf16[512,256]{1,0:T(8,128)(2,1)} %bitcast.50), custom_call_target="tpu_custom_call" | custom-call | tf_op jit(solution)/shard_map/pallas_call | solution.py:63
  2.9 5.4 %all-to-all-start = ((bf16[4,3,64,512]{3,2,1,0:T(8,128)(2,1)}), bf16[4,3,64,512]{3,2,1,0:T(8,128)(2,1)S(1)}, u32[]{:S(2)}, u32[]{:S(2)}) async-start(bf16[4,3,64,512]{3,2,1,0:T(8,128)(2,1)} %shard_map.77.token), calls=%async_computation | async-start | bytes 1572864 | tf_op jit(solution)/shard_map/all_to_all | solution.py:25
  9.8 1.7 %collective-permute-start.1 = (bf16[3,256,512]{2,1,0:T(8,128)(2,1)}, bf16[3,256,512]{2,1,0:T(8,128)(2,1)S(1)}, u32[]{:S(2)}, u32[]{:S(2)}) collective-permute-start(bf16[3,256,512]{2,1,0:T(8,128)(2,1)} %refs_1_.1), channel_id=1, source_target_pairs={{0,96},{16,112},{32,0},{48,16},{64,32},{80,48},{96,64},{112,80},{1... | collective-permute-start | bytes 2359304 | tf_op jit(solution)/shard_map/ppermute | solution.py:16
  11.5 5.3 %shard_map.78.token.upper = bf16[8,512,768]{2,1,0:T(8,128)(2,1)} custom-call(bf16[4,256,24,256]{3,2,1,0:T(8,128)(2,1)} %src.3, bf16[4,3,64,512]{3,2,1,0:T(8,128)(2,1)} %shard_map.77.token), custom_call_target="tpu_custom_call" | custom-call | bytes 12582912 | tf_op jit(solution)/shard_map/pallas_call | solution.py:86
  16.9 3.7 %all-to-all-done = bf16[4,3,64,512]{3,2,1,0:T(8,128)(2,1)S(1)} async-done(((bf16[4,3,64,512]{3,2,1,0:T(8,128)(2,1)}), bf16[4,3,64,512]{3,2,1,0:T(8,128)(2,1)S(1)}, u32[]{:S(2)}, u32[]{:S(2)}) %all-to-all-start) | async-done | bytes 786464 | tf_op jit(solution)/shard_map/all_to_all | solution.py:25
  20.6 2.0 %broadcast_in_dim.6 = bf16[4,4,3,64,512]{4,3,2,1,0:T(8,128)(2,1)} broadcast(bf16[4,3,64,512]{3,2,1,0:T(8,128)(2,1)S(1)} %all-to-all-done), dimensions={1,2,3,4} | broadcast | bytes 3932160 | tf_op jit(solution)/shard_map/broadcast_in_dim | solution.py:30
  22.6 4.6 %all-to-all-start.1 = ((bf16[4,4,3,64,512]{4,3,2,1,0:T(8,128)(2,1)}), bf16[4,4,3,64,512]{4,3,2,1,0:T(8,128)(2,1)}, u32[]{:S(2)}, u32[]{:S(2)}) async-start(bf16[4,4,3,64,512]{4,3,2,1,0:T(8,128)(2,1)} %broadcast_in_dim.6), calls=%async_computation.1 | async-start | bytes 6291456 | tf_op jit(solution)/shard_map/all_to_all | solution.py:31
  27.3 5.4 %shard_map.79.lower = bf16[8,512,768]{2,1,0:T(8,128)(2,1)} custom-call(bf16[4,256,24,256]{3,2,1,0:T(8,128)(2,1)} %src.3, bf16[8,512,768]{2,1,0:T(8,128)(2,1)} %shard_map.78.token.upper), custom_call_target="tpu_custom_call" | custom-call | bytes 12582912 | tf_op jit(solution)/shard_map/pallas_call | solution.py:86
  35.4 1.7 %collective-permute-start.6 = (bf16[3,128,512]{2,1,0:T(8,128)(2,1)S(1)}, bf16[3,128,512]{2,1,0:T(8,128)(2,1)S(1)}, u32[]{:S(2)}, u32[]{:S(2)}) collective-permute-start(bf16[3,128,512]{2,1,0:T(8,128)(2,1)S(1)} %slice.24), channel_id=1, source_target_pairs={{0,96},{16,112},{32,0},{48,16},{64,32},{80,48},{96,64},{112,80},{1... | collective-permute-start | bytes 1179656 | tf_op jit(solution)/shard_map/ppermute | solution.py:16
  37.2 12.4 %shard_map.80.before = f32[1024,512]{1,0:T(8,128)S(1)} custom-call(s32[6]{0:T(128)S(1)} %stack.88.order, bf16[8,512,768]{2,1,0:T(8,128)(2,1)} %shard_map.78.token.upper, bf16[8,512,768]{2,1,0:T(8,128)(2,1)} %shard_map.79.lower, bf16[3,256,512]{2,1,0:T(8,128)(2,1)} %refs_1_.1, bf16[3,256,512]{2,1,0:T(8,128)(2,1)} %refs_1_.1, bf16[3,256,512]{2,1,0:T(8,128)(2,1)} %copy-done.2, ...), custom_call_target="tpu_custom_call" | custom-call | flops 4831838208 | bytes 16252928 | tf_op jit(solution)/shard_map/pallas_call | solution.py:184
  52.1 6.1 %shard_map.81 = (bf16[16,128,128]{2,1,0:T(8,128)(2,1)}, bf16[16,128,128]{2,1,0:T(8,128)(2,1)}) custom-call(s32[2]{0:T(128)S(1)} %pad_add_fusion.1.order, bf16[8,512,768]{2,1,0:T(8,128)(2,1)} %shard_map.78.token.upper, bf16[8,512,768]{2,1,0:T(8,128)(2,1)} %shard_map.79.lower, f32[1024,512]{1,0:T(8,128)S(1)} %shard_map.80.before, f32[8,128]{1,0:T(8,128)S(1)} %slice.28.token, ...), custom_call_target="tpu_custom_call" | custom-call | flops 1610612736 | bytes 6815744 | tf_op jit(solution)/shard_map/pallas_call | solution.py:184
  58.2 5.8 %all-to-all-done.1 = bf16[4,4,3,64,512]{4,3,2,1,0:T(8,128)(2,1)} async-done(((bf16[4,4,3,64,512]{4,3,2,1,0:T(8,128)(2,1)}), bf16[4,4,3,64,512]{4,3,2,1,0:T(8,128)(2,1)}, u32[]{:S(2)}, u32[]{:S(2)}) %all-to-all-start.1) | async-done | bytes 3145760 | tf_op jit(solution)/shard_map/all_to_all | solution.py:31
  64.0 3.7 %all-to-all-start.2 = ((bf16[16,128,128]{2,1,0:T(8,128)(2,1)}), bf16[16,128,128]{2,1,0:T(8,128)(2,1)S(1)}, u32[]{:S(2)}, u32[]{:S(2)}) async-start(bf16[16,128,128]{2,1,0:T(8,128)(2,1)} %get-tuple-element.48), calls=%async_computation.2 | async-start | bytes 1048576 | tf_op jit(solution)/shard_map/all_to_all | solution.py:257
  68.6 9.6 %all-to-all-done.2 = bf16[16,128,128]{2,1,0:T(8,128)(2,1)S(1)} async-done(((bf16[16,128,128]{2,1,0:T(8,128)(2,1)}), bf16[16,128,128]{2,1,0:T(8,128)(2,1)S(1)}, u32[]{:S(2)}, u32[]{:S(2)}) %all-to-all-start.2) | async-done | bytes 524320 | tf_op jit(solution)/shard_map/all_to_all | solution.py:257
  80.6 2.3 %collective-permute-start.11 = (bf16[2,128,128]{2,1,0:T(8,128)(2,1)S(1)}, bf16[2,128,128]{2,1,0:T(8,128)(2,1)S(1)}, u32[]{:S(2)}, u32[]{:S(2)}) collective-permute-start(bf16[2,128,128]{2,1,0:T(8,128)(2,1)S(1)} %pad_maximum_fusion.1.own), channel_id=1, source_target_pairs={{0,96},{16,112},{32,0},{48,16},{64,32},{80,48},{96,64},{112,80},{1... | collective-permute-start | bytes 196616 | tf_op jit(solution)/shard_map/ppermute | solution.py:16
  84.2 3.6 %all-to-all-start.3 = ((bf16[16,128,128]{2,1,0:T(8,128)(2,1)}), bf16[16,128,128]{2,1,0:T(8,128)(2,1)S(1)}, u32[]{:S(2)}, u32[]{:S(2)}) async-start(bf16[16,128,128]{2,1,0:T(8,128)(2,1)} %get-tuple-element.50), calls=%async_computation.3 | async-start | bytes 1048576 | tf_op jit(solution)/shard_map/all_to_all | solution.py:257
  88.7 1.7 %shard_map.82 = (bf16[128,128]{1,0:T(8,128)(2,1)S(1)}, bf16[128,128]{1,0:T(8,128)(2,1)S(1)}, bf16[128,128]{1,0:T(8,128)(2,1)S(1)}, bf16[128,128]{1,0:T(8,128)(2,1)S(1)}) custom-call(s32[8]{0:T(128)S(1)} %stack.81.order, s32[4]{0:T(128)S(1)} %pad_add_fusion.targets, bf16[2,128,128]{2,1,0:T(8,128)(2,1)S(1)} %pad_maximum_fusion.1.own, ...), custom_call_target="tpu_custom_call" | custom-call | flops 134217728 | bytes 1048576 | tf_op jit(solution)/shard_map/pallas_call | solution.py:234
  90.4 2.2 %collective-permute-start.15 = (bf16[128,128]{1,0:T(8,128)(2,1)S(1)}, bf16[128,128]{1,0:T(8,128)(2,1)S(1)}, u32[]{:S(2)}, u32[]{:S(2)}) collective-permute-start(bf16[128,128]{1,0:T(8,128)(2,1)S(1)} %get-tuple-element.56), channel_id=1, source_target_pairs={{0,3},{1,0},{2,1},{3,2},{4,7},{5,4},{6,5},{7,6},{8,11},{9,8},{10,9... | collective-permute-start | bytes 98312 | tf_op jit(solution)/shard_map/ppermute | solution.py:36
  94.4 2.6 %collective-permute-done.15 = bf16[128,128]{1,0:T(8,128)(2,1)S(1)} collective-permute-done((bf16[128,128]{1,0:T(8,128)(2,1)S(1)}, bf16[128,128]{1,0:T(8,128)(2,1)S(1)}, u32[]{:S(2)}, u32[]{:S(2)}) %collective-permute-start.15) | collective-permute-done | bytes 32800 | tf_op jit(solution)/shard_map/ppermute | solution.py:36
  97.0 2.4 %collective-permute-done.14 = bf16[128,128]{1,0:T(8,128)(2,1)S(1)} collective-permute-done((bf16[128,128]{1,0:T(8,128)(2,1)S(1)}, bf16[128,128]{1,0:T(8,128)(2,1)S(1)}, u32[]{:S(2)}, u32[]{:S(2)}) %collective-permute-start.14) | collective-permute-done | bytes 32800 | tf_op jit(solution)/shard_map/ppermute | solution.py:36
  101.6 2.6 %collective-permute-start.18 = (bf16[2,128,128]{2,1,0:T(8,128)(2,1)S(1)}, bf16[2,128,128]{2,1,0:T(8,128)(2,1)S(1)}, u32[]{:S(2)}, u32[]{:S(2)}) collective-permute-start(bf16[2,128,128]{2,1,0:T(8,128)(2,1)S(1)} %pad_maximum_fusion.2.own), channel_id=1, source_target_pairs={{0,96},{16,112},{32,0},{48,16},{64,32},{80,48},{96,64},{112,80},{1... | collective-permute-start | bytes 196616 | tf_op jit(solution)/shard_map/ppermute | solution.py:16
  107.0 3.0 %collective-permute-done.19.three = bf16[2,128,128]{2,1,0:T(8,128)(2,1)S(1)} collective-permute-done((bf16[2,128,128]{2,1,0:T(8,128)(2,1)S(1)}, bf16[2,128,128]{2,1,0:T(8,128)(2,1)S(1)}, u32[]{:S(2)}, u32[]{:S(2)}) %collective-permute-start.19) | collective-permute-done | bytes 65568 | tf_op jit(solution)/shard_map/ppermute | solution.py:16
  110.0 1.7 %shard_map.83 = (bf16[128,128]{1,0:T(8,128)(2,1)S(1)}, bf16[128,128]{1,0:T(8,128)(2,1)S(1)}, bf16[128,128]{1,0:T(8,128)(2,1)S(1)}, bf16[128,128]{1,0:T(8,128)(2,1)S(1)}) custom-call(s32[8]{0:T(128)S(1)} %stack.81.order, s32[4]{0:T(128)S(1)} %pad_add_fusion.targets, bf16[2,128,128]{2,1,0:T(8,128)(2,1)S(1)} %pad_maximum_fusion.2.own, ...), custom_call_target="tpu_custom_call" | custom-call | flops 134217728 | bytes 1048576 | tf_op jit(solution)/shard_map/pallas_call | solution.py:234
  115.0 6.9 %all-to-all-start.4 = ((bf16[16,128,128]{2,1,0:T(8,128)(2,1)}), bf16[16,128,128]{2,1,0:T(8,128)(2,1)S(1)}, u32[]{:S(2)}, u32[]{:S(2)}) async-start(bf16[16,128,128]{2,1,0:T(8,128)(2,1)} %broadcast_in_dim.7), calls=%async_computation.4 | async-start | bytes 1048576 | tf_op jit(solution)/shard_map/all_to_all | solution.py:262
  123.5 3.2 %collective-permute-start.25 = (bf16[2,128,128]{2,1,0:T(8,128)(2,1)S(1)}, bf16[2,128,128]{2,1,0:T(8,128)(2,1)S(1)}, u32[]{:S(2)}, u32[]{:S(2)}) collective-permute-start(bf16[2,128,128]{2,1,0:T(8,128)(2,1)S(1)} %pad_maximum_fusion.3.own), channel_id=1, source_target_pairs={{0,96},{16,112},{32,0},{48,16},{64,32},{80,48},{96,64},{112,80},{1... | collective-permute-start | bytes 196616 | tf_op jit(solution)/shard_map/ppermute | solution.py:16
  126.7 2.2 %collective-permute-done.24.one = bf16[2,128,128]{2,1,0:T(8,128)(2,1)S(1)} collective-permute-done((bf16[2,128,128]{2,1,0:T(8,128)(2,1)S(1)}, bf16[2,128,128]{2,1,0:T(8,128)(2,1)S(1)}, u32[]{:S(2)}, u32[]{:S(2)}) %collective-permute-start.24) | collective-permute-done | bytes 65568 | tf_op jit(solution)/shard_map/ppermute | solution.py:16
  129.5 2.9 %collective-permute-done.26.three = bf16[2,128,128]{2,1,0:T(8,128)(2,1)S(1)} collective-permute-done((bf16[2,128,128]{2,1,0:T(8,128)(2,1)S(1)}, bf16[2,128,128]{2,1,0:T(8,128)(2,1)S(1)}, u32[]{:S(2)}, u32[]{:S(2)}) %collective-permute-start.26) | collective-permute-done | bytes 65568 | tf_op jit(solution)/shard_map/ppermute | solution.py:16
  134.8 3.2 %collective-permute-start.29 = (bf16[128,128]{1,0:T(8,128)(2,1)S(1)}, bf16[128,128]{1,0:T(8,128)(2,1)S(1)}, u32[]{:S(2)}, u32[]{:S(2)}) collective-permute-start(bf16[128,128]{1,0:T(8,128)(2,1)S(1)} %get-tuple-element.69), channel_id=1, source_target_pairs={{0,3},{1,0},{2,1},{3,2},{4,7},{5,4},{6,5},{7,6},{8,11},{9,8},{10,9... | collective-permute-start | bytes 98312 | tf_op jit(solution)/shard_map/ppermute | solution.py:36
  139.8 3.7 %collective-permute-done.28 = bf16[128,128]{1,0:T(8,128)(2,1)S(1)} collective-permute-done((bf16[128,128]{1,0:T(8,128)(2,1)S(1)}, bf16[128,128]{1,0:T(8,128)(2,1)S(1)}, u32[]{:S(2)}, u32[]{:S(2)}) %collective-permute-start.28) | collective-permute-done | bytes 32800 | tf_op jit(solution)/shard_map/ppermute | solution.py:36
  144.9 5.3 %all-to-all-start.5 = ((bf16[16,128,128]{2,1,0:T(8,128)(2,1)}), bf16[16,128,128]{2,1,0:T(8,128)(2,1)S(1)}, u32[]{:S(2)}, u32[]{:S(2)}) async-start(bf16[16,128,128]{2,1,0:T(8,128)(2,1)} %broadcast_in_dim.8), calls=%async_computation.5 | async-start | bytes 1048576 | tf_op jit(solution)/shard_map/all_to_all | solution.py:262
  150.6 9.7 %all-to-all-done.5 = bf16[16,128,128]{2,1,0:T(8,128)(2,1)S(1)} async-done(((bf16[16,128,128]{2,1,0:T(8,128)(2,1)}), bf16[16,128,128]{2,1,0:T(8,128)(2,1)S(1)}, u32[]{:S(2)}, u32[]{:S(2)}) %all-to-all-start.5) | async-done | bytes 524320 | tf_op jit(solution)/shard_map/all_to_all | solution.py:262
  165.7 2.4 %collective-permute-done.33 = bf16[32,512]{1,0:T(8,128)(2,1)S(1)} collective-permute-done((bf16[32,512]{1,0:T(8,128)(2,1)S(1)}, bf16[32,512]{1,0:T(8,128)(2,1)S(1)}, u32[]{:S(2)}, u32[]{:S(2)}) %collective-permute-start.33) | collective-permute-done | bytes 32800 | tf_op jit(solution)/shard_map/ppermute | solution.py:16
  (95 shorter events, 37.2 us)
Async XLA Ops:
  2.9 17.7 %all-to-all-start = ((bf16[4,3,64,512]{3,2,1,0:T(8,128)(2,1)}), bf16[4,3,64,512]{3,2,1,0:T(8,128)(2,1)S(1)}, u32[]{:S(2)}, u32[]{:S(2)}) async-start(bf16[4,3,64,512]{3,2,1,0:T(8,128)(2,1)} %shard_map.77.token), calls=%async_computation | async-start | bytes 1572864 | tf_op jit(solution)/shard_map/all_to_all | solution.py:25
  8.3 24.4 %collective-permute-start = (bf16[3,256,512]{2,1,0:T(8,128)(2,1)}, bf16[3,256,512]{2,1,0:T(8,128)(2,1)S(1)}, u32[]{:S(2)}, u32[]{:S(2)}) collective-permute-start(bf16[3,256,512]{2,1,0:T(8,128)(2,1)} %refs_1_.1), channel_id=1, source_target_pairs={{0,32},{16,48},{32,64},{48,80},{64,96},{80,112},{96,0},{112,16},{1... | collective-permute-start | bytes 2359304 | tf_op jit(solution)/shard_map/ppermute | solution.py:16
  9.8 22.9 %collective-permute-start.1 = (bf16[3,256,512]{2,1,0:T(8,128)(2,1)}, bf16[3,256,512]{2,1,0:T(8,128)(2,1)S(1)}, u32[]{:S(2)}, u32[]{:S(2)}) collective-permute-start(bf16[3,256,512]{2,1,0:T(8,128)(2,1)} %refs_1_.1), channel_id=1, source_target_pairs={{0,96},{16,112},{32,0},{48,16},{64,32},{80,48},{96,64},{112,80},{1... | collective-permute-start | bytes 2359304 | tf_op jit(solution)/shard_map/ppermute | solution.py:16
  11.5 21.2 %collective-permute-start.2 = (bf16[3,256,512]{2,1,0:T(8,128)(2,1)}, bf16[3,256,512]{2,1,0:T(8,128)(2,1)S(1)}, u32[]{:S(2)}, u32[]{:S(2)}) collective-permute-start(bf16[3,256,512]{2,1,0:T(8,128)(2,1)} %refs_1_.1), channel_id=1, source_target_pairs={{0,16},{16,0},{32,48},{48,32},{64,80},{80,64},{96,112},{112,96},{1... | collective-permute-start | bytes 2359304 | tf_op jit(solution)/shard_map/ppermute | solution.py:20
  22.6 41.4 %all-to-all-start.1 = ((bf16[4,4,3,64,512]{4,3,2,1,0:T(8,128)(2,1)}), bf16[4,4,3,64,512]{4,3,2,1,0:T(8,128)(2,1)}, u32[]{:S(2)}, u32[]{:S(2)}) async-start(bf16[4,4,3,64,512]{4,3,2,1,0:T(8,128)(2,1)} %broadcast_in_dim.6), calls=%async_computation.1 | async-start | bytes 6291456 | tf_op jit(solution)/shard_map/all_to_all | solution.py:31
  33.8 15.7 %collective-permute-start.5 = (bf16[3,128,512]{2,1,0:T(8,128)(2,1)S(1)}, bf16[3,128,512]{2,1,0:T(8,128)(2,1)S(1)}, u32[]{:S(2)}, u32[]{:S(2)}) collective-permute-start(bf16[3,128,512]{2,1,0:T(8,128)(2,1)S(1)} %slice.23), channel_id=1, source_target_pairs={{0,32},{16,48},{32,64},{48,80},{64,96},{80,112},{96,0},{112,16},{1... | collective-permute-start | bytes 1179656 | tf_op jit(solution)/shard_map/ppermute | solution.py:16
  35.4 14.2 %collective-permute-start.6 = (bf16[3,128,512]{2,1,0:T(8,128)(2,1)S(1)}, bf16[3,128,512]{2,1,0:T(8,128)(2,1)S(1)}, u32[]{:S(2)}, u32[]{:S(2)}) collective-permute-start(bf16[3,128,512]{2,1,0:T(8,128)(2,1)S(1)} %slice.24), channel_id=1, source_target_pairs={{0,96},{16,112},{32,0},{48,16},{64,32},{80,48},{96,64},{112,80},{1... | collective-permute-start | bytes 1179656 | tf_op jit(solution)/shard_map/ppermute | solution.py:16
  64.0 14.2 %all-to-all-start.2 = ((bf16[16,128,128]{2,1,0:T(8,128)(2,1)}), bf16[16,128,128]{2,1,0:T(8,128)(2,1)S(1)}, u32[]{:S(2)}, u32[]{:S(2)}) async-start(bf16[16,128,128]{2,1,0:T(8,128)(2,1)} %get-tuple-element.48), calls=%async_computation.2 | async-start | bytes 1048576 | tf_op jit(solution)/shard_map/all_to_all | solution.py:257
  79.6 8.2 %collective-permute-start.10 = (bf16[2,128,128]{2,1,0:T(8,128)(2,1)S(1)}, bf16[2,128,128]{2,1,0:T(8,128)(2,1)S(1)}, u32[]{:S(2)}, u32[]{:S(2)}) collective-permute-start(bf16[2,128,128]{2,1,0:T(8,128)(2,1)S(1)} %pad_maximum_fusion.1.own), channel_id=1, source_target_pairs={{0,32},{16,48},{32,64},{48,80},{64,96},{80,112},{96,0},{112,16},{1... | collective-permute-start | bytes 196616 | tf_op jit(solution)/shard_map/ppermute | solution.py:16
  80.6 7.2 %collective-permute-start.11 = (bf16[2,128,128]{2,1,0:T(8,128)(2,1)S(1)}, bf16[2,128,128]{2,1,0:T(8,128)(2,1)S(1)}, u32[]{:S(2)}, u32[]{:S(2)}) collective-permute-start(bf16[2,128,128]{2,1,0:T(8,128)(2,1)S(1)} %pad_maximum_fusion.1.own), channel_id=1, source_target_pairs={{0,96},{16,112},{32,0},{48,16},{64,32},{80,48},{96,64},{112,80},{1... | collective-permute-start | bytes 196616 | tf_op jit(solution)/shard_map/ppermute | solution.py:16
  82.9 5.8 %collective-permute-start.12 = (bf16[2,128,128]{2,1,0:T(8,128)(2,1)S(1)}, bf16[2,128,128]{2,1,0:T(8,128)(2,1)S(1)}, u32[]{:S(2)}, u32[]{:S(2)}) collective-permute-start(bf16[2,128,128]{2,1,0:T(8,128)(2,1)S(1)} %pad_maximum_fusion.1.own), channel_id=1, source_target_pairs={{0,64},{16,80},{32,96},{48,112},{64,0},{80,16},{96,32},{112,48},{1... | collective-permute-start | bytes 196616 | tf_op jit(solution)/shard_map/ppermute | solution.py:16
  84.2 29.9 %all-to-all-start.3 = ((bf16[16,128,128]{2,1,0:T(8,128)(2,1)}), bf16[16,128,128]{2,1,0:T(8,128)(2,1)S(1)}, u32[]{:S(2)}, u32[]{:S(2)}) async-start(bf16[16,128,128]{2,1,0:T(8,128)(2,1)} %get-tuple-element.50), calls=%async_computation.3 | async-start | bytes 1048576 | tf_op jit(solution)/shard_map/all_to_all | solution.py:257
  90.4 6.6 %collective-permute-start.15 = (bf16[128,128]{1,0:T(8,128)(2,1)S(1)}, bf16[128,128]{1,0:T(8,128)(2,1)S(1)}, u32[]{:S(2)}, u32[]{:S(2)}) collective-permute-start(bf16[128,128]{1,0:T(8,128)(2,1)S(1)} %get-tuple-element.56), channel_id=1, source_target_pairs={{0,3},{1,0},{2,1},{3,2},{4,7},{5,4},{6,5},{7,6},{8,11},{9,8},{10,9... | collective-permute-start | bytes 98312 | tf_op jit(solution)/shard_map/ppermute | solution.py:36
  92.7 6.7 %collective-permute-start.14 = (bf16[128,128]{1,0:T(8,128)(2,1)S(1)}, bf16[128,128]{1,0:T(8,128)(2,1)S(1)}, u32[]{:S(2)}, u32[]{:S(2)}) collective-permute-start(bf16[128,128]{1,0:T(8,128)(2,1)S(1)} %get-tuple-element.55), channel_id=1, source_target_pairs={{0,2},{1,3},{2,0},{3,1},{4,6},{5,7},{6,4},{7,5},{8,10},{9,11},{10,... | collective-permute-start | bytes 98312 | tf_op jit(solution)/shard_map/ppermute | solution.py:36
  93.5 5.9 %collective-permute-start.13 = (bf16[128,128]{1,0:T(8,128)(2,1)S(1)}, bf16[128,128]{1,0:T(8,128)(2,1)S(1)}, u32[]{:S(2)}, u32[]{:S(2)}) collective-permute-start(bf16[128,128]{1,0:T(8,128)(2,1)S(1)} %get-tuple-element.54), channel_id=1, source_target_pairs={{0,1},{1,2},{2,3},{3,0},{4,5},{5,6},{6,7},{7,4},{8,9},{9,10},{10,1... | collective-permute-start | bytes 98312 | tf_op jit(solution)/shard_map/ppermute | solution.py:36
  100.9 5.5 %collective-permute-start.17 = (bf16[2,128,128]{2,1,0:T(8,128)(2,1)S(1)}, bf16[2,128,128]{2,1,0:T(8,128)(2,1)S(1)}, u32[]{:S(2)}, u32[]{:S(2)}) collective-permute-start(bf16[2,128,128]{2,1,0:T(8,128)(2,1)S(1)} %pad_maximum_fusion.2.own), channel_id=1, source_target_pairs={{0,32},{16,48},{32,64},{48,80},{64,96},{80,112},{96,0},{112,16},{1... | collective-permute-start | bytes 196616 | tf_op jit(solution)/shard_map/ppermute | solution.py:16
  101.6 5.4 %collective-permute-start.18 = (bf16[2,128,128]{2,1,0:T(8,128)(2,1)S(1)}, bf16[2,128,128]{2,1,0:T(8,128)(2,1)S(1)}, u32[]{:S(2)}, u32[]{:S(2)}) collective-permute-start(bf16[2,128,128]{2,1,0:T(8,128)(2,1)S(1)} %pad_maximum_fusion.2.own), channel_id=1, source_target_pairs={{0,96},{16,112},{32,0},{48,16},{64,32},{80,48},{96,64},{112,80},{1... | collective-permute-start | bytes 196616 | tf_op jit(solution)/shard_map/ppermute | solution.py:16
  104.2 5.8 %collective-permute-start.19 = (bf16[2,128,128]{2,1,0:T(8,128)(2,1)S(1)}, bf16[2,128,128]{2,1,0:T(8,128)(2,1)S(1)}, u32[]{:S(2)}, u32[]{:S(2)}) collective-permute-start(bf16[2,128,128]{2,1,0:T(8,128)(2,1)S(1)} %pad_maximum_fusion.2.own), channel_id=1, source_target_pairs={{0,64},{16,80},{32,96},{48,112},{64,0},{80,16},{96,32},{112,48},{1... | collective-permute-start | bytes 196616 | tf_op jit(solution)/shard_map/ppermute | solution.py:16
  111.7 10.3 %collective-permute-start.22 = (bf16[128,128]{1,0:T(8,128)(2,1)S(1)}, bf16[128,128]{1,0:T(8,128)(2,1)S(1)}, u32[]{:S(2)}, u32[]{:S(2)}) collective-permute-start(bf16[128,128]{1,0:T(8,128)(2,1)S(1)} %get-tuple-element.60), channel_id=1, source_target_pairs={{0,3},{1,0},{2,1},{3,2},{4,7},{5,4},{6,5},{7,6},{8,11},{9,8},{10,9... | collective-permute-start | bytes 98312 | tf_op jit(solution)/shard_map/ppermute | solution.py:36
  113.0 9.0 %collective-permute-start.21 = (bf16[128,128]{1,0:T(8,128)(2,1)S(1)}, bf16[128,128]{1,0:T(8,128)(2,1)S(1)}, u32[]{:S(2)}, u32[]{:S(2)}) collective-permute-start(bf16[128,128]{1,0:T(8,128)(2,1)S(1)} %get-tuple-element.59), channel_id=1, source_target_pairs={{0,2},{1,3},{2,0},{3,1},{4,6},{5,7},{6,4},{7,5},{8,10},{9,11},{10,... | collective-permute-start | bytes 98312 | tf_op jit(solution)/shard_map/ppermute | solution.py:36
  114.1 7.9 %collective-permute-start.20 = (bf16[128,128]{1,0:T(8,128)(2,1)S(1)}, bf16[128,128]{1,0:T(8,128)(2,1)S(1)}, u32[]{:S(2)}, u32[]{:S(2)}) collective-permute-start(bf16[128,128]{1,0:T(8,128)(2,1)S(1)} %get-tuple-element.58), channel_id=1, source_target_pairs={{0,1},{1,2},{2,3},{3,0},{4,5},{5,6},{6,7},{7,4},{8,9},{9,10},{10,1... | collective-permute-start | bytes 98312 | tf_op jit(solution)/shard_map/ppermute | solution.py:36
  115.0 19.2 %all-to-all-start.4 = ((bf16[16,128,128]{2,1,0:T(8,128)(2,1)}), bf16[16,128,128]{2,1,0:T(8,128)(2,1)S(1)}, u32[]{:S(2)}, u32[]{:S(2)}) async-start(bf16[16,128,128]{2,1,0:T(8,128)(2,1)} %broadcast_in_dim.7), calls=%async_computation.4 | async-start | bytes 1048576 | tf_op jit(solution)/shard_map/all_to_all | solution.py:262
  123.4 5.5 %collective-permute-start.24 = (bf16[2,128,128]{2,1,0:T(8,128)(2,1)S(1)}, bf16[2,128,128]{2,1,0:T(8,128)(2,1)S(1)}, u32[]{:S(2)}, u32[]{:S(2)}) collective-permute-start(bf16[2,128,128]{2,1,0:T(8,128)(2,1)S(1)} %pad_maximum_fusion.3.own), channel_id=1, source_target_pairs={{0,32},{16,48},{32,64},{48,80},{64,96},{80,112},{96,0},{112,16},{1... | collective-permute-start | bytes 196616 | tf_op jit(solution)/shard_map/ppermute | solution.py:16
  123.5 6.1 %collective-permute-start.25 = (bf16[2,128,128]{2,1,0:T(8,128)(2,1)S(1)}, bf16[2,128,128]{2,1,0:T(8,128)(2,1)S(1)}, u32[]{:S(2)}, u32[]{:S(2)}) collective-permute-start(bf16[2,128,128]{2,1,0:T(8,128)(2,1)S(1)} %pad_maximum_fusion.3.own), channel_id=1, source_target_pairs={{0,96},{16,112},{32,0},{48,16},{64,32},{80,48},{96,64},{112,80},{1... | collective-permute-start | bytes 196616 | tf_op jit(solution)/shard_map/ppermute | solution.py:16
  126.7 5.8 %collective-permute-start.26 = (bf16[2,128,128]{2,1,0:T(8,128)(2,1)S(1)}, bf16[2,128,128]{2,1,0:T(8,128)(2,1)S(1)}, u32[]{:S(2)}, u32[]{:S(2)}) collective-permute-start(bf16[2,128,128]{2,1,0:T(8,128)(2,1)S(1)} %pad_maximum_fusion.3.own), channel_id=1, source_target_pairs={{0,64},{16,80},{32,96},{48,112},{64,0},{80,16},{96,32},{112,48},{1... | collective-permute-start | bytes 196616 | tf_op jit(solution)/shard_map/ppermute | solution.py:16
  134.8 4.9 %collective-permute-start.29 = (bf16[128,128]{1,0:T(8,128)(2,1)S(1)}, bf16[128,128]{1,0:T(8,128)(2,1)S(1)}, u32[]{:S(2)}, u32[]{:S(2)}) collective-permute-start(bf16[128,128]{1,0:T(8,128)(2,1)S(1)} %get-tuple-element.69), channel_id=1, source_target_pairs={{0,3},{1,0},{2,1},{3,2},{4,7},{5,4},{6,5},{7,6},{8,11},{9,8},{10,9... | collective-permute-start | bytes 98312 | tf_op jit(solution)/shard_map/ppermute | solution.py:36
  138.0 5.4 %collective-permute-start.28 = (bf16[128,128]{1,0:T(8,128)(2,1)S(1)}, bf16[128,128]{1,0:T(8,128)(2,1)S(1)}, u32[]{:S(2)}, u32[]{:S(2)}) collective-permute-start(bf16[128,128]{1,0:T(8,128)(2,1)S(1)} %get-tuple-element.68), channel_id=1, source_target_pairs={{0,2},{1,3},{2,0},{3,1},{4,6},{5,7},{6,4},{7,5},{8,10},{9,11},{10,... | collective-permute-start | bytes 98312 | tf_op jit(solution)/shard_map/ppermute | solution.py:36
  138.9 5.1 %collective-permute-start.27 = (bf16[128,128]{1,0:T(8,128)(2,1)S(1)}, bf16[128,128]{1,0:T(8,128)(2,1)S(1)}, u32[]{:S(2)}, u32[]{:S(2)}) collective-permute-start(bf16[128,128]{1,0:T(8,128)(2,1)S(1)} %get-tuple-element.67), channel_id=1, source_target_pairs={{0,1},{1,2},{2,3},{3,0},{4,5},{5,6},{6,7},{7,4},{8,9},{9,10},{10,1... | collective-permute-start | bytes 98312 | tf_op jit(solution)/shard_map/ppermute | solution.py:36
  144.9 15.4 %all-to-all-start.5 = ((bf16[16,128,128]{2,1,0:T(8,128)(2,1)}), bf16[16,128,128]{2,1,0:T(8,128)(2,1)S(1)}, u32[]{:S(2)}, u32[]{:S(2)}) async-start(bf16[16,128,128]{2,1,0:T(8,128)(2,1)} %broadcast_in_dim.8), calls=%async_computation.5 | async-start | bytes 1048576 | tf_op jit(solution)/shard_map/all_to_all | solution.py:262
  162.5 5.6 %collective-permute-start.33 = (bf16[32,512]{1,0:T(8,128)(2,1)S(1)}, bf16[32,512]{1,0:T(8,128)(2,1)S(1)}, u32[]{:S(2)}, u32[]{:S(2)}) collective-permute-start(bf16[32,512]{1,0:T(8,128)(2,1)S(1)} %get-tuple-element.72), channel_id=1, source_target_pairs={{0,64},{16,80},{32,96},{48,112},{64,0},{80,16},{96,32},{112,48},{1... | collective-permute-start | bytes 98312 | tf_op jit(solution)/shard_map/ppermute | solution.py:16
  162.6 5.5 %collective-permute-start.32 = (bf16[32,512]{1,0:T(8,128)(2,1)S(1)}, bf16[32,512]{1,0:T(8,128)(2,1)S(1)}, u32[]{:S(2)}, u32[]{:S(2)}) collective-permute-start(bf16[32,512]{1,0:T(8,128)(2,1)S(1)} %get-tuple-element.72), channel_id=1, source_target_pairs={{0,96},{16,112},{32,0},{48,16},{64,32},{80,48},{96,64},{112,80},{1... | collective-permute-start | bytes 98312 | tf_op jit(solution)/shard_map/ppermute | solution.py:16
  164.1 5.1 %collective-permute-start.31 = (bf16[32,512]{1,0:T(8,128)(2,1)S(1)}, bf16[32,512]{1,0:T(8,128)(2,1)S(1)}, u32[]{:S(2)}, u32[]{:S(2)}) collective-permute-start(bf16[32,512]{1,0:T(8,128)(2,1)S(1)} %get-tuple-element.72), channel_id=1, source_target_pairs={{0,32},{16,48},{32,64},{48,80},{64,96},{80,112},{96,0},{112,16},{1... | collective-permute-start | bytes 98312 | tf_op jit(solution)/shard_map/ppermute | solution.py:16
  (12 other events, 73.9 us)
